TPU v7x, 32 devices: a whole 2x2x4 slice. The times are simulated.
32 devices in a mesh: wide: 8 (over y, x, core), eight: 4 (over z).
Axes of the slice: x: 2, y: 2, z: 4, core: 2. Of those that a mesh axis runs over, the one named last changes fastest.
Arguments:
- multipliers: float32 [64, 1024, 256], P(('wide', 'eight')), may hold values from -6 to 6
- gap: float32 [64, 1024, 256], P(('wide', 'eight'))
- flexibility: bfloat16 [64, 1024, 1024], P(('wide', 'eight'))
- dirichlet: bfloat16 [64, 1024, 1024], P(('wide', 'eight'))
- side: int32 [64, 8], P(('wide', 'eight')), may hold values from 0 to 3
- powers: int32 [64], P(('wide', 'eight')), may hold values from 1 to 3, as said below
- active: int32 [3, 64, 1024], P(None, ('wide', 'eight')), may hold values 0 or 1
Outputs:
- solution: float32 [64, 1024, 256], P(('wide', 'eight'))
- steps: float32 [3, 256], replicated
- centres: float32 [3, 1024, 256], replicated
Inputs may be any that keep to these rules, and one draw needn't show every extreme that they name: `powers`: some subdomain has 3 applications in every draw.
All inputs are finite; a program needn't handle non-finite values. No bound on the sum of `active` on one device may be relied on, other than what follows from the above.
Results may differ from a plain program's by a relative error of at most 0.0075.
Values may be sent and summed in bfloat16 or wider, within the bound.
No kernel may reach another device: no remote copies, remote signals or barrier semaphores. Data moves between devices by JAX's collectives and lax.ppermute only.
A program may use at most 128 MiB of HBM per device.

v0:
```python
import functools

import jax
import jax.numpy as jnp
from jax import lax
from jax.experimental import pallas as pl
from jax.experimental.pallas import tpu as pltpu
from jax.sharding import PartitionSpec as P


ITERS = 3
EXTRA = 16
F32 = jnp.float32
BF16 = jnp.bfloat16
VMEM = pl.BlockSpec(memory_space=pltpu.VMEM)
ANY = pl.BlockSpec(memory_space=pl.ANY)
SMEM = pl.BlockSpec(memory_space=pltpu.SMEM)


def call(kernel, outs, n_smem, ins, flops, nbytes, scratch=(), vmem=16, anys=(), any_outs=(), aliases=None):
    return pl.pallas_call(
        kernel,
        out_shape=outs,
        in_specs=[
            SMEM if i < n_smem else ANY if i in anys else VMEM for i in range(len(ins))
        ],
        out_specs=[ANY if i in any_outs else VMEM for i in range(len(outs))],
        scratch_shapes=list(scratch),
        input_output_aliases=aliases or {},
        compiler_params=pltpu.CompilerParams(vmem_limit_bytes=vmem << 20),
        cost_estimate=pl.CostEstimate(flops=flops, bytes_accessed=nbytes, transcendentals=0),
    )(*ins)


def sds(shape, dtype):
    return jax.ShapeDtypeStruct(shape, dtype)


def stage_bits(size):
    total = size.bit_length() - 1
    groups = [1]
    left = total - 1
    while left > 0:
        take = 2 if left >= 2 else 1
        groups.append(take)
        left -= take
    return groups


def pack_products(inner, square, most):
    shape = (EXTRA, inner.shape[1])
    row = lax.broadcasted_iota(jnp.int32, shape, 0)
    ih = inner.astype(BF16).astype(F32)
    sh = square.astype(BF16).astype(F32)
    tile = jnp.zeros(shape, F32)
    for i, value in enumerate((ih, inner - ih, sh, square - sh, most)):
        tile = jnp.where(row == i, jnp.broadcast_to(value, shape), tile)
    return tile.astype(BF16)


def unpack_products(tiles):
    vals = []
    for tile in tiles:
        t = tile.astype(F32)
        vals.append((t[0:1] + t[1:2], t[2:3] + t[3:4], t[4:5]))
    return (
        tree([v[0] for v in vals]),
        tree([v[1] for v in vals]),
        functools.reduce(jnp.maximum, [v[2] for v in vals]),
    )


def tree(items):
    items = list(items)
    while len(items) > 1:
        items = [items[i] + items[i + 1] for i in range(0, len(items), 2)]
    return items[0]


def send_partial(chunk, wide, w, part, tile, keep_ref, send_ref):
    for k in range(wide):
        total = part(pl.ds(pl.multiple_of(jnp.bitwise_xor(w, k) * chunk, chunk), chunk))
        out = send_ref if k % 2 else keep_ref
        out[pl.ds((k // 2) * chunk, chunk), :] = total.astype(BF16)
    if tile is not None:
        tail = pl.ds((wide // 2) * chunk, EXTRA)
        keep_ref[tail, :] = tile
        send_ref[tail, :] = tile


def send_halo(info, disp_ref, za_ref, zb_ref, theirs=None, base_ref=None):
    subs, rows_all, _ = disp_ref.shape
    zodd = jnp.bitwise_and(info[1], 1)
    za_ref[...] = disp_ref[(1 - zodd) * (subs - 1)]
    zb_ref[...] = disp_ref[zodd * (subs - 1)]
    if theirs is None:
        return
    blocks = theirs.shape[1]
    height = rows_all // blocks
    cap = base_ref.shape[0]
    odd = jnp.bitwise_and(info[0], 1)
    count = jnp.int32(0)
    for s in range(subs):

        def block(b, n, s=s):
            need = theirs[s, b] == odd
            rows = pl.ds(pl.multiple_of(b * height, height), height)

            @pl.when(need & (n < cap))
            def _():
                base_ref[n] = disp_ref[s, rows, :]

            return n + need.astype(jnp.int32)

        count = lax.fori_loop(0, blocks, block, count)


def first_kernel(chunk, wide, info, lam_ref, half_ref, keep_ref, send_ref):
    subs = lam_ref.shape[0]
    half_ref[...] = lam_ref[...].astype(BF16)
    send_partial(
        chunk, wide, info[0], lambda rows: tree([lam_ref[s, rows, :] for s in range(subs)]),
        None, keep_ref, send_ref,
    )


def flex_kernel(packed, info, *refs):
    theirs = base_ref = None
    if packed:
        theirs, half_ref, flex_ref, disp_ref, za_ref, zb_ref, base_ref = refs
    else:
        half_ref, flex_ref, disp_ref, za_ref, zb_ref = refs
    for s in range(half_ref.shape[0]):
        disp_ref[s] = jnp.dot(
            flex_ref[s], half_ref[s], preferred_element_type=F32
        ).astype(BF16)
    send_halo(info, disp_ref, za_ref, zb_ref, theirs, base_ref)


def update_kernel(chunk, wide, step, last, info, lam_ref, dir_ref, alpha_ref, floor_ref, *refs):
    centre_refs = refs[:wide]
    refs = refs[wide:]
    if step:
        refs = refs[1:]
    if last:
        lam_out, stack_ref, mean, sem = refs
    else:
        lam_out, stack_ref, half_ref, keep_ref, send_ref, mean, sem = refs
    w = info[0]
    subs, _, cols = lam_ref.shape
    alpha = jnp.broadcast_to(alpha_ref[0:1, :], (chunk, cols))
    for k in range(wide):
        rows = pl.ds(pl.multiple_of(jnp.bitwise_xor(w, k) * chunk, chunk), chunk)
        centre = centre_refs[k][...].astype(F32)
        mean[rows, :] = centre
        total = None
        for s in range(subs):
            trial = lam_ref[s, rows, :] + alpha * dir_ref[s, rows, :].astype(F32)
            low = floor_ref[s, rows, :]
            low = jnp.concatenate([low] * (cols // low.shape[1]), axis=1)
            new = jnp.maximum(trial - centre, low)
            lam_out[s, rows, :] = new
            if not last:
                half_ref[s, rows, :] = new.astype(BF16)
                total = new if total is None else total + new
        if not last:
            out = send_ref if k % 2 else keep_ref
            out[pl.ds((k // 2) * chunk, chunk), :] = total.astype(BF16)
    copy = pltpu.make_async_copy(mean, stack_ref.at[step], sem)
    copy.start()
    copy.wait()


def direct_kernel(chunk, wide, packed, info, side, powers, gap_ref, disp_ref, chip_ref, off_ref, za_ref, zb_ref, diri_ref, after_ref, dir_ref, keep_ref, send_ref, jump, work):
    w = info[0]
    odd = jnp.bitwise_and(w, 1)
    zodd = jnp.bitwise_and(info[1], 1)
    subs, rows_all, cols = gap_ref.shape
    blocks = side.shape[1]
    height = rows_all // blocks
    inner = jnp.zeros((8, cols), F32)
    square = jnp.zeros((8, cols), F32)
    count = jnp.int32(0)
    for s in range(subs):

        def block(b, n, s=s):
            face = side[s, b]
            rows = pl.ds(pl.multiple_of(b * height, height), height)

            def put(source):
                value = gap_ref[s, rows, :] - (
                    disp_ref[s, rows, :].astype(F32) - source.astype(F32)
                )
                jump[rows, :] = value
                work[s, rows, :] = value.astype(BF16)

            pl.when(face == odd)(lambda: put(chip_ref[s, rows, :]))
            away = face == 1 - odd
            if packed:
                slot = jnp.minimum(n, off_ref.shape[0] - 1)
                pl.when(away)(lambda: put(off_ref[slot]))
            else:
                pl.when(away)(lambda: put(off_ref[s, rows, :]))
            if s + 1 < subs:
                pl.when(face == 2)(lambda: put(disp_ref[s + 1, rows, :]))
            else:
                pl.when((face == 2) & (zodd == 0))(lambda: put(za_ref[rows, :]))
                pl.when((face == 2) & (zodd == 1))(lambda: put(zb_ref[rows, :]))
            if s > 0:
                pl.when(face == 3)(lambda: put(disp_ref[s - 1, rows, :]))
            else:
                pl.when((face == 3) & (zodd == 1))(lambda: put(za_ref[rows, :]))
                pl.when((face == 3) & (zodd == 0))(lambda: put(zb_ref[rows, :]))
            return n + away.astype(jnp.int32)

        count = lax.fori_loop(0, blocks, block, count)

        def level(i, carry, s=s):
            work[s] = jnp.dot(
                diri_ref[s], work[s], preferred_element_type=F32
            ).astype(BF16)
            return carry

        lax.fori_loop(0, powers[s], level, 0)
        direct = work[s]
        dir_ref[s] = direct
        dfloat = direct.astype(F32)
        inner = inner + jnp.sum((jump[...] * dfloat).reshape(rows_all // 8, 8, cols), axis=0)
        square = square + jnp.sum((dfloat * dfloat).reshape(rows_all // 8, 8, cols), axis=0)
    tile = pack_products(
        jnp.sum(inner, axis=0, keepdims=True),
        jnp.sum(square, axis=0, keepdims=True),
        jnp.broadcast_to(count.astype(F32), (1, cols)),
    )
    send_partial(
        chunk, wide, w, lambda rows: tree([work[s, rows, :].astype(F32) for s in range(subs)]),
        tile, keep_ref, send_ref,
    )


def add_kernel(chunk, chunks, ways_in, ways_out, extra, *refs):
    ins, outs = refs[:ways_in], refs[ways_in:]
    for c in range(chunks):
        rows = pl.ds(c * chunk, chunk)
        total = tree([r[rows, :].astype(F32) for r in ins]).astype(BF16)
        outs[c % ways_out][pl.ds((c // ways_out) * chunk, chunk), :] = total
    if extra:
        tail = pl.ds(chunks * chunk, EXTRA)
        tiles = [r[tail, :] for r in ins]
        tile = pack_products(*unpack_products(tiles))
        for o in outs:
            o[pl.ds((chunks // ways_out) * chunk, EXTRA), :] = tile


def centre_kernel(chunk, ways, count, *refs):
    dirs, lams = refs[:ways], refs[ways : 2 * ways]
    centre_ref, alpha_ref = refs[2 * ways :]
    rows = pl.ds(0, chunk)
    tail = pl.ds(chunk, EXTRA)
    inner, square, most = unpack_products([r[tail, :] for r in dirs])
    alpha = inner / (square + 1e-06)
    row = lax.broadcasted_iota(jnp.int32, alpha_ref.shape, 0)
    alpha_ref[...] = jnp.where(
        row == 0, jnp.broadcast_to(alpha, row.shape), jnp.broadcast_to(most, row.shape)
    )
    dsum = tree([r[rows, :].astype(F32) for r in dirs])
    lsum = tree([r[rows, :].astype(F32) for r in lams])
    centre_ref[...] = ((lsum + alpha * dsum) / count).astype(BF16)


def swap(x, axis, mask):
    n = lax.axis_size(axis)
    return lax.ppermute(x, axis, [(i, i ^ mask) for i in range(n)])


def stage(parts, g, chunk, wide, extra):
    groups = stage_bits(wide)
    shift = sum(groups[:g])
    ways = 1 << groups[g]
    chunks = wide >> (shift + groups[g])
    cols = parts[0].shape[1]
    got = [parts[0]] + [swap(parts[q], "wide", q << shift) for q in range(1, ways)]
    nxt = 1 << groups[g + 1] if g + 1 < len(groups) else 1
    shape = sds(((chunks // nxt) * chunk + (EXTRA if extra else 0), cols), BF16)
    return call(
        functools.partial(add_kernel, chunk, chunks, ways, nxt, extra),
        [shape] * nxt, 0, got, chunks * chunk * cols * ways,
        chunks * chunk * cols * 2 * (ways + 1), vmem=8,
    )


def scatter(parts, first, chunk, wide, extra):
    for g in range(first, len(stage_bits(wide))):
        parts = stage(parts, g, chunk, wide, extra)
    return parts[0]


def across(x):
    size = lax.axis_size("eight")
    return [x] + [swap(x, "eight", q) for q in range(1, size)]


def gather(centre, wide):
    groups = stage_bits(wide)
    have = {0: centre}
    shift = wide.bit_length() - 1
    for bits in reversed(groups):
        shift -= bits
        new = dict(have)
        for q in range(1, 1 << bits):
            for k, v in have.items():
                new[k ^ (q << shift)] = swap(v, "wide", q << shift)
        have = new
    return [have[k] for k in range(wide)]


def body(multipliers, gap, flexibility, dirichlet, side, powers, active):
    subs, rows, cols = multipliers.shape
    blocks = side.shape[1]
    wide = lax.axis_size("wide")
    eight = lax.axis_size("eight")
    count = wide * eight * subs
    chunk = rows // wide
    cap = -(-subs * blocks * 9 // 16)
    away = [(i, (i + 1) % wide if i % 2 else (i - 1) % wide) for i in range(wide)]
    pairs_a = [(i, i ^ 1) for i in range(eight) if i ^ 1 < eight]
    pairs_b = [(i, i + 1 if i % 2 else i - 1) for i in range(1, eight - 1 + eight % 2)]
    info = jnp.stack([lax.axis_index("wide"), lax.axis_index("eight")]).astype(jnp.int32)
    theirs = lax.ppermute(side, "wide", away)
    lanes = 128
    floor = jnp.where(
        jnp.broadcast_to(active[..., None], active.shape + (lanes,)) == 1, 0.0, -jnp.inf
    ).astype(F32)

    full = sds((subs, rows, cols), F32)
    half = sds((subs, rows, cols), BF16)
    one = sds((rows, cols), BF16)
    base = sds((cap, rows // blocks, cols), BF16)
    part = sds(((wide // 2) * chunk, cols), BF16)
    message = sds(((wide // 2) * chunk + EXTRA, cols), BF16)
    stack = sds((ITERS, rows, cols), F32)
    mm = 2 * subs * rows * rows * cols
    op_bytes = 2 * subs * rows * rows
    arr = subs * rows * cols

    def search(half_lam, lkeep, lsend, packed):
        ins = [info] + ([theirs] if packed else []) + [half_lam, flexibility]
        sends = call(
            functools.partial(flex_kernel, packed), [half, one, one] + ([base] if packed else []),
            len(ins) - 2, ins, mm, op_bytes + arr * 6,
        )
        lams = stage([lkeep, lsend], 0, chunk, wide, False)
        lams, sends = lax.optimization_barrier((lams, sends))
        own = scatter(lams, 1, chunk, wide, False)
        disp, za, zb = sends[:3]
        off = lax.ppermute(sends[-1] if packed else disp, "wide", away)
        za = lax.ppermute(za, "eight", pairs_a)
        zb = lax.ppermute(zb, "eight", pairs_b)
        chip = swap(disp, "wide", 1)
        lam_parts = across(own)
        direct, dkeep, dsend = call(
            functools.partial(direct_kernel, chunk, wide, packed), [half, message, message], 3,
            [info, side, powers, gap, disp, chip, off, za, zb, dirichlet, own],
            2 * mm, op_bytes + arr * 16,
            scratch=[pltpu.VMEM((rows, cols), F32), pltpu.VMEM((subs, rows, cols), BF16)],
        )
        dirs = stage([dkeep, dsend], 0, chunk, wide, True)
        dir_parts = across(scatter(dirs, 1, chunk, wide, True))
        centre, alpha = call(
            functools.partial(centre_kernel, chunk, eight, float(count)),
            [sds((chunk, cols), BF16), sds((8, cols), F32)], 0, dir_parts + lam_parts,
            chunk * cols * 10, chunk * cols * 20, vmem=8,
        )
        return direct, alpha, gather(centre, wide)

    def update(step, lam, direct, alpha, pieces, centres):
        last = step == ITERS - 1
        ins = [info, lam, direct, alpha, floor[step], *pieces]
        aliases, anys = {}, ()
        if step:
            aliases, anys = {len(ins): 1}, (len(ins),)
            ins.append(centres)
        return call(
            functools.partial(update_kernel, chunk, wide, step, last),
            [full, stack] + ([] if last else [half, part, part]), 1, ins, arr * 6, arr * 16,
            scratch=[pltpu.VMEM((rows, cols), F32), pltpu.SemaphoreType.DMA],
            anys=anys, any_outs=(1,), aliases=aliases,
        )

    first = call(
        functools.partial(first_kernel, chunk, wide), [half, part, part], 1, [info, multipliers],
        arr * 2, arr * 8,
    )
    direct, alpha, pieces = search(*first, False)

    def rest(packed, direct, alpha, pieces):
        alphas = [alpha[0]]
        lam, centres = multipliers, None
        for step in range(ITERS - 1):
            lam, centres, *sums = update(step, lam, direct, alpha, pieces, centres)
            direct, alpha, pieces = search(*sums, packed)
            alphas.append(alpha[0])
        lam, centres = update(ITERS - 1, lam, direct, alpha, pieces, centres)
        return lam, jnp.stack(alphas), centres

    return lax.cond(
        alpha[1, 0] <= cap,
        functools.partial(rest, True),
        functools.partial(rest, False),
        direct, alpha, pieces,
    )


def solution(mesh):
    return jax.shard_map(
        body,
        mesh=mesh,
        in_specs=(
            P(("wide", "eight"), None, None),
            P(("wide", "eight"), None, None),
            P(("wide", "eight"), None, None),
            P(("wide", "eight"), None, None),
            P(("wide", "eight"), None),
            P(("wide", "eight")),
            P(None, ("wide", "eight"), None),
        ),
        out_specs=(P(("wide", "eight"), None, None), P(), P()),
        check_vma=False,
    )
```

profile of v0, /device:TPU:0, one launch (start us, length us, event | category | flops | bytes accessed | tf_op | source)
XLA Modules:
  0.0 222.6 jit_solution(10818284813884351156)
XLA Ops:
  0.7 1.9 shard_map.96
  3.3 3.9 %shard_map.98 = (bf16[2,1024,256]{2,1,0:T(8,128)(2,1)S(1)}, bf16[1024,256]{1,0:T(8,128)(2,1)S(1)}, bf16[1024,256]{1,0:T(8,128)(2,1)S(1)}) custom-call(s32[2]{0:T(128)S(1)} %pad_add_fusion.info, bf16[2,1024,256]{2,1,0:T(8,128)(2,1)S(1)} %get-tuple-element.266.refs_0_, bf16[2,1024,1024]{2,1,0:T(8,128)(2,1)} %refs_1_.1), custom_call_target="tpu_custom_call" | custom-call | flops 1073741824 | bytes 7340032 | tf_op jit(solution)/shard_map/pallas_call | solution.py:21
  7.3 3.7 %collective-permute-start.102 = (bf16[2,1024,256]{2,1,0:T(8,128)(2,1)S(1)}, bf16[2,1024,256]{2,1,0:T(8,128)(2,1)S(1)}, u32[]{:S(2)}, u32[]{:S(2)}) collective-permute-start(bf16[2,1024,256]{2,1,0:T(8,128)(2,1)S(1)} %get-tuple-element.270.disp_ref), channel_id=1, source_target_pairs={{0,28},{4,8},{8,4},{12,16},{16,12},{20,24},{24,20},{28,0},{1,29},{... | collective-permute-start | bytes 3145736 | tf_op jit(solution)/shard_map/ppermute | solution.py:356
  11.0 1.6 collective-permute-start.103
  13.3 21.5 %collective-permute-done.105.refs_1_ = bf16[128,256]{1,0:T(8,128)(2,1)S(1)} collective-permute-done((bf16[128,256]{1,0:T(8,128)(2,1)S(1)}, bf16[128,256]{1,0:T(8,128)(2,1)S(1)}, u32[]{:S(2)}, u32[]{:S(2)}) %collective-permute-start.105) | collective-permute-done | bytes 65568 | tf_op jit(solution)/shard_map/ppermute | solution.py:273
  34.9 1.8 collective-permute-start.106
  36.7 2.9 %collective-permute-done.106.refs_2_ = bf16[128,256]{1,0:T(8,128)(2,1)S(1)} collective-permute-done((bf16[128,256]{1,0:T(8,128)(2,1)S(1)}, bf16[128,256]{1,0:T(8,128)(2,1)S(1)}, u32[]{:S(2)}, u32[]{:S(2)}) %collective-permute-start.106) | collective-permute-done | bytes 65568 | tf_op jit(solution)/shard_map/ppermute | solution.py:273
  39.6 2.9 %collective-permute-start.107 = (bf16[128,256]{1,0:T(8,128)(2,1)S(1)}, bf16[128,256]{1,0:T(8,128)(2,1)S(1)}, u32[]{:S(2)}, u32[]{:S(2)}) collective-permute-start(bf16[128,256]{1,0:T(8,128)(2,1)S(1)} %get-tuple-element.276), channel_id=1, source_target_pairs={{0,24},{4,28},{8,16},{12,20},{16,8},{20,12},{24,0},{28,4},{1,25},{... | collective-permute-start | bytes 196616 | tf_op jit(solution)/shard_map/ppermute | solution.py:273
  42.4 2.3 %collective-permute-done.107.refs_3_ = bf16[128,256]{1,0:T(8,128)(2,1)S(1)} collective-permute-done((bf16[128,256]{1,0:T(8,128)(2,1)S(1)}, bf16[128,256]{1,0:T(8,128)(2,1)S(1)}, u32[]{:S(2)}, u32[]{:S(2)}) %collective-permute-start.107) | collective-permute-done | bytes 65568 | tf_op jit(solution)/shard_map/ppermute | solution.py:273
  44.9 4.0 %shard_map.100 = (bf16[2,1024,256]{2,1,0:T(8,128)(2,1)S(1)}, bf16[528,256]{1,0:T(8,128)(2,1)S(1)}, bf16[528,256]{1,0:T(8,128)(2,1)S(1)}) custom-call(s32[2]{0:T(128)S(1)} %pad_add_fusion.info, s32[2,8]{1,0:T(2,128)S(1)} %copy-done.4, s32[2]{0:T(128)S(1)} %copy-done.6, f32[2,1024,256]{2,1,0:T(8,128)S(1)} %copy-done.2, ...), custom_call_target="tpu_custom_call" | custom-call | flops 2147483648 | bytes 12582912 | tf_op jit(solution)/shard_map/pallas_call | solution.py:21
  52.6 1.5 collective-permute-start.110
  56.9 2.4 %collective-permute-done.111.refs_3_ = bf16[144,256]{1,0:T(8,128)(2,1)S(1)} collective-permute-done((bf16[144,256]{1,0:T(8,128)(2,1)S(1)}, bf16[144,256]{1,0:T(8,128)(2,1)S(1)}, u32[]{:S(2)}, u32[]{:S(2)}) %collective-permute-start.111) | collective-permute-done | bytes 73760 | tf_op jit(solution)/shard_map/ppermute | solution.py:273
  60.3 3.0 %collective-permute-start.113 = (bf16[144,256]{1,0:T(8,128)(2,1)S(1)}, bf16[144,256]{1,0:T(8,128)(2,1)S(1)}, u32[]{:S(2)}, u32[]{:S(2)}) collective-permute-start(bf16[144,256]{1,0:T(8,128)(2,1)S(1)} %shard_map.102.refs_0_), channel_id=1, source_target_pairs={{0,2},{1,3},{2,0},{3,1},{4,6},{5,7},{6,4},{7,5},{8,10},{9,11},{10,... | collective-permute-start | bytes 221192 | tf_op jit(solution)/shard_map/ppermute | solution.py:273
  63.9 1.7 collective-permute-start.116
  65.6 1.6 collective-permute-start.117
  67.1 6.6 %collective-permute-done.116.refs_6_ = bf16[128,256]{1,0:T(8,128)(2,1)S(1)} collective-permute-done((bf16[128,256]{1,0:T(8,128)(2,1)S(1)}, bf16[128,256]{1,0:T(8,128)(2,1)S(1)}, u32[]{:S(2)}, u32[]{:S(2)}) %collective-permute-start.116) | collective-permute-done | bytes 65568 | tf_op jit(solution)/shard_map/ppermute | solution.py:273
  79.3 2.2 %collective-permute-done.123 = bf16[128,256]{1,0:T(8,128)(2,1)S(1)} collective-permute-done((bf16[128,256]{1,0:T(8,128)(2,1)S(1)}, bf16[128,256]{1,0:T(8,128)(2,1)S(1)}, u32[]{:S(2)}, u32[]{:S(2)}) %collective-permute-start.123) | collective-permute-done | bytes 65568 | tf_op jit(solution)/shard_map/ppermute | solution.py:273
  83.7 137.6 %conditional.1 = (f32[2,1024,256]{2,1,0:T(8,128)S(1)}, f32[3,1024,256]{2,1,0:T(8,128)}, f32[3,256]{1,0:T(4,128)S(1)}) conditional(s32[]{:T(128)} %bitcast.8, (f32[3,2,1024,128]{3,2,1,0:T(8,128)S(1)}, s32[2]{0:T(128)S(1)}, f32[2,1024,256]{2,1,0:T(8,128)S(1)}, bf16[2,1024,256]{2,1,0:T(8,128)(2,1)S(1)}, f32[8,256]{1,0:T(8,128)S(1)}, ...), branch_computations={%region_0.1_spmd, %region_1.2_spmd} | conditional | flops 6454117888 | bytes 116865000 | solution.py:406
  84.1 2.0 branch_1_fun.17
  86.7 2.3 %branch_1_fun.19 = (bf16[2,1024,256]{2,1,0:T(8,128)(2,1)S(1)}, bf16[1024,256]{1,0:T(8,128)(2,1)S(1)}, bf16[1024,256]{1,0:T(8,128)(2,1)S(1)}, bf16[9,128,256]{2,1,0:T(8,128)(2,1)S(1)}) custom-call(s32[2]{0:T(128)S(1)} %get-tuple-element.150.info, s32[2,8]{1,0:T(2,128)S(1)} %get-tuple-element.173.refs_0_, ...), custom_call_target="tpu_custom_call" | custom-call | flops 1073741824 | bytes 7340032 | tf_op jit(solution)/shard_map/cond/branch_1_fun/pallas_call | solution.py:21
  93.3 13.1 %collective-permute-done.55.refs_1_ = bf16[128,256]{1,0:T(8,128)(2,1)S(1)} collective-permute-done((bf16[128,256]{1,0:T(8,128)(2,1)S(1)}, bf16[128,256]{1,0:T(8,128)(2,1)S(1)}, u32[]{:S(2)}, u32[]{:S(2)}) %collective-permute-start.55) | collective-permute-done | bytes 65568 | tf_op jit(solution)/shard_map/cond/branch_1_fun/ppermute | solution.py:273
  107.4 3.3 %collective-permute-done.56.refs_2_ = bf16[128,256]{1,0:T(8,128)(2,1)S(1)} collective-permute-done((bf16[128,256]{1,0:T(8,128)(2,1)S(1)}, bf16[128,256]{1,0:T(8,128)(2,1)S(1)}, u32[]{:S(2)}, u32[]{:S(2)}) %collective-permute-start.56) | collective-permute-done | bytes 65568 | tf_op jit(solution)/shard_map/cond/branch_1_fun/ppermute | solution.py:273
  111.6 4.2 %collective-permute-done.57.refs_3_ = bf16[128,256]{1,0:T(8,128)(2,1)S(1)} collective-permute-done((bf16[128,256]{1,0:T(8,128)(2,1)S(1)}, bf16[128,256]{1,0:T(8,128)(2,1)S(1)}, u32[]{:S(2)}, u32[]{:S(2)}) %collective-permute-start.57) | collective-permute-done | bytes 65568 | tf_op jit(solution)/shard_map/cond/branch_1_fun/ppermute | solution.py:273
  115.9 4.0 %branch_1_fun.21 = (bf16[2,1024,256]{2,1,0:T(8,128)(2,1)S(1)}, bf16[528,256]{1,0:T(8,128)(2,1)S(1)}, bf16[528,256]{1,0:T(8,128)(2,1)S(1)}) custom-call(s32[2]{0:T(128)S(1)} %get-tuple-element.150.info, s32[2,8]{1,0:T(2,128)S(1)} %get-tuple-element.164.side, s32[2]{0:T(128)S(1)} %get-tuple-element.165.powers, f32[2,1024,256]{2,1,0:T(8,128)S(1)} %get-tuple-element.166.gap_ref, ...), custom_call_target="tpu_custom_call" | custom-call | flops 2147483648 | bytes 12582912 | tf_op jit(solution)/shard_map/cond/branch_1_fun/pallas_call | solution.py:21
  120.0 1.5 collective-permute-done.58.refs_1_
  123.2 1.9 collective-permute-start.61
  126.0 1.6 collective-permute-done.60.refs_2_
  129.6 2.6 %collective-permute-start.63 = (bf16[144,256]{1,0:T(8,128)(2,1)S(1)}, bf16[144,256]{1,0:T(8,128)(2,1)S(1)}, u32[]{:S(2)}, u32[]{:S(2)}) collective-permute-start(bf16[144,256]{1,0:T(8,128)(2,1)S(1)} %branch_1_fun.23.refs_0_), channel_id=1, source_target_pairs={{0,2},{1,3},{2,0},{3,1},{4,6},{5,7},{6,4},{7,5},{8,10},{9,11},{10,... | collective-permute-start | bytes 221192 | tf_op jit(solution)/shard_map/cond/branch_1_fun/ppermute | solution.py:273
  133.0 1.5 collective-permute-start.66
  134.5 1.5 collective-permute-start.67
  136.0 6.9 %collective-permute-done.66.refs_6_ = bf16[128,256]{1,0:T(8,128)(2,1)S(1)} collective-permute-done((bf16[128,256]{1,0:T(8,128)(2,1)S(1)}, bf16[128,256]{1,0:T(8,128)(2,1)S(1)}, u32[]{:S(2)}, u32[]{:S(2)}) %collective-permute-start.66) | collective-permute-done | bytes 65568 | tf_op jit(solution)/shard_map/cond/branch_1_fun/ppermute | solution.py:273
  143.9 1.5 collective-permute-start.71
  148.2 2.4 %collective-permute-done.73.refs_6_ = bf16[128,256]{1,0:T(8,128)(2,1)S(1)} collective-permute-done((bf16[128,256]{1,0:T(8,128)(2,1)S(1)}, bf16[128,256]{1,0:T(8,128)(2,1)S(1)}, u32[]{:S(2)}, u32[]{:S(2)}) %collective-permute-start.73) | collective-permute-done | bytes 65568 | tf_op jit(solution)/shard_map/cond/branch_1_fun/ppermute | solution.py:273
  151.8 2.0 branch_1_fun.25
  154.1 2.3 %branch_1_fun.27 = (bf16[2,1024,256]{2,1,0:T(8,128)(2,1)S(1)}, bf16[1024,256]{1,0:T(8,128)(2,1)S(1)}, bf16[1024,256]{1,0:T(8,128)(2,1)S(1)}, bf16[9,128,256]{2,1,0:T(8,128)(2,1)S(1)}) custom-call(s32[2]{0:T(128)S(1)} %get-tuple-element.150.info, s32[2,8]{1,0:T(2,128)S(1)} %get-tuple-element.173.refs_0_, ...), custom_call_target="tpu_custom_call" | custom-call | flops 1073741824 | bytes 7340032 | tf_op jit(solution)/shard_map/cond/branch_1_fun/pallas_call | solution.py:21
  160.6 13.2 %collective-permute-done.80.refs_1_ = bf16[128,256]{1,0:T(8,128)(2,1)S(1)} collective-permute-done((bf16[128,256]{1,0:T(8,128)(2,1)S(1)}, bf16[128,256]{1,0:T(8,128)(2,1)S(1)}, u32[]{:S(2)}, u32[]{:S(2)}) %collective-permute-start.80) | collective-permute-done | bytes 65568 | tf_op jit(solution)/shard_map/cond/branch_1_fun/ppermute | solution.py:273
  174.2 3.9 %collective-permute-done.81.refs_2_ = bf16[128,256]{1,0:T(8,128)(2,1)S(1)} collective-permute-done((bf16[128,256]{1,0:T(8,128)(2,1)S(1)}, bf16[128,256]{1,0:T(8,128)(2,1)S(1)}, u32[]{:S(2)}, u32[]{:S(2)}) %collective-permute-start.81) | collective-permute-done | bytes 65568 | tf_op jit(solution)/shard_map/cond/branch_1_fun/ppermute | solution.py:273
  179.3 4.0 %collective-permute-done.82.refs_3_ = bf16[128,256]{1,0:T(8,128)(2,1)S(1)} collective-permute-done((bf16[128,256]{1,0:T(8,128)(2,1)S(1)}, bf16[128,256]{1,0:T(8,128)(2,1)S(1)}, u32[]{:S(2)}, u32[]{:S(2)}) %collective-permute-start.82) | collective-permute-done | bytes 65568 | tf_op jit(solution)/shard_map/cond/branch_1_fun/ppermute | solution.py:273
  183.4 4.0 %branch_1_fun.29 = (bf16[2,1024,256]{2,1,0:T(8,128)(2,1)S(1)}, bf16[528,256]{1,0:T(8,128)(2,1)S(1)}, bf16[528,256]{1,0:T(8,128)(2,1)S(1)}) custom-call(s32[2]{0:T(128)S(1)} %get-tuple-element.150.info, s32[2,8]{1,0:T(2,128)S(1)} %get-tuple-element.164.side, s32[2]{0:T(128)S(1)} %get-tuple-element.165.powers, f32[2,1024,256]{2,1,0:T(8,128)S(1)} %get-tuple-element.166.gap_ref, ...), custom_call_target="tpu_custom_call" | custom-call | flops 2147483648 | bytes 12582912 | tf_op jit(solution)/shard_map/cond/branch_1_fun/pallas_call | solution.py:21
  187.5 1.5 collective-permute-done.83.refs_1_
  190.9 1.7 collective-permute-start.86
  193.5 1.9 collective-permute-done.85.refs_2_
  197.3 2.7 %collective-permute-start.88 = (bf16[144,256]{1,0:T(8,128)(2,1)S(1)}, bf16[144,256]{1,0:T(8,128)(2,1)S(1)}, u32[]{:S(2)}, u32[]{:S(2)}) collective-permute-start(bf16[144,256]{1,0:T(8,128)(2,1)S(1)} %branch_1_fun.31.refs_0_), channel_id=1, source_target_pairs={{0,2},{1,3},{2,0},{3,1},{4,6},{5,7},{6,4},{7,5},{8,10},{9,11},{10,... | collective-permute-start | bytes 221192 | tf_op jit(solution)/shard_map/cond/branch_1_fun/ppermute | solution.py:273
  202.0 1.8 collective-permute-start.92
  203.8 6.8 %collective-permute-done.91.refs_6_ = bf16[128,256]{1,0:T(8,128)(2,1)S(1)} collective-permute-done((bf16[128,256]{1,0:T(8,128)(2,1)S(1)}, bf16[128,256]{1,0:T(8,128)(2,1)S(1)}, u32[]{:S(2)}, u32[]{:S(2)}) %collective-permute-start.91) | collective-permute-done | bytes 65568 | tf_op jit(solution)/shard_map/cond/branch_1_fun/ppermute | solution.py:273
  211.3 1.7 collective-permute-start.96
  215.6 2.6 %collective-permute-done.98.refs_6_ = bf16[128,256]{1,0:T(8,128)(2,1)S(1)} collective-permute-done((bf16[128,256]{1,0:T(8,128)(2,1)S(1)}, bf16[128,256]{1,0:T(8,128)(2,1)S(1)}, u32[]{:S(2)}, u32[]{:S(2)}) %collective-permute-start.98) | collective-permute-done | bytes 65568 | tf_op jit(solution)/shard_map/cond/branch_1_fun/ppermute | solution.py:273
  219.4 1.9 branch_1_fun.33
  (157 shorter events, 52.7 us)
Async XLA Ops:
  7.2 37.6 %collective-permute-start.101 = (bf16[2,1024,256]{2,1,0:T(8,128)(2,1)S(1)}, bf16[2,1024,256]{2,1,0:T(8,128)(2,1)S(1)}, u32[]{:S(2)}, u32[]{:S(2)}) collective-permute-start(bf16[2,1024,256]{2,1,0:T(8,128)(2,1)S(1)} %get-tuple-element.270.disp_ref), channel_id=1, source_target_pairs={{0,4},{4,0},{8,12},{12,8},{16,20},{20,16},{24,28},{28,24},{1,5},{5... | collective-permute-start | bytes 3145736 | tf_op jit(solution)/shard_map/ppermute | solution.py:273
  7.3 37.5 %collective-permute-start.102 = (bf16[2,1024,256]{2,1,0:T(8,128)(2,1)S(1)}, bf16[2,1024,256]{2,1,0:T(8,128)(2,1)S(1)}, u32[]{:S(2)}, u32[]{:S(2)}) collective-permute-start(bf16[2,1024,256]{2,1,0:T(8,128)(2,1)S(1)} %get-tuple-element.270.disp_ref), channel_id=1, source_target_pairs={{0,28},{4,8},{8,4},{12,16},{16,12},{20,24},{24,20},{28,0},{1,29},{... | collective-permute-start | bytes 3145736 | tf_op jit(solution)/shard_map/ppermute | solution.py:356
  11.0 33.8 %collective-permute-start.103 = (bf16[1024,256]{1,0:T(8,128)(2,1)S(1)}, bf16[1024,256]{1,0:T(8,128)(2,1)S(1)}, u32[]{:S(2)}, u32[]{:S(2)}) collective-permute-start(bf16[1024,256]{1,0:T(8,128)(2,1)S(1)} %get-tuple-element.271), channel_id=1, source_target_pairs={{0,1},{1,0},{2,3},{3,2},{4,5},{5,4},{6,7},{7,6},{8,9},{9,8},{10,11... | collective-permute-start | bytes 1572872 | tf_op jit(solution)/shard_map/ppermute | solution.py:357
  12.6 32.3 %collective-permute-start.104 = (bf16[1024,256]{1,0:T(8,128)(2,1)S(1)}, bf16[1024,256]{1,0:T(8,128)(2,1)S(1)}, u32[]{:S(2)}, u32[]{:S(2)}) collective-permute-start(bf16[1024,256]{1,0:T(8,128)(2,1)S(1)} %get-tuple-element.272), channel_id=1, source_target_pairs={{1,2},{2,1},{5,6},{6,5},{9,10},{10,9},{13,14},{14,13},{17,18},{18,... | collective-permute-start | bytes 1572872 | tf_op jit(solution)/shard_map/ppermute | solution.py:358
  13.2 21.6 %collective-permute-start.105 = (bf16[128,256]{1,0:T(8,128)(2,1)S(1)}, bf16[128,256]{1,0:T(8,128)(2,1)S(1)}, u32[]{:S(2)}, u32[]{:S(2)}) collective-permute-start(bf16[128,256]{1,0:T(8,128)(2,1)S(1)} %get-tuple-element.274), channel_id=1, source_target_pairs={{0,8},{4,12},{8,0},{12,4},{16,24},{20,28},{24,16},{28,20},{1,9},{5... | collective-permute-start | bytes 196616 | tf_op jit(solution)/shard_map/ppermute | solution.py:273
  34.9 4.7 %collective-permute-start.106 = (bf16[128,256]{1,0:T(8,128)(2,1)S(1)}, bf16[128,256]{1,0:T(8,128)(2,1)S(1)}, u32[]{:S(2)}, u32[]{:S(2)}) collective-permute-start(bf16[128,256]{1,0:T(8,128)(2,1)S(1)} %get-tuple-element.275), channel_id=1, source_target_pairs={{0,16},{4,20},{8,24},{12,28},{16,0},{20,4},{24,8},{28,12},{1,17},{... | collective-permute-start | bytes 196616 | tf_op jit(solution)/shard_map/ppermute | solution.py:273
  39.6 5.2 %collective-permute-start.107 = (bf16[128,256]{1,0:T(8,128)(2,1)S(1)}, bf16[128,256]{1,0:T(8,128)(2,1)S(1)}, u32[]{:S(2)}, u32[]{:S(2)}) collective-permute-start(bf16[128,256]{1,0:T(8,128)(2,1)S(1)} %get-tuple-element.276), channel_id=1, source_target_pairs={{0,24},{4,28},{8,16},{12,20},{16,8},{20,12},{24,0},{28,4},{1,25},{... | collective-permute-start | bytes 196616 | tf_op jit(solution)/shard_map/ppermute | solution.py:273
  54.1 5.3 %collective-permute-start.111 = (bf16[144,256]{1,0:T(8,128)(2,1)S(1)}, bf16[144,256]{1,0:T(8,128)(2,1)S(1)}, u32[]{:S(2)}, u32[]{:S(2)}) collective-permute-start(bf16[144,256]{1,0:T(8,128)(2,1)S(1)} %get-tuple-element.282), channel_id=1, source_target_pairs={{0,24},{4,28},{8,16},{12,20},{16,8},{20,12},{24,0},{28,4},{1,25},{... | collective-permute-start | bytes 221192 | tf_op jit(solution)/shard_map/ppermute | solution.py:273
  54.7 10.9 %collective-permute-start.115 = (bf16[128,256]{1,0:T(8,128)(2,1)S(1)}, bf16[128,256]{1,0:T(8,128)(2,1)S(1)}, u32[]{:S(2)}, u32[]{:S(2)}) collective-permute-start(bf16[128,256]{1,0:T(8,128)(2,1)S(1)} %shard_map.99.after_ref.refs_4_), channel_id=1, source_target_pairs={{0,1},{1,0},{2,3},{3,2},{4,5},{5,4},{6,7},{7,6},{8,9},{9,8},{10,11... | collective-permute-start | bytes 196616 | tf_op jit(solution)/shard_map/ppermute | solution.py:273
  59.4 14.4 %collective-permute-start.112 = (bf16[144,256]{1,0:T(8,128)(2,1)S(1)}, bf16[144,256]{1,0:T(8,128)(2,1)S(1)}, u32[]{:S(2)}, u32[]{:S(2)}) collective-permute-start(bf16[144,256]{1,0:T(8,128)(2,1)S(1)} %shard_map.102.refs_0_), channel_id=1, source_target_pairs={{0,1},{1,0},{2,3},{3,2},{4,5},{5,4},{6,7},{7,6},{8,9},{9,8},{10,11... | collective-permute-start | bytes 221192 | tf_op jit(solution)/shard_map/ppermute | solution.py:273
  60.3 13.5 %collective-permute-start.113 = (bf16[144,256]{1,0:T(8,128)(2,1)S(1)}, bf16[144,256]{1,0:T(8,128)(2,1)S(1)}, u32[]{:S(2)}, u32[]{:S(2)}) collective-permute-start(bf16[144,256]{1,0:T(8,128)(2,1)S(1)} %shard_map.102.refs_0_), channel_id=1, source_target_pairs={{0,2},{1,3},{2,0},{3,1},{4,6},{5,7},{6,4},{7,5},{8,10},{9,11},{10,... | collective-permute-start | bytes 221192 | tf_op jit(solution)/shard_map/ppermute | solution.py:273
  63.3 10.5 %collective-permute-start.114 = (bf16[144,256]{1,0:T(8,128)(2,1)S(1)}, bf16[144,256]{1,0:T(8,128)(2,1)S(1)}, u32[]{:S(2)}, u32[]{:S(2)}) collective-permute-start(bf16[144,256]{1,0:T(8,128)(2,1)S(1)} %shard_map.102.refs_0_), channel_id=1, source_target_pairs={{0,3},{1,2},{2,1},{3,0},{4,7},{5,6},{6,5},{7,4},{8,11},{9,10},{10,... | collective-permute-start | bytes 221192 | tf_op jit(solution)/shard_map/ppermute | solution.py:273
  63.9 9.9 %collective-permute-start.116 = (bf16[128,256]{1,0:T(8,128)(2,1)S(1)}, bf16[128,256]{1,0:T(8,128)(2,1)S(1)}, u32[]{:S(2)}, u32[]{:S(2)}) collective-permute-start(bf16[128,256]{1,0:T(8,128)(2,1)S(1)} %shard_map.99.after_ref.refs_4_), channel_id=1, source_target_pairs={{0,2},{1,3},{2,0},{3,1},{4,6},{5,7},{6,4},{7,5},{8,10},{9,11},{10,... | collective-permute-start | bytes 196616 | tf_op jit(solution)/shard_map/ppermute | solution.py:273
  65.6 8.2 %collective-permute-start.117 = (bf16[128,256]{1,0:T(8,128)(2,1)S(1)}, bf16[128,256]{1,0:T(8,128)(2,1)S(1)}, u32[]{:S(2)}, u32[]{:S(2)}) collective-permute-start(bf16[128,256]{1,0:T(8,128)(2,1)S(1)} %shard_map.99.after_ref.refs_4_), channel_id=1, source_target_pairs={{0,3},{1,2},{2,1},{3,0},{4,7},{5,6},{6,5},{7,4},{8,11},{9,10},{10,... | collective-permute-start | bytes 196616 | tf_op jit(solution)/shard_map/ppermute | solution.py:273
  73.9 4.7 %collective-permute-start.119 = (bf16[128,256]{1,0:T(8,128)(2,1)S(1)}, bf16[128,256]{1,0:T(8,128)(2,1)S(1)}, u32[]{:S(2)}, u32[]{:S(2)}) collective-permute-start(bf16[128,256]{1,0:T(8,128)(2,1)S(1)} %get-tuple-element.285), channel_id=1, source_target_pairs={{0,8},{4,12},{8,0},{12,4},{16,24},{20,28},{24,16},{28,20},{1,9},{5... | collective-permute-start | bytes 196616 | tf_op jit(solution)/shard_map/ppermute | solution.py:273
  76.3 5.2 %collective-permute-start.123 = (bf16[128,256]{1,0:T(8,128)(2,1)S(1)}, bf16[128,256]{1,0:T(8,128)(2,1)S(1)}, u32[]{:S(2)}, u32[]{:S(2)}) collective-permute-start(bf16[128,256]{1,0:T(8,128)(2,1)S(1)} %get-tuple-element.285), channel_id=1, source_target_pairs={{0,24},{4,28},{8,16},{12,20},{16,8},{20,12},{24,0},{28,4},{1,25},{... | collective-permute-start | bytes 196616 | tf_op jit(solution)/shard_map/ppermute | solution.py:273
  77.4 6.2 %collective-permute-start.125 = (s32[2,8]{1,0:T(2,128)S(1)}, s32[2,8]{1,0:T(2,128)S(1)}, u32[]{:S(2)}, u32[]{:S(2)}) collective-permute-start(s32[2,8]{1,0:T(2,128)S(1)} %copy-done.4), channel_id=1, source_target_pairs={{0,28},{4,8},{8,4},{12,16},{16,12},{20,24},{24,20},{28,0},{1,29},{... | collective-permute-start | bytes 200 | tf_op jit(solution)/shard_map/ppermute | solution.py:329
  77.4 5.3 %collective-permute-start.118 = (bf16[128,256]{1,0:T(8,128)(2,1)S(1)}, bf16[128,256]{1,0:T(8,128)(2,1)S(1)}, u32[]{:S(2)}, u32[]{:S(2)}) collective-permute-start(bf16[128,256]{1,0:T(8,128)(2,1)S(1)} %get-tuple-element.285), channel_id=1, source_target_pairs={{0,4},{4,0},{8,12},{12,8},{16,20},{20,16},{24,28},{28,24},{1,5},{5... | collective-permute-start | bytes 196616 | tf_op jit(solution)/shard_map/ppermute | solution.py:273
  89.1 26.8 %collective-permute-start.51 = (bf16[2,1024,256]{2,1,0:T(8,128)(2,1)S(1)}, bf16[2,1024,256]{2,1,0:T(8,128)(2,1)S(1)}, u32[]{:S(2)}, u32[]{:S(2)}) collective-permute-start(bf16[2,1024,256]{2,1,0:T(8,128)(2,1)S(1)} %get-tuple-element.180.disp_ref), channel_id=1, source_target_pairs={{0,4},{4,0},{8,12},{12,8},{16,20},{20,16},{24,28},{28,24},{1,5},{5... | collective-permute-start | bytes 3145736 | tf_op jit(solution)/shard_map/cond/branch_1_fun/ppermute | solution.py:273
  89.2 26.7 %collective-permute-start.52 = (bf16[9,128,256]{2,1,0:T(8,128)(2,1)S(1)}, bf16[9,128,256]{2,1,0:T(8,128)(2,1)S(1)}, u32[]{:S(2)}, u32[]{:S(2)}) collective-permute-start(bf16[9,128,256]{2,1,0:T(8,128)(2,1)S(1)} %get-tuple-element.181), channel_id=1, source_target_pairs={{0,28},{4,8},{8,4},{12,16},{16,12},{20,24},{24,20},{28,0},{1,29},{... | collective-permute-start | bytes 1769480 | tf_op jit(solution)/shard_map/cond/branch_1_fun/ppermute | solution.py:356
  90.4 25.5 %collective-permute-start.53 = (bf16[1024,256]{1,0:T(8,128)(2,1)S(1)}, bf16[1024,256]{1,0:T(8,128)(2,1)S(1)}, u32[]{:S(2)}, u32[]{:S(2)}) collective-permute-start(bf16[1024,256]{1,0:T(8,128)(2,1)S(1)} %get-tuple-element.182), channel_id=1, source_target_pairs={{0,1},{1,0},{2,3},{3,2},{4,5},{5,4},{6,7},{7,6},{8,9},{9,8},{10,11... | collective-permute-start | bytes 1572872 | tf_op jit(solution)/shard_map/cond/branch_1_fun/ppermute | solution.py:357
  91.6 24.3 %collective-permute-start.54 = (bf16[1024,256]{1,0:T(8,128)(2,1)S(1)}, bf16[1024,256]{1,0:T(8,128)(2,1)S(1)}, u32[]{:S(2)}, u32[]{:S(2)}) collective-permute-start(bf16[1024,256]{1,0:T(8,128)(2,1)S(1)} %get-tuple-element.183), channel_id=1, source_target_pairs={{1,2},{2,1},{5,6},{6,5},{9,10},{10,9},{13,14},{14,13},{17,18},{18,... | collective-permute-start | bytes 1572872 | tf_op jit(solution)/shard_map/cond/branch_1_fun/ppermute | solution.py:358
  92.3 14.1 %collective-permute-start.55 = (bf16[128,256]{1,0:T(8,128)(2,1)S(1)}, bf16[128,256]{1,0:T(8,128)(2,1)S(1)}, u32[]{:S(2)}, u32[]{:S(2)}) collective-permute-start(bf16[128,256]{1,0:T(8,128)(2,1)S(1)} %get-tuple-element.186), channel_id=1, source_target_pairs={{0,8},{4,12},{8,0},{12,4},{16,24},{20,28},{24,16},{28,20},{1,9},{5... | collective-permute-start | bytes 196616 | tf_op jit(solution)/shard_map/cond/branch_1_fun/ppermute | solution.py:273
  110.6 5.2 %collective-permute-start.57 = (bf16[128,256]{1,0:T(8,128)(2,1)S(1)}, bf16[128,256]{1,0:T(8,128)(2,1)S(1)}, u32[]{:S(2)}, u32[]{:S(2)}) collective-permute-start(bf16[128,256]{1,0:T(8,128)(2,1)S(1)} %get-tuple-element.188), channel_id=1, source_target_pairs={{0,24},{4,28},{8,16},{12,20},{16,8},{20,12},{24,0},{28,4},{1,25},{... | collective-permute-start | bytes 196616 | tf_op jit(solution)/shard_map/cond/branch_1_fun/ppermute | solution.py:273
  122.5 5.1 %collective-permute-start.60 = (bf16[144,256]{1,0:T(8,128)(2,1)S(1)}, bf16[144,256]{1,0:T(8,128)(2,1)S(1)}, u32[]{:S(2)}, u32[]{:S(2)}) collective-permute-start(bf16[144,256]{1,0:T(8,128)(2,1)S(1)} %get-tuple-element.194), channel_id=1, source_target_pairs={{0,16},{4,20},{8,24},{12,28},{16,0},{20,4},{24,8},{28,12},{1,17},{... | collective-permute-start | bytes 221192 | tf_op jit(solution)/shard_map/cond/branch_1_fun/ppermute | solution.py:273
  123.2 5.3 %collective-permute-start.61 = (bf16[144,256]{1,0:T(8,128)(2,1)S(1)}, bf16[144,256]{1,0:T(8,128)(2,1)S(1)}, u32[]{:S(2)}, u32[]{:S(2)}) collective-permute-start(bf16[144,256]{1,0:T(8,128)(2,1)S(1)} %get-tuple-element.195), channel_id=1, source_target_pairs={{0,24},{4,28},{8,16},{12,20},{16,8},{20,12},{24,0},{28,4},{1,25},{... | collective-permute-start | bytes 221192 | tf_op jit(solution)/shard_map/cond/branch_1_fun/ppermute | solution.py:273
  125.1 9.4 %collective-permute-start.65 = (bf16[128,256]{1,0:T(8,128)(2,1)S(1)}, bf16[128,256]{1,0:T(8,128)(2,1)S(1)}, u32[]{:S(2)}, u32[]{:S(2)}) collective-permute-start(bf16[128,256]{1,0:T(8,128)(2,1)S(1)} %branch_1_fun.20.after_ref.refs_4_), channel_id=1, source_target_pairs={{0,1},{1,0},{2,3},{3,2},{4,5},{5,4},{6,7},{7,6},{8,9},{9,8},{10,11... | collective-permute-start | bytes 196616 | tf_op jit(solution)/shard_map/cond/branch_1_fun/ppermute | solution.py:273
  128.5 14.4 %collective-permute-start.62 = (bf16[144,256]{1,0:T(8,128)(2,1)S(1)}, bf16[144,256]{1,0:T(8,128)(2,1)S(1)}, u32[]{:S(2)}, u32[]{:S(2)}) collective-permute-start(bf16[144,256]{1,0:T(8,128)(2,1)S(1)} %branch_1_fun.23.refs_0_), channel_id=1, source_target_pairs={{0,1},{1,0},{2,3},{3,2},{4,5},{5,4},{6,7},{7,6},{8,9},{9,8},{10,11... | collective-permute-start | bytes 221192 | tf_op jit(solution)/shard_map/cond/branch_1_fun/ppermute | solution.py:273
  129.6 13.3 %collective-permute-start.63 = (bf16[144,256]{1,0:T(8,128)(2,1)S(1)}, bf16[144,256]{1,0:T(8,128)(2,1)S(1)}, u32[]{:S(2)}, u32[]{:S(2)}) collective-permute-start(bf16[144,256]{1,0:T(8,128)(2,1)S(1)} %branch_1_fun.23.refs_0_), channel_id=1, source_target_pairs={{0,2},{1,3},{2,0},{3,1},{4,6},{5,7},{6,4},{7,5},{8,10},{9,11},{10,... | collective-permute-start | bytes 221192 | tf_op jit(solution)/shard_map/cond/branch_1_fun/ppermute | solution.py:273
  132.2 10.8 %collective-permute-start.64 = (bf16[144,256]{1,0:T(8,128)(2,1)S(1)}, bf16[144,256]{1,0:T(8,128)(2,1)S(1)}, u32[]{:S(2)}, u32[]{:S(2)}) collective-permute-start(bf16[144,256]{1,0:T(8,128)(2,1)S(1)} %branch_1_fun.23.refs_0_), channel_id=1, source_target_pairs={{0,3},{1,2},{2,1},{3,0},{4,7},{5,6},{6,5},{7,4},{8,11},{9,10},{10,... | collective-permute-start | bytes 221192 | tf_op jit(solution)/shard_map/cond/branch_1_fun/ppermute | solution.py:273
  133.0 9.9 %collective-permute-start.66 = (bf16[128,256]{1,0:T(8,128)(2,1)S(1)}, bf16[128,256]{1,0:T(8,128)(2,1)S(1)}, u32[]{:S(2)}, u32[]{:S(2)}) collective-permute-start(bf16[128,256]{1,0:T(8,128)(2,1)S(1)} %branch_1_fun.20.after_ref.refs_4_), channel_id=1, source_target_pairs={{0,2},{1,3},{2,0},{3,1},{4,6},{5,7},{6,4},{7,5},{8,10},{9,11},{10,... | collective-permute-start | bytes 196616 | tf_op jit(solution)/shard_map/cond/branch_1_fun/ppermute | solution.py:273
  134.5 8.4 %collective-permute-start.67 = (bf16[128,256]{1,0:T(8,128)(2,1)S(1)}, bf16[128,256]{1,0:T(8,128)(2,1)S(1)}, u32[]{:S(2)}, u32[]{:S(2)}) collective-permute-start(bf16[128,256]{1,0:T(8,128)(2,1)S(1)} %branch_1_fun.20.after_ref.refs_4_), channel_id=1, source_target_pairs={{0,3},{1,2},{2,1},{3,0},{4,7},{5,6},{6,5},{7,4},{8,11},{9,10},{10,... | collective-permute-start | bytes 196616 | tf_op jit(solution)/shard_map/cond/branch_1_fun/ppermute | solution.py:273
  145.4 5.2 %collective-permute-start.73 = (bf16[128,256]{1,0:T(8,128)(2,1)S(1)}, bf16[128,256]{1,0:T(8,128)(2,1)S(1)}, u32[]{:S(2)}, u32[]{:S(2)}) collective-permute-start(bf16[128,256]{1,0:T(8,128)(2,1)S(1)} %get-tuple-element.197.refs_0_), channel_id=1, source_target_pairs={{0,24},{4,28},{8,16},{12,20},{16,8},{20,12},{24,0},{28,4},{1,25},{... | collective-permute-start | bytes 196616 | tf_op jit(solution)/shard_map/cond/branch_1_fun/ppermute | solution.py:273
  156.4 26.9 %collective-permute-start.76 = (bf16[2,1024,256]{2,1,0:T(8,128)(2,1)S(1)}, bf16[2,1024,256]{2,1,0:T(8,128)(2,1)S(1)}, u32[]{:S(2)}, u32[]{:S(2)}) collective-permute-start(bf16[2,1024,256]{2,1,0:T(8,128)(2,1)S(1)} %get-tuple-element.211.disp_ref), channel_id=1, source_target_pairs={{0,4},{4,0},{8,12},{12,8},{16,20},{20,16},{24,28},{28,24},{1,5},{5... | collective-permute-start | bytes 3145736 | tf_op jit(solution)/shard_map/cond/branch_1_fun/ppermute | solution.py:273
  156.8 26.5 %collective-permute-start.77 = (bf16[9,128,256]{2,1,0:T(8,128)(2,1)S(1)}, bf16[9,128,256]{2,1,0:T(8,128)(2,1)S(1)}, u32[]{:S(2)}, u32[]{:S(2)}) collective-permute-start(bf16[9,128,256]{2,1,0:T(8,128)(2,1)S(1)} %get-tuple-element.212), channel_id=1, source_target_pairs={{0,28},{4,8},{8,4},{12,16},{16,12},{20,24},{24,20},{28,0},{1,29},{... | collective-permute-start | bytes 1769480 | tf_op jit(solution)/shard_map/cond/branch_1_fun/ppermute | solution.py:356
  157.8 25.5 %collective-permute-start.78 = (bf16[1024,256]{1,0:T(8,128)(2,1)S(1)}, bf16[1024,256]{1,0:T(8,128)(2,1)S(1)}, u32[]{:S(2)}, u32[]{:S(2)}) collective-permute-start(bf16[1024,256]{1,0:T(8,128)(2,1)S(1)} %get-tuple-element.213), channel_id=1, source_target_pairs={{0,1},{1,0},{2,3},{3,2},{4,5},{5,4},{6,7},{7,6},{8,9},{9,8},{10,11... | collective-permute-start | bytes 1572872 | tf_op jit(solution)/shard_map/cond/branch_1_fun/ppermute | solution.py:357
  159.0 24.3 %collective-permute-start.79 = (bf16[1024,256]{1,0:T(8,128)(2,1)S(1)}, bf16[1024,256]{1,0:T(8,128)(2,1)S(1)}, u32[]{:S(2)}, u32[]{:S(2)}) collective-permute-start(bf16[1024,256]{1,0:T(8,128)(2,1)S(1)} %get-tuple-element.214), channel_id=1, source_target_pairs={{1,2},{2,1},{5,6},{6,5},{9,10},{10,9},{13,14},{14,13},{17,18},{18,... | collective-permute-start | bytes 1572872 | tf_op jit(solution)/shard_map/cond/branch_1_fun/ppermute | solution.py:358
  159.7 14.1 %collective-permute-start.80 = (bf16[128,256]{1,0:T(8,128)(2,1)S(1)}, bf16[128,256]{1,0:T(8,128)(2,1)S(1)}, u32[]{:S(2)}, u32[]{:S(2)}) collective-permute-start(bf16[128,256]{1,0:T(8,128)(2,1)S(1)} %get-tuple-element.216), channel_id=1, source_target_pairs={{0,8},{4,12},{8,0},{12,4},{16,24},{20,28},{24,16},{28,20},{1,9},{5... | collective-permute-start | bytes 196616 | tf_op jit(solution)/shard_map/cond/branch_1_fun/ppermute | solution.py:273
  178.1 5.2 %collective-permute-start.82 = (bf16[128,256]{1,0:T(8,128)(2,1)S(1)}, bf16[128,256]{1,0:T(8,128)(2,1)S(1)}, u32[]{:S(2)}, u32[]{:S(2)}) collective-permute-start(bf16[128,256]{1,0:T(8,128)(2,1)S(1)} %get-tuple-element.218), channel_id=1, source_target_pairs={{0,24},{4,28},{8,16},{12,20},{16,8},{20,12},{24,0},{28,4},{1,25},{... | collective-permute-start | bytes 196616 | tf_op jit(solution)/shard_map/cond/branch_1_fun/ppermute | solution.py:273
  190.2 5.1 %collective-permute-start.85 = (bf16[144,256]{1,0:T(8,128)(2,1)S(1)}, bf16[144,256]{1,0:T(8,128)(2,1)S(1)}, u32[]{:S(2)}, u32[]{:S(2)}) collective-permute-start(bf16[144,256]{1,0:T(8,128)(2,1)S(1)} %get-tuple-element.224), channel_id=1, source_target_pairs={{0,16},{4,20},{8,24},{12,28},{16,0},{20,4},{24,8},{28,12},{1,17},{... | collective-permute-start | bytes 221192 | tf_op jit(solution)/shard_map/cond/branch_1_fun/ppermute | solution.py:273
  190.9 5.3 %collective-permute-start.86 = (bf16[144,256]{1,0:T(8,128)(2,1)S(1)}, bf16[144,256]{1,0:T(8,128)(2,1)S(1)}, u32[]{:S(2)}, u32[]{:S(2)}) collective-permute-start(bf16[144,256]{1,0:T(8,128)(2,1)S(1)} %get-tuple-element.225), channel_id=1, source_target_pairs={{0,24},{4,28},{8,16},{12,20},{16,8},{20,12},{24,0},{28,4},{1,25},{... | collective-permute-start | bytes 221192 | tf_op jit(solution)/shard_map/cond/branch_1_fun/ppermute | solution.py:273
  192.6 9.4 %collective-permute-start.90 = (bf16[128,256]{1,0:T(8,128)(2,1)S(1)}, bf16[128,256]{1,0:T(8,128)(2,1)S(1)}, u32[]{:S(2)}, u32[]{:S(2)}) collective-permute-start(bf16[128,256]{1,0:T(8,128)(2,1)S(1)} %branch_1_fun.28.after_ref.refs_4_), channel_id=1, source_target_pairs={{0,1},{1,0},{2,3},{3,2},{4,5},{5,4},{6,7},{7,6},{8,9},{9,8},{10,11... | collective-permute-start | bytes 196616 | tf_op jit(solution)/shard_map/cond/branch_1_fun/ppermute | solution.py:273
  196.2 14.4 %collective-permute-start.87 = (bf16[144,256]{1,0:T(8,128)(2,1)S(1)}, bf16[144,256]{1,0:T(8,128)(2,1)S(1)}, u32[]{:S(2)}, u32[]{:S(2)}) collective-permute-start(bf16[144,256]{1,0:T(8,128)(2,1)S(1)} %branch_1_fun.31.refs_0_), channel_id=1, source_target_pairs={{0,1},{1,0},{2,3},{3,2},{4,5},{5,4},{6,7},{7,6},{8,9},{9,8},{10,11... | collective-permute-start | bytes 221192 | tf_op jit(solution)/shard_map/cond/branch_1_fun/ppermute | solution.py:273
  197.3 13.3 %collective-permute-start.88 = (bf16[144,256]{1,0:T(8,128)(2,1)S(1)}, bf16[144,256]{1,0:T(8,128)(2,1)S(1)}, u32[]{:S(2)}, u32[]{:S(2)}) collective-permute-start(bf16[144,256]{1,0:T(8,128)(2,1)S(1)} %branch_1_fun.31.refs_0_), channel_id=1, source_target_pairs={{0,2},{1,3},{2,0},{3,1},{4,6},{5,7},{6,4},{7,5},{8,10},{9,11},{10,... | collective-permute-start | bytes 221192 | tf_op jit(solution)/shard_map/cond/branch_1_fun/ppermute | solution.py:273
  200.0 10.7 %collective-permute-start.89 = (bf16[144,256]{1,0:T(8,128)(2,1)S(1)}, bf16[144,256]{1,0:T(8,128)(2,1)S(1)}, u32[]{:S(2)}, u32[]{:S(2)}) collective-permute-start(bf16[144,256]{1,0:T(8,128)(2,1)S(1)} %branch_1_fun.31.refs_0_), channel_id=1, source_target_pairs={{0,3},{1,2},{2,1},{3,0},{4,7},{5,6},{6,5},{7,4},{8,11},{9,10},{10,... | collective-permute-start | bytes 221192 | tf_op jit(solution)/shard_map/cond/branch_1_fun/ppermute | solution.py:273
  200.7 10.0 %collective-permute-start.91 = (bf16[128,256]{1,0:T(8,128)(2,1)S(1)}, bf16[128,256]{1,0:T(8,128)(2,1)S(1)}, u32[]{:S(2)}, u32[]{:S(2)}) collective-permute-start(bf16[128,256]{1,0:T(8,128)(2,1)S(1)} %branch_1_fun.28.after_ref.refs_4_), channel_id=1, source_target_pairs={{0,2},{1,3},{2,0},{3,1},{4,6},{5,7},{6,4},{7,5},{8,10},{9,11},{10,... | collective-permute-start | bytes 196616 | tf_op jit(solution)/shard_map/cond/branch_1_fun/ppermute | solution.py:273
  202.0 8.6 %collective-permute-start.92 = (bf16[128,256]{1,0:T(8,128)(2,1)S(1)}, bf16[128,256]{1,0:T(8,128)(2,1)S(1)}, u32[]{:S(2)}, u32[]{:S(2)}) collective-permute-start(bf16[128,256]{1,0:T(8,128)(2,1)S(1)} %branch_1_fun.28.after_ref.refs_4_), channel_id=1, source_target_pairs={{0,3},{1,2},{2,1},{3,0},{4,7},{5,6},{6,5},{7,4},{8,11},{9,10},{10,... | collective-permute-start | bytes 196616 | tf_op jit(solution)/shard_map/cond/branch_1_fun/ppermute | solution.py:273
  213.0 5.2 %collective-permute-start.98 = (bf16[128,256]{1,0:T(8,128)(2,1)S(1)}, bf16[128,256]{1,0:T(8,128)(2,1)S(1)}, u32[]{:S(2)}, u32[]{:S(2)}) collective-permute-start(bf16[128,256]{1,0:T(8,128)(2,1)S(1)} %get-tuple-element.227.refs_0_), channel_id=1, source_target_pairs={{0,24},{4,28},{8,16},{12,20},{16,8},{20,12},{24,0},{28,4},{1,25},{... | collective-permute-start | bytes 196616 | tf_op jit(solution)/shard_map/cond/branch_1_fun/ppermute | solution.py:273
  (37 other events, 376.3 us)
where the time goes:
time: 223 us
  waiting for transfers between devices  116 us (52%)
  starting transfers between devices  72.4 us (32%)
  Pallas kernels  29.3 us (13%)
  local copies, waits for them, and re-layouts  2.95 us (1%)
    ppermute x66, waiting for transfers between devices, swap(): return lax.ppermute(x, axis, [(i, i ^ mask) for i in range(n)])  116 us
    ppermute x66, starting transfers between devices, swap(): return lax.ppermute(x, axis, [(i, i ^ mask) for i in range(n)])  60.4 us
    pallas_call x25, Pallas kernels, call(): pl.pallas_call(kernel, out_shape=outs, in_specs=[SMEM if i < n_smem else...  29.3 us
    ppermute x3, starting transfers between devices, search(): off = lax.ppermute(sends[-1] if packed else disp, 'wide', away)  5.84 us
  transfers between devices with their start and end apart: 76, of which 34 were waited for; matrix products, arithmetic and copies ran while one was open for 1% of the time, Pallas kernels for 4%

commit v1 on v0

--- a/solution.py
+++ b/solution.py
@@ -88,31 +88,40 @@
         send_ref[tail, :] = tile
 
 
-def send_halo(info, disp_ref, za_ref, zb_ref, theirs=None, base_ref=None):
-    subs, rows_all, _ = disp_ref.shape
+def pack_blocks(table, row, face, source, disp_ref, out_ref, count):
+    blocks = table.shape[1]
+    height = disp_ref.shape[1] // blocks
+    cap = out_ref.shape[0]
+
+    def block(b, n):
+        need = table[row, b] == face
+        rows = pl.ds(pl.multiple_of(b * height, height), height)
+
+        @pl.when(need & (n < cap))
+        def _():
+            out_ref[n] = disp_ref[source, rows, :]
+
+        return n + need.astype(jnp.int32)
+
+    return lax.fori_loop(0, blocks, block, count)
+
+
+def send_halo(info, disp_ref, outs, tables):
+    last = disp_ref.shape[0] - 1
+    odd = jnp.bitwise_and(info[0], 1)
     zodd = jnp.bitwise_and(info[1], 1)
-    za_ref[...] = disp_ref[(1 - zodd) * (subs - 1)]
-    zb_ref[...] = disp_ref[zodd * (subs - 1)]
-    if theirs is None:
+    za_ref, zb_ref = outs[:2]
+    zero = jnp.int32(0)
+    if not tables:
+        za_ref[...] = disp_ref[(1 - zodd) * last]
+        zb_ref[...] = disp_ref[zodd * last]
         return
-    blocks = theirs.shape[1]
-    height = rows_all // blocks
-    cap = base_ref.shape[0]
-    odd = jnp.bitwise_and(info[0], 1)
-    count = jnp.int32(0)
-    for s in range(subs):
-
-        def block(b, n, s=s):
-            need = theirs[s, b] == odd
-            rows = pl.ds(pl.multiple_of(b * height, height), height)
-
-            @pl.when(need & (n < cap))
-            def _():
-                base_ref[n] = disp_ref[s, rows, :]
-
-            return n + need.astype(jnp.int32)
-
-        count = lax.fori_loop(0, blocks, block, count)
+    theirs, ta, tb = tables
+    count = zero
+    for s in range(last + 1):
+        count = pack_blocks(theirs, s, odd, s, disp_ref, outs[2], count)
+    pack_blocks(ta, zodd * last, 3 - zodd, (1 - zodd) * last, disp_ref, za_ref, zero)
+    pack_blocks(tb, (1 - zodd) * last, 2 + zodd, zodd * last, disp_ref, zb_ref, zero)
 
 
 def first_kernel(chunk, wide, info, lam_ref, half_ref, keep_ref, send_ref):
@@ -124,66 +133,82 @@
     )
 
 
-def flex_kernel(packed, info, *refs):
-    theirs = base_ref = None
-    if packed:
-        theirs, half_ref, flex_ref, disp_ref, za_ref, zb_ref, base_ref = refs
+def flex_kernel(step, packed, info, *refs):
+    tables, refs = refs[: 3 * packed], refs[3 * packed :]
+    half_ref, flex_ref, *refs = refs
+    if step:
+        mean_ref, *refs = refs
+        if step > 1:
+            refs = refs[1:]
+        disp_ref, *outs, stack_ref, sem = refs
+        copy = pltpu.make_async_copy(mean_ref, stack_ref.at[step - 1], sem)
+        copy.start()
     else:
-        half_ref, flex_ref, disp_ref, za_ref, zb_ref = refs
+        disp_ref, *outs = refs
     for s in range(half_ref.shape[0]):
         disp_ref[s] = jnp.dot(
             flex_ref[s], half_ref[s], preferred_element_type=F32
         ).astype(BF16)
-    send_halo(info, disp_ref, za_ref, zb_ref, theirs, base_ref)
+    send_halo(info, disp_ref, outs, tables)
+    if step:
+        copy.wait()
 
 
 def update_kernel(chunk, wide, step, last, info, lam_ref, dir_ref, alpha_ref, floor_ref, *refs):
     centre_refs = refs[:wide]
     refs = refs[wide:]
-    if step:
-        refs = refs[1:]
     if last:
-        lam_out, stack_ref, mean, sem = refs
+        _, lam_out, stack_ref, new_ref, mean_ref, sems = refs
     else:
-        lam_out, stack_ref, half_ref, keep_ref, send_ref, mean, sem = refs
+        new_ref, mean_ref, half_ref, keep_ref, send_ref = refs
     w = info[0]
     subs, _, cols = lam_ref.shape
     alpha = jnp.broadcast_to(alpha_ref[0:1, :], (chunk, cols))
+    copies = []
+
+    def send(src, dst):
+        copies.append(pltpu.make_async_copy(src, dst, sems.at[len(copies)]))
+        copies[-1].start()
+
     for k in range(wide):
         rows = pl.ds(pl.multiple_of(jnp.bitwise_xor(w, k) * chunk, chunk), chunk)
         centre = centre_refs[k][...].astype(F32)
-        mean[rows, :] = centre
+        mean_ref[rows, :] = centre
         total = None
         for s in range(subs):
             trial = lam_ref[s, rows, :] + alpha * dir_ref[s, rows, :].astype(F32)
             low = floor_ref[s, rows, :]
             low = jnp.concatenate([low] * (cols // low.shape[1]), axis=1)
             new = jnp.maximum(trial - centre, low)
-            lam_out[s, rows, :] = new
-            if not last:
+            new_ref[s, rows, :] = new
+            if last:
+                send(new_ref.at[s, rows, :], lam_out.at[s, rows, :])
+            else:
                 half_ref[s, rows, :] = new.astype(BF16)
                 total = new if total is None else total + new
-        if not last:
+        if last:
+            send(mean_ref.at[rows, :], stack_ref.at[step, rows, :])
+        else:
             out = send_ref if k % 2 else keep_ref
             out[pl.ds((k // 2) * chunk, chunk), :] = total.astype(BF16)
-    copy = pltpu.make_async_copy(mean, stack_ref.at[step], sem)
-    copy.start()
-    copy.wait()
-
-
-def direct_kernel(chunk, wide, packed, info, side, powers, gap_ref, disp_ref, chip_ref, off_ref, za_ref, zb_ref, diri_ref, after_ref, dir_ref, keep_ref, send_ref, jump, work):
-    w = info[0]
+    for copy in copies:
+        copy.wait()
+
+
+def direct_kernel(chunk, wide, eight, caps, packed, info, side, powers, gap_ref, disp_ref, chip_ref, off_ref, za_ref, zb_ref, diri_ref, after_ref, dir_ref, keep_ref, send_ref, jump, work):
+    w, z = info[0], info[1]
     odd = jnp.bitwise_and(w, 1)
-    zodd = jnp.bitwise_and(info[1], 1)
+    zodd = jnp.bitwise_and(z, 1)
     subs, rows_all, cols = gap_ref.shape
     blocks = side.shape[1]
     height = rows_all // blocks
     inner = jnp.zeros((8, cols), F32)
     square = jnp.zeros((8, cols), F32)
-    count = jnp.int32(0)
+    counts = (jnp.int32(0),) * 3
     for s in range(subs):
 
-        def block(b, n, s=s):
+        def block(b, ns, s=s):
+            n, above, below = ns
             face = side[s, b]
             rows = pl.ds(pl.multiple_of(b * height, height), height)
 
@@ -194,26 +219,30 @@
                 jump[rows, :] = value
                 work[s, rows, :] = value.astype(BF16)
 
+            def take(ref, slot):
+                if packed:
+                    return ref[jnp.minimum(slot, ref.shape[0] - 1)]
+                return ref[s, rows, :] if len(ref.shape) == 3 else ref[rows, :]
+
             pl.when(face == odd)(lambda: put(chip_ref[s, rows, :]))
             away = face == 1 - odd
-            if packed:
-                slot = jnp.minimum(n, off_ref.shape[0] - 1)
-                pl.when(away)(lambda: put(off_ref[slot]))
-            else:
-                pl.when(away)(lambda: put(off_ref[s, rows, :]))
+            pl.when(away)(lambda: put(take(off_ref, n)))
+            n = n + away.astype(jnp.int32)
             if s + 1 < subs:
                 pl.when(face == 2)(lambda: put(disp_ref[s + 1, rows, :]))
             else:
-                pl.when((face == 2) & (zodd == 0))(lambda: put(za_ref[rows, :]))
-                pl.when((face == 2) & (zodd == 1))(lambda: put(zb_ref[rows, :]))
+                pl.when((face == 2) & (zodd == 0))(lambda: put(take(za_ref, above)))
+                pl.when((face == 2) & (zodd == 1))(lambda: put(take(zb_ref, above)))
+                above = above + (face == 2).astype(jnp.int32)
             if s > 0:
                 pl.when(face == 3)(lambda: put(disp_ref[s - 1, rows, :]))
             else:
-                pl.when((face == 3) & (zodd == 1))(lambda: put(za_ref[rows, :]))
-                pl.when((face == 3) & (zodd == 0))(lambda: put(zb_ref[rows, :]))
-            return n + away.astype(jnp.int32)
-
-        count = lax.fori_loop(0, blocks, block, count)
+                pl.when((face == 3) & (zodd == 1))(lambda: put(take(za_ref, below)))
+                pl.when((face == 3) & (zodd == 0))(lambda: put(take(zb_ref, below)))
+                below = below + (face == 3).astype(jnp.int32)
+            return n, above, below
+
+        counts = lax.fori_loop(0, blocks, block, counts)
 
         def level(i, carry, s=s):
             work[s] = jnp.dot(
@@ -227,10 +256,17 @@
         dfloat = direct.astype(F32)
         inner = inner + jnp.sum((jump[...] * dfloat).reshape(rows_all // 8, 8, cols), axis=0)
         square = square + jnp.sum((dfloat * dfloat).reshape(rows_all // 8, 8, cols), axis=0)
+    n, above, below = counts
+    excess = jnp.maximum(
+        n - caps[0],
+        jnp.maximum(
+            jnp.where(z < eight - 1, above, 0) - caps[1], jnp.where(z > 0, below, 0) - caps[1]
+        ),
+    )
     tile = pack_products(
         jnp.sum(inner, axis=0, keepdims=True),
         jnp.sum(square, axis=0, keepdims=True),
-        jnp.broadcast_to(count.astype(F32), (1, cols)),
+        jnp.broadcast_to(excess.astype(F32), (1, cols)),
     )
     send_partial(
         chunk, wide, w, lambda rows: tree([work[s, rows, :].astype(F32) for s in range(subs)]),
@@ -321,12 +357,16 @@
     eight = lax.axis_size("eight")
     count = wide * eight * subs
     chunk = rows // wide
-    cap = -(-subs * blocks * 9 // 16)
+    caps = (-(-subs * blocks * 9 // 16), -(-blocks * 3 // 4))
     away = [(i, (i + 1) % wide if i % 2 else (i - 1) % wide) for i in range(wide)]
     pairs_a = [(i, i ^ 1) for i in range(eight) if i ^ 1 < eight]
     pairs_b = [(i, i + 1 if i % 2 else i - 1) for i in range(1, eight - 1 + eight % 2)]
     info = jnp.stack([lax.axis_index("wide"), lax.axis_index("eight")]).astype(jnp.int32)
-    theirs = lax.ppermute(side, "wide", away)
+    tables = [
+        lax.ppermute(side, "wide", away),
+        lax.ppermute(side, "eight", pairs_a),
+        lax.ppermute(side, "eight", pairs_b),
+    ]
     lanes = 128
     floor = jnp.where(
         jnp.broadcast_to(active[..., None], active.shape + (lanes,)) == 1, 0.0, -jnp.inf
@@ -335,7 +375,7 @@
     full = sds((subs, rows, cols), F32)
     half = sds((subs, rows, cols), BF16)
     one = sds((rows, cols), BF16)
-    base = sds((cap, rows // blocks, cols), BF16)
+    few = [sds((cap, rows // blocks, cols), BF16) for cap in (caps[1], caps[1], caps[0])]
     part = sds(((wide // 2) * chunk, cols), BF16)
     message = sds(((wide // 2) * chunk + EXTRA, cols), BF16)
     stack = sds((ITERS, rows, cols), F32)
@@ -343,23 +383,38 @@
     op_bytes = 2 * subs * rows * rows
     arr = subs * rows * cols
 
-    def search(half_lam, lkeep, lsend, packed):
-        ins = [info] + ([theirs] if packed else []) + [half_lam, flexibility]
+    def search(step, sums, centres, packed, tables):
+        mean, half_lam, lkeep, lsend = sums
+        ins = [info] + (tables if packed else []) + [half_lam, flexibility]
+        n_smem = len(ins) - 2
+        outs = [half] + (few if packed else [one, one])
+        spots = {}
+        if step:
+            ins.append(mean)
+            if step > 1:
+                spots = dict(anys=(len(ins),), aliases={len(ins): len(outs)})
+                ins.append(centres)
+            spots |= dict(any_outs=(len(outs),), scratch=[pltpu.SemaphoreType.DMA])
+            outs = outs + [stack]
         sends = call(
-            functools.partial(flex_kernel, packed), [half, one, one] + ([base] if packed else []),
-            len(ins) - 2, ins, mm, op_bytes + arr * 6,
+            functools.partial(flex_kernel, step, packed), outs, n_smem, ins, mm,
+            op_bytes + arr * 6, **spots,
         )
+        if step:
+            *sends, centres = sends
         lams = stage([lkeep, lsend], 0, chunk, wide, False)
         lams, sends = lax.optimization_barrier((lams, sends))
         own = scatter(lams, 1, chunk, wide, False)
         disp, za, zb = sends[:3]
-        off = lax.ppermute(sends[-1] if packed else disp, "wide", away)
+        off = lax.ppermute(sends[3] if packed else disp, "wide", away)
         za = lax.ppermute(za, "eight", pairs_a)
         zb = lax.ppermute(zb, "eight", pairs_b)
         chip = swap(disp, "wide", 1)
         lam_parts = across(own)
+        if not step:
+            own, tables = lax.optimization_barrier((own, tables))
         direct, dkeep, dsend = call(
-            functools.partial(direct_kernel, chunk, wide, packed), [half, message, message], 3,
+            functools.partial(direct_kernel, chunk, wide, eight, caps, packed), [half, message, message], 3,
             [info, side, powers, gap, disp, chip, off, za, zb, dirichlet, own],
             2 * mm, op_bytes + arr * 16,
             scratch=[pltpu.VMEM((rows, cols), F32), pltpu.VMEM((subs, rows, cols), BF16)],
@@ -371,43 +426,46 @@
             [sds((chunk, cols), BF16), sds((8, cols), F32)], 0, dir_parts + lam_parts,
             chunk * cols * 10, chunk * cols * 20, vmem=8,
         )
-        return direct, alpha, gather(centre, wide)
-
-    def update(step, lam, direct, alpha, pieces, centres):
-        last = step == ITERS - 1
+        return (direct, alpha, gather(centre, wide)), centres, tables
+
+    def update(step, lam, found, centres):
+        direct, alpha, pieces = found
         ins = [info, lam, direct, alpha, floor[step], *pieces]
-        aliases, anys = {}, ()
-        if step:
-            aliases, anys = {len(ins): 1}, (len(ins),)
-            ins.append(centres)
+        kernel = functools.partial(update_kernel, chunk, wide, step, step == ITERS - 1)
+        if step < ITERS - 1:
+            outs = [full, sds((rows, cols), F32), half, part, part]
+            return call(kernel, outs, 1, ins, arr * 6, arr * 16)
         return call(
-            functools.partial(update_kernel, chunk, wide, step, last),
-            [full, stack] + ([] if last else [half, part, part]), 1, ins, arr * 6, arr * 16,
-            scratch=[pltpu.VMEM((rows, cols), F32), pltpu.SemaphoreType.DMA],
-            anys=anys, any_outs=(1,), aliases=aliases,
+            kernel, [full, stack], 1, ins + [centres], arr * 6, arr * 16,
+            scratch=[
+                pltpu.VMEM((subs, rows, cols), F32),
+                pltpu.VMEM((rows, cols), F32),
+                pltpu.SemaphoreType.DMA((wide * (subs + 1),)),
+            ],
+            anys=(len(ins),), any_outs=(0, 1), aliases={len(ins): 1},
         )
 
-    first = call(
+    sums = call(
         functools.partial(first_kernel, chunk, wide), [half, part, part], 1, [info, multipliers],
         arr * 2, arr * 8,
     )
-    direct, alpha, pieces = search(*first, False)
-
-    def rest(packed, direct, alpha, pieces):
-        alphas = [alpha[0]]
+    found, _, tables = search(0, [None, *sums], None, False, tables)
+
+    def rest(packed, tables, found):
+        alphas = [found[1][0]]
         lam, centres = multipliers, None
-        for step in range(ITERS - 1):
-            lam, centres, *sums = update(step, lam, direct, alpha, pieces, centres)
-            direct, alpha, pieces = search(*sums, packed)
-            alphas.append(alpha[0])
-        lam, centres = update(ITERS - 1, lam, direct, alpha, pieces, centres)
+        for step in range(1, ITERS):
+            lam, *sums = update(step - 1, lam, found, centres)
+            found, centres, _ = search(step, sums, centres, packed, tables)
+            alphas.append(found[1][0])
+        lam, centres = update(ITERS - 1, lam, found, centres)
         return lam, jnp.stack(alphas), centres
 
     return lax.cond(
-        alpha[1, 0] <= cap,
+        found[1][1, 0] <= 0,
         functools.partial(rest, True),
         functools.partial(rest, False),
-        direct, alpha, pieces,
+        tables, found,
     )
 
 

time: 223 us -> 217 us (0.973)
  waiting for transfers between devices: 116 us -> 88.2 us
  starting transfers between devices: 72.4 us -> 92.4 us
    ppermute x66, waiting for transfers between devices: 116 us -> 82.8 us  [swap(): return lax.ppermute(x, axis, [(i, i ^ mask) for i in range(n)])]
    ppermute x4 -> x6, starting transfers between devices: 5.84 us -> 23.2 us  [the longest x1 16 us: body(): lax.ppermute(side, 'eight', pairs_a)]
    ppermute x4 -> x6, waiting for transfers between devices: 0.01 us -> 5.41 us  [the longest x1 3.84 us: body(): lax.ppermute(side, 'wide', away)]
    ppermute x66, starting transfers between devices: 60.4 us -> 63.7 us  [swap(): return lax.ppermute(x, axis, [(i, i ^ mask) for i in range(n)])]
  transfers between devices with their start and end apart: 76 -> 78, of which waited for: 34 -> 35; matrix products, arithmetic and copies ran while one was open for 1% -> 0% of each run, Pallas kernels for 4% -> 4%
where the time goes in v1:
time: 217 us
  starting transfers between devices  92.4 us (43%)
  waiting for transfers between devices  88.2 us (41%)
  Pallas kernels  30.7 us (14%)
  local copies, waits for them, and re-layouts  2.95 us (1%)
    ppermute x66, waiting for transfers between devices, swap(): return lax.ppermute(x, axis, [(i, i ^ mask) for i in range(n)])  82.8 us
    ppermute x66, starting transfers between devices, swap(): return lax.ppermute(x, axis, [(i, i ^ mask) for i in range(n)])  63.7 us
    pallas_call x25, Pallas kernels, call(): pl.pallas_call(kernel, out_shape=outs, in_specs=[SMEM if i < n_smem else...  30.7 us
    ppermute x1, starting transfers between devices, body(): lax.ppermute(side, 'eight', pairs_a)  16 us
    ppermute x3, starting transfers between devices, search(): off = lax.ppermute(sends[3] if packed else disp, 'wide', away)  6.5 us
  transfers between devices with their start and end apart: 78, of which 35 were waited for; matrix products, arithmetic and copies ran while one was open for 0% of the time, Pallas kernels for 4%

profile of v1, /device:TPU:0, one launch (start us, length us, event | category | flops | bytes accessed | tf_op | source)
XLA Modules:
  0.0 216.8 jit_solution(15964883051609001114)
XLA Ops:
  0.7 1.9 shard_map.96
  3.3 3.9 %shard_map.98 = (bf16[2,1024,256]{2,1,0:T(8,128)(2,1)S(1)}, bf16[1024,256]{1,0:T(8,128)(2,1)S(1)}, bf16[1024,256]{1,0:T(8,128)(2,1)S(1)}) custom-call(s32[2]{0:T(128)S(1)} %pad_add_fusion.info, bf16[2,1024,256]{2,1,0:T(8,128)(2,1)S(1)} %get-tuple-element.280.refs_0_, bf16[2,1024,1024]{2,1,0:T(8,128)(2,1)} %refs_1_.1), custom_call_target="tpu_custom_call" | custom-call | flops 1073741824 | bytes 7340032 | tf_op jit(solution)/shard_map/pallas_call | solution.py:21
  7.2 3.7 %collective-permute-start.102 = (bf16[2,1024,256]{2,1,0:T(8,128)(2,1)S(1)}, bf16[2,1024,256]{2,1,0:T(8,128)(2,1)S(1)}, u32[]{:S(2)}, u32[]{:S(2)}) collective-permute-start(bf16[2,1024,256]{2,1,0:T(8,128)(2,1)S(1)} %get-tuple-element.284.disp_ref), channel_id=1, source_target_pairs={{0,28},{4,8},{8,4},{12,16},{16,12},{20,24},{24,20},{28,0},{1,29},{... | collective-permute-start | bytes 3145736 | tf_op jit(solution)/shard_map/ppermute | solution.py:409
  10.9 1.6 collective-permute-start.103
  13.9 16.0 %collective-permute-start.109 = (s32[2,8]{1,0:T(2,128)S(1)}, s32[2,8]{1,0:T(2,128)S(1)}, u32[]{:S(2)}, u32[]{:S(2)}) collective-permute-start(s32[2,8]{1,0:T(2,128)S(1)} %copy-done.4), channel_id=1, source_target_pairs={{0,1},{1,0},{2,3},{3,2},{4,5},{5,4},{6,7},{7,6},{8,9},{9,8},{10,11... | collective-permute-start | bytes 200 | tf_op jit(solution)/shard_map/ppermute | solution.py:367
  29.9 1.6 collective-permute-done.109
  31.5 4.3 %collective-permute-done.105.refs_1_ = bf16[128,256]{1,0:T(8,128)(2,1)S(1)} collective-permute-done((bf16[128,256]{1,0:T(8,128)(2,1)S(1)}, bf16[128,256]{1,0:T(8,128)(2,1)S(1)}, u32[]{:S(2)}, u32[]{:S(2)}) %collective-permute-start.105) | collective-permute-done | bytes 65568 | tf_op jit(solution)/shard_map/ppermute | solution.py:309
  36.6 3.4 %collective-permute-done.106.refs_2_ = bf16[128,256]{1,0:T(8,128)(2,1)S(1)} collective-permute-done((bf16[128,256]{1,0:T(8,128)(2,1)S(1)}, bf16[128,256]{1,0:T(8,128)(2,1)S(1)}, u32[]{:S(2)}, u32[]{:S(2)}) %collective-permute-start.106) | collective-permute-done | bytes 65568 | tf_op jit(solution)/shard_map/ppermute | solution.py:309
  40.0 1.8 collective-permute-start.107
  41.8 3.4 %collective-permute-done.107.refs_3_ = bf16[128,256]{1,0:T(8,128)(2,1)S(1)} collective-permute-done((bf16[128,256]{1,0:T(8,128)(2,1)S(1)}, bf16[128,256]{1,0:T(8,128)(2,1)S(1)}, u32[]{:S(2)}, u32[]{:S(2)}) %collective-permute-start.107) | collective-permute-done | bytes 65568 | tf_op jit(solution)/shard_map/ppermute | solution.py:309
  45.2 3.8 %collective-permute-done.108 = s32[2,8]{1,0:T(2,128)S(1)} collective-permute-done((s32[2,8]{1,0:T(2,128)S(1)}, s32[2,8]{1,0:T(2,128)S(1)}, u32[]{:S(2)}, u32[]{:S(2)}) %collective-permute-start.108) | collective-permute-done | bytes 96 | tf_op jit(solution)/shard_map/ppermute | solution.py:366
  49.1 4.0 %shard_map.100 = (bf16[2,1024,256]{2,1,0:T(8,128)(2,1)S(1)}, bf16[528,256]{1,0:T(8,128)(2,1)S(1)}, bf16[528,256]{1,0:T(8,128)(2,1)S(1)}) custom-call(s32[2]{0:T(128)S(1)} %pad_add_fusion.info, s32[2,8]{1,0:T(2,128)S(1)} %copy-done.4, s32[2]{0:T(128)S(1)} %copy-done.6, f32[2,1024,256]{2,1,0:T(8,128)S(1)} %copy-done.2, ...), custom_call_target="tpu_custom_call" | custom-call | flops 2147483648 | bytes 12582912 | tf_op jit(solution)/shard_map/pallas_call | solution.py:21
  56.4 2.1 collective-permute-start.114
  58.5 2.9 %collective-permute-start.120 = (bf16[128,256]{1,0:T(8,128)(2,1)S(1)}, bf16[128,256]{1,0:T(8,128)(2,1)S(1)}, u32[]{:S(2)}, u32[]{:S(2)}) collective-permute-start(bf16[128,256]{1,0:T(8,128)(2,1)S(1)} %shard_map.99.after_ref.refs_4_), channel_id=1, source_target_pairs={{0,3},{1,2},{2,1},{3,0},{4,7},{5,6},{6,5},{7,4},{8,11},{9,10},{10,... | collective-permute-start | bytes 196616 | tf_op jit(solution)/shard_map/ppermute | solution.py:309
  61.7 3.5 %collective-permute-start.117 = (bf16[144,256]{1,0:T(8,128)(2,1)S(1)}, bf16[144,256]{1,0:T(8,128)(2,1)S(1)}, u32[]{:S(2)}, u32[]{:S(2)}) collective-permute-start(bf16[144,256]{1,0:T(8,128)(2,1)S(1)} %shard_map.102.refs_0_), channel_id=1, source_target_pairs={{0,3},{1,2},{2,1},{3,0},{4,7},{5,6},{6,5},{7,4},{8,11},{9,10},{10,... | collective-permute-start | bytes 221192 | tf_op jit(solution)/shard_map/ppermute | solution.py:309
  66.1 2.0 collective-permute-start.119
  68.1 2.0 collective-permute-start.118
  70.2 3.5 %collective-permute-done.119.refs_6_ = bf16[128,256]{1,0:T(8,128)(2,1)S(1)} collective-permute-done((bf16[128,256]{1,0:T(8,128)(2,1)S(1)}, bf16[128,256]{1,0:T(8,128)(2,1)S(1)}, u32[]{:S(2)}, u32[]{:S(2)}) %collective-permute-start.119) | collective-permute-done | bytes 65568 | tf_op jit(solution)/shard_map/ppermute | solution.py:309
  73.8 2.4 %collective-permute-start.126 = (bf16[128,256]{1,0:T(8,128)(2,1)S(1)}, bf16[128,256]{1,0:T(8,128)(2,1)S(1)}, u32[]{:S(2)}, u32[]{:S(2)}) collective-permute-start(bf16[128,256]{1,0:T(8,128)(2,1)S(1)} %get-tuple-element.300), channel_id=1, source_target_pairs={{0,24},{4,28},{8,16},{12,20},{16,8},{20,12},{24,0},{28,4},{1,25},{... | collective-permute-start | bytes 196616 | tf_op jit(solution)/shard_map/ppermute | solution.py:309
  77.4 1.8 collective-permute-done.126
  83.1 132.3 %conditional.1 = (f32[2,1024,256]{2,1,0:T(8,128)S(1)}, f32[3,1024,256]{2,1,0:T(8,128)}, f32[3,256]{1,0:T(4,128)S(1)}) conditional(s32[]{:T(128)} %bitcast.8, (f32[3,2,1024,128]{3,2,1,0:T(8,128)S(1)}, s32[2]{0:T(128)S(1)}, f32[2,1024,256]{2,1,0:T(8,128)S(1)}, bf16[2,1024,256]{2,1,0:T(8,128)(2,1)S(1)}, f32[8,256]{1,0:T(8,128)S(1)}, ...), branch_computations={%region_0.1_spmd, %region_1.2_spmd} | conditional | flops 6454117888 | bytes 116865000 | solution.py:464
  85.2 2.4 %branch_1_fun.19 = (bf16[2,1024,256]{2,1,0:T(8,128)(2,1)S(1)}, bf16[6,128,256]{2,1,0:T(8,128)(2,1)S(1)}, bf16[6,128,256]{2,1,0:T(8,128)(2,1)S(1)}, bf16[9,128,256]{2,1,0:T(8,128)(2,1)S(1)}, f32[3,1024,256]{2,1,0:T(8,128)}) custom-call(s32[2]{0:T(128)S(1)} %get-tuple-element.156.info, s32[2,8]{1,0:T(2,128)S(1)} %get-tuple-element.179.refs_0_, ...), custom_call_target="tpu_custom_call" | custom-call | flops 1073741824 | bytes 7340032 | tf_op jit(solution)/shard_map/cond/branch_1_fun/pallas_call | solution.py:21
  91.6 13.5 %collective-permute-done.55.refs_1_ = bf16[128,256]{1,0:T(8,128)(2,1)S(1)} collective-permute-done((bf16[128,256]{1,0:T(8,128)(2,1)S(1)}, bf16[128,256]{1,0:T(8,128)(2,1)S(1)}, u32[]{:S(2)}, u32[]{:S(2)}) %collective-permute-start.55) | collective-permute-done | bytes 65568 | tf_op jit(solution)/shard_map/cond/branch_1_fun/ppermute | solution.py:309
  106.3 3.0 %collective-permute-done.56.refs_2_ = bf16[128,256]{1,0:T(8,128)(2,1)S(1)} collective-permute-done((bf16[128,256]{1,0:T(8,128)(2,1)S(1)}, bf16[128,256]{1,0:T(8,128)(2,1)S(1)}, u32[]{:S(2)}, u32[]{:S(2)}) %collective-permute-start.56) | collective-permute-done | bytes 65568 | tf_op jit(solution)/shard_map/cond/branch_1_fun/ppermute | solution.py:309
  110.6 4.0 %collective-permute-done.57.refs_3_ = bf16[128,256]{1,0:T(8,128)(2,1)S(1)} collective-permute-done((bf16[128,256]{1,0:T(8,128)(2,1)S(1)}, bf16[128,256]{1,0:T(8,128)(2,1)S(1)}, u32[]{:S(2)}, u32[]{:S(2)}) %collective-permute-start.57) | collective-permute-done | bytes 65568 | tf_op jit(solution)/shard_map/cond/branch_1_fun/ppermute | solution.py:309
  114.6 4.1 %branch_1_fun.21 = (bf16[2,1024,256]{2,1,0:T(8,128)(2,1)S(1)}, bf16[528,256]{1,0:T(8,128)(2,1)S(1)}, bf16[528,256]{1,0:T(8,128)(2,1)S(1)}) custom-call(s32[2]{0:T(128)S(1)} %get-tuple-element.156.info, s32[2,8]{1,0:T(2,128)S(1)} %get-tuple-element.170.side, s32[2]{0:T(128)S(1)} %get-tuple-element.171.powers, f32[2,1024,256]{2,1,0:T(8,128)S(1)} %get-tuple-element.172.gap_ref, ...), custom_call_target="tpu_custom_call" | custom-call | flops 2147483648 | bytes 12582912 | tf_op jit(solution)/shard_map/cond/branch_1_fun/pallas_call | solution.py:21
  118.8 1.5 collective-permute-done.58.refs_1_
  122.2 1.7 collective-permute-start.61
  123.9 2.2 collective-permute-start.67
  127.5 3.0 %collective-permute-start.64 = (bf16[144,256]{1,0:T(8,128)(2,1)S(1)}, bf16[144,256]{1,0:T(8,128)(2,1)S(1)}, u32[]{:S(2)}, u32[]{:S(2)}) collective-permute-start(bf16[144,256]{1,0:T(8,128)(2,1)S(1)} %branch_1_fun.23.refs_0_), channel_id=1, source_target_pairs={{0,3},{1,2},{2,1},{3,0},{4,7},{5,6},{6,5},{7,4},{8,11},{9,10},{10,... | collective-permute-start | bytes 221192 | tf_op jit(solution)/shard_map/cond/branch_1_fun/ppermute | solution.py:309
  133.4 2.0 collective-permute-start.65
  135.4 3.4 %collective-permute-done.66.refs_6_ = bf16[128,256]{1,0:T(8,128)(2,1)S(1)} collective-permute-done((bf16[128,256]{1,0:T(8,128)(2,1)S(1)}, bf16[128,256]{1,0:T(8,128)(2,1)S(1)}, u32[]{:S(2)}, u32[]{:S(2)}) %collective-permute-start.66) | collective-permute-done | bytes 65568 | tf_op jit(solution)/shard_map/cond/branch_1_fun/ppermute | solution.py:309
  138.9 1.7 collective-permute-start.73
  142.5 1.8 collective-permute-done.73.refs_6_
  148.4 2.4 %branch_1_fun.27 = (bf16[2,1024,256]{2,1,0:T(8,128)(2,1)S(1)}, bf16[6,128,256]{2,1,0:T(8,128)(2,1)S(1)}, bf16[6,128,256]{2,1,0:T(8,128)(2,1)S(1)}, bf16[9,128,256]{2,1,0:T(8,128)(2,1)S(1)}, f32[3,1024,256]{2,1,0:T(8,128)}) custom-call(s32[2]{0:T(128)S(1)} %get-tuple-element.156.info, ...), custom_call_target="tpu_custom_call", output_to_operand_aliasing={{4}: (7, {})} | custom-call | flops 1073741824 | bytes 7340032 | tf_op jit(solution)/shard_map/cond/branch_1_fun/pallas_call | solution.py:21
  154.8 13.7 %collective-permute-done.80.refs_1_ = bf16[128,256]{1,0:T(8,128)(2,1)S(1)} collective-permute-done((bf16[128,256]{1,0:T(8,128)(2,1)S(1)}, bf16[128,256]{1,0:T(8,128)(2,1)S(1)}, u32[]{:S(2)}, u32[]{:S(2)}) %collective-permute-start.80) | collective-permute-done | bytes 65568 | tf_op jit(solution)/shard_map/cond/branch_1_fun/ppermute | solution.py:309
  169.8 2.9 %collective-permute-done.81.refs_2_ = bf16[128,256]{1,0:T(8,128)(2,1)S(1)} collective-permute-done((bf16[128,256]{1,0:T(8,128)(2,1)S(1)}, bf16[128,256]{1,0:T(8,128)(2,1)S(1)}, u32[]{:S(2)}, u32[]{:S(2)}) %collective-permute-start.81) | collective-permute-done | bytes 65568 | tf_op jit(solution)/shard_map/cond/branch_1_fun/ppermute | solution.py:309
  174.2 3.7 %collective-permute-done.82.refs_3_ = bf16[128,256]{1,0:T(8,128)(2,1)S(1)} collective-permute-done((bf16[128,256]{1,0:T(8,128)(2,1)S(1)}, bf16[128,256]{1,0:T(8,128)(2,1)S(1)}, u32[]{:S(2)}, u32[]{:S(2)}) %collective-permute-start.82) | collective-permute-done | bytes 65568 | tf_op jit(solution)/shard_map/cond/branch_1_fun/ppermute | solution.py:309
  178.0 4.3 %branch_1_fun.29 = (bf16[2,1024,256]{2,1,0:T(8,128)(2,1)S(1)}, bf16[528,256]{1,0:T(8,128)(2,1)S(1)}, bf16[528,256]{1,0:T(8,128)(2,1)S(1)}) custom-call(s32[2]{0:T(128)S(1)} %get-tuple-element.156.info, s32[2,8]{1,0:T(2,128)S(1)} %get-tuple-element.170.side, s32[2]{0:T(128)S(1)} %get-tuple-element.171.powers, f32[2,1024,256]{2,1,0:T(8,128)S(1)} %get-tuple-element.172.gap_ref, ...), custom_call_target="tpu_custom_call" | custom-call | flops 2147483648 | bytes 12582912 | tf_op jit(solution)/shard_map/cond/branch_1_fun/pallas_call | solution.py:21
  182.4 1.5 collective-permute-done.83.refs_1_
  186.1 1.5 collective-permute-start.86
  187.6 1.9 collective-permute-start.92
  191.4 2.4 %collective-permute-start.89 = (bf16[144,256]{1,0:T(8,128)(2,1)S(1)}, bf16[144,256]{1,0:T(8,128)(2,1)S(1)}, u32[]{:S(2)}, u32[]{:S(2)}) collective-permute-start(bf16[144,256]{1,0:T(8,128)(2,1)S(1)} %branch_1_fun.31.refs_0_), channel_id=1, source_target_pairs={{0,3},{1,2},{2,1},{3,0},{4,7},{5,6},{6,5},{7,4},{8,11},{9,10},{10,... | collective-permute-start | bytes 221192 | tf_op jit(solution)/shard_map/cond/branch_1_fun/ppermute | solution.py:309
  193.8 2.1 collective-permute-start.87
  196.7 2.0 collective-permute-start.90
  198.7 4.0 %collective-permute-done.91.refs_6_ = bf16[128,256]{1,0:T(8,128)(2,1)S(1)} collective-permute-done((bf16[128,256]{1,0:T(8,128)(2,1)S(1)}, bf16[128,256]{1,0:T(8,128)(2,1)S(1)}, u32[]{:S(2)}, u32[]{:S(2)}) %collective-permute-start.91) | collective-permute-done | bytes 65568 | tf_op jit(solution)/shard_map/cond/branch_1_fun/ppermute | solution.py:309
  206.4 1.7 collective-permute-done.98.refs_6_
  210.6 4.5 %branch_1_fun.33 = (f32[2,1024,256]{2,1,0:T(8,128)S(1)}, f32[3,1024,256]{2,1,0:T(8,128)}) custom-call(s32[2]{0:T(128)S(1)} %get-tuple-element.156.info, f32[2,1024,256]{2,1,0:T(8,128)S(1)} %get-tuple-element.207.lam_ref, bf16[2,1024,256]{2,1,0:T(8,128)(2,1)S(1)} %get-tuple-element.229.dir_ref, ...), custom_call_target="tpu_custom_call", output_to_operand_aliasing={{1}: (13, {})} | custom-call | flops 3145728 | bytes 8388608 | tf_op jit(solution)/shard_map/cond/branch_1_fun/pallas_call | solution.py:21
  (161 shorter events, 52.0 us)
Async XLA Ops:
  7.2 41.8 %collective-permute-start.102 = (bf16[2,1024,256]{2,1,0:T(8,128)(2,1)S(1)}, bf16[2,1024,256]{2,1,0:T(8,128)(2,1)S(1)}, u32[]{:S(2)}, u32[]{:S(2)}) collective-permute-start(bf16[2,1024,256]{2,1,0:T(8,128)(2,1)S(1)} %get-tuple-element.284.disp_ref), channel_id=1, source_target_pairs={{0,28},{4,8},{8,4},{12,16},{16,12},{20,24},{24,20},{28,0},{1,29},{... | collective-permute-start | bytes 3145736 | tf_op jit(solution)/shard_map/ppermute | solution.py:409
  10.9 38.1 %collective-permute-start.101 = (bf16[2,1024,256]{2,1,0:T(8,128)(2,1)S(1)}, bf16[2,1024,256]{2,1,0:T(8,128)(2,1)S(1)}, u32[]{:S(2)}, u32[]{:S(2)}) collective-permute-start(bf16[2,1024,256]{2,1,0:T(8,128)(2,1)S(1)} %get-tuple-element.284.disp_ref), channel_id=1, source_target_pairs={{0,4},{4,0},{8,12},{12,8},{16,20},{20,16},{24,28},{28,24},{1,5},{5... | collective-permute-start | bytes 3145736 | tf_op jit(solution)/shard_map/ppermute | solution.py:309
  10.9 38.1 %collective-permute-start.103 = (bf16[1024,256]{1,0:T(8,128)(2,1)S(1)}, bf16[1024,256]{1,0:T(8,128)(2,1)S(1)}, u32[]{:S(2)}, u32[]{:S(2)}) collective-permute-start(bf16[1024,256]{1,0:T(8,128)(2,1)S(1)} %get-tuple-element.285), channel_id=1, source_target_pairs={{0,1},{1,0},{2,3},{3,2},{4,5},{5,4},{6,7},{7,6},{8,9},{9,8},{10,11... | collective-permute-start | bytes 1572872 | tf_op jit(solution)/shard_map/ppermute | solution.py:410
  12.5 36.6 %collective-permute-start.104 = (bf16[1024,256]{1,0:T(8,128)(2,1)S(1)}, bf16[1024,256]{1,0:T(8,128)(2,1)S(1)}, u32[]{:S(2)}, u32[]{:S(2)}) collective-permute-start(bf16[1024,256]{1,0:T(8,128)(2,1)S(1)} %get-tuple-element.286), channel_id=1, source_target_pairs={{1,2},{2,1},{5,6},{6,5},{9,10},{10,9},{13,14},{14,13},{17,18},{18,... | collective-permute-start | bytes 1572872 | tf_op jit(solution)/shard_map/ppermute | solution.py:411
  13.9 17.6 %collective-permute-start.109 = (s32[2,8]{1,0:T(2,128)S(1)}, s32[2,8]{1,0:T(2,128)S(1)}, u32[]{:S(2)}, u32[]{:S(2)}) collective-permute-start(s32[2,8]{1,0:T(2,128)S(1)} %copy-done.4), channel_id=1, source_target_pairs={{0,1},{1,0},{2,3},{3,2},{4,5},{5,4},{6,7},{7,6},{8,9},{9,8},{10,11... | collective-permute-start | bytes 200 | tf_op jit(solution)/shard_map/ppermute | solution.py:367
  40.0 5.2 %collective-permute-start.107 = (bf16[128,256]{1,0:T(8,128)(2,1)S(1)}, bf16[128,256]{1,0:T(8,128)(2,1)S(1)}, u32[]{:S(2)}, u32[]{:S(2)}) collective-permute-start(bf16[128,256]{1,0:T(8,128)(2,1)S(1)} %get-tuple-element.290), channel_id=1, source_target_pairs={{0,24},{4,28},{8,16},{12,20},{16,8},{20,12},{24,0},{28,4},{1,25},{... | collective-permute-start | bytes 196616 | tf_op jit(solution)/shard_map/ppermute | solution.py:309
  54.9 6.4 %collective-permute-start.112 = (bf16[144,256]{1,0:T(8,128)(2,1)S(1)}, bf16[144,256]{1,0:T(8,128)(2,1)S(1)}, u32[]{:S(2)}, u32[]{:S(2)}) collective-permute-start(bf16[144,256]{1,0:T(8,128)(2,1)S(1)} %get-tuple-element.295), channel_id=1, source_target_pairs={{0,8},{4,12},{8,0},{12,4},{16,24},{20,28},{24,16},{28,20},{1,9},{5... | collective-permute-start | bytes 221192 | tf_op jit(solution)/shard_map/ppermute | solution.py:309
  55.0 6.4 %collective-permute-start.113 = (bf16[144,256]{1,0:T(8,128)(2,1)S(1)}, bf16[144,256]{1,0:T(8,128)(2,1)S(1)}, u32[]{:S(2)}, u32[]{:S(2)}) collective-permute-start(bf16[144,256]{1,0:T(8,128)(2,1)S(1)} %get-tuple-element.296), channel_id=1, source_target_pairs={{0,16},{4,20},{8,24},{12,28},{16,0},{20,4},{24,8},{28,12},{1,17},{... | collective-permute-start | bytes 221192 | tf_op jit(solution)/shard_map/ppermute | solution.py:309
  56.4 5.3 %collective-permute-start.114 = (bf16[144,256]{1,0:T(8,128)(2,1)S(1)}, bf16[144,256]{1,0:T(8,128)(2,1)S(1)}, u32[]{:S(2)}, u32[]{:S(2)}) collective-permute-start(bf16[144,256]{1,0:T(8,128)(2,1)S(1)} %get-tuple-element.297), channel_id=1, source_target_pairs={{0,24},{4,28},{8,16},{12,20},{16,8},{20,12},{24,0},{28,4},{1,25},{... | collective-permute-start | bytes 221192 | tf_op jit(solution)/shard_map/ppermute | solution.py:309
  58.5 9.6 %collective-permute-start.120 = (bf16[128,256]{1,0:T(8,128)(2,1)S(1)}, bf16[128,256]{1,0:T(8,128)(2,1)S(1)}, u32[]{:S(2)}, u32[]{:S(2)}) collective-permute-start(bf16[128,256]{1,0:T(8,128)(2,1)S(1)} %shard_map.99.after_ref.refs_4_), channel_id=1, source_target_pairs={{0,3},{1,2},{2,1},{3,0},{4,7},{5,6},{6,5},{7,4},{8,11},{9,10},{10,... | collective-permute-start | bytes 196616 | tf_op jit(solution)/shard_map/ppermute | solution.py:309
  61.7 12.0 %collective-permute-start.117 = (bf16[144,256]{1,0:T(8,128)(2,1)S(1)}, bf16[144,256]{1,0:T(8,128)(2,1)S(1)}, u32[]{:S(2)}, u32[]{:S(2)}) collective-permute-start(bf16[144,256]{1,0:T(8,128)(2,1)S(1)} %shard_map.102.refs_0_), channel_id=1, source_target_pairs={{0,3},{1,2},{2,1},{3,0},{4,7},{5,6},{6,5},{7,4},{8,11},{9,10},{10,... | collective-permute-start | bytes 221192 | tf_op jit(solution)/shard_map/ppermute | solution.py:309
  65.2 8.5 %collective-permute-start.116 = (bf16[144,256]{1,0:T(8,128)(2,1)S(1)}, bf16[144,256]{1,0:T(8,128)(2,1)S(1)}, u32[]{:S(2)}, u32[]{:S(2)}) collective-permute-start(bf16[144,256]{1,0:T(8,128)(2,1)S(1)} %shard_map.102.refs_0_), channel_id=1, source_target_pairs={{0,2},{1,3},{2,0},{3,1},{4,6},{5,7},{6,4},{7,5},{8,10},{9,11},{10,... | collective-permute-start | bytes 221192 | tf_op jit(solution)/shard_map/ppermute | solution.py:309
  65.2 8.5 %collective-permute-start.115 = (bf16[144,256]{1,0:T(8,128)(2,1)S(1)}, bf16[144,256]{1,0:T(8,128)(2,1)S(1)}, u32[]{:S(2)}, u32[]{:S(2)}) collective-permute-start(bf16[144,256]{1,0:T(8,128)(2,1)S(1)} %shard_map.102.refs_0_), channel_id=1, source_target_pairs={{0,1},{1,0},{2,3},{3,2},{4,5},{5,4},{6,7},{7,6},{8,9},{9,8},{10,11... | collective-permute-start | bytes 221192 | tf_op jit(solution)/shard_map/ppermute | solution.py:309
  66.1 7.6 %collective-permute-start.119 = (bf16[128,256]{1,0:T(8,128)(2,1)S(1)}, bf16[128,256]{1,0:T(8,128)(2,1)S(1)}, u32[]{:S(2)}, u32[]{:S(2)}) collective-permute-start(bf16[128,256]{1,0:T(8,128)(2,1)S(1)} %shard_map.99.after_ref.refs_4_), channel_id=1, source_target_pairs={{0,2},{1,3},{2,0},{3,1},{4,6},{5,7},{6,4},{7,5},{8,10},{9,11},{10,... | collective-permute-start | bytes 196616 | tf_op jit(solution)/shard_map/ppermute | solution.py:309
  68.1 5.6 %collective-permute-start.118 = (bf16[128,256]{1,0:T(8,128)(2,1)S(1)}, bf16[128,256]{1,0:T(8,128)(2,1)S(1)}, u32[]{:S(2)}, u32[]{:S(2)}) collective-permute-start(bf16[128,256]{1,0:T(8,128)(2,1)S(1)} %shard_map.99.after_ref.refs_4_), channel_id=1, source_target_pairs={{0,1},{1,0},{2,3},{3,2},{4,5},{5,4},{6,7},{7,6},{8,9},{9,8},{10,11... | collective-permute-start | bytes 196616 | tf_op jit(solution)/shard_map/ppermute | solution.py:309
  73.8 5.3 %collective-permute-start.126 = (bf16[128,256]{1,0:T(8,128)(2,1)S(1)}, bf16[128,256]{1,0:T(8,128)(2,1)S(1)}, u32[]{:S(2)}, u32[]{:S(2)}) collective-permute-start(bf16[128,256]{1,0:T(8,128)(2,1)S(1)} %get-tuple-element.300), channel_id=1, source_target_pairs={{0,24},{4,28},{8,16},{12,20},{16,8},{20,12},{24,0},{28,4},{1,25},{... | collective-permute-start | bytes 196616 | tf_op jit(solution)/shard_map/ppermute | solution.py:309
  87.7 26.9 %collective-permute-start.51 = (bf16[2,1024,256]{2,1,0:T(8,128)(2,1)S(1)}, bf16[2,1024,256]{2,1,0:T(8,128)(2,1)S(1)}, u32[]{:S(2)}, u32[]{:S(2)}) collective-permute-start(bf16[2,1024,256]{2,1,0:T(8,128)(2,1)S(1)} %get-tuple-element.189.disp_ref), channel_id=1, source_target_pairs={{0,4},{4,0},{8,12},{12,8},{16,20},{20,16},{24,28},{28,24},{1,5},{5... | collective-permute-start | bytes 3145736 | tf_op jit(solution)/shard_map/cond/branch_1_fun/ppermute | solution.py:309
  87.8 26.8 %collective-permute-start.52 = (bf16[9,128,256]{2,1,0:T(8,128)(2,1)S(1)}, bf16[9,128,256]{2,1,0:T(8,128)(2,1)S(1)}, u32[]{:S(2)}, u32[]{:S(2)}) collective-permute-start(bf16[9,128,256]{2,1,0:T(8,128)(2,1)S(1)} %get-tuple-element.190), channel_id=1, source_target_pairs={{0,28},{4,8},{8,4},{12,16},{16,12},{20,24},{24,20},{28,0},{1,29},{... | collective-permute-start | bytes 1769480 | tf_op jit(solution)/shard_map/cond/branch_1_fun/ppermute | solution.py:409
  89.3 25.3 %collective-permute-start.53 = (bf16[6,128,256]{2,1,0:T(8,128)(2,1)S(1)}, bf16[6,128,256]{2,1,0:T(8,128)(2,1)S(1)}, u32[]{:S(2)}, u32[]{:S(2)}) collective-permute-start(bf16[6,128,256]{2,1,0:T(8,128)(2,1)S(1)} %get-tuple-element.191), channel_id=1, source_target_pairs={{0,1},{1,0},{2,3},{3,2},{4,5},{5,4},{6,7},{7,6},{8,9},{9,8},{10,11... | collective-permute-start | bytes 1179656 | tf_op jit(solution)/shard_map/cond/branch_1_fun/ppermute | solution.py:410
  90.1 24.5 %collective-permute-start.54 = (bf16[6,128,256]{2,1,0:T(8,128)(2,1)S(1)}, bf16[6,128,256]{2,1,0:T(8,128)(2,1)S(1)}, u32[]{:S(2)}, u32[]{:S(2)}) collective-permute-start(bf16[6,128,256]{2,1,0:T(8,128)(2,1)S(1)} %get-tuple-element.192), channel_id=1, source_target_pairs={{1,2},{2,1},{5,6},{6,5},{9,10},{10,9},{13,14},{14,13},{17,18},{18,... | collective-permute-start | bytes 1179656 | tf_op jit(solution)/shard_map/cond/branch_1_fun/ppermute | solution.py:411
  90.8 14.3 %collective-permute-start.55 = (bf16[128,256]{1,0:T(8,128)(2,1)S(1)}, bf16[128,256]{1,0:T(8,128)(2,1)S(1)}, u32[]{:S(2)}, u32[]{:S(2)}) collective-permute-start(bf16[128,256]{1,0:T(8,128)(2,1)S(1)} %get-tuple-element.195), channel_id=1, source_target_pairs={{0,8},{4,12},{8,0},{12,4},{16,24},{20,28},{24,16},{28,20},{1,9},{5... | collective-permute-start | bytes 196616 | tf_op jit(solution)/shard_map/cond/branch_1_fun/ppermute | solution.py:309
  109.4 5.2 %collective-permute-start.57 = (bf16[128,256]{1,0:T(8,128)(2,1)S(1)}, bf16[128,256]{1,0:T(8,128)(2,1)S(1)}, u32[]{:S(2)}, u32[]{:S(2)}) collective-permute-start(bf16[128,256]{1,0:T(8,128)(2,1)S(1)} %get-tuple-element.197), channel_id=1, source_target_pairs={{0,24},{4,28},{8,16},{12,20},{16,8},{20,12},{24,0},{28,4},{1,25},{... | collective-permute-start | bytes 196616 | tf_op jit(solution)/shard_map/cond/branch_1_fun/ppermute | solution.py:309
  120.4 5.7 %collective-permute-start.59 = (bf16[144,256]{1,0:T(8,128)(2,1)S(1)}, bf16[144,256]{1,0:T(8,128)(2,1)S(1)}, u32[]{:S(2)}, u32[]{:S(2)}) collective-permute-start(bf16[144,256]{1,0:T(8,128)(2,1)S(1)} %get-tuple-element.202), channel_id=1, source_target_pairs={{0,8},{4,12},{8,0},{12,4},{16,24},{20,28},{24,16},{28,20},{1,9},{5... | collective-permute-start | bytes 221192 | tf_op jit(solution)/shard_map/cond/branch_1_fun/ppermute | solution.py:309
  121.1 5.1 %collective-permute-start.60 = (bf16[144,256]{1,0:T(8,128)(2,1)S(1)}, bf16[144,256]{1,0:T(8,128)(2,1)S(1)}, u32[]{:S(2)}, u32[]{:S(2)}) collective-permute-start(bf16[144,256]{1,0:T(8,128)(2,1)S(1)} %get-tuple-element.203), channel_id=1, source_target_pairs={{0,16},{4,20},{8,24},{12,28},{16,0},{20,4},{24,8},{28,12},{1,17},{... | collective-permute-start | bytes 221192 | tf_op jit(solution)/shard_map/cond/branch_1_fun/ppermute | solution.py:309
  122.2 5.3 %collective-permute-start.61 = (bf16[144,256]{1,0:T(8,128)(2,1)S(1)}, bf16[144,256]{1,0:T(8,128)(2,1)S(1)}, u32[]{:S(2)}, u32[]{:S(2)}) collective-permute-start(bf16[144,256]{1,0:T(8,128)(2,1)S(1)} %get-tuple-element.204), channel_id=1, source_target_pairs={{0,24},{4,28},{8,16},{12,20},{16,8},{20,12},{24,0},{28,4},{1,25},{... | collective-permute-start | bytes 221192 | tf_op jit(solution)/shard_map/cond/branch_1_fun/ppermute | solution.py:309
  123.9 9.5 %collective-permute-start.67 = (bf16[128,256]{1,0:T(8,128)(2,1)S(1)}, bf16[128,256]{1,0:T(8,128)(2,1)S(1)}, u32[]{:S(2)}, u32[]{:S(2)}) collective-permute-start(bf16[128,256]{1,0:T(8,128)(2,1)S(1)} %branch_1_fun.20.after_ref.refs_4_), channel_id=1, source_target_pairs={{0,3},{1,2},{2,1},{3,0},{4,7},{5,6},{6,5},{7,4},{8,11},{9,10},{10,... | collective-permute-start | bytes 196616 | tf_op jit(solution)/shard_map/cond/branch_1_fun/ppermute | solution.py:309
  127.5 11.3 %collective-permute-start.64 = (bf16[144,256]{1,0:T(8,128)(2,1)S(1)}, bf16[144,256]{1,0:T(8,128)(2,1)S(1)}, u32[]{:S(2)}, u32[]{:S(2)}) collective-permute-start(bf16[144,256]{1,0:T(8,128)(2,1)S(1)} %branch_1_fun.23.refs_0_), channel_id=1, source_target_pairs={{0,3},{1,2},{2,1},{3,0},{4,7},{5,6},{6,5},{7,4},{8,11},{9,10},{10,... | collective-permute-start | bytes 221192 | tf_op jit(solution)/shard_map/cond/branch_1_fun/ppermute | solution.py:309
  130.5 8.3 %collective-permute-start.63 = (bf16[144,256]{1,0:T(8,128)(2,1)S(1)}, bf16[144,256]{1,0:T(8,128)(2,1)S(1)}, u32[]{:S(2)}, u32[]{:S(2)}) collective-permute-start(bf16[144,256]{1,0:T(8,128)(2,1)S(1)} %branch_1_fun.23.refs_0_), channel_id=1, source_target_pairs={{0,2},{1,3},{2,0},{3,1},{4,6},{5,7},{6,4},{7,5},{8,10},{9,11},{10,... | collective-permute-start | bytes 221192 | tf_op jit(solution)/shard_map/cond/branch_1_fun/ppermute | solution.py:309
  130.5 8.3 %collective-permute-start.62 = (bf16[144,256]{1,0:T(8,128)(2,1)S(1)}, bf16[144,256]{1,0:T(8,128)(2,1)S(1)}, u32[]{:S(2)}, u32[]{:S(2)}) collective-permute-start(bf16[144,256]{1,0:T(8,128)(2,1)S(1)} %branch_1_fun.23.refs_0_), channel_id=1, source_target_pairs={{0,1},{1,0},{2,3},{3,2},{4,5},{5,4},{6,7},{7,6},{8,9},{9,8},{10,11... | collective-permute-start | bytes 221192 | tf_op jit(solution)/shard_map/cond/branch_1_fun/ppermute | solution.py:309
  132.0 6.9 %collective-permute-start.66 = (bf16[128,256]{1,0:T(8,128)(2,1)S(1)}, bf16[128,256]{1,0:T(8,128)(2,1)S(1)}, u32[]{:S(2)}, u32[]{:S(2)}) collective-permute-start(bf16[128,256]{1,0:T(8,128)(2,1)S(1)} %branch_1_fun.20.after_ref.refs_4_), channel_id=1, source_target_pairs={{0,2},{1,3},{2,0},{3,1},{4,6},{5,7},{6,4},{7,5},{8,10},{9,11},{10,... | collective-permute-start | bytes 196616 | tf_op jit(solution)/shard_map/cond/branch_1_fun/ppermute | solution.py:309
  133.4 5.4 %collective-permute-start.65 = (bf16[128,256]{1,0:T(8,128)(2,1)S(1)}, bf16[128,256]{1,0:T(8,128)(2,1)S(1)}, u32[]{:S(2)}, u32[]{:S(2)}) collective-permute-start(bf16[128,256]{1,0:T(8,128)(2,1)S(1)} %branch_1_fun.20.after_ref.refs_4_), channel_id=1, source_target_pairs={{0,1},{1,0},{2,3},{3,2},{4,5},{5,4},{6,7},{7,6},{8,9},{9,8},{10,11... | collective-permute-start | bytes 196616 | tf_op jit(solution)/shard_map/cond/branch_1_fun/ppermute | solution.py:309
  138.9 5.3 %collective-permute-start.73 = (bf16[128,256]{1,0:T(8,128)(2,1)S(1)}, bf16[128,256]{1,0:T(8,128)(2,1)S(1)}, u32[]{:S(2)}, u32[]{:S(2)}) collective-permute-start(bf16[128,256]{1,0:T(8,128)(2,1)S(1)} %get-tuple-element.206.refs_0_), channel_id=1, source_target_pairs={{0,24},{4,28},{8,16},{12,20},{16,8},{20,12},{24,0},{28,4},{1,25},{... | collective-permute-start | bytes 196616 | tf_op jit(solution)/shard_map/cond/branch_1_fun/ppermute | solution.py:309
  150.9 27.1 %collective-permute-start.76 = (bf16[2,1024,256]{2,1,0:T(8,128)(2,1)S(1)}, bf16[2,1024,256]{2,1,0:T(8,128)(2,1)S(1)}, u32[]{:S(2)}, u32[]{:S(2)}) collective-permute-start(bf16[2,1024,256]{2,1,0:T(8,128)(2,1)S(1)} %get-tuple-element.221.disp_ref), channel_id=1, source_target_pairs={{0,4},{4,0},{8,12},{12,8},{16,20},{20,16},{24,28},{28,24},{1,5},{5... | collective-permute-start | bytes 3145736 | tf_op jit(solution)/shard_map/cond/branch_1_fun/ppermute | solution.py:309
  151.3 26.6 %collective-permute-start.77 = (bf16[9,128,256]{2,1,0:T(8,128)(2,1)S(1)}, bf16[9,128,256]{2,1,0:T(8,128)(2,1)S(1)}, u32[]{:S(2)}, u32[]{:S(2)}) collective-permute-start(bf16[9,128,256]{2,1,0:T(8,128)(2,1)S(1)} %get-tuple-element.222), channel_id=1, source_target_pairs={{0,28},{4,8},{8,4},{12,16},{16,12},{20,24},{24,20},{28,0},{1,29},{... | collective-permute-start | bytes 1769480 | tf_op jit(solution)/shard_map/cond/branch_1_fun/ppermute | solution.py:409
  152.7 25.3 %collective-permute-start.78 = (bf16[6,128,256]{2,1,0:T(8,128)(2,1)S(1)}, bf16[6,128,256]{2,1,0:T(8,128)(2,1)S(1)}, u32[]{:S(2)}, u32[]{:S(2)}) collective-permute-start(bf16[6,128,256]{2,1,0:T(8,128)(2,1)S(1)} %get-tuple-element.223), channel_id=1, source_target_pairs={{0,1},{1,0},{2,3},{3,2},{4,5},{5,4},{6,7},{7,6},{8,9},{9,8},{10,11... | collective-permute-start | bytes 1179656 | tf_op jit(solution)/shard_map/cond/branch_1_fun/ppermute | solution.py:410
  153.8 24.2 %collective-permute-start.79 = (bf16[6,128,256]{2,1,0:T(8,128)(2,1)S(1)}, bf16[6,128,256]{2,1,0:T(8,128)(2,1)S(1)}, u32[]{:S(2)}, u32[]{:S(2)}) collective-permute-start(bf16[6,128,256]{2,1,0:T(8,128)(2,1)S(1)} %get-tuple-element.224), channel_id=1, source_target_pairs={{1,2},{2,1},{5,6},{6,5},{9,10},{10,9},{13,14},{14,13},{17,18},{18,... | collective-permute-start | bytes 1179656 | tf_op jit(solution)/shard_map/cond/branch_1_fun/ppermute | solution.py:411
  154.5 14.0 %collective-permute-start.80 = (bf16[128,256]{1,0:T(8,128)(2,1)S(1)}, bf16[128,256]{1,0:T(8,128)(2,1)S(1)}, u32[]{:S(2)}, u32[]{:S(2)}) collective-permute-start(bf16[128,256]{1,0:T(8,128)(2,1)S(1)} %get-tuple-element.226), channel_id=1, source_target_pairs={{0,8},{4,12},{8,0},{12,4},{16,24},{20,28},{24,16},{28,20},{1,9},{5... | collective-permute-start | bytes 196616 | tf_op jit(solution)/shard_map/cond/branch_1_fun/ppermute | solution.py:309
  172.7 5.2 %collective-permute-start.82 = (bf16[128,256]{1,0:T(8,128)(2,1)S(1)}, bf16[128,256]{1,0:T(8,128)(2,1)S(1)}, u32[]{:S(2)}, u32[]{:S(2)}) collective-permute-start(bf16[128,256]{1,0:T(8,128)(2,1)S(1)} %get-tuple-element.228), channel_id=1, source_target_pairs={{0,24},{4,28},{8,16},{12,20},{16,8},{20,12},{24,0},{28,4},{1,25},{... | collective-permute-start | bytes 196616 | tf_op jit(solution)/shard_map/cond/branch_1_fun/ppermute | solution.py:309
  184.0 5.4 %collective-permute-start.84 = (bf16[144,256]{1,0:T(8,128)(2,1)S(1)}, bf16[144,256]{1,0:T(8,128)(2,1)S(1)}, u32[]{:S(2)}, u32[]{:S(2)}) collective-permute-start(bf16[144,256]{1,0:T(8,128)(2,1)S(1)} %get-tuple-element.233), channel_id=1, source_target_pairs={{0,8},{4,12},{8,0},{12,4},{16,24},{20,28},{24,16},{28,20},{1,9},{5... | collective-permute-start | bytes 221192 | tf_op jit(solution)/shard_map/cond/branch_1_fun/ppermute | solution.py:309
  184.9 5.1 %collective-permute-start.85 = (bf16[144,256]{1,0:T(8,128)(2,1)S(1)}, bf16[144,256]{1,0:T(8,128)(2,1)S(1)}, u32[]{:S(2)}, u32[]{:S(2)}) collective-permute-start(bf16[144,256]{1,0:T(8,128)(2,1)S(1)} %get-tuple-element.234), channel_id=1, source_target_pairs={{0,16},{4,20},{8,24},{12,28},{16,0},{20,4},{24,8},{28,12},{1,17},{... | collective-permute-start | bytes 221192 | tf_op jit(solution)/shard_map/cond/branch_1_fun/ppermute | solution.py:309
  186.1 5.3 %collective-permute-start.86 = (bf16[144,256]{1,0:T(8,128)(2,1)S(1)}, bf16[144,256]{1,0:T(8,128)(2,1)S(1)}, u32[]{:S(2)}, u32[]{:S(2)}) collective-permute-start(bf16[144,256]{1,0:T(8,128)(2,1)S(1)} %get-tuple-element.235), channel_id=1, source_target_pairs={{0,24},{4,28},{8,16},{12,20},{16,8},{20,12},{24,0},{28,4},{1,25},{... | collective-permute-start | bytes 221192 | tf_op jit(solution)/shard_map/cond/branch_1_fun/ppermute | solution.py:309
  187.6 9.1 %collective-permute-start.92 = (bf16[128,256]{1,0:T(8,128)(2,1)S(1)}, bf16[128,256]{1,0:T(8,128)(2,1)S(1)}, u32[]{:S(2)}, u32[]{:S(2)}) collective-permute-start(bf16[128,256]{1,0:T(8,128)(2,1)S(1)} %branch_1_fun.28.after_ref.refs_4_), channel_id=1, source_target_pairs={{0,3},{1,2},{2,1},{3,0},{4,7},{5,6},{6,5},{7,4},{8,11},{9,10},{10,... | collective-permute-start | bytes 196616 | tf_op jit(solution)/shard_map/cond/branch_1_fun/ppermute | solution.py:309
  191.4 11.3 %collective-permute-start.89 = (bf16[144,256]{1,0:T(8,128)(2,1)S(1)}, bf16[144,256]{1,0:T(8,128)(2,1)S(1)}, u32[]{:S(2)}, u32[]{:S(2)}) collective-permute-start(bf16[144,256]{1,0:T(8,128)(2,1)S(1)} %branch_1_fun.31.refs_0_), channel_id=1, source_target_pairs={{0,3},{1,2},{2,1},{3,0},{4,7},{5,6},{6,5},{7,4},{8,11},{9,10},{10,... | collective-permute-start | bytes 221192 | tf_op jit(solution)/shard_map/cond/branch_1_fun/ppermute | solution.py:309
  193.8 9.0 %collective-permute-start.88 = (bf16[144,256]{1,0:T(8,128)(2,1)S(1)}, bf16[144,256]{1,0:T(8,128)(2,1)S(1)}, u32[]{:S(2)}, u32[]{:S(2)}) collective-permute-start(bf16[144,256]{1,0:T(8,128)(2,1)S(1)} %branch_1_fun.31.refs_0_), channel_id=1, source_target_pairs={{0,2},{1,3},{2,0},{3,1},{4,6},{5,7},{6,4},{7,5},{8,10},{9,11},{10,... | collective-permute-start | bytes 221192 | tf_op jit(solution)/shard_map/cond/branch_1_fun/ppermute | solution.py:309
  193.8 9.0 %collective-permute-start.87 = (bf16[144,256]{1,0:T(8,128)(2,1)S(1)}, bf16[144,256]{1,0:T(8,128)(2,1)S(1)}, u32[]{:S(2)}, u32[]{:S(2)}) collective-permute-start(bf16[144,256]{1,0:T(8,128)(2,1)S(1)} %branch_1_fun.31.refs_0_), channel_id=1, source_target_pairs={{0,1},{1,0},{2,3},{3,2},{4,5},{5,4},{6,7},{7,6},{8,9},{9,8},{10,11... | collective-permute-start | bytes 221192 | tf_op jit(solution)/shard_map/cond/branch_1_fun/ppermute | solution.py:309
  195.8 6.9 %collective-permute-start.91 = (bf16[128,256]{1,0:T(8,128)(2,1)S(1)}, bf16[128,256]{1,0:T(8,128)(2,1)S(1)}, u32[]{:S(2)}, u32[]{:S(2)}) collective-permute-start(bf16[128,256]{1,0:T(8,128)(2,1)S(1)} %branch_1_fun.28.after_ref.refs_4_), channel_id=1, source_target_pairs={{0,2},{1,3},{2,0},{3,1},{4,6},{5,7},{6,4},{7,5},{8,10},{9,11},{10,... | collective-permute-start | bytes 196616 | tf_op jit(solution)/shard_map/cond/branch_1_fun/ppermute | solution.py:309
  196.7 6.0 %collective-permute-start.90 = (bf16[128,256]{1,0:T(8,128)(2,1)S(1)}, bf16[128,256]{1,0:T(8,128)(2,1)S(1)}, u32[]{:S(2)}, u32[]{:S(2)}) collective-permute-start(bf16[128,256]{1,0:T(8,128)(2,1)S(1)} %branch_1_fun.28.after_ref.refs_4_), channel_id=1, source_target_pairs={{0,1},{1,0},{2,3},{3,2},{4,5},{5,4},{6,7},{7,6},{8,9},{9,8},{10,11... | collective-permute-start | bytes 196616 | tf_op jit(solution)/shard_map/cond/branch_1_fun/ppermute | solution.py:309
  202.8 5.3 %collective-permute-start.98 = (bf16[128,256]{1,0:T(8,128)(2,1)S(1)}, bf16[128,256]{1,0:T(8,128)(2,1)S(1)}, u32[]{:S(2)}, u32[]{:S(2)}) collective-permute-start(bf16[128,256]{1,0:T(8,128)(2,1)S(1)} %get-tuple-element.237.refs_0_), channel_id=1, source_target_pairs={{0,24},{4,28},{8,16},{12,20},{16,8},{20,12},{24,0},{28,4},{1,25},{... | collective-permute-start | bytes 196616 | tf_op jit(solution)/shard_map/cond/branch_1_fun/ppermute | solution.py:309
  (39 other events, 340.9 us)

commit v2 on v1

--- a/solution.py
+++ b/solution.py
@@ -13,18 +13,18 @@
 F32 = jnp.float32
 BF16 = jnp.bfloat16
 VMEM = pl.BlockSpec(memory_space=pltpu.VMEM)
-ANY = pl.BlockSpec(memory_space=pl.ANY)
+HBM = pl.BlockSpec(memory_space=pltpu.HBM)
 SMEM = pl.BlockSpec(memory_space=pltpu.SMEM)
 
 
-def call(kernel, outs, n_smem, ins, flops, nbytes, scratch=(), vmem=16, anys=(), any_outs=(), aliases=None):
+def call(kernel, outs, n_smem, ins, flops, nbytes, scratch=(), vmem=16, hbm_ins=(), hbm_outs=(), aliases=None):
     return pl.pallas_call(
         kernel,
         out_shape=outs,
         in_specs=[
-            SMEM if i < n_smem else ANY if i in anys else VMEM for i in range(len(ins))
+            SMEM if i < n_smem else HBM if i in hbm_ins else VMEM for i in range(len(ins))
         ],
-        out_specs=[ANY if i in any_outs else VMEM for i in range(len(outs))],
+        out_specs=[HBM if i in hbm_outs else VMEM for i in range(len(outs))],
         scratch_shapes=list(scratch),
         input_output_aliases=aliases or {},
         compiler_params=pltpu.CompilerParams(vmem_limit_bytes=vmem << 20),
@@ -145,10 +145,14 @@
         copy.start()
     else:
         disp_ref, *outs = refs
-    for s in range(half_ref.shape[0]):
+
+    def product(s, carry):
         disp_ref[s] = jnp.dot(
             flex_ref[s], half_ref[s], preferred_element_type=F32
         ).astype(BF16)
+        return carry
+
+    lax.fori_loop(0, half_ref.shape[0], product, 0)
     send_halo(info, disp_ref, outs, tables)
     if step:
         copy.wait()
@@ -158,18 +162,13 @@
     centre_refs = refs[:wide]
     refs = refs[wide:]
     if last:
-        _, lam_out, stack_ref, new_ref, mean_ref, sems = refs
+        _, new_ref, stack_ref, mean_ref, sems = refs
     else:
         new_ref, mean_ref, half_ref, keep_ref, send_ref = refs
     w = info[0]
     subs, _, cols = lam_ref.shape
     alpha = jnp.broadcast_to(alpha_ref[0:1, :], (chunk, cols))
     copies = []
-
-    def send(src, dst):
-        copies.append(pltpu.make_async_copy(src, dst, sems.at[len(copies)]))
-        copies[-1].start()
-
     for k in range(wide):
         rows = pl.ds(pl.multiple_of(jnp.bitwise_xor(w, k) * chunk, chunk), chunk)
         centre = centre_refs[k][...].astype(F32)
@@ -181,13 +180,16 @@
             low = jnp.concatenate([low] * (cols // low.shape[1]), axis=1)
             new = jnp.maximum(trial - centre, low)
             new_ref[s, rows, :] = new
-            if last:
-                send(new_ref.at[s, rows, :], lam_out.at[s, rows, :])
-            else:
+            if not last:
                 half_ref[s, rows, :] = new.astype(BF16)
                 total = new if total is None else total + new
         if last:
-            send(mean_ref.at[rows, :], stack_ref.at[step, rows, :])
+            copies.append(
+                pltpu.make_async_copy(
+                    mean_ref.at[rows, :], stack_ref.at[step, rows, :], sems.at[k]
+                )
+            )
+            copies[-1].start()
         else:
             out = send_ref if k % 2 else keep_ref
             out[pl.ds((k // 2) * chunk, chunk), :] = total.astype(BF16)
@@ -202,8 +204,6 @@
     subs, rows_all, cols = gap_ref.shape
     blocks = side.shape[1]
     height = rows_all // blocks
-    inner = jnp.zeros((8, cols), F32)
-    square = jnp.zeros((8, cols), F32)
     counts = (jnp.int32(0),) * 3
     for s in range(subs):
 
@@ -216,7 +216,7 @@
                 value = gap_ref[s, rows, :] - (
                     disp_ref[s, rows, :].astype(F32) - source.astype(F32)
                 )
-                jump[rows, :] = value
+                jump[s, rows, :] = value
                 work[s, rows, :] = value.astype(BF16)
 
             def take(ref, slot):
@@ -244,7 +244,8 @@
 
         counts = lax.fori_loop(0, blocks, block, counts)
 
-        def level(i, carry, s=s):
+    def apply(s, sums):
+        def level(i, carry):
             work[s] = jnp.dot(
                 diri_ref[s], work[s], preferred_element_type=F32
             ).astype(BF16)
@@ -254,8 +255,14 @@
         direct = work[s]
         dir_ref[s] = direct
         dfloat = direct.astype(F32)
-        inner = inner + jnp.sum((jump[...] * dfloat).reshape(rows_all // 8, 8, cols), axis=0)
-        square = square + jnp.sum((dfloat * dfloat).reshape(rows_all // 8, 8, cols), axis=0)
+        split = (rows_all // 8, 8, cols)
+        return (
+            sums[0] + jnp.sum((jump[s] * dfloat).reshape(split), axis=0),
+            sums[1] + jnp.sum((dfloat * dfloat).reshape(split), axis=0),
+        )
+
+    zeros = jnp.zeros((8, cols), F32)
+    inner, square = lax.fori_loop(0, subs, apply, (zeros, zeros))
     n, above, below = counts
     excess = jnp.maximum(
         n - caps[0],
@@ -289,8 +296,8 @@
 
 
 def centre_kernel(chunk, ways, count, *refs):
-    dirs, lams = refs[:ways], refs[ways : 2 * ways]
-    centre_ref, alpha_ref = refs[2 * ways :]
+    dirs, lams = refs[:ways], refs[ways:-2]
+    centre_ref, alpha_ref = refs[-2:]
     rows = pl.ds(0, chunk)
     tail = pl.ds(chunk, EXTRA)
     inner, square, most = unpack_products([r[tail, :] for r in dirs])
@@ -334,6 +341,18 @@
 def across(x):
     size = lax.axis_size("eight")
     return [x] + [swap(x, "eight", q) for q in range(1, size)]
+
+
+def across_steps(x, chunk):
+    size = lax.axis_size("eight")
+    q = 1
+    while 2 * q < size:
+        (x,) = call(
+            functools.partial(add_kernel, chunk, 1, 2, 1, False), [sds(x.shape, BF16)], 0,
+            [x, swap(x, "eight", q)], 2 * x.size, 6 * x.size, vmem=8,
+        )
+        q *= 2
+    return [x, swap(x, "eight", q)]
 
 
 def gather(centre, wide):
@@ -367,10 +386,10 @@
         lax.ppermute(side, "eight", pairs_a),
         lax.ppermute(side, "eight", pairs_b),
     ]
-    lanes = 128
-    floor = jnp.where(
-        jnp.broadcast_to(active[..., None], active.shape + (lanes,)) == 1, 0.0, -jnp.inf
-    ).astype(F32)
+
+    def low_of(flags):
+        wide_flags = jnp.broadcast_to(flags[..., None], flags.shape + (128,))
+        return jnp.where(wide_flags == 1, 0.0, -jnp.inf).astype(F32)
 
     full = sds((subs, rows, cols), F32)
     half = sds((subs, rows, cols), BF16)
@@ -383,7 +402,7 @@
     op_bytes = 2 * subs * rows * rows
     arr = subs * rows * cols
 
-    def search(step, sums, centres, packed, tables):
+    def search(step, sums, centres, packed):
         mean, half_lam, lkeep, lsend = sums
         ins = [info] + (tables if packed else []) + [half_lam, flexibility]
         n_smem = len(ins) - 2
@@ -392,9 +411,9 @@
         if step:
             ins.append(mean)
             if step > 1:
-                spots = dict(anys=(len(ins),), aliases={len(ins): len(outs)})
+                spots = dict(hbm_ins=(len(ins),), aliases={len(ins): len(outs)})
                 ins.append(centres)
-            spots |= dict(any_outs=(len(outs),), scratch=[pltpu.SemaphoreType.DMA])
+            spots |= dict(hbm_outs=(len(outs),), scratch=[pltpu.SemaphoreType.DMA])
             outs = outs + [stack]
         sends = call(
             functools.partial(flex_kernel, step, packed), outs, n_smem, ins, mm,
@@ -410,14 +429,12 @@
         za = lax.ppermute(za, "eight", pairs_a)
         zb = lax.ppermute(zb, "eight", pairs_b)
         chip = swap(disp, "wide", 1)
-        lam_parts = across(own)
-        if not step:
-            own, tables = lax.optimization_barrier((own, tables))
+        lam_parts = across_steps(own, chunk)
         direct, dkeep, dsend = call(
             functools.partial(direct_kernel, chunk, wide, eight, caps, packed), [half, message, message], 3,
             [info, side, powers, gap, disp, chip, off, za, zb, dirichlet, own],
             2 * mm, op_bytes + arr * 16,
-            scratch=[pltpu.VMEM((rows, cols), F32), pltpu.VMEM((subs, rows, cols), BF16)],
+            scratch=[pltpu.VMEM((subs, rows, cols), F32), pltpu.VMEM((subs, rows, cols), BF16)],
         )
         dirs = stage([dkeep, dsend], 0, chunk, wide, True)
         dir_parts = across(scatter(dirs, 1, chunk, wide, True))
@@ -426,47 +443,44 @@
             [sds((chunk, cols), BF16), sds((8, cols), F32)], 0, dir_parts + lam_parts,
             chunk * cols * 10, chunk * cols * 20, vmem=8,
         )
-        return (direct, alpha, gather(centre, wide)), centres, tables
-
-    def update(step, lam, found, centres):
+        return (direct, alpha, gather(centre, wide)), centres
+
+    def update(step, lam, found, centres, low):
         direct, alpha, pieces = found
-        ins = [info, lam, direct, alpha, floor[step], *pieces]
+        ins = [info, lam, direct, alpha, low, *pieces]
         kernel = functools.partial(update_kernel, chunk, wide, step, step == ITERS - 1)
         if step < ITERS - 1:
             outs = [full, sds((rows, cols), F32), half, part, part]
             return call(kernel, outs, 1, ins, arr * 6, arr * 16)
         return call(
             kernel, [full, stack], 1, ins + [centres], arr * 6, arr * 16,
-            scratch=[
-                pltpu.VMEM((subs, rows, cols), F32),
-                pltpu.VMEM((rows, cols), F32),
-                pltpu.SemaphoreType.DMA((wide * (subs + 1),)),
-            ],
-            anys=(len(ins),), any_outs=(0, 1), aliases={len(ins): 1},
-        )
-
-    sums = call(
-        functools.partial(first_kernel, chunk, wide), [half, part, part], 1, [info, multipliers],
-        arr * 2, arr * 8,
-    )
-    found, _, tables = search(0, [None, *sums], None, False, tables)
-
-    def rest(packed, tables, found):
+            scratch=[pltpu.VMEM((rows, cols), F32), pltpu.SemaphoreType.DMA((wide,))],
+            hbm_ins=(len(ins),), hbm_outs=(1,), aliases={len(ins): 1},
+        )
+
+    def start():
+        return call(
+            functools.partial(first_kernel, chunk, wide), [half, part, part], 1,
+            [info, multipliers], arr * 2, arr * 8,
+        )
+
+    first, _ = search(0, [None, *start()], None, True)
+
+    def rest(packed, found):
         alphas = [found[1][0]]
         lam, centres = multipliers, None
         for step in range(1, ITERS):
-            lam, *sums = update(step - 1, lam, found, centres)
-            found, centres, _ = search(step, sums, centres, packed, tables)
+            lam, *sums = update(step - 1, lam, found, centres, low_of(active[step - 1]))
+            found, centres = search(step, sums, centres, packed)
             alphas.append(found[1][0])
-        lam, centres = update(ITERS - 1, lam, found, centres)
+        lam, centres = update(ITERS - 1, lam, found, centres, low_of(active[ITERS - 1]))
         return lam, jnp.stack(alphas), centres
 
-    return lax.cond(
-        found[1][1, 0] <= 0,
-        functools.partial(rest, True),
-        functools.partial(rest, False),
-        tables, found,
-    )
+    def again(found):
+        found, _ = search(0, [None, *start()], None, False)
+        return rest(False, found)
+
+    return lax.cond(first[1][1, 0] <= 0, functools.partial(rest, True), again, first)
 
 
 def solution(mesh):

time: 217 us -> 214 us (0.986)
  starting transfers between devices: 92.4 us -> 69.9 us
  waiting for transfers between devices: 88.2 us -> 109 us
    ppermute x66 -> x63, waiting for transfers between devices: 82.8 us -> 108 us  [swap(): return lax.ppermute(x, axis, [(i, i ^ mask) for i in range(n)])]
    ppermute x1, starting transfers between devices: 16 us -> 1.58 us  [body(): lax.ppermute(side, 'eight', pairs_a)]
    ppermute x66 -> x63, starting transfers between devices: 63.7 us -> 55.1 us  [swap(): return lax.ppermute(x, axis, [(i, i ^ mask) for i in range(n)])]
    ppermute x3, starting transfers between devices: 6.5 us -> 2.36 us  [search(): off = lax.ppermute(sends[3] if packed else disp, 'wide', away)]
    ppermute x1, waiting for transfers between devices: 3.84 us -> 0.01 us  [body(): lax.ppermute(side, 'wide', away)]
    ppermute x1, starting transfers between devices: 0.01 us -> 3.54 us  [body(): lax.ppermute(side, 'wide', away)]
    pallas_call x25 -> x28, Pallas kernels: 30.7 us -> 29.8 us  [call(): pl.pallas_call(kernel, out_shape=outs, in_specs=[SMEM if i < n_smem else...]
  transfers between devices with their start and end apart: 78 -> 75, of which waited for: 35 -> 32; matrix products, arithmetic and copies ran while one was open for 0% -> 0% of each run, Pallas kernels for 4% -> 4%
where the time goes in v2:
time: 214 us; the launch traced here: 213 us
  waiting for transfers between devices  109 us (51%)
  starting transfers between devices  69.9 us (33%)
  Pallas kernels  29.8 us (14%)
    ppermute x63, waiting for transfers between devices, swap(): return lax.ppermute(x, axis, [(i, i ^ mask) for i in range(n)])  108 us
    ppermute x63, starting transfers between devices, swap(): return lax.ppermute(x, axis, [(i, i ^ mask) for i in range(n)])  55.1 us
    pallas_call x28, Pallas kernels, call(): pl.pallas_call(kernel, out_shape=outs, in_specs=[SMEM if i < n_smem else...  29.8 us
    ppermute x3, starting transfers between devices, search(): za = lax.ppermute(za, 'eight', pairs_a)  4.62 us
  transfers between devices with their start and end apart: 75, of which 32 were waited for; matrix products, arithmetic and copies ran while one was open for 0% of the time, Pallas kernels for 4%

profile of v2, /device:TPU:0, one launch (start us, length us, event | category | flops | bytes accessed | tf_op | source)
XLA Modules:
  0.0 213.4 jit_solution(1866309468311400992)
XLA Ops:
  0.7 1.9 shard_map.96
  3.3 3.5 %collective-permute-start.121 = (s32[2,8]{1,0:T(2,128)}, s32[2,8]{1,0:T(2,128)S(1)}, u32[]{:S(2)}, u32[]{:S(2)}) collective-permute-start(s32[2,8]{1,0:T(2,128)} %side.1), channel_id=1, source_target_pairs={{0,28},{4,8},{8,4},{12,16},{16,12},{20,24},{24,20},{28,0},{1,29},{... | collective-permute-start | bytes 200 | tf_op jit(solution)/shard_map/ppermute | solution.py:385
  6.8 1.6 collective-permute-start.122
  9.0 1.5 collective-permute-done.122.refs_1_
  10.6 4.2 %shard_map.98 = (bf16[2,1024,256]{2,1,0:T(8,128)(2,1)S(1)}, bf16[6,128,256]{2,1,0:T(8,128)(2,1)S(1)}, bf16[6,128,256]{2,1,0:T(8,128)(2,1)S(1)}, bf16[9,128,256]{2,1,0:T(8,128)(2,1)S(1)}) custom-call(s32[2]{0:T(128)S(1)} %pad_add_fusion.info, s32[2,8]{1,0:T(2,128)S(1)} %collective-permute-done.121.refs_0_, s32[2,8]{1,0:T(2,128)S(1)} %collective-permute-done.122.refs_1_, ...), custom_call_target="tpu_custom_call" | custom-call | flops 1073741824 | bytes 7340032 | tf_op jit(solution)/shard_map/pallas_call | solution.py:21
  15.5 4.6 %collective-permute-start.126 = (bf16[6,128,256]{2,1,0:T(8,128)(2,1)S(1)}, bf16[6,128,256]{2,1,0:T(8,128)(2,1)S(1)}, u32[]{:S(2)}, u32[]{:S(2)}) collective-permute-start(bf16[6,128,256]{2,1,0:T(8,128)(2,1)S(1)} %get-tuple-element.281), channel_id=1, source_target_pairs={{0,1},{1,0},{2,3},{3,2},{4,5},{5,4},{6,7},{7,6},{8,9},{9,8},{10,11... | collective-permute-start | bytes 1179656 | tf_op jit(solution)/shard_map/ppermute | solution.py:429
  20.8 1.5 collective-permute-start.128
  22.4 9.6 %collective-permute-done.128.refs_1_ = bf16[128,256]{1,0:T(8,128)(2,1)S(1)} collective-permute-done((bf16[128,256]{1,0:T(8,128)(2,1)S(1)}, bf16[128,256]{1,0:T(8,128)(2,1)S(1)}, u32[]{:S(2)}, u32[]{:S(2)}) %collective-permute-start.128) | collective-permute-done | bytes 65568 | tf_op jit(solution)/shard_map/ppermute | solution.py:316
  32.8 3.4 %collective-permute-done.129.refs_2_ = bf16[128,256]{1,0:T(8,128)(2,1)S(1)} collective-permute-done((bf16[128,256]{1,0:T(8,128)(2,1)S(1)}, bf16[128,256]{1,0:T(8,128)(2,1)S(1)}, u32[]{:S(2)}, u32[]{:S(2)}) %collective-permute-start.129) | collective-permute-done | bytes 65568 | tf_op jit(solution)/shard_map/ppermute | solution.py:316
  36.9 4.5 %collective-permute-done.130.refs_3_ = bf16[128,256]{1,0:T(8,128)(2,1)S(1)} collective-permute-done((bf16[128,256]{1,0:T(8,128)(2,1)S(1)}, bf16[128,256]{1,0:T(8,128)(2,1)S(1)}, u32[]{:S(2)}, u32[]{:S(2)}) %collective-permute-start.130) | collective-permute-done | bytes 65568 | tf_op jit(solution)/shard_map/ppermute | solution.py:316
  41.5 4.1 %shard_map.100 = (bf16[2,1024,256]{2,1,0:T(8,128)(2,1)S(1)}, bf16[528,256]{1,0:T(8,128)(2,1)S(1)}, bf16[528,256]{1,0:T(8,128)(2,1)S(1)}) custom-call(s32[2]{0:T(128)S(1)} %pad_add_fusion.info, s32[2,8]{1,0:T(2,128)S(1)} %copy-done.5, s32[2]{0:T(128)S(1)} %copy-done.6, f32[2,1024,256]{2,1,0:T(8,128)S(1)} %copy-done.2, ...), custom_call_target="tpu_custom_call" | custom-call | flops 2147483648 | bytes 12582912 | tf_op jit(solution)/shard_map/pallas_call | solution.py:21
  45.7 1.5 collective-permute-done.131.refs_1_
  48.7 2.2 %collective-permute-start.134 = (bf16[144,256]{1,0:T(8,128)(2,1)S(1)}, bf16[144,256]{1,0:T(8,128)(2,1)S(1)}, u32[]{:S(2)}, u32[]{:S(2)}) collective-permute-start(bf16[144,256]{1,0:T(8,128)(2,1)S(1)} %get-tuple-element.292), channel_id=1, source_target_pairs={{0,24},{4,28},{8,16},{12,20},{16,8},{20,12},{24,0},{28,4},{1,25},{... | collective-permute-start | bytes 221192 | tf_op jit(solution)/shard_map/ppermute | solution.py:316
  50.9 3.9 %collective-permute-start.138 = (bf16[128,256]{1,0:T(8,128)(2,1)S(1)}, bf16[128,256]{1,0:T(8,128)(2,1)S(1)}, u32[]{:S(2)}, u32[]{:S(2)}) collective-permute-start(bf16[128,256]{1,0:T(8,128)(2,1)S(1)} %shard_map.99.after_ref.refs_0_), channel_id=1, source_target_pairs={{0,1},{1,0},{2,3},{3,2},{4,5},{5,4},{6,7},{7,6},{8,9},{9,8},{10,11... | collective-permute-start | bytes 196616 | tf_op jit(solution)/shard_map/ppermute | solution.py:316
  54.8 3.5 %collective-permute-start.135 = (bf16[144,256]{1,0:T(8,128)(2,1)S(1)}, bf16[144,256]{1,0:T(8,128)(2,1)S(1)}, u32[]{:S(2)}, u32[]{:S(2)}) collective-permute-start(bf16[144,256]{1,0:T(8,128)(2,1)S(1)} %shard_map.102.refs_0_), channel_id=1, source_target_pairs={{0,1},{1,0},{2,3},{3,2},{4,5},{5,4},{6,7},{7,6},{8,9},{9,8},{10,11... | collective-permute-start | bytes 221192 | tf_op jit(solution)/shard_map/ppermute | solution.py:316
  58.3 1.7 collective-permute-start.136
  60.1 1.4 collective-permute-start.137
  61.5 2.1 collective-permute-start.139
  63.6 6.2 %collective-permute-done.139.refs_5_ = bf16[128,256]{1,0:T(8,128)(2,1)S(1)} collective-permute-done((bf16[128,256]{1,0:T(8,128)(2,1)S(1)}, bf16[128,256]{1,0:T(8,128)(2,1)S(1)}, u32[]{:S(2)}, u32[]{:S(2)}) %collective-permute-start.139) | collective-permute-done | bytes 65568 | tf_op jit(solution)/shard_map/ppermute | solution.py:316
  70.9 1.7 collective-permute-start.143
  75.7 2.0 collective-permute-done.145
  79.0 133.8 %conditional.1 = (f32[2,1024,256]{2,1,0:T(8,128)}, f32[3,1024,256]{2,1,0:T(8,128)}, f32[3,256]{1,0:T(4,128)S(1)}) conditional(s32[]{:T(128)} %bitcast.8, (s32[2]{0:T(128)S(1)}, f32[2,1024,256]{2,1,0:T(8,128)S(1)}, bf16[2,1024,1024]{2,1,0:T(8,128)(2,1)S(1)}, s32[2,8]{1,0:T(2,128)S(1)}, s32[2]{0:T(128)S(1)}, /*index=5*/f32[2,1024,256]{2,1,0:T(8,128)S(1)}, ...), branch_computations={%region_0.1_spmd, %region_1.2_spmd} | conditional | flops 9677715456 | bytes 160488160 | solution.py:483
  81.3 2.6 %branch_1_fun.21 = (bf16[2,1024,256]{2,1,0:T(8,128)(2,1)S(1)}, bf16[6,128,256]{2,1,0:T(8,128)(2,1)S(1)}, bf16[6,128,256]{2,1,0:T(8,128)(2,1)S(1)}, bf16[9,128,256]{2,1,0:T(8,128)(2,1)S(1)}, f32[3,1024,256]{2,1,0:T(8,128)}) custom-call(s32[2]{0:T(128)S(1)} %get-tuple-element.152.info, s32[2,8]{1,0:T(2,128)S(1)} %get-tuple-element.175.refs_0_, ...), custom_call_target="tpu_custom_call" | custom-call | flops 1073741824 | bytes 7340032 | tf_op jit(solution)/shard_map/cond/branch_1_fun/pallas_call | solution.py:21
  87.0 14.0 %collective-permute-done.77.refs_1_ = bf16[128,256]{1,0:T(8,128)(2,1)S(1)} collective-permute-done((bf16[128,256]{1,0:T(8,128)(2,1)S(1)}, bf16[128,256]{1,0:T(8,128)(2,1)S(1)}, u32[]{:S(2)}, u32[]{:S(2)}) %collective-permute-start.77) | collective-permute-done | bytes 65568 | tf_op jit(solution)/shard_map/cond/branch_1_fun/ppermute | solution.py:316
  101.6 3.6 %collective-permute-done.78.refs_2_ = bf16[128,256]{1,0:T(8,128)(2,1)S(1)} collective-permute-done((bf16[128,256]{1,0:T(8,128)(2,1)S(1)}, bf16[128,256]{1,0:T(8,128)(2,1)S(1)}, u32[]{:S(2)}, u32[]{:S(2)}) %collective-permute-start.78) | collective-permute-done | bytes 65568 | tf_op jit(solution)/shard_map/cond/branch_1_fun/ppermute | solution.py:316
  106.2 4.1 %collective-permute-done.79.refs_3_ = bf16[128,256]{1,0:T(8,128)(2,1)S(1)} collective-permute-done((bf16[128,256]{1,0:T(8,128)(2,1)S(1)}, bf16[128,256]{1,0:T(8,128)(2,1)S(1)}, u32[]{:S(2)}, u32[]{:S(2)}) %collective-permute-start.79) | collective-permute-done | bytes 65568 | tf_op jit(solution)/shard_map/cond/branch_1_fun/ppermute | solution.py:316
  110.5 4.1 %branch_1_fun.23 = (bf16[2,1024,256]{2,1,0:T(8,128)(2,1)S(1)}, bf16[528,256]{1,0:T(8,128)(2,1)S(1)}, bf16[528,256]{1,0:T(8,128)(2,1)S(1)}) custom-call(s32[2]{0:T(128)S(1)} %get-tuple-element.152.info, s32[2,8]{1,0:T(2,128)S(1)} %get-tuple-element.166.side, s32[2]{0:T(128)S(1)} %get-tuple-element.167.powers, f32[2,1024,256]{2,1,0:T(8,128)S(1)} %get-tuple-element.168.gap_ref, ...), custom_call_target="tpu_custom_call" | custom-call | flops 2147483648 | bytes 12582912 | tf_op jit(solution)/shard_map/cond/branch_1_fun/pallas_call | solution.py:21
  114.7 1.5 collective-permute-done.80.refs_1_
  117.9 1.9 collective-permute-start.83
  120.7 2.7 %collective-permute-done.82.refs_2_ = bf16[144,256]{1,0:T(8,128)(2,1)S(1)} collective-permute-done((bf16[144,256]{1,0:T(8,128)(2,1)S(1)}, bf16[144,256]{1,0:T(8,128)(2,1)S(1)}, u32[]{:S(2)}, u32[]{:S(2)}) %collective-permute-start.82) | collective-permute-done | bytes 73760 | tf_op jit(solution)/shard_map/cond/branch_1_fun/ppermute | solution.py:316
  123.5 3.7 %collective-permute-start.85 = (bf16[144,256]{1,0:T(8,128)(2,1)S(1)}, bf16[144,256]{1,0:T(8,128)(2,1)S(1)}, u32[]{:S(2)}, u32[]{:S(2)}) collective-permute-start(bf16[144,256]{1,0:T(8,128)(2,1)S(1)} %branch_1_fun.25.refs_0_), channel_id=1, source_target_pairs={{0,2},{1,3},{2,0},{3,1},{4,6},{5,7},{6,4},{7,5},{8,10},{9,11},{10,... | collective-permute-start | bytes 221192 | tf_op jit(solution)/shard_map/cond/branch_1_fun/ppermute | solution.py:316
  128.8 6.7 %collective-permute-done.88.refs_5_ = bf16[128,256]{1,0:T(8,128)(2,1)S(1)} collective-permute-done((bf16[128,256]{1,0:T(8,128)(2,1)S(1)}, bf16[128,256]{1,0:T(8,128)(2,1)S(1)}, u32[]{:S(2)}, u32[]{:S(2)}) %collective-permute-start.88) | collective-permute-done | bytes 65568 | tf_op jit(solution)/shard_map/cond/branch_1_fun/ppermute | solution.py:316
  136.0 2.1 collective-permute-start.92
  140.8 2.4 %collective-permute-done.94.refs_6_ = bf16[128,256]{1,0:T(8,128)(2,1)S(1)} collective-permute-done((bf16[128,256]{1,0:T(8,128)(2,1)S(1)}, bf16[128,256]{1,0:T(8,128)(2,1)S(1)}, u32[]{:S(2)}, u32[]{:S(2)}) %collective-permute-start.94) | collective-permute-done | bytes 65568 | tf_op jit(solution)/shard_map/cond/branch_1_fun/ppermute | solution.py:316
  146.1 2.6 %branch_1_fun.30 = (bf16[2,1024,256]{2,1,0:T(8,128)(2,1)S(1)}, bf16[6,128,256]{2,1,0:T(8,128)(2,1)S(1)}, bf16[6,128,256]{2,1,0:T(8,128)(2,1)S(1)}, bf16[9,128,256]{2,1,0:T(8,128)(2,1)S(1)}, f32[3,1024,256]{2,1,0:T(8,128)}) custom-call(s32[2]{0:T(128)S(1)} %get-tuple-element.152.info, ...), custom_call_target="tpu_custom_call", output_to_operand_aliasing={{4}: (7, {})} | custom-call | flops 1073741824 | bytes 7340032 | tf_op jit(solution)/shard_map/cond/branch_1_fun/pallas_call | solution.py:21
  151.7 13.9 %collective-permute-done.101.refs_1_ = bf16[128,256]{1,0:T(8,128)(2,1)S(1)} collective-permute-done((bf16[128,256]{1,0:T(8,128)(2,1)S(1)}, bf16[128,256]{1,0:T(8,128)(2,1)S(1)}, u32[]{:S(2)}, u32[]{:S(2)}) %collective-permute-start.101) | collective-permute-done | bytes 65568 | tf_op jit(solution)/shard_map/cond/branch_1_fun/ppermute | solution.py:316
  165.7 4.3 %collective-permute-done.102.refs_2_ = bf16[128,256]{1,0:T(8,128)(2,1)S(1)} collective-permute-done((bf16[128,256]{1,0:T(8,128)(2,1)S(1)}, bf16[128,256]{1,0:T(8,128)(2,1)S(1)}, u32[]{:S(2)}, u32[]{:S(2)}) %collective-permute-start.102) | collective-permute-done | bytes 65568 | tf_op jit(solution)/shard_map/cond/branch_1_fun/ppermute | solution.py:316
  169.9 1.6 collective-permute-start.103
  171.6 3.5 %collective-permute-done.103.refs_3_ = bf16[128,256]{1,0:T(8,128)(2,1)S(1)} collective-permute-done((bf16[128,256]{1,0:T(8,128)(2,1)S(1)}, bf16[128,256]{1,0:T(8,128)(2,1)S(1)}, u32[]{:S(2)}, u32[]{:S(2)}) %collective-permute-start.103) | collective-permute-done | bytes 65568 | tf_op jit(solution)/shard_map/cond/branch_1_fun/ppermute | solution.py:316
  175.2 4.1 %branch_1_fun.32 = (bf16[2,1024,256]{2,1,0:T(8,128)(2,1)S(1)}, bf16[528,256]{1,0:T(8,128)(2,1)S(1)}, bf16[528,256]{1,0:T(8,128)(2,1)S(1)}) custom-call(s32[2]{0:T(128)S(1)} %get-tuple-element.152.info, s32[2,8]{1,0:T(2,128)S(1)} %get-tuple-element.166.side, s32[2]{0:T(128)S(1)} %get-tuple-element.167.powers, f32[2,1024,256]{2,1,0:T(8,128)S(1)} %get-tuple-element.168.gap_ref, ...), custom_call_target="tpu_custom_call" | custom-call | flops 2147483648 | bytes 12582912 | tf_op jit(solution)/shard_map/cond/branch_1_fun/pallas_call | solution.py:21
  179.4 1.5 collective-permute-done.104.refs_1_
  181.0 1.8 collective-permute-start.105
  185.4 3.3 %collective-permute-done.106.refs_2_ = bf16[144,256]{1,0:T(8,128)(2,1)S(1)} collective-permute-done((bf16[144,256]{1,0:T(8,128)(2,1)S(1)}, bf16[144,256]{1,0:T(8,128)(2,1)S(1)}, u32[]{:S(2)}, u32[]{:S(2)}) %collective-permute-start.106) | collective-permute-done | bytes 73760 | tf_op jit(solution)/shard_map/cond/branch_1_fun/ppermute | solution.py:316
  188.8 3.3 %collective-permute-start.109 = (bf16[144,256]{1,0:T(8,128)(2,1)S(1)}, bf16[144,256]{1,0:T(8,128)(2,1)S(1)}, u32[]{:S(2)}, u32[]{:S(2)}) collective-permute-start(bf16[144,256]{1,0:T(8,128)(2,1)S(1)} %branch_1_fun.34.refs_0_), channel_id=1, source_target_pairs={{0,2},{1,3},{2,0},{3,1},{4,6},{5,7},{6,4},{7,5},{8,10},{9,11},{10,... | collective-permute-start | bytes 221192 | tf_op jit(solution)/shard_map/cond/branch_1_fun/ppermute | solution.py:316
  193.8 6.7 %collective-permute-done.112.refs_5_ = bf16[128,256]{1,0:T(8,128)(2,1)S(1)} collective-permute-done((bf16[128,256]{1,0:T(8,128)(2,1)S(1)}, bf16[128,256]{1,0:T(8,128)(2,1)S(1)}, u32[]{:S(2)}, u32[]{:S(2)}) %collective-permute-start.112) | collective-permute-done | bytes 65568 | tf_op jit(solution)/shard_map/cond/branch_1_fun/ppermute | solution.py:316
  201.2 1.8 collective-permute-start.116
  206.2 2.0 collective-permute-done.118.refs_6_
  209.8 3.0 %branch_1_fun.37 = (f32[2,1024,256]{2,1,0:T(8,128)}, f32[3,1024,256]{2,1,0:T(8,128)}) custom-call(s32[2]{0:T(128)S(1)} %get-tuple-element.152.info, f32[2,1024,256]{2,1,0:T(8,128)S(1)} %get-tuple-element.203.lam_ref, bf16[2,1024,256]{2,1,0:T(8,128)(2,1)S(1)} %get-tuple-element.225.dir_ref, ...), custom_call_target="tpu_custom_call", output_to_operand_aliasing={{1}: (13, {})} | custom-call | flops 3145728 | bytes 8388608 | tf_op jit(solution)/shard_map/cond/branch_1_fun/pallas_call | solution.py:21
  (157 shorter events, 41.7 us)
Async XLA Ops:
  2.7 12.1 %collective-permute-start.120 = (bf16[512,256]{1,0:T(8,128)(2,1)S(1)}, bf16[512,256]{1,0:T(8,128)(2,1)S(1)}, u32[]{:S(2)}, u32[]{:S(2)}) collective-permute-start(bf16[512,256]{1,0:T(8,128)(2,1)S(1)} %get-tuple-element.269), channel_id=1, source_target_pairs={{0,4},{4,0},{8,12},{12,8},{16,20},{20,16},{24,28},{28,24},{1,5},{5... | collective-permute-start | bytes 786440 | tf_op jit(solution)/shard_map/ppermute | solution.py:316
  3.3 5.8 %collective-permute-start.121 = (s32[2,8]{1,0:T(2,128)}, s32[2,8]{1,0:T(2,128)S(1)}, u32[]{:S(2)}, u32[]{:S(2)}) collective-permute-start(s32[2,8]{1,0:T(2,128)} %side.1), channel_id=1, source_target_pairs={{0,28},{4,8},{8,4},{12,16},{16,12},{20,24},{24,20},{28,0},{1,29},{... | collective-permute-start | bytes 200 | tf_op jit(solution)/shard_map/ppermute | solution.py:385
  14.8 26.7 %collective-permute-start.124 = (bf16[2,1024,256]{2,1,0:T(8,128)(2,1)S(1)}, bf16[2,1024,256]{2,1,0:T(8,128)(2,1)S(1)}, u32[]{:S(2)}, u32[]{:S(2)}) collective-permute-start(bf16[2,1024,256]{2,1,0:T(8,128)(2,1)S(1)} %get-tuple-element.279.disp_ref), channel_id=1, source_target_pairs={{0,4},{4,0},{8,12},{12,8},{16,20},{20,16},{24,28},{28,24},{1,5},{5... | collective-permute-start | bytes 3145736 | tf_op jit(solution)/shard_map/ppermute | solution.py:316
  14.9 26.6 %collective-permute-start.125 = (bf16[9,128,256]{2,1,0:T(8,128)(2,1)S(1)}, bf16[9,128,256]{2,1,0:T(8,128)(2,1)S(1)}, u32[]{:S(2)}, u32[]{:S(2)}) collective-permute-start(bf16[9,128,256]{2,1,0:T(8,128)(2,1)S(1)} %get-tuple-element.280), channel_id=1, source_target_pairs={{0,28},{4,8},{8,4},{12,16},{16,12},{20,24},{24,20},{28,0},{1,29},{... | collective-permute-start | bytes 1769480 | tf_op jit(solution)/shard_map/ppermute | solution.py:428
  15.5 25.9 %collective-permute-start.126 = (bf16[6,128,256]{2,1,0:T(8,128)(2,1)S(1)}, bf16[6,128,256]{2,1,0:T(8,128)(2,1)S(1)}, u32[]{:S(2)}, u32[]{:S(2)}) collective-permute-start(bf16[6,128,256]{2,1,0:T(8,128)(2,1)S(1)} %get-tuple-element.281), channel_id=1, source_target_pairs={{0,1},{1,0},{2,3},{3,2},{4,5},{5,4},{6,7},{7,6},{8,9},{9,8},{10,11... | collective-permute-start | bytes 1179656 | tf_op jit(solution)/shard_map/ppermute | solution.py:429
  20.2 21.3 %collective-permute-start.127 = (bf16[6,128,256]{2,1,0:T(8,128)(2,1)S(1)}, bf16[6,128,256]{2,1,0:T(8,128)(2,1)S(1)}, u32[]{:S(2)}, u32[]{:S(2)}) collective-permute-start(bf16[6,128,256]{2,1,0:T(8,128)(2,1)S(1)} %get-tuple-element.282), channel_id=1, source_target_pairs={{1,2},{2,1},{5,6},{6,5},{9,10},{10,9},{13,14},{14,13},{17,18},{18,... | collective-permute-start | bytes 1179656 | tf_op jit(solution)/shard_map/ppermute | solution.py:430
  20.8 11.1 %collective-permute-start.128 = (bf16[128,256]{1,0:T(8,128)(2,1)S(1)}, bf16[128,256]{1,0:T(8,128)(2,1)S(1)}, u32[]{:S(2)}, u32[]{:S(2)}) collective-permute-start(bf16[128,256]{1,0:T(8,128)(2,1)S(1)} %get-tuple-element.284), channel_id=1, source_target_pairs={{0,8},{4,12},{8,0},{12,4},{16,24},{20,28},{24,16},{28,20},{1,9},{5... | collective-permute-start | bytes 196616 | tf_op jit(solution)/shard_map/ppermute | solution.py:316
  36.2 5.2 %collective-permute-start.130 = (bf16[128,256]{1,0:T(8,128)(2,1)S(1)}, bf16[128,256]{1,0:T(8,128)(2,1)S(1)}, u32[]{:S(2)}, u32[]{:S(2)}) collective-permute-start(bf16[128,256]{1,0:T(8,128)(2,1)S(1)} %get-tuple-element.286), channel_id=1, source_target_pairs={{0,24},{4,28},{8,16},{12,20},{16,8},{20,12},{24,0},{28,4},{1,25},{... | collective-permute-start | bytes 196616 | tf_op jit(solution)/shard_map/ppermute | solution.py:316
  47.3 7.4 %collective-permute-start.132 = (bf16[144,256]{1,0:T(8,128)(2,1)S(1)}, bf16[144,256]{1,0:T(8,128)(2,1)S(1)}, u32[]{:S(2)}, u32[]{:S(2)}) collective-permute-start(bf16[144,256]{1,0:T(8,128)(2,1)S(1)} %get-tuple-element.290), channel_id=1, source_target_pairs={{0,8},{4,12},{8,0},{12,4},{16,24},{20,28},{24,16},{28,20},{1,9},{5... | collective-permute-start | bytes 221192 | tf_op jit(solution)/shard_map/ppermute | solution.py:316
  47.8 7.0 %collective-permute-start.133 = (bf16[144,256]{1,0:T(8,128)(2,1)S(1)}, bf16[144,256]{1,0:T(8,128)(2,1)S(1)}, u32[]{:S(2)}, u32[]{:S(2)}) collective-permute-start(bf16[144,256]{1,0:T(8,128)(2,1)S(1)} %get-tuple-element.291), channel_id=1, source_target_pairs={{0,16},{4,20},{8,24},{12,28},{16,0},{20,4},{24,8},{28,12},{1,17},{... | collective-permute-start | bytes 221192 | tf_op jit(solution)/shard_map/ppermute | solution.py:316
  48.7 6.1 %collective-permute-start.134 = (bf16[144,256]{1,0:T(8,128)(2,1)S(1)}, bf16[144,256]{1,0:T(8,128)(2,1)S(1)}, u32[]{:S(2)}, u32[]{:S(2)}) collective-permute-start(bf16[144,256]{1,0:T(8,128)(2,1)S(1)} %get-tuple-element.292), channel_id=1, source_target_pairs={{0,24},{4,28},{8,16},{12,20},{16,8},{20,12},{24,0},{28,4},{1,25},{... | collective-permute-start | bytes 221192 | tf_op jit(solution)/shard_map/ppermute | solution.py:316
  50.9 10.6 %collective-permute-start.138 = (bf16[128,256]{1,0:T(8,128)(2,1)S(1)}, bf16[128,256]{1,0:T(8,128)(2,1)S(1)}, u32[]{:S(2)}, u32[]{:S(2)}) collective-permute-start(bf16[128,256]{1,0:T(8,128)(2,1)S(1)} %shard_map.99.after_ref.refs_0_), channel_id=1, source_target_pairs={{0,1},{1,0},{2,3},{3,2},{4,5},{5,4},{6,7},{7,6},{8,9},{9,8},{10,11... | collective-permute-start | bytes 196616 | tf_op jit(solution)/shard_map/ppermute | solution.py:316
  54.8 14.9 %collective-permute-start.135 = (bf16[144,256]{1,0:T(8,128)(2,1)S(1)}, bf16[144,256]{1,0:T(8,128)(2,1)S(1)}, u32[]{:S(2)}, u32[]{:S(2)}) collective-permute-start(bf16[144,256]{1,0:T(8,128)(2,1)S(1)} %shard_map.102.refs_0_), channel_id=1, source_target_pairs={{0,1},{1,0},{2,3},{3,2},{4,5},{5,4},{6,7},{7,6},{8,9},{9,8},{10,11... | collective-permute-start | bytes 221192 | tf_op jit(solution)/shard_map/ppermute | solution.py:316
  58.3 11.4 %collective-permute-start.136 = (bf16[144,256]{1,0:T(8,128)(2,1)S(1)}, bf16[144,256]{1,0:T(8,128)(2,1)S(1)}, u32[]{:S(2)}, u32[]{:S(2)}) collective-permute-start(bf16[144,256]{1,0:T(8,128)(2,1)S(1)} %shard_map.102.refs_0_), channel_id=1, source_target_pairs={{0,2},{1,3},{2,0},{3,1},{4,6},{5,7},{6,4},{7,5},{8,10},{9,11},{10,... | collective-permute-start | bytes 221192 | tf_op jit(solution)/shard_map/ppermute | solution.py:316
  60.1 9.7 %collective-permute-start.137 = (bf16[144,256]{1,0:T(8,128)(2,1)S(1)}, bf16[144,256]{1,0:T(8,128)(2,1)S(1)}, u32[]{:S(2)}, u32[]{:S(2)}) collective-permute-start(bf16[144,256]{1,0:T(8,128)(2,1)S(1)} %shard_map.102.refs_0_), channel_id=1, source_target_pairs={{0,3},{1,2},{2,1},{3,0},{4,7},{5,6},{6,5},{7,4},{8,11},{9,10},{10,... | collective-permute-start | bytes 221192 | tf_op jit(solution)/shard_map/ppermute | solution.py:316
  61.5 8.3 %collective-permute-start.139 = (bf16[128,256]{1,0:T(8,128)(2,1)S(1)}, bf16[128,256]{1,0:T(8,128)(2,1)S(1)}, u32[]{:S(2)}, u32[]{:S(2)}) collective-permute-start(bf16[128,256]{1,0:T(8,128)(2,1)S(1)} %shard_map.103.refs_4_), channel_id=1, source_target_pairs={{0,2},{1,3},{2,0},{3,1},{4,6},{5,7},{6,4},{7,5},{8,10},{9,11},{10,... | collective-permute-start | bytes 196616 | tf_op jit(solution)/shard_map/ppermute | solution.py:316
  72.6 5.2 %collective-permute-start.145 = (bf16[128,256]{1,0:T(8,128)(2,1)S(1)}, bf16[128,256]{1,0:T(8,128)(2,1)S(1)}, u32[]{:S(2)}, u32[]{:S(2)}) collective-permute-start(bf16[128,256]{1,0:T(8,128)(2,1)S(1)} %get-tuple-element.295), channel_id=1, source_target_pairs={{0,24},{4,28},{8,16},{12,20},{16,8},{20,12},{24,0},{28,4},{1,25},{... | collective-permute-start | bytes 196616 | tf_op jit(solution)/shard_map/ppermute | solution.py:316
  73.4 5.5 %collective-permute-start.140 = (bf16[128,256]{1,0:T(8,128)(2,1)S(1)}, bf16[128,256]{1,0:T(8,128)(2,1)S(1)}, u32[]{:S(2)}, u32[]{:S(2)}) collective-permute-start(bf16[128,256]{1,0:T(8,128)(2,1)S(1)} %get-tuple-element.295), channel_id=1, source_target_pairs={{0,4},{4,0},{8,12},{12,8},{16,20},{20,16},{24,28},{28,24},{1,5},{5... | collective-permute-start | bytes 196616 | tf_op jit(solution)/shard_map/ppermute | solution.py:316
  84.0 26.5 %collective-permute-start.73 = (bf16[2,1024,256]{2,1,0:T(8,128)(2,1)S(1)}, bf16[2,1024,256]{2,1,0:T(8,128)(2,1)S(1)}, u32[]{:S(2)}, u32[]{:S(2)}) collective-permute-start(bf16[2,1024,256]{2,1,0:T(8,128)(2,1)S(1)} %get-tuple-element.185.disp_ref), channel_id=1, source_target_pairs={{0,4},{4,0},{8,12},{12,8},{16,20},{20,16},{24,28},{28,24},{1,5},{5... | collective-permute-start | bytes 3145736 | tf_op jit(solution)/shard_map/cond/branch_1_fun/ppermute | solution.py:316
  84.1 26.4 %collective-permute-start.74 = (bf16[9,128,256]{2,1,0:T(8,128)(2,1)S(1)}, bf16[9,128,256]{2,1,0:T(8,128)(2,1)S(1)}, u32[]{:S(2)}, u32[]{:S(2)}) collective-permute-start(bf16[9,128,256]{2,1,0:T(8,128)(2,1)S(1)} %get-tuple-element.186), channel_id=1, source_target_pairs={{0,28},{4,8},{8,4},{12,16},{16,12},{20,24},{24,20},{28,0},{1,29},{... | collective-permute-start | bytes 1769480 | tf_op jit(solution)/shard_map/cond/branch_1_fun/ppermute | solution.py:428
  85.0 25.4 %collective-permute-start.75 = (bf16[6,128,256]{2,1,0:T(8,128)(2,1)S(1)}, bf16[6,128,256]{2,1,0:T(8,128)(2,1)S(1)}, u32[]{:S(2)}, u32[]{:S(2)}) collective-permute-start(bf16[6,128,256]{2,1,0:T(8,128)(2,1)S(1)} %get-tuple-element.187), channel_id=1, source_target_pairs={{0,1},{1,0},{2,3},{3,2},{4,5},{5,4},{6,7},{7,6},{8,9},{9,8},{10,11... | collective-permute-start | bytes 1179656 | tf_op jit(solution)/shard_map/cond/branch_1_fun/ppermute | solution.py:429
  85.0 25.5 %collective-permute-start.76 = (bf16[6,128,256]{2,1,0:T(8,128)(2,1)S(1)}, bf16[6,128,256]{2,1,0:T(8,128)(2,1)S(1)}, u32[]{:S(2)}, u32[]{:S(2)}) collective-permute-start(bf16[6,128,256]{2,1,0:T(8,128)(2,1)S(1)} %get-tuple-element.188), channel_id=1, source_target_pairs={{1,2},{2,1},{5,6},{6,5},{9,10},{10,9},{13,14},{14,13},{17,18},{18,... | collective-permute-start | bytes 1179656 | tf_op jit(solution)/shard_map/cond/branch_1_fun/ppermute | solution.py:430
  85.7 15.3 %collective-permute-start.77 = (bf16[128,256]{1,0:T(8,128)(2,1)S(1)}, bf16[128,256]{1,0:T(8,128)(2,1)S(1)}, u32[]{:S(2)}, u32[]{:S(2)}) collective-permute-start(bf16[128,256]{1,0:T(8,128)(2,1)S(1)} %get-tuple-element.191), channel_id=1, source_target_pairs={{0,8},{4,12},{8,0},{12,4},{16,24},{20,28},{24,16},{28,20},{1,9},{5... | collective-permute-start | bytes 196616 | tf_op jit(solution)/shard_map/cond/branch_1_fun/ppermute | solution.py:316
  105.2 5.2 %collective-permute-start.79 = (bf16[128,256]{1,0:T(8,128)(2,1)S(1)}, bf16[128,256]{1,0:T(8,128)(2,1)S(1)}, u32[]{:S(2)}, u32[]{:S(2)}) collective-permute-start(bf16[128,256]{1,0:T(8,128)(2,1)S(1)} %get-tuple-element.193), channel_id=1, source_target_pairs={{0,24},{4,28},{8,16},{12,20},{16,8},{20,12},{24,0},{28,4},{1,25},{... | collective-permute-start | bytes 196616 | tf_op jit(solution)/shard_map/cond/branch_1_fun/ppermute | solution.py:316
  117.6 5.7 %collective-permute-start.82 = (bf16[144,256]{1,0:T(8,128)(2,1)S(1)}, bf16[144,256]{1,0:T(8,128)(2,1)S(1)}, u32[]{:S(2)}, u32[]{:S(2)}) collective-permute-start(bf16[144,256]{1,0:T(8,128)(2,1)S(1)} %get-tuple-element.199), channel_id=1, source_target_pairs={{0,16},{4,20},{8,24},{12,28},{16,0},{20,4},{24,8},{28,12},{1,17},{... | collective-permute-start | bytes 221192 | tf_op jit(solution)/shard_map/cond/branch_1_fun/ppermute | solution.py:316
  117.9 5.4 %collective-permute-start.83 = (bf16[144,256]{1,0:T(8,128)(2,1)S(1)}, bf16[144,256]{1,0:T(8,128)(2,1)S(1)}, u32[]{:S(2)}, u32[]{:S(2)}) collective-permute-start(bf16[144,256]{1,0:T(8,128)(2,1)S(1)} %get-tuple-element.200), channel_id=1, source_target_pairs={{0,24},{4,28},{8,16},{12,20},{16,8},{20,12},{24,0},{28,4},{1,25},{... | collective-permute-start | bytes 221192 | tf_op jit(solution)/shard_map/cond/branch_1_fun/ppermute | solution.py:316
  119.8 8.0 %collective-permute-start.87 = (bf16[128,256]{1,0:T(8,128)(2,1)S(1)}, bf16[128,256]{1,0:T(8,128)(2,1)S(1)}, u32[]{:S(2)}, u32[]{:S(2)}) collective-permute-start(bf16[128,256]{1,0:T(8,128)(2,1)S(1)} %branch_1_fun.22.after_ref.refs_0_), channel_id=1, source_target_pairs={{0,1},{1,0},{2,3},{3,2},{4,5},{5,4},{6,7},{7,6},{8,9},{9,8},{10,11... | collective-permute-start | bytes 196616 | tf_op jit(solution)/shard_map/cond/branch_1_fun/ppermute | solution.py:316
  123.4 12.1 %collective-permute-start.84 = (bf16[144,256]{1,0:T(8,128)(2,1)S(1)}, bf16[144,256]{1,0:T(8,128)(2,1)S(1)}, u32[]{:S(2)}, u32[]{:S(2)}) collective-permute-start(bf16[144,256]{1,0:T(8,128)(2,1)S(1)} %branch_1_fun.25.refs_0_), channel_id=1, source_target_pairs={{0,1},{1,0},{2,3},{3,2},{4,5},{5,4},{6,7},{7,6},{8,9},{9,8},{10,11... | collective-permute-start | bytes 221192 | tf_op jit(solution)/shard_map/cond/branch_1_fun/ppermute | solution.py:316
  123.5 12.0 %collective-permute-start.85 = (bf16[144,256]{1,0:T(8,128)(2,1)S(1)}, bf16[144,256]{1,0:T(8,128)(2,1)S(1)}, u32[]{:S(2)}, u32[]{:S(2)}) collective-permute-start(bf16[144,256]{1,0:T(8,128)(2,1)S(1)} %branch_1_fun.25.refs_0_), channel_id=1, source_target_pairs={{0,2},{1,3},{2,0},{3,1},{4,6},{5,7},{6,4},{7,5},{8,10},{9,11},{10,... | collective-permute-start | bytes 221192 | tf_op jit(solution)/shard_map/cond/branch_1_fun/ppermute | solution.py:316
  127.2 8.3 %collective-permute-start.86 = (bf16[144,256]{1,0:T(8,128)(2,1)S(1)}, bf16[144,256]{1,0:T(8,128)(2,1)S(1)}, u32[]{:S(2)}, u32[]{:S(2)}) collective-permute-start(bf16[144,256]{1,0:T(8,128)(2,1)S(1)} %branch_1_fun.25.refs_0_), channel_id=1, source_target_pairs={{0,3},{1,2},{2,1},{3,0},{4,7},{5,6},{6,5},{7,4},{8,11},{9,10},{10,... | collective-permute-start | bytes 221192 | tf_op jit(solution)/shard_map/cond/branch_1_fun/ppermute | solution.py:316
  127.9 7.6 %collective-permute-start.88 = (bf16[128,256]{1,0:T(8,128)(2,1)S(1)}, bf16[128,256]{1,0:T(8,128)(2,1)S(1)}, u32[]{:S(2)}, u32[]{:S(2)}) collective-permute-start(bf16[128,256]{1,0:T(8,128)(2,1)S(1)} %branch_1_fun.26.refs_4_), channel_id=1, source_target_pairs={{0,2},{1,3},{2,0},{3,1},{4,6},{5,7},{6,4},{7,5},{8,10},{9,11},{10,... | collective-permute-start | bytes 196616 | tf_op jit(solution)/shard_map/cond/branch_1_fun/ppermute | solution.py:316
  136.0 4.8 %collective-permute-start.92 = (bf16[128,256]{1,0:T(8,128)(2,1)S(1)}, bf16[128,256]{1,0:T(8,128)(2,1)S(1)}, u32[]{:S(2)}, u32[]{:S(2)}) collective-permute-start(bf16[128,256]{1,0:T(8,128)(2,1)S(1)} %get-tuple-element.202.refs_0_), channel_id=1, source_target_pairs={{0,16},{4,20},{8,24},{12,28},{16,0},{20,4},{24,8},{28,12},{1,17},{... | collective-permute-start | bytes 196616 | tf_op jit(solution)/shard_map/cond/branch_1_fun/ppermute | solution.py:316
  138.0 5.2 %collective-permute-start.94 = (bf16[128,256]{1,0:T(8,128)(2,1)S(1)}, bf16[128,256]{1,0:T(8,128)(2,1)S(1)}, u32[]{:S(2)}, u32[]{:S(2)}) collective-permute-start(bf16[128,256]{1,0:T(8,128)(2,1)S(1)} %get-tuple-element.202.refs_0_), channel_id=1, source_target_pairs={{0,24},{4,28},{8,16},{12,20},{16,8},{20,12},{24,0},{28,4},{1,25},{... | collective-permute-start | bytes 196616 | tf_op jit(solution)/shard_map/cond/branch_1_fun/ppermute | solution.py:316
  148.8 26.4 %collective-permute-start.97 = (bf16[2,1024,256]{2,1,0:T(8,128)(2,1)S(1)}, bf16[2,1024,256]{2,1,0:T(8,128)(2,1)S(1)}, u32[]{:S(2)}, u32[]{:S(2)}) collective-permute-start(bf16[2,1024,256]{2,1,0:T(8,128)(2,1)S(1)} %get-tuple-element.217.disp_ref), channel_id=1, source_target_pairs={{0,4},{4,0},{8,12},{12,8},{16,20},{20,16},{24,28},{28,24},{1,5},{5... | collective-permute-start | bytes 3145736 | tf_op jit(solution)/shard_map/cond/branch_1_fun/ppermute | solution.py:316
  149.2 26.0 %collective-permute-start.98 = (bf16[9,128,256]{2,1,0:T(8,128)(2,1)S(1)}, bf16[9,128,256]{2,1,0:T(8,128)(2,1)S(1)}, u32[]{:S(2)}, u32[]{:S(2)}) collective-permute-start(bf16[9,128,256]{2,1,0:T(8,128)(2,1)S(1)} %get-tuple-element.218), channel_id=1, source_target_pairs={{0,28},{4,8},{8,4},{12,16},{16,12},{20,24},{24,20},{28,0},{1,29},{... | collective-permute-start | bytes 1769480 | tf_op jit(solution)/shard_map/cond/branch_1_fun/ppermute | solution.py:428
  150.0 25.1 %collective-permute-start.99 = (bf16[6,128,256]{2,1,0:T(8,128)(2,1)S(1)}, bf16[6,128,256]{2,1,0:T(8,128)(2,1)S(1)}, u32[]{:S(2)}, u32[]{:S(2)}) collective-permute-start(bf16[6,128,256]{2,1,0:T(8,128)(2,1)S(1)} %get-tuple-element.219), channel_id=1, source_target_pairs={{0,1},{1,0},{2,3},{3,2},{4,5},{5,4},{6,7},{7,6},{8,9},{9,8},{10,11... | collective-permute-start | bytes 1179656 | tf_op jit(solution)/shard_map/cond/branch_1_fun/ppermute | solution.py:429
  150.0 25.1 %collective-permute-start.100 = (bf16[6,128,256]{2,1,0:T(8,128)(2,1)S(1)}, bf16[6,128,256]{2,1,0:T(8,128)(2,1)S(1)}, u32[]{:S(2)}, u32[]{:S(2)}) collective-permute-start(bf16[6,128,256]{2,1,0:T(8,128)(2,1)S(1)} %get-tuple-element.220), channel_id=1, source_target_pairs={{1,2},{2,1},{5,6},{6,5},{9,10},{10,9},{13,14},{14,13},{17,18},{18,... | collective-permute-start | bytes 1179656 | tf_op jit(solution)/shard_map/cond/branch_1_fun/ppermute | solution.py:430
  150.7 15.0 %collective-permute-start.101 = (bf16[128,256]{1,0:T(8,128)(2,1)S(1)}, bf16[128,256]{1,0:T(8,128)(2,1)S(1)}, u32[]{:S(2)}, u32[]{:S(2)}) collective-permute-start(bf16[128,256]{1,0:T(8,128)(2,1)S(1)} %get-tuple-element.222), channel_id=1, source_target_pairs={{0,8},{4,12},{8,0},{12,4},{16,24},{20,28},{24,16},{28,20},{1,9},{5... | collective-permute-start | bytes 196616 | tf_op jit(solution)/shard_map/cond/branch_1_fun/ppermute | solution.py:316
  169.9 5.2 %collective-permute-start.103 = (bf16[128,256]{1,0:T(8,128)(2,1)S(1)}, bf16[128,256]{1,0:T(8,128)(2,1)S(1)}, u32[]{:S(2)}, u32[]{:S(2)}) collective-permute-start(bf16[128,256]{1,0:T(8,128)(2,1)S(1)} %get-tuple-element.224), channel_id=1, source_target_pairs={{0,24},{4,28},{8,16},{12,20},{16,8},{20,12},{24,0},{28,4},{1,25},{... | collective-permute-start | bytes 196616 | tf_op jit(solution)/shard_map/cond/branch_1_fun/ppermute | solution.py:316
  182.8 5.9 %collective-permute-start.106 = (bf16[144,256]{1,0:T(8,128)(2,1)S(1)}, bf16[144,256]{1,0:T(8,128)(2,1)S(1)}, u32[]{:S(2)}, u32[]{:S(2)}) collective-permute-start(bf16[144,256]{1,0:T(8,128)(2,1)S(1)} %get-tuple-element.230), channel_id=1, source_target_pairs={{0,16},{4,20},{8,24},{12,28},{16,0},{20,4},{24,8},{28,12},{1,17},{... | collective-permute-start | bytes 221192 | tf_op jit(solution)/shard_map/cond/branch_1_fun/ppermute | solution.py:316
  183.2 5.4 %collective-permute-start.107 = (bf16[144,256]{1,0:T(8,128)(2,1)S(1)}, bf16[144,256]{1,0:T(8,128)(2,1)S(1)}, u32[]{:S(2)}, u32[]{:S(2)}) collective-permute-start(bf16[144,256]{1,0:T(8,128)(2,1)S(1)} %get-tuple-element.231), channel_id=1, source_target_pairs={{0,24},{4,28},{8,16},{12,20},{16,8},{20,12},{24,0},{28,4},{1,25},{... | collective-permute-start | bytes 221192 | tf_op jit(solution)/shard_map/cond/branch_1_fun/ppermute | solution.py:316
  184.5 8.6 %collective-permute-start.111 = (bf16[128,256]{1,0:T(8,128)(2,1)S(1)}, bf16[128,256]{1,0:T(8,128)(2,1)S(1)}, u32[]{:S(2)}, u32[]{:S(2)}) collective-permute-start(bf16[128,256]{1,0:T(8,128)(2,1)S(1)} %branch_1_fun.31.after_ref.refs_0_), channel_id=1, source_target_pairs={{0,1},{1,0},{2,3},{3,2},{4,5},{5,4},{6,7},{7,6},{8,9},{9,8},{10,11... | collective-permute-start | bytes 196616 | tf_op jit(solution)/shard_map/cond/branch_1_fun/ppermute | solution.py:316
  188.7 11.7 %collective-permute-start.108 = (bf16[144,256]{1,0:T(8,128)(2,1)S(1)}, bf16[144,256]{1,0:T(8,128)(2,1)S(1)}, u32[]{:S(2)}, u32[]{:S(2)}) collective-permute-start(bf16[144,256]{1,0:T(8,128)(2,1)S(1)} %branch_1_fun.34.refs_0_), channel_id=1, source_target_pairs={{0,1},{1,0},{2,3},{3,2},{4,5},{5,4},{6,7},{7,6},{8,9},{9,8},{10,11... | collective-permute-start | bytes 221192 | tf_op jit(solution)/shard_map/cond/branch_1_fun/ppermute | solution.py:316
  188.8 11.7 %collective-permute-start.109 = (bf16[144,256]{1,0:T(8,128)(2,1)S(1)}, bf16[144,256]{1,0:T(8,128)(2,1)S(1)}, u32[]{:S(2)}, u32[]{:S(2)}) collective-permute-start(bf16[144,256]{1,0:T(8,128)(2,1)S(1)} %branch_1_fun.34.refs_0_), channel_id=1, source_target_pairs={{0,2},{1,3},{2,0},{3,1},{4,6},{5,7},{6,4},{7,5},{8,10},{9,11},{10,... | collective-permute-start | bytes 221192 | tf_op jit(solution)/shard_map/cond/branch_1_fun/ppermute | solution.py:316
  192.1 8.3 %collective-permute-start.110 = (bf16[144,256]{1,0:T(8,128)(2,1)S(1)}, bf16[144,256]{1,0:T(8,128)(2,1)S(1)}, u32[]{:S(2)}, u32[]{:S(2)}) collective-permute-start(bf16[144,256]{1,0:T(8,128)(2,1)S(1)} %branch_1_fun.34.refs_0_), channel_id=1, source_target_pairs={{0,3},{1,2},{2,1},{3,0},{4,7},{5,6},{6,5},{7,4},{8,11},{9,10},{10,... | collective-permute-start | bytes 221192 | tf_op jit(solution)/shard_map/cond/branch_1_fun/ppermute | solution.py:316
  193.2 7.2 %collective-permute-start.112 = (bf16[128,256]{1,0:T(8,128)(2,1)S(1)}, bf16[128,256]{1,0:T(8,128)(2,1)S(1)}, u32[]{:S(2)}, u32[]{:S(2)}) collective-permute-start(bf16[128,256]{1,0:T(8,128)(2,1)S(1)} %branch_1_fun.35.refs_4_), channel_id=1, source_target_pairs={{0,2},{1,3},{2,0},{3,1},{4,6},{5,7},{6,4},{7,5},{8,10},{9,11},{10,... | collective-permute-start | bytes 196616 | tf_op jit(solution)/shard_map/cond/branch_1_fun/ppermute | solution.py:316
  201.2 5.0 %collective-permute-start.116 = (bf16[128,256]{1,0:T(8,128)(2,1)S(1)}, bf16[128,256]{1,0:T(8,128)(2,1)S(1)}, u32[]{:S(2)}, u32[]{:S(2)}) collective-permute-start(bf16[128,256]{1,0:T(8,128)(2,1)S(1)} %get-tuple-element.233.refs_0_), channel_id=1, source_target_pairs={{0,16},{4,20},{8,24},{12,28},{16,0},{20,4},{24,8},{28,12},{1,17},{... | collective-permute-start | bytes 196616 | tf_op jit(solution)/shard_map/cond/branch_1_fun/ppermute | solution.py:316
  203.0 5.2 %collective-permute-start.118 = (bf16[128,256]{1,0:T(8,128)(2,1)S(1)}, bf16[128,256]{1,0:T(8,128)(2,1)S(1)}, u32[]{:S(2)}, u32[]{:S(2)}) collective-permute-start(bf16[128,256]{1,0:T(8,128)(2,1)S(1)} %get-tuple-element.233.refs_0_), channel_id=1, source_target_pairs={{0,24},{4,28},{8,16},{12,20},{16,8},{20,12},{24,0},{28,4},{1,25},{... | collective-permute-start | bytes 196616 | tf_op jit(solution)/shard_map/cond/branch_1_fun/ppermute | solution.py:316
  (35 other events, 358.1 us)

commit v3 on v2

--- a/solution.py
+++ b/solution.py
@@ -88,19 +88,22 @@
         send_ref[tail, :] = tile
 
 
-def pack_blocks(table, row, face, source, disp_ref, out_ref, count):
+def pack_blocks(table, row, face, source, disp_ref, outs, count):
     blocks = table.shape[1]
     height = disp_ref.shape[1] // blocks
-    cap = out_ref.shape[0]
 
     def block(b, n):
         need = table[row, b] == face
         rows = pl.ds(pl.multiple_of(b * height, height), height)
-
-        @pl.when(need & (n < cap))
-        def _():
-            out_ref[n] = disp_ref[source, rows, :]
-
+        low = 0
+        for out_ref in outs:
+            high = low + out_ref.shape[0]
+
+            @pl.when(need & (n >= low) & (n < high))
+            def _(out_ref=out_ref, low=low):
+                out_ref[n - low] = disp_ref[source, rows, :]
+
+            low = high
         return n + need.astype(jnp.int32)
 
     return lax.fori_loop(0, blocks, block, count)
@@ -119,32 +122,46 @@
     theirs, ta, tb = tables
     count = zero
     for s in range(last + 1):
-        count = pack_blocks(theirs, s, odd, s, disp_ref, outs[2], count)
-    pack_blocks(ta, zodd * last, 3 - zodd, (1 - zodd) * last, disp_ref, za_ref, zero)
-    pack_blocks(tb, (1 - zodd) * last, 2 + zodd, zodd * last, disp_ref, zb_ref, zero)
-
-
-def first_kernel(chunk, wide, info, lam_ref, half_ref, keep_ref, send_ref):
+        count = pack_blocks(theirs, s, odd, s, disp_ref, outs[2:], count)
+    pack_blocks(ta, zodd * last, 3 - zodd, (1 - zodd) * last, disp_ref, [za_ref], zero)
+    pack_blocks(tb, (1 - zodd) * last, 2 + zodd, zodd * last, disp_ref, [zb_ref], zero)
+
+
+def open_kernel(chunk, wide, info, lam_ref, flex_ref, keep_ref, send_ref, disp_ref, flex, half, sems):
     subs = lam_ref.shape[0]
-    half_ref[...] = lam_ref[...].astype(BF16)
+
+    def fetch(s):
+        return pltpu.make_async_copy(flex_ref.at[s], flex.at[s], sems.at[s])
+
+    for s in range(subs):
+        fetch(s).start()
+    half[...] = lam_ref[...].astype(BF16)
     send_partial(
         chunk, wide, info[0], lambda rows: tree([lam_ref[s, rows, :] for s in range(subs)]),
         None, keep_ref, send_ref,
     )
 
+    def product(s, carry):
+        fetch(s).wait()
+        disp_ref[s] = jnp.dot(flex[s], half[s], preferred_element_type=F32).astype(BF16)
+        return carry
+
+    lax.fori_loop(0, subs, product, 0)
+
+
+def halo_kernel(packed, info, *refs):
+    tables, (disp_ref, *outs) = refs[: 3 * packed], refs[3 * packed :]
+    send_halo(info, disp_ref, outs, tables)
+
 
 def flex_kernel(step, packed, info, *refs):
     tables, refs = refs[: 3 * packed], refs[3 * packed :]
-    half_ref, flex_ref, *refs = refs
-    if step:
-        mean_ref, *refs = refs
-        if step > 1:
-            refs = refs[1:]
-        disp_ref, *outs, stack_ref, sem = refs
-        copy = pltpu.make_async_copy(mean_ref, stack_ref.at[step - 1], sem)
-        copy.start()
-    else:
-        disp_ref, *outs = refs
+    half_ref, flex_ref, mean_ref, *refs = refs
+    if step > 1:
+        refs = refs[1:]
+    disp_ref, *outs, stack_ref, sem = refs
+    copy = pltpu.make_async_copy(mean_ref, stack_ref.at[step - 1], sem)
+    copy.start()
 
     def product(s, carry):
         disp_ref[s] = jnp.dot(
@@ -154,21 +171,25 @@
 
     lax.fori_loop(0, half_ref.shape[0], product, 0)
     send_halo(info, disp_ref, outs, tables)
-    if step:
-        copy.wait()
+    copy.wait()
 
 
 def update_kernel(chunk, wide, step, last, info, lam_ref, dir_ref, alpha_ref, floor_ref, *refs):
     centre_refs = refs[:wide]
     refs = refs[wide:]
     if last:
-        _, new_ref, stack_ref, mean_ref, sems = refs
+        _, lam_out, stack_ref, new_ref, mean_ref, sems = refs
     else:
         new_ref, mean_ref, half_ref, keep_ref, send_ref = refs
     w = info[0]
     subs, _, cols = lam_ref.shape
     alpha = jnp.broadcast_to(alpha_ref[0:1, :], (chunk, cols))
     copies = []
+
+    def send(src, dst):
+        copies.append(pltpu.make_async_copy(src, dst, sems.at[len(copies)]))
+        copies[-1].start()
+
     for k in range(wide):
         rows = pl.ds(pl.multiple_of(jnp.bitwise_xor(w, k) * chunk, chunk), chunk)
         centre = centre_refs[k][...].astype(F32)
@@ -180,16 +201,13 @@
             low = jnp.concatenate([low] * (cols // low.shape[1]), axis=1)
             new = jnp.maximum(trial - centre, low)
             new_ref[s, rows, :] = new
-            if not last:
+            if last:
+                send(new_ref.at[s, rows, :], lam_out.at[s, rows, :])
+            else:
                 half_ref[s, rows, :] = new.astype(BF16)
                 total = new if total is None else total + new
         if last:
-            copies.append(
-                pltpu.make_async_copy(
-                    mean_ref.at[rows, :], stack_ref.at[step, rows, :], sems.at[k]
-                )
-            )
-            copies[-1].start()
+            send(mean_ref.at[rows, :], stack_ref.at[step, rows, :])
         else:
             out = send_ref if k % 2 else keep_ref
             out[pl.ds((k // 2) * chunk, chunk), :] = total.astype(BF16)
@@ -197,7 +215,9 @@
         copy.wait()
 
 
-def direct_kernel(chunk, wide, eight, caps, packed, info, side, powers, gap_ref, disp_ref, chip_ref, off_ref, za_ref, zb_ref, diri_ref, after_ref, dir_ref, keep_ref, send_ref, jump, work):
+def direct_kernel(chunk, wide, eight, caps, packed, info, side, powers, gap_ref, disp_ref, chip_ref, za_ref, zb_ref, *refs):
+    offs, refs = refs[: 1 + packed], refs[1 + packed :]
+    diri_ref, _, dir_ref, keep_ref, send_ref, jump, work = refs
     w, z = info[0], info[1]
     odd = jnp.bitwise_and(w, 1)
     zodd = jnp.bitwise_and(z, 1)
@@ -226,7 +246,10 @@
 
             pl.when(face == odd)(lambda: put(chip_ref[s, rows, :]))
             away = face == 1 - odd
-            pl.when(away)(lambda: put(take(off_ref, n)))
+            half = offs[0].shape[0] if packed else subs * blocks
+            pl.when(away & (n < half))(lambda: put(take(offs[0], n)))
+            if packed:
+                pl.when(away & (n >= half))(lambda: put(take(offs[1], n - half)))
             n = n + away.astype(jnp.int32)
             if s + 1 < subs:
                 pl.when(face == 2)(lambda: put(disp_ref[s + 1, rows, :]))
@@ -394,7 +417,7 @@
     full = sds((subs, rows, cols), F32)
     half = sds((subs, rows, cols), BF16)
     one = sds((rows, cols), BF16)
-    few = [sds((cap, rows // blocks, cols), BF16) for cap in (caps[1], caps[1], caps[0])]
+    few = [sds((cap, rows // blocks, cols), BF16) for cap in (caps[1], caps[1], -(-caps[0] // 2), caps[0] // 2)]
     part = sds(((wide // 2) * chunk, cols), BF16)
     message = sds(((wide // 2) * chunk + EXTRA, cols), BF16)
     stack = sds((ITERS, rows, cols), F32)
@@ -403,36 +426,47 @@
     arr = subs * rows * cols
 
     def search(step, sums, centres, packed):
-        mean, half_lam, lkeep, lsend = sums
-        ins = [info] + (tables if packed else []) + [half_lam, flexibility]
-        n_smem = len(ins) - 2
-        outs = [half] + (few if packed else [one, one])
-        spots = {}
+        head = [info] + (tables if packed else [])
+        outs = few if packed else [one, one]
         if step:
-            ins.append(mean)
-            if step > 1:
-                spots = dict(hbm_ins=(len(ins),), aliases={len(ins): len(outs)})
-                ins.append(centres)
-            spots |= dict(hbm_outs=(len(outs),), scratch=[pltpu.SemaphoreType.DMA])
-            outs = outs + [stack]
-        sends = call(
-            functools.partial(flex_kernel, step, packed), outs, n_smem, ins, mm,
-            op_bytes + arr * 6, **spots,
-        )
-        if step:
-            *sends, centres = sends
+            mean, half_lam, lkeep, lsend = sums
+            ins = head + [half_lam, flexibility, mean] + ([centres] if step > 1 else [])
+            *sends, centres = call(
+                functools.partial(flex_kernel, step, packed), [half, *outs, stack], len(head), ins,
+                mm, op_bytes + arr * 6, scratch=[pltpu.SemaphoreType.DMA],
+                hbm_ins=(len(head) + 3,), hbm_outs=(len(outs) + 1,),
+                aliases={len(head) + 3: len(outs) + 1} if step > 1 else None,
+            )
+        else:
+            lkeep, lsend, disp = call(
+                functools.partial(open_kernel, chunk, wide), [part, part, half], 1,
+                [info, multipliers, flexibility], mm, op_bytes + arr * 6,
+                scratch=[
+                    pltpu.VMEM((subs, rows, rows), BF16),
+                    pltpu.VMEM((subs, rows, cols), BF16),
+                    pltpu.SemaphoreType.DMA((subs,)),
+                ],
+                hbm_ins=(2,),
+            )
+            sends = [disp, *call(
+                functools.partial(halo_kernel, packed), outs, len(head), head + [disp],
+                arr, arr * 4, vmem=8,
+            )]
         lams = stage([lkeep, lsend], 0, chunk, wide, False)
         lams, sends = lax.optimization_barrier((lams, sends))
+        disp, za, zb = sends[:3]
+        offs = sends[3:] if packed else [disp]
+        if packed:
+            offs[0] = lax.ppermute(offs[0], "wide", away)
         own = scatter(lams, 1, chunk, wide, False)
-        disp, za, zb = sends[:3]
-        off = lax.ppermute(sends[3] if packed else disp, "wide", away)
+        offs[-1] = lax.ppermute(offs[-1], "wide", away)
         za = lax.ppermute(za, "eight", pairs_a)
         zb = lax.ppermute(zb, "eight", pairs_b)
         chip = swap(disp, "wide", 1)
         lam_parts = across_steps(own, chunk)
         direct, dkeep, dsend = call(
             functools.partial(direct_kernel, chunk, wide, eight, caps, packed), [half, message, message], 3,
-            [info, side, powers, gap, disp, chip, off, za, zb, dirichlet, own],
+            [info, side, powers, gap, disp, chip, za, zb, *offs, dirichlet, own],
             2 * mm, op_bytes + arr * 16,
             scratch=[pltpu.VMEM((subs, rows, cols), F32), pltpu.VMEM((subs, rows, cols), BF16)],
         )
@@ -454,17 +488,15 @@
             return call(kernel, outs, 1, ins, arr * 6, arr * 16)
         return call(
             kernel, [full, stack], 1, ins + [centres], arr * 6, arr * 16,
-            scratch=[pltpu.VMEM((rows, cols), F32), pltpu.SemaphoreType.DMA((wide,))],
-            hbm_ins=(len(ins),), hbm_outs=(1,), aliases={len(ins): 1},
+            scratch=[
+                pltpu.VMEM((subs, rows, cols), F32),
+                pltpu.VMEM((rows, cols), F32),
+                pltpu.SemaphoreType.DMA((wide * (subs + 1),)),
+            ],
+            hbm_ins=(len(ins),), hbm_outs=(0, 1), aliases={len(ins): 1},
         )
 
-    def start():
-        return call(
-            functools.partial(first_kernel, chunk, wide), [half, part, part], 1,
-            [info, multipliers], arr * 2, arr * 8,
-        )
-
-    first, _ = search(0, [None, *start()], None, True)
+    first, _ = search(0, None, None, True)
 
     def rest(packed, found):
         alphas = [found[1][0]]
@@ -477,7 +509,7 @@
         return lam, jnp.stack(alphas), centres
 
     def again(found):
-        found, _ = search(0, [None, *start()], None, False)
+        found, _ = search(0, None, None, False)
         return rest(False, found)
 
     return lax.cond(first[1][1, 0] <= 0, functools.partial(rest, True), again, first)

time: 214 us -> 204 us (0.953)
  waiting for transfers between devices: 109 us -> 93.6 us
  starting transfers between devices: 69.9 us -> 76 us
    ppermute x63, waiting for transfers between devices: 108 us -> 55.3 us  [swap(): return lax.ppermute(x, axis, [(i, i ^ mask) for i in range(n)])]
    ppermute x3 -> x6, waiting for transfers between devices: 0.01 us -> 37 us  [the longest x3 36.9 us: search(): offs[-1] = lax.ppermute(offs[-1], 'wide', away)]
    ppermute x63, starting transfers between devices: 55.1 us -> 62.9 us  [swap(): return lax.ppermute(x, axis, [(i, i ^ mask) for i in range(n)])]
  transfers between devices with their start and end apart: 75 -> 78, of which waited for: 32 -> 33; matrix products, arithmetic and copies ran while one was open for 0% -> 0% of each run, Pallas kernels for 4% -> 3%
where the time goes in v3:
time: 204 us
  waiting for transfers between devices  93.6 us (46%)
  starting transfers between devices  76 us (37%)
  Pallas kernels  30.4 us (15%)
  local copies, waits for them, and re-layouts  2.11 us (1%)
    ppermute x63, starting transfers between devices, swap(): return lax.ppermute(x, axis, [(i, i ^ mask) for i in range(n)])  62.9 us
    ppermute x63, waiting for transfers between devices, swap(): return lax.ppermute(x, axis, [(i, i ^ mask) for i in range(n)])  55.3 us
    ppermute x3, waiting for transfers between devices, search(): offs[-1] = lax.ppermute(offs[-1], 'wide', away)  36.9 us
    pallas_call x28, Pallas kernels, call(): pl.pallas_call(kernel, out_shape=outs, in_specs=[SMEM if i < n_smem else...  30.4 us
    ppermute x3, starting transfers between devices, search(): za = lax.ppermute(za, 'eight', pairs_a)  4.51 us
  transfers between devices with their start and end apart: 78, of which 33 were waited for; matrix products, arithmetic and copies ran while one was open for 0% of the time, Pallas kernels for 3%

profile of v3, /device:TPU:0, one launch (start us, length us, event | category | flops | bytes accessed | tf_op | source)
XLA Modules:
  0.0 204.3 jit_solution(12328437681081641546)
XLA Ops:
  0.7 5.5 %shard_map.96 = (bf16[512,256]{1,0:T(8,128)(2,1)S(1)}, bf16[512,256]{1,0:T(8,128)(2,1)S(1)}, bf16[2,1024,256]{2,1,0:T(8,128)(2,1)S(1)}) custom-call(s32[2]{0:T(128)S(1)} %pad_add_fusion.info, f32[2,1024,256]{2,1,0:T(8,128)} %lam_ref.1, bf16[2,1024,1024]{2,1,0:T(8,128)(2,1)} %flex_ref.1), custom_call_target="tpu_custom_call" | custom-call | flops 1073741824 | bytes 7340032 | tf_op jit(solution)/shard_map/pallas_call | solution.py:21
  6.8 3.5 %collective-permute-start.123 = (s32[2,8]{1,0:T(2,128)S(1)}, s32[2,8]{1,0:T(2,128)S(1)}, u32[]{:S(2)}, u32[]{:S(2)}) collective-permute-start(s32[2,8]{1,0:T(2,128)S(1)} %copy-done.5), channel_id=1, source_target_pairs={{0,28},{4,8},{8,4},{12,16},{16,12},{20,24},{24,20},{28,0},{1,29},{... | collective-permute-start | bytes 200 | tf_op jit(solution)/shard_map/ppermute | solution.py:408
  10.4 1.6 collective-permute-start.124
  12.6 1.3 collective-permute-done.124.refs_1_
  16.7 4.5 %collective-permute-start.127 = (bf16[6,128,256]{2,1,0:T(8,128)(2,1)S(1)}, bf16[6,128,256]{2,1,0:T(8,128)(2,1)S(1)}, u32[]{:S(2)}, u32[]{:S(2)}) collective-permute-start(bf16[6,128,256]{2,1,0:T(8,128)(2,1)S(1)} %get-tuple-element.284), channel_id=1, source_target_pairs={{0,1},{1,0},{2,3},{3,2},{4,5},{5,4},{6,7},{7,6},{8,9},{9,8},{10,11... | collective-permute-start | bytes 1179656 | tf_op jit(solution)/shard_map/ppermute | solution.py:463
  21.9 2.4 %collective-permute-start.133 = (bf16[128,256]{1,0:T(8,128)(2,1)S(1)}, bf16[128,256]{1,0:T(8,128)(2,1)S(1)}, u32[]{:S(2)}, u32[]{:S(2)}) collective-permute-start(bf16[128,256]{1,0:T(8,128)(2,1)S(1)} %get-tuple-element.291), channel_id=1, source_target_pairs={{0,24},{4,28},{8,16},{12,20},{16,8},{20,12},{24,0},{28,4},{1,25},{... | collective-permute-start | bytes 196616 | tf_op jit(solution)/shard_map/ppermute | solution.py:339
  24.3 2.8 %collective-permute-done.133.refs_3_ = bf16[128,256]{1,0:T(8,128)(2,1)S(1)} collective-permute-done((bf16[128,256]{1,0:T(8,128)(2,1)S(1)}, bf16[128,256]{1,0:T(8,128)(2,1)S(1)}, u32[]{:S(2)}, u32[]{:S(2)}) %collective-permute-start.133) | collective-permute-done | bytes 65568 | tf_op jit(solution)/shard_map/ppermute | solution.py:339
  27.6 12.1 %collective-permute-done.130.refs_1_ = bf16[4,128,256]{2,1,0:T(8,128)(2,1)S(1)} collective-permute-done((bf16[4,128,256]{2,1,0:T(8,128)(2,1)S(1)}, bf16[4,128,256]{2,1,0:T(8,128)(2,1)S(1)}, u32[]{:S(2)}, u32[]{:S(2)}) %collective-permute-start.130) | collective-permute-done | bytes 262176 | tf_op jit(solution)/shard_map/ppermute | solution.py:462
  39.8 4.2 %shard_map.100 = (bf16[2,1024,256]{2,1,0:T(8,128)(2,1)S(1)}, bf16[528,256]{1,0:T(8,128)(2,1)S(1)}, bf16[528,256]{1,0:T(8,128)(2,1)S(1)}) custom-call(s32[2]{0:T(128)S(1)} %pad_add_fusion.info, s32[2,8]{1,0:T(2,128)S(1)} %copy-done.5, s32[2]{0:T(128)S(1)} %copy-done.6, f32[2,1024,256]{2,1,0:T(8,128)S(1)} %copy-done.2, ...), custom_call_target="tpu_custom_call" | custom-call | flops 2147483648 | bytes 12582912 | tf_op jit(solution)/shard_map/pallas_call | solution.py:21
  44.0 1.5 collective-permute-start.134
  47.1 3.3 %collective-permute-start.137 = (bf16[144,256]{1,0:T(8,128)(2,1)S(1)}, bf16[144,256]{1,0:T(8,128)(2,1)S(1)}, u32[]{:S(2)}, u32[]{:S(2)}) collective-permute-start(bf16[144,256]{1,0:T(8,128)(2,1)S(1)} %get-tuple-element.297), channel_id=1, source_target_pairs={{0,24},{4,28},{8,16},{12,20},{16,8},{20,12},{24,0},{28,4},{1,25},{... | collective-permute-start | bytes 221192 | tf_op jit(solution)/shard_map/ppermute | solution.py:339
  50.3 1.4 collective-permute-start.141
  51.7 1.3 collective-permute-done.136.refs_2_
  53.1 3.8 %collective-permute-start.138 = (bf16[144,256]{1,0:T(8,128)(2,1)S(1)}, bf16[144,256]{1,0:T(8,128)(2,1)S(1)}, u32[]{:S(2)}, u32[]{:S(2)}) collective-permute-start(bf16[144,256]{1,0:T(8,128)(2,1)S(1)} %shard_map.102.refs_0_), channel_id=1, source_target_pairs={{0,1},{1,0},{2,3},{3,2},{4,5},{5,4},{6,7},{7,6},{8,9},{9,8},{10,11... | collective-permute-start | bytes 221192 | tf_op jit(solution)/shard_map/ppermute | solution.py:339
  57.0 2.4 %collective-permute-start.140 = (bf16[144,256]{1,0:T(8,128)(2,1)S(1)}, bf16[144,256]{1,0:T(8,128)(2,1)S(1)}, u32[]{:S(2)}, u32[]{:S(2)}) collective-permute-start(bf16[144,256]{1,0:T(8,128)(2,1)S(1)} %shard_map.102.refs_0_), channel_id=1, source_target_pairs={{0,3},{1,2},{2,1},{3,0},{4,7},{5,6},{6,5},{7,4},{8,11},{9,10},{10,... | collective-permute-start | bytes 221192 | tf_op jit(solution)/shard_map/ppermute | solution.py:339
  60.0 7.9 %collective-permute-done.142.refs_5_ = bf16[128,256]{1,0:T(8,128)(2,1)S(1)} collective-permute-done((bf16[128,256]{1,0:T(8,128)(2,1)S(1)}, bf16[128,256]{1,0:T(8,128)(2,1)S(1)}, u32[]{:S(2)}, u32[]{:S(2)}) %collective-permute-start.142) | collective-permute-done | bytes 65568 | tf_op jit(solution)/shard_map/ppermute | solution.py:339
  69.1 2.4 %collective-permute-start.148 = (bf16[128,256]{1,0:T(8,128)(2,1)S(1)}, bf16[128,256]{1,0:T(8,128)(2,1)S(1)}, u32[]{:S(2)}, u32[]{:S(2)}) collective-permute-start(bf16[128,256]{1,0:T(8,128)(2,1)S(1)} %get-tuple-element.300), channel_id=1, source_target_pairs={{0,24},{4,28},{8,16},{12,20},{16,8},{20,12},{24,0},{28,4},{1,25},{... | collective-permute-start | bytes 196616 | tf_op jit(solution)/shard_map/ppermute | solution.py:339
  75.6 128.1 %conditional.1 = (f32[2,1024,256]{2,1,0:T(8,128)}, f32[3,1024,256]{2,1,0:T(8,128)}, f32[3,256]{1,0:T(4,128)S(1)}) conditional(s32[]{:T(128)} %bitcast.8, (s32[2]{0:T(128)S(1)}, f32[2,1024,256]{2,1,0:T(8,128)S(1)}, bf16[2,1024,1024]{2,1,0:T(8,128)(2,1)S(1)}, s32[2,8]{1,0:T(2,128)S(1)}, s32[2]{0:T(128)S(1)}, /*index=5*/f32[2,1024,256]{2,1,0:T(8,128)S(1)}, ...), branch_computations={%region_0.1_spmd, %region_1.2_spmd} | conditional | flops 9677191168 | bytes 158391008 | solution.py:515
  77.8 2.7 %branch_1_fun.21 = (bf16[2,1024,256]{2,1,0:T(8,128)(2,1)S(1)}, bf16[6,128,256]{2,1,0:T(8,128)(2,1)S(1)}, bf16[6,128,256]{2,1,0:T(8,128)(2,1)S(1)}, bf16[5,128,25...) custom-call(s32[2]{0:T(128)S(1)} %get-tuple-element.151.info, ...), custom_call_target="tpu_custom_call" | custom-call | flops 1073741824 | bytes 7340032 | tf_op jit(solution)/shard_map/cond/branch_1_fun/pallas_call | solution.py:21
  80.7 1.4 collective-permute-start.78
  82.1 1.5 collective-permute-start.79
  85.2 2.4 %collective-permute-start.80 = (bf16[128,256]{1,0:T(8,128)(2,1)S(1)}, bf16[128,256]{1,0:T(8,128)(2,1)S(1)}, u32[]{:S(2)}, u32[]{:S(2)}) collective-permute-start(bf16[128,256]{1,0:T(8,128)(2,1)S(1)} %get-tuple-element.194), channel_id=1, source_target_pairs={{0,24},{4,28},{8,16},{12,20},{16,8},{20,12},{24,0},{28,4},{1,25},{... | collective-permute-start | bytes 196616 | tf_op jit(solution)/shard_map/cond/branch_1_fun/ppermute | solution.py:339
  87.6 2.8 %collective-permute-done.80.refs_3_ = bf16[128,256]{1,0:T(8,128)(2,1)S(1)} collective-permute-done((bf16[128,256]{1,0:T(8,128)(2,1)S(1)}, bf16[128,256]{1,0:T(8,128)(2,1)S(1)}, u32[]{:S(2)}, u32[]{:S(2)}) %collective-permute-start.80) | collective-permute-done | bytes 65568 | tf_op jit(solution)/shard_map/cond/branch_1_fun/ppermute | solution.py:339
  90.8 12.2 %collective-permute-done.77.refs_1_ = bf16[4,128,256]{2,1,0:T(8,128)(2,1)S(1)} collective-permute-done((bf16[4,128,256]{2,1,0:T(8,128)(2,1)S(1)}, bf16[4,128,256]{2,1,0:T(8,128)(2,1)S(1)}, u32[]{:S(2)}, u32[]{:S(2)}) %collective-permute-start.77) | collective-permute-done | bytes 262176 | tf_op jit(solution)/shard_map/cond/branch_1_fun/ppermute | solution.py:462
  103.0 4.2 %branch_1_fun.23 = (bf16[2,1024,256]{2,1,0:T(8,128)(2,1)S(1)}, bf16[528,256]{1,0:T(8,128)(2,1)S(1)}, bf16[528,256]{1,0:T(8,128)(2,1)S(1)}) custom-call(s32[2]{0:T(128)S(1)} %get-tuple-element.151.info, s32[2,8]{1,0:T(2,128)S(1)} %get-tuple-element.165.side, s32[2]{0:T(128)S(1)} %get-tuple-element.166.powers, f32[2,1024,256]{2,1,0:T(8,128)S(1)} %get-tuple-element.167.gap_ref, ...), custom_call_target="tpu_custom_call" | custom-call | flops 2147483648 | bytes 12582912 | tf_op jit(solution)/shard_map/cond/branch_1_fun/pallas_call | solution.py:21
  107.2 2.6 %collective-permute-start.81 = (bf16[528,256]{1,0:T(8,128)(2,1)S(1)}, bf16[528,256]{1,0:T(8,128)(2,1)S(1)}, u32[]{:S(2)}, u32[]{:S(2)}) collective-permute-start(bf16[528,256]{1,0:T(8,128)(2,1)S(1)} %get-tuple-element.197), channel_id=1, source_target_pairs={{0,4},{4,0},{8,12},{12,8},{16,20},{20,16},{24,28},{28,24},{1,5},{5... | collective-permute-start | bytes 811016 | tf_op jit(solution)/shard_map/cond/branch_1_fun/ppermute | solution.py:339
  111.2 3.4 %collective-permute-start.84 = (bf16[144,256]{1,0:T(8,128)(2,1)S(1)}, bf16[144,256]{1,0:T(8,128)(2,1)S(1)}, u32[]{:S(2)}, u32[]{:S(2)}) collective-permute-start(bf16[144,256]{1,0:T(8,128)(2,1)S(1)} %get-tuple-element.201), channel_id=1, source_target_pairs={{0,24},{4,28},{8,16},{12,20},{16,8},{20,12},{24,0},{28,4},{1,25},{... | collective-permute-start | bytes 221192 | tf_op jit(solution)/shard_map/cond/branch_1_fun/ppermute | solution.py:339
  115.9 1.3 collective-permute-done.83.refs_2_
  117.3 2.0 collective-permute-start.85
  119.7 2.1 %collective-permute-start.87 = (bf16[144,256]{1,0:T(8,128)(2,1)S(1)}, bf16[144,256]{1,0:T(8,128)(2,1)S(1)}, u32[]{:S(2)}, u32[]{:S(2)}) collective-permute-start(bf16[144,256]{1,0:T(8,128)(2,1)S(1)} %branch_1_fun.25.refs_0_), channel_id=1, source_target_pairs={{0,3},{1,2},{2,1},{3,0},{4,7},{5,6},{6,5},{7,4},{8,11},{9,10},{10,... | collective-permute-start | bytes 221192 | tf_op jit(solution)/shard_map/cond/branch_1_fun/ppermute | solution.py:339
  121.8 1.4 collective-permute-start.89
  123.2 7.1 %collective-permute-done.89.refs_5_ = bf16[128,256]{1,0:T(8,128)(2,1)S(1)} collective-permute-done((bf16[128,256]{1,0:T(8,128)(2,1)S(1)}, bf16[128,256]{1,0:T(8,128)(2,1)S(1)}, u32[]{:S(2)}, u32[]{:S(2)}) %collective-permute-start.89) | collective-permute-done | bytes 65568 | tf_op jit(solution)/shard_map/cond/branch_1_fun/ppermute | solution.py:339
  132.3 1.6 collective-permute-start.95
  135.9 1.6 collective-permute-done.95.refs_6_
  140.4 2.7 %branch_1_fun.30 = (bf16[2,1024,256]{2,1,0:T(8,128)(2,1)S(1)}, bf16[6,128,256]{2,1,0:T(8,128)(2,1)S(1)}, bf16[6,128,256]{2,1,0:T(8,128)(2,1)S(1)}, bf16[5,128,25...) custom-call(s32[2]{0:T(128)S(1)} %get-tuple-element.151.info, ...), custom_call_target="tpu_custom_call", output_to_operand_aliasing={{5}: (7, {})} | custom-call | flops 1073741824 | bytes 7340032 | tf_op jit(solution)/shard_map/cond/branch_1_fun/pallas_call | solution.py:21
  146.5 1.4 collective-permute-done.103.refs_1_
  147.9 1.6 collective-permute-start.105
  149.6 3.5 %collective-permute-done.105.refs_3_ = bf16[128,256]{1,0:T(8,128)(2,1)S(1)} collective-permute-done((bf16[128,256]{1,0:T(8,128)(2,1)S(1)}, bf16[128,256]{1,0:T(8,128)(2,1)S(1)}, u32[]{:S(2)}, u32[]{:S(2)}) %collective-permute-start.105) | collective-permute-done | bytes 65568 | tf_op jit(solution)/shard_map/cond/branch_1_fun/ppermute | solution.py:339
  153.1 12.6 %collective-permute-done.102.refs_1_ = bf16[4,128,256]{2,1,0:T(8,128)(2,1)S(1)} collective-permute-done((bf16[4,128,256]{2,1,0:T(8,128)(2,1)S(1)}, bf16[4,128,256]{2,1,0:T(8,128)(2,1)S(1)}, u32[]{:S(2)}, u32[]{:S(2)}) %collective-permute-start.102) | collective-permute-done | bytes 262176 | tf_op jit(solution)/shard_map/cond/branch_1_fun/ppermute | solution.py:462
  165.7 4.2 %branch_1_fun.32 = (bf16[2,1024,256]{2,1,0:T(8,128)(2,1)S(1)}, bf16[528,256]{1,0:T(8,128)(2,1)S(1)}, bf16[528,256]{1,0:T(8,128)(2,1)S(1)}) custom-call(s32[2]{0:T(128)S(1)} %get-tuple-element.151.info, s32[2,8]{1,0:T(2,128)S(1)} %get-tuple-element.165.side, s32[2]{0:T(128)S(1)} %get-tuple-element.166.powers, f32[2,1024,256]{2,1,0:T(8,128)S(1)} %get-tuple-element.167.gap_ref, ...), custom_call_target="tpu_custom_call" | custom-call | flops 2147483648 | bytes 12582912 | tf_op jit(solution)/shard_map/cond/branch_1_fun/pallas_call | solution.py:21
  169.9 2.0 collective-permute-start.106
  173.3 3.4 %collective-permute-start.109 = (bf16[144,256]{1,0:T(8,128)(2,1)S(1)}, bf16[144,256]{1,0:T(8,128)(2,1)S(1)}, u32[]{:S(2)}, u32[]{:S(2)}) collective-permute-start(bf16[144,256]{1,0:T(8,128)(2,1)S(1)} %get-tuple-element.234), channel_id=1, source_target_pairs={{0,24},{4,28},{8,16},{12,20},{16,8},{20,12},{24,0},{28,4},{1,25},{... | collective-permute-start | bytes 221192 | tf_op jit(solution)/shard_map/cond/branch_1_fun/ppermute | solution.py:339
  178.1 1.3 collective-permute-done.108.refs_2_
  179.5 2.5 %collective-permute-start.110 = (bf16[144,256]{1,0:T(8,128)(2,1)S(1)}, bf16[144,256]{1,0:T(8,128)(2,1)S(1)}, u32[]{:S(2)}, u32[]{:S(2)}) collective-permute-start(bf16[144,256]{1,0:T(8,128)(2,1)S(1)} %branch_1_fun.34.refs_0_), channel_id=1, source_target_pairs={{0,1},{1,0},{2,3},{3,2},{4,5},{5,4},{6,7},{7,6},{8,9},{9,8},{10,11... | collective-permute-start | bytes 221192 | tf_op jit(solution)/shard_map/cond/branch_1_fun/ppermute | solution.py:339
  182.0 2.4 %collective-permute-start.112 = (bf16[144,256]{1,0:T(8,128)(2,1)S(1)}, bf16[144,256]{1,0:T(8,128)(2,1)S(1)}, u32[]{:S(2)}, u32[]{:S(2)}) collective-permute-start(bf16[144,256]{1,0:T(8,128)(2,1)S(1)} %branch_1_fun.34.refs_0_), channel_id=1, source_target_pairs={{0,3},{1,2},{2,1},{3,0},{4,7},{5,6},{6,5},{7,4},{8,11},{9,10},{10,... | collective-permute-start | bytes 221192 | tf_op jit(solution)/shard_map/cond/branch_1_fun/ppermute | solution.py:339
  185.4 7.6 %collective-permute-done.114.refs_5_ = bf16[128,256]{1,0:T(8,128)(2,1)S(1)} collective-permute-done((bf16[128,256]{1,0:T(8,128)(2,1)S(1)}, bf16[128,256]{1,0:T(8,128)(2,1)S(1)}, u32[]{:S(2)}, u32[]{:S(2)}) %collective-permute-start.114) | collective-permute-done | bytes 65568 | tf_op jit(solution)/shard_map/cond/branch_1_fun/ppermute | solution.py:339
  194.5 2.1 %collective-permute-start.120 = (bf16[128,256]{1,0:T(8,128)(2,1)S(1)}, bf16[128,256]{1,0:T(8,128)(2,1)S(1)}, u32[]{:S(2)}, u32[]{:S(2)}) collective-permute-start(bf16[128,256]{1,0:T(8,128)(2,1)S(1)} %get-tuple-element.236.refs_0_), channel_id=1, source_target_pairs={{0,24},{4,28},{8,16},{12,20},{16,8},{20,12},{24,0},{28,4},{1,25},{... | collective-permute-start | bytes 196616 | tf_op jit(solution)/shard_map/cond/branch_1_fun/ppermute | solution.py:339
  201.3 2.4 %branch_1_fun.37 = (f32[2,1024,256]{2,1,0:T(8,128)}, f32[3,1024,256]{2,1,0:T(8,128)}) custom-call(s32[2]{0:T(128)S(1)} %get-tuple-element.151.info, f32[2,1024,256]{2,1,0:T(8,128)S(1)} %get-tuple-element.204.lam_ref, bf16[2,1024,256]{2,1,0:T(8,128)(2,1)S(1)} %get-tuple-element.228.dir_ref, ...), custom_call_target="tpu_custom_call", output_to_operand_aliasing={{1}: (13, {})} | custom-call | flops 3145728 | bytes 8388608 | tf_op jit(solution)/shard_map/cond/branch_1_fun/pallas_call | solution.py:21
  (163 shorter events, 40.0 us)
Async XLA Ops:
  6.3 9.0 %collective-permute-start.122 = (bf16[512,256]{1,0:T(8,128)(2,1)S(1)}, bf16[512,256]{1,0:T(8,128)(2,1)S(1)}, u32[]{:S(2)}, u32[]{:S(2)}) collective-permute-start(bf16[512,256]{1,0:T(8,128)(2,1)S(1)} %get-tuple-element.273), channel_id=1, source_target_pairs={{0,4},{4,0},{8,12},{12,8},{16,20},{20,16},{24,28},{28,24},{1,5},{5... | collective-permute-start | bytes 786440 | tf_op jit(solution)/shard_map/ppermute | solution.py:339
  6.8 5.8 %collective-permute-start.123 = (s32[2,8]{1,0:T(2,128)S(1)}, s32[2,8]{1,0:T(2,128)S(1)}, u32[]{:S(2)}, u32[]{:S(2)}) collective-permute-start(s32[2,8]{1,0:T(2,128)S(1)} %copy-done.5), channel_id=1, source_target_pairs={{0,28},{4,8},{8,4},{12,16},{16,12},{20,24},{24,20},{28,0},{1,29},{... | collective-permute-start | bytes 200 | tf_op jit(solution)/shard_map/ppermute | solution.py:408
  15.3 24.4 %collective-permute-start.126 = (bf16[2,1024,256]{2,1,0:T(8,128)(2,1)S(1)}, bf16[2,1024,256]{2,1,0:T(8,128)(2,1)S(1)}, u32[]{:S(2)}, u32[]{:S(2)}) collective-permute-start(bf16[2,1024,256]{2,1,0:T(8,128)(2,1)S(1)} %get-tuple-element.283.refs_3_.disp_ref), channel_id=1, source_target_pairs={{0,4},{4,0},{8,12},{12,8},{16,20},{20,16},{24,28},{28,24},{1,5},{5... | collective-permute-start | bytes 3145736 | tf_op jit(solution)/shard_map/ppermute | solution.py:339
  15.4 6.5 %collective-permute-start.131 = (bf16[128,256]{1,0:T(8,128)(2,1)S(1)}, bf16[128,256]{1,0:T(8,128)(2,1)S(1)}, u32[]{:S(2)}, u32[]{:S(2)}) collective-permute-start(bf16[128,256]{1,0:T(8,128)(2,1)S(1)} %get-tuple-element.289), channel_id=1, source_target_pairs={{0,8},{4,12},{8,0},{12,4},{16,24},{20,28},{24,16},{28,20},{1,9},{5... | collective-permute-start | bytes 196616 | tf_op jit(solution)/shard_map/ppermute | solution.py:339
  15.5 8.8 %collective-permute-start.132 = (bf16[128,256]{1,0:T(8,128)(2,1)S(1)}, bf16[128,256]{1,0:T(8,128)(2,1)S(1)}, u32[]{:S(2)}, u32[]{:S(2)}) collective-permute-start(bf16[128,256]{1,0:T(8,128)(2,1)S(1)} %get-tuple-element.290), channel_id=1, source_target_pairs={{0,16},{4,20},{8,24},{12,28},{16,0},{20,4},{24,8},{28,12},{1,17},{... | collective-permute-start | bytes 196616 | tf_op jit(solution)/shard_map/ppermute | solution.py:339
  16.7 23.1 %collective-permute-start.127 = (bf16[6,128,256]{2,1,0:T(8,128)(2,1)S(1)}, bf16[6,128,256]{2,1,0:T(8,128)(2,1)S(1)}, u32[]{:S(2)}, u32[]{:S(2)}) collective-permute-start(bf16[6,128,256]{2,1,0:T(8,128)(2,1)S(1)} %get-tuple-element.284), channel_id=1, source_target_pairs={{0,1},{1,0},{2,3},{3,2},{4,5},{5,4},{6,7},{7,6},{8,9},{9,8},{10,11... | collective-permute-start | bytes 1179656 | tf_op jit(solution)/shard_map/ppermute | solution.py:463
  21.2 18.6 %collective-permute-start.128 = (bf16[6,128,256]{2,1,0:T(8,128)(2,1)S(1)}, bf16[6,128,256]{2,1,0:T(8,128)(2,1)S(1)}, u32[]{:S(2)}, u32[]{:S(2)}) collective-permute-start(bf16[6,128,256]{2,1,0:T(8,128)(2,1)S(1)} %get-tuple-element.285), channel_id=1, source_target_pairs={{1,2},{2,1},{5,6},{6,5},{9,10},{10,9},{13,14},{14,13},{17,18},{18,... | collective-permute-start | bytes 1179656 | tf_op jit(solution)/shard_map/ppermute | solution.py:464
  21.9 5.2 %collective-permute-start.133 = (bf16[128,256]{1,0:T(8,128)(2,1)S(1)}, bf16[128,256]{1,0:T(8,128)(2,1)S(1)}, u32[]{:S(2)}, u32[]{:S(2)}) collective-permute-start(bf16[128,256]{1,0:T(8,128)(2,1)S(1)} %get-tuple-element.291), channel_id=1, source_target_pairs={{0,24},{4,28},{8,16},{12,20},{16,8},{20,12},{24,0},{28,4},{1,25},{... | collective-permute-start | bytes 196616 | tf_op jit(solution)/shard_map/ppermute | solution.py:339
  24.3 15.4 %collective-permute-start.129 = (bf16[5,128,256]{2,1,0:T(8,128)(2,1)S(1)}, bf16[5,128,256]{2,1,0:T(8,128)(2,1)S(1)}, u32[]{:S(2)}, u32[]{:S(2)}) collective-permute-start(bf16[5,128,256]{2,1,0:T(8,128)(2,1)S(1)} %get-tuple-element.286), channel_id=1, source_target_pairs={{0,28},{4,8},{8,4},{12,16},{16,12},{20,24},{24,20},{28,0},{1,29},{... | collective-permute-start | bytes 983048 | tf_op jit(solution)/shard_map/ppermute | solution.py:460
  27.1 12.6 %collective-permute-start.130 = (bf16[4,128,256]{2,1,0:T(8,128)(2,1)S(1)}, bf16[4,128,256]{2,1,0:T(8,128)(2,1)S(1)}, u32[]{:S(2)}, u32[]{:S(2)}) collective-permute-start(bf16[4,128,256]{2,1,0:T(8,128)(2,1)S(1)} %get-tuple-element.287), channel_id=1, source_target_pairs={{0,28},{4,8},{8,4},{12,16},{16,12},{20,24},{24,20},{28,0},{1,29},{... | collective-permute-start | bytes 786440 | tf_op jit(solution)/shard_map/ppermute | solution.py:462
  46.8 5.0 %collective-permute-start.135 = (bf16[144,256]{1,0:T(8,128)(2,1)S(1)}, bf16[144,256]{1,0:T(8,128)(2,1)S(1)}, u32[]{:S(2)}, u32[]{:S(2)}) collective-permute-start(bf16[144,256]{1,0:T(8,128)(2,1)S(1)} %get-tuple-element.295), channel_id=1, source_target_pairs={{0,8},{4,12},{8,0},{12,4},{16,24},{20,28},{24,16},{28,20},{1,9},{5... | collective-permute-start | bytes 221192 | tf_op jit(solution)/shard_map/ppermute | solution.py:339
  46.9 6.2 %collective-permute-start.136 = (bf16[144,256]{1,0:T(8,128)(2,1)S(1)}, bf16[144,256]{1,0:T(8,128)(2,1)S(1)}, u32[]{:S(2)}, u32[]{:S(2)}) collective-permute-start(bf16[144,256]{1,0:T(8,128)(2,1)S(1)} %get-tuple-element.296), channel_id=1, source_target_pairs={{0,16},{4,20},{8,24},{12,28},{16,0},{20,4},{24,8},{28,12},{1,17},{... | collective-permute-start | bytes 221192 | tf_op jit(solution)/shard_map/ppermute | solution.py:339
  47.1 6.0 %collective-permute-start.137 = (bf16[144,256]{1,0:T(8,128)(2,1)S(1)}, bf16[144,256]{1,0:T(8,128)(2,1)S(1)}, u32[]{:S(2)}, u32[]{:S(2)}) collective-permute-start(bf16[144,256]{1,0:T(8,128)(2,1)S(1)} %get-tuple-element.297), channel_id=1, source_target_pairs={{0,24},{4,28},{8,16},{12,20},{16,8},{20,12},{24,0},{28,4},{1,25},{... | collective-permute-start | bytes 221192 | tf_op jit(solution)/shard_map/ppermute | solution.py:339
  50.3 9.1 %collective-permute-start.141 = (bf16[128,256]{1,0:T(8,128)(2,1)S(1)}, bf16[128,256]{1,0:T(8,128)(2,1)S(1)}, u32[]{:S(2)}, u32[]{:S(2)}) collective-permute-start(bf16[128,256]{1,0:T(8,128)(2,1)S(1)} %shard_map.99.refs_3_.refs_0_), channel_id=1, source_target_pairs={{0,1},{1,0},{2,3},{3,2},{4,5},{5,4},{6,7},{7,6},{8,9},{9,8},{10,11... | collective-permute-start | bytes 196616 | tf_op jit(solution)/shard_map/ppermute | solution.py:339
  53.1 14.8 %collective-permute-start.138 = (bf16[144,256]{1,0:T(8,128)(2,1)S(1)}, bf16[144,256]{1,0:T(8,128)(2,1)S(1)}, u32[]{:S(2)}, u32[]{:S(2)}) collective-permute-start(bf16[144,256]{1,0:T(8,128)(2,1)S(1)} %shard_map.102.refs_0_), channel_id=1, source_target_pairs={{0,1},{1,0},{2,3},{3,2},{4,5},{5,4},{6,7},{7,6},{8,9},{9,8},{10,11... | collective-permute-start | bytes 221192 | tf_op jit(solution)/shard_map/ppermute | solution.py:339
  57.0 10.9 %collective-permute-start.139 = (bf16[144,256]{1,0:T(8,128)(2,1)S(1)}, bf16[144,256]{1,0:T(8,128)(2,1)S(1)}, u32[]{:S(2)}, u32[]{:S(2)}) collective-permute-start(bf16[144,256]{1,0:T(8,128)(2,1)S(1)} %shard_map.102.refs_0_), channel_id=1, source_target_pairs={{0,2},{1,3},{2,0},{3,1},{4,6},{5,7},{6,4},{7,5},{8,10},{9,11},{10,... | collective-permute-start | bytes 221192 | tf_op jit(solution)/shard_map/ppermute | solution.py:339
  57.0 10.9 %collective-permute-start.140 = (bf16[144,256]{1,0:T(8,128)(2,1)S(1)}, bf16[144,256]{1,0:T(8,128)(2,1)S(1)}, u32[]{:S(2)}, u32[]{:S(2)}) collective-permute-start(bf16[144,256]{1,0:T(8,128)(2,1)S(1)} %shard_map.102.refs_0_), channel_id=1, source_target_pairs={{0,3},{1,2},{2,1},{3,0},{4,7},{5,6},{6,5},{7,4},{8,11},{9,10},{10,... | collective-permute-start | bytes 221192 | tf_op jit(solution)/shard_map/ppermute | solution.py:339
  59.4 8.4 %collective-permute-start.142 = (bf16[128,256]{1,0:T(8,128)(2,1)S(1)}, bf16[128,256]{1,0:T(8,128)(2,1)S(1)}, u32[]{:S(2)}, u32[]{:S(2)}) collective-permute-start(bf16[128,256]{1,0:T(8,128)(2,1)S(1)} %shard_map.103.refs_4_), channel_id=1, source_target_pairs={{0,2},{1,3},{2,0},{3,1},{4,6},{5,7},{6,4},{7,5},{8,10},{9,11},{10,... | collective-permute-start | bytes 196616 | tf_op jit(solution)/shard_map/ppermute | solution.py:339
  69.1 5.2 %collective-permute-start.148 = (bf16[128,256]{1,0:T(8,128)(2,1)S(1)}, bf16[128,256]{1,0:T(8,128)(2,1)S(1)}, u32[]{:S(2)}, u32[]{:S(2)}) collective-permute-start(bf16[128,256]{1,0:T(8,128)(2,1)S(1)} %get-tuple-element.300), channel_id=1, source_target_pairs={{0,24},{4,28},{8,16},{12,20},{16,8},{20,12},{24,0},{28,4},{1,25},{... | collective-permute-start | bytes 196616 | tf_op jit(solution)/shard_map/ppermute | solution.py:339
  80.6 22.4 %collective-permute-start.73 = (bf16[2,1024,256]{2,1,0:T(8,128)(2,1)S(1)}, bf16[2,1024,256]{2,1,0:T(8,128)(2,1)S(1)}, u32[]{:S(2)}, u32[]{:S(2)}) collective-permute-start(bf16[2,1024,256]{2,1,0:T(8,128)(2,1)S(1)} %get-tuple-element.185.disp_ref), channel_id=1, source_target_pairs={{0,4},{4,0},{8,12},{12,8},{16,20},{20,16},{24,28},{28,24},{1,5},{5... | collective-permute-start | bytes 3145736 | tf_op jit(solution)/shard_map/cond/branch_1_fun/ppermute | solution.py:339
  82.1 5.4 %collective-permute-start.79 = (bf16[128,256]{1,0:T(8,128)(2,1)S(1)}, bf16[128,256]{1,0:T(8,128)(2,1)S(1)}, u32[]{:S(2)}, u32[]{:S(2)}) collective-permute-start(bf16[128,256]{1,0:T(8,128)(2,1)S(1)} %get-tuple-element.193), channel_id=1, source_target_pairs={{0,16},{4,20},{8,24},{12,28},{16,0},{20,4},{24,8},{28,12},{1,17},{... | collective-permute-start | bytes 196616 | tf_op jit(solution)/shard_map/cond/branch_1_fun/ppermute | solution.py:339
  83.7 19.3 %collective-permute-start.74 = (bf16[6,128,256]{2,1,0:T(8,128)(2,1)S(1)}, bf16[6,128,256]{2,1,0:T(8,128)(2,1)S(1)}, u32[]{:S(2)}, u32[]{:S(2)}) collective-permute-start(bf16[6,128,256]{2,1,0:T(8,128)(2,1)S(1)} %get-tuple-element.186), channel_id=1, source_target_pairs={{0,1},{1,0},{2,3},{3,2},{4,5},{5,4},{6,7},{7,6},{8,9},{9,8},{10,11... | collective-permute-start | bytes 1179656 | tf_op jit(solution)/shard_map/cond/branch_1_fun/ppermute | solution.py:463
  83.7 19.3 %collective-permute-start.75 = (bf16[6,128,256]{2,1,0:T(8,128)(2,1)S(1)}, bf16[6,128,256]{2,1,0:T(8,128)(2,1)S(1)}, u32[]{:S(2)}, u32[]{:S(2)}) collective-permute-start(bf16[6,128,256]{2,1,0:T(8,128)(2,1)S(1)} %get-tuple-element.187), channel_id=1, source_target_pairs={{1,2},{2,1},{5,6},{6,5},{9,10},{10,9},{13,14},{14,13},{17,18},{18,... | collective-permute-start | bytes 1179656 | tf_op jit(solution)/shard_map/cond/branch_1_fun/ppermute | solution.py:464
  85.2 5.2 %collective-permute-start.80 = (bf16[128,256]{1,0:T(8,128)(2,1)S(1)}, bf16[128,256]{1,0:T(8,128)(2,1)S(1)}, u32[]{:S(2)}, u32[]{:S(2)}) collective-permute-start(bf16[128,256]{1,0:T(8,128)(2,1)S(1)} %get-tuple-element.194), channel_id=1, source_target_pairs={{0,24},{4,28},{8,16},{12,20},{16,8},{20,12},{24,0},{28,4},{1,25},{... | collective-permute-start | bytes 196616 | tf_op jit(solution)/shard_map/cond/branch_1_fun/ppermute | solution.py:339
  87.6 15.4 %collective-permute-start.76 = (bf16[5,128,256]{2,1,0:T(8,128)(2,1)S(1)}, bf16[5,128,256]{2,1,0:T(8,128)(2,1)S(1)}, u32[]{:S(2)}, u32[]{:S(2)}) collective-permute-start(bf16[5,128,256]{2,1,0:T(8,128)(2,1)S(1)} %get-tuple-element.188), channel_id=1, source_target_pairs={{0,28},{4,8},{8,4},{12,16},{16,12},{20,24},{24,20},{28,0},{1,29},{... | collective-permute-start | bytes 983048 | tf_op jit(solution)/shard_map/cond/branch_1_fun/ppermute | solution.py:460
  90.3 12.6 %collective-permute-start.77 = (bf16[4,128,256]{2,1,0:T(8,128)(2,1)S(1)}, bf16[4,128,256]{2,1,0:T(8,128)(2,1)S(1)}, u32[]{:S(2)}, u32[]{:S(2)}) collective-permute-start(bf16[4,128,256]{2,1,0:T(8,128)(2,1)S(1)} %get-tuple-element.189), channel_id=1, source_target_pairs={{0,28},{4,8},{8,4},{12,16},{16,12},{20,24},{24,20},{28,0},{1,29},{... | collective-permute-start | bytes 786440 | tf_op jit(solution)/shard_map/cond/branch_1_fun/ppermute | solution.py:462
  111.1 6.2 %collective-permute-start.83 = (bf16[144,256]{1,0:T(8,128)(2,1)S(1)}, bf16[144,256]{1,0:T(8,128)(2,1)S(1)}, u32[]{:S(2)}, u32[]{:S(2)}) collective-permute-start(bf16[144,256]{1,0:T(8,128)(2,1)S(1)} %get-tuple-element.200), channel_id=1, source_target_pairs={{0,16},{4,20},{8,24},{12,28},{16,0},{20,4},{24,8},{28,12},{1,17},{... | collective-permute-start | bytes 221192 | tf_op jit(solution)/shard_map/cond/branch_1_fun/ppermute | solution.py:339
  111.2 6.1 %collective-permute-start.84 = (bf16[144,256]{1,0:T(8,128)(2,1)S(1)}, bf16[144,256]{1,0:T(8,128)(2,1)S(1)}, u32[]{:S(2)}, u32[]{:S(2)}) collective-permute-start(bf16[144,256]{1,0:T(8,128)(2,1)S(1)} %get-tuple-element.201), channel_id=1, source_target_pairs={{0,24},{4,28},{8,16},{12,20},{16,8},{20,12},{24,0},{28,4},{1,25},{... | collective-permute-start | bytes 221192 | tf_op jit(solution)/shard_map/cond/branch_1_fun/ppermute | solution.py:339
  114.6 7.2 %collective-permute-start.88 = (bf16[128,256]{1,0:T(8,128)(2,1)S(1)}, bf16[128,256]{1,0:T(8,128)(2,1)S(1)}, u32[]{:S(2)}, u32[]{:S(2)}) collective-permute-start(bf16[128,256]{1,0:T(8,128)(2,1)S(1)} %branch_1_fun.22.refs_3_.refs_0_), channel_id=1, source_target_pairs={{0,1},{1,0},{2,3},{3,2},{4,5},{5,4},{6,7},{7,6},{8,9},{9,8},{10,11... | collective-permute-start | bytes 196616 | tf_op jit(solution)/shard_map/cond/branch_1_fun/ppermute | solution.py:339
  117.3 13.0 %collective-permute-start.85 = (bf16[144,256]{1,0:T(8,128)(2,1)S(1)}, bf16[144,256]{1,0:T(8,128)(2,1)S(1)}, u32[]{:S(2)}, u32[]{:S(2)}) collective-permute-start(bf16[144,256]{1,0:T(8,128)(2,1)S(1)} %branch_1_fun.25.refs_0_), channel_id=1, source_target_pairs={{0,1},{1,0},{2,3},{3,2},{4,5},{5,4},{6,7},{7,6},{8,9},{9,8},{10,11... | collective-permute-start | bytes 221192 | tf_op jit(solution)/shard_map/cond/branch_1_fun/ppermute | solution.py:339
  119.3 11.0 %collective-permute-start.86 = (bf16[144,256]{1,0:T(8,128)(2,1)S(1)}, bf16[144,256]{1,0:T(8,128)(2,1)S(1)}, u32[]{:S(2)}, u32[]{:S(2)}) collective-permute-start(bf16[144,256]{1,0:T(8,128)(2,1)S(1)} %branch_1_fun.25.refs_0_), channel_id=1, source_target_pairs={{0,2},{1,3},{2,0},{3,1},{4,6},{5,7},{6,4},{7,5},{8,10},{9,11},{10,... | collective-permute-start | bytes 221192 | tf_op jit(solution)/shard_map/cond/branch_1_fun/ppermute | solution.py:339
  119.7 10.6 %collective-permute-start.87 = (bf16[144,256]{1,0:T(8,128)(2,1)S(1)}, bf16[144,256]{1,0:T(8,128)(2,1)S(1)}, u32[]{:S(2)}, u32[]{:S(2)}) collective-permute-start(bf16[144,256]{1,0:T(8,128)(2,1)S(1)} %branch_1_fun.25.refs_0_), channel_id=1, source_target_pairs={{0,3},{1,2},{2,1},{3,0},{4,7},{5,6},{6,5},{7,4},{8,11},{9,10},{10,... | collective-permute-start | bytes 221192 | tf_op jit(solution)/shard_map/cond/branch_1_fun/ppermute | solution.py:339
  121.8 8.5 %collective-permute-start.89 = (bf16[128,256]{1,0:T(8,128)(2,1)S(1)}, bf16[128,256]{1,0:T(8,128)(2,1)S(1)}, u32[]{:S(2)}, u32[]{:S(2)}) collective-permute-start(bf16[128,256]{1,0:T(8,128)(2,1)S(1)} %branch_1_fun.26.refs_4_), channel_id=1, source_target_pairs={{0,2},{1,3},{2,0},{3,1},{4,6},{5,7},{6,4},{7,5},{8,10},{9,11},{10,... | collective-permute-start | bytes 196616 | tf_op jit(solution)/shard_map/cond/branch_1_fun/ppermute | solution.py:339
  132.3 5.2 %collective-permute-start.95 = (bf16[128,256]{1,0:T(8,128)(2,1)S(1)}, bf16[128,256]{1,0:T(8,128)(2,1)S(1)}, u32[]{:S(2)}, u32[]{:S(2)}) collective-permute-start(bf16[128,256]{1,0:T(8,128)(2,1)S(1)} %get-tuple-element.203.refs_0_), channel_id=1, source_target_pairs={{0,24},{4,28},{8,16},{12,20},{16,8},{20,12},{24,0},{28,4},{1,25},{... | collective-permute-start | bytes 196616 | tf_op jit(solution)/shard_map/cond/branch_1_fun/ppermute | solution.py:339
  143.2 22.5 %collective-permute-start.98 = (bf16[2,1024,256]{2,1,0:T(8,128)(2,1)S(1)}, bf16[2,1024,256]{2,1,0:T(8,128)(2,1)S(1)}, u32[]{:S(2)}, u32[]{:S(2)}) collective-permute-start(bf16[2,1024,256]{2,1,0:T(8,128)(2,1)S(1)} %get-tuple-element.219.disp_ref), channel_id=1, source_target_pairs={{0,4},{4,0},{8,12},{12,8},{16,20},{20,16},{24,28},{28,24},{1,5},{5... | collective-permute-start | bytes 3145736 | tf_op jit(solution)/shard_map/cond/branch_1_fun/ppermute | solution.py:339
  145.8 19.9 %collective-permute-start.99 = (bf16[6,128,256]{2,1,0:T(8,128)(2,1)S(1)}, bf16[6,128,256]{2,1,0:T(8,128)(2,1)S(1)}, u32[]{:S(2)}, u32[]{:S(2)}) collective-permute-start(bf16[6,128,256]{2,1,0:T(8,128)(2,1)S(1)} %get-tuple-element.220), channel_id=1, source_target_pairs={{0,1},{1,0},{2,3},{3,2},{4,5},{5,4},{6,7},{7,6},{8,9},{9,8},{10,11... | collective-permute-start | bytes 1179656 | tf_op jit(solution)/shard_map/cond/branch_1_fun/ppermute | solution.py:463
  145.9 19.9 %collective-permute-start.100 = (bf16[6,128,256]{2,1,0:T(8,128)(2,1)S(1)}, bf16[6,128,256]{2,1,0:T(8,128)(2,1)S(1)}, u32[]{:S(2)}, u32[]{:S(2)}) collective-permute-start(bf16[6,128,256]{2,1,0:T(8,128)(2,1)S(1)} %get-tuple-element.221), channel_id=1, source_target_pairs={{1,2},{2,1},{5,6},{6,5},{9,10},{10,9},{13,14},{14,13},{17,18},{18,... | collective-permute-start | bytes 1179656 | tf_op jit(solution)/shard_map/cond/branch_1_fun/ppermute | solution.py:464
  147.9 5.2 %collective-permute-start.105 = (bf16[128,256]{1,0:T(8,128)(2,1)S(1)}, bf16[128,256]{1,0:T(8,128)(2,1)S(1)}, u32[]{:S(2)}, u32[]{:S(2)}) collective-permute-start(bf16[128,256]{1,0:T(8,128)(2,1)S(1)} %get-tuple-element.227), channel_id=1, source_target_pairs={{0,24},{4,28},{8,16},{12,20},{16,8},{20,12},{24,0},{28,4},{1,25},{... | collective-permute-start | bytes 196616 | tf_op jit(solution)/shard_map/cond/branch_1_fun/ppermute | solution.py:339
  149.6 16.2 %collective-permute-start.101 = (bf16[5,128,256]{2,1,0:T(8,128)(2,1)S(1)}, bf16[5,128,256]{2,1,0:T(8,128)(2,1)S(1)}, u32[]{:S(2)}, u32[]{:S(2)}) collective-permute-start(bf16[5,128,256]{2,1,0:T(8,128)(2,1)S(1)} %get-tuple-element.222), channel_id=1, source_target_pairs={{0,28},{4,8},{8,4},{12,16},{16,12},{20,24},{24,20},{28,0},{1,29},{... | collective-permute-start | bytes 983048 | tf_op jit(solution)/shard_map/cond/branch_1_fun/ppermute | solution.py:460
  153.1 12.6 %collective-permute-start.102 = (bf16[4,128,256]{2,1,0:T(8,128)(2,1)S(1)}, bf16[4,128,256]{2,1,0:T(8,128)(2,1)S(1)}, u32[]{:S(2)}, u32[]{:S(2)}) collective-permute-start(bf16[4,128,256]{2,1,0:T(8,128)(2,1)S(1)} %get-tuple-element.223), channel_id=1, source_target_pairs={{0,28},{4,8},{8,4},{12,16},{16,12},{20,24},{24,20},{28,0},{1,29},{... | collective-permute-start | bytes 786440 | tf_op jit(solution)/shard_map/cond/branch_1_fun/ppermute | solution.py:462
  173.3 6.2 %collective-permute-start.108 = (bf16[144,256]{1,0:T(8,128)(2,1)S(1)}, bf16[144,256]{1,0:T(8,128)(2,1)S(1)}, u32[]{:S(2)}, u32[]{:S(2)}) collective-permute-start(bf16[144,256]{1,0:T(8,128)(2,1)S(1)} %get-tuple-element.233), channel_id=1, source_target_pairs={{0,16},{4,20},{8,24},{12,28},{16,0},{20,4},{24,8},{28,12},{1,17},{... | collective-permute-start | bytes 221192 | tf_op jit(solution)/shard_map/cond/branch_1_fun/ppermute | solution.py:339
  173.3 6.1 %collective-permute-start.109 = (bf16[144,256]{1,0:T(8,128)(2,1)S(1)}, bf16[144,256]{1,0:T(8,128)(2,1)S(1)}, u32[]{:S(2)}, u32[]{:S(2)}) collective-permute-start(bf16[144,256]{1,0:T(8,128)(2,1)S(1)} %get-tuple-element.234), channel_id=1, source_target_pairs={{0,24},{4,28},{8,16},{12,20},{16,8},{20,12},{24,0},{28,4},{1,25},{... | collective-permute-start | bytes 221192 | tf_op jit(solution)/shard_map/cond/branch_1_fun/ppermute | solution.py:339
  176.7 7.7 %collective-permute-start.113 = (bf16[128,256]{1,0:T(8,128)(2,1)S(1)}, bf16[128,256]{1,0:T(8,128)(2,1)S(1)}, u32[]{:S(2)}, u32[]{:S(2)}) collective-permute-start(bf16[128,256]{1,0:T(8,128)(2,1)S(1)} %branch_1_fun.31.refs_3_.refs_0_), channel_id=1, source_target_pairs={{0,1},{1,0},{2,3},{3,2},{4,5},{5,4},{6,7},{7,6},{8,9},{9,8},{10,11... | collective-permute-start | bytes 196616 | tf_op jit(solution)/shard_map/cond/branch_1_fun/ppermute | solution.py:339
  179.5 13.5 %collective-permute-start.110 = (bf16[144,256]{1,0:T(8,128)(2,1)S(1)}, bf16[144,256]{1,0:T(8,128)(2,1)S(1)}, u32[]{:S(2)}, u32[]{:S(2)}) collective-permute-start(bf16[144,256]{1,0:T(8,128)(2,1)S(1)} %branch_1_fun.34.refs_0_), channel_id=1, source_target_pairs={{0,1},{1,0},{2,3},{3,2},{4,5},{5,4},{6,7},{7,6},{8,9},{9,8},{10,11... | collective-permute-start | bytes 221192 | tf_op jit(solution)/shard_map/cond/branch_1_fun/ppermute | solution.py:339
  182.0 11.0 %collective-permute-start.111 = (bf16[144,256]{1,0:T(8,128)(2,1)S(1)}, bf16[144,256]{1,0:T(8,128)(2,1)S(1)}, u32[]{:S(2)}, u32[]{:S(2)}) collective-permute-start(bf16[144,256]{1,0:T(8,128)(2,1)S(1)} %branch_1_fun.34.refs_0_), channel_id=1, source_target_pairs={{0,2},{1,3},{2,0},{3,1},{4,6},{5,7},{6,4},{7,5},{8,10},{9,11},{10,... | collective-permute-start | bytes 221192 | tf_op jit(solution)/shard_map/cond/branch_1_fun/ppermute | solution.py:339
  182.0 11.0 %collective-permute-start.112 = (bf16[144,256]{1,0:T(8,128)(2,1)S(1)}, bf16[144,256]{1,0:T(8,128)(2,1)S(1)}, u32[]{:S(2)}, u32[]{:S(2)}) collective-permute-start(bf16[144,256]{1,0:T(8,128)(2,1)S(1)} %branch_1_fun.34.refs_0_), channel_id=1, source_target_pairs={{0,3},{1,2},{2,1},{3,0},{4,7},{5,6},{6,5},{7,4},{8,11},{9,10},{10,... | collective-permute-start | bytes 221192 | tf_op jit(solution)/shard_map/cond/branch_1_fun/ppermute | solution.py:339
  184.4 8.5 %collective-permute-start.114 = (bf16[128,256]{1,0:T(8,128)(2,1)S(1)}, bf16[128,256]{1,0:T(8,128)(2,1)S(1)}, u32[]{:S(2)}, u32[]{:S(2)}) collective-permute-start(bf16[128,256]{1,0:T(8,128)(2,1)S(1)} %branch_1_fun.35.refs_4_), channel_id=1, source_target_pairs={{0,2},{1,3},{2,0},{3,1},{4,6},{5,7},{6,4},{7,5},{8,10},{9,11},{10,... | collective-permute-start | bytes 196616 | tf_op jit(solution)/shard_map/cond/branch_1_fun/ppermute | solution.py:339
  194.5 5.2 %collective-permute-start.120 = (bf16[128,256]{1,0:T(8,128)(2,1)S(1)}, bf16[128,256]{1,0:T(8,128)(2,1)S(1)}, u32[]{:S(2)}, u32[]{:S(2)}) collective-permute-start(bf16[128,256]{1,0:T(8,128)(2,1)S(1)} %get-tuple-element.236.refs_0_), channel_id=1, source_target_pairs={{0,24},{4,28},{8,16},{12,20},{16,8},{20,12},{24,0},{28,4},{1,25},{... | collective-permute-start | bytes 196616 | tf_op jit(solution)/shard_map/cond/branch_1_fun/ppermute | solution.py:339
  (38 other events, 366.5 us)

commit v4 on v3

--- a/solution.py
+++ b/solution.py
@@ -106,7 +106,7 @@
             low = high
         return n + need.astype(jnp.int32)
 
-    return lax.fori_loop(0, blocks, block, count)
+    return lax.fori_loop(0, blocks, block, count, unroll=True)
 
 
 def send_halo(info, disp_ref, outs, tables):
@@ -244,25 +244,39 @@
                     return ref[jnp.minimum(slot, ref.shape[0] - 1)]
                 return ref[s, rows, :] if len(ref.shape) == 3 else ref[rows, :]
 
-            pl.when(face == odd)(lambda: put(chip_ref[s, rows, :]))
             away = face == 1 - odd
-            half = offs[0].shape[0] if packed else subs * blocks
-            pl.when(away & (n < half))(lambda: put(take(offs[0], n)))
-            if packed:
-                pl.when(away & (n >= half))(lambda: put(take(offs[1], n - half)))
+            size = offs[0].shape[0] if packed else subs * blocks
+            up = (face == 2).astype(jnp.int32)
+            down = (face == 3).astype(jnp.int32)
+
+            @pl.when(face < 2)
+            def _():
+                pl.when(face == odd)(lambda: put(chip_ref[s, rows, :]))
+                pl.when(away & (n < size))(lambda: put(take(offs[0], n)))
+                if packed:
+                    pl.when(away & (n >= size))(lambda: put(take(offs[1], n - size)))
+
+            @pl.when(face == 2)
+            def _():
+                if s + 1 < subs:
+                    put(disp_ref[s + 1, rows, :])
+                else:
+                    pl.when(zodd == 0)(lambda: put(take(za_ref, above)))
+                    pl.when(zodd == 1)(lambda: put(take(zb_ref, above)))
+
+            @pl.when(face == 3)
+            def _():
+                if s > 0:
+                    put(disp_ref[s - 1, rows, :])
+                else:
+                    pl.when(zodd == 1)(lambda: put(take(za_ref, below)))
+                    pl.when(zodd == 0)(lambda: put(take(zb_ref, below)))
+
             n = n + away.astype(jnp.int32)
-            if s + 1 < subs:
-                pl.when(face == 2)(lambda: put(disp_ref[s + 1, rows, :]))
-            else:
-                pl.when((face == 2) & (zodd == 0))(lambda: put(take(za_ref, above)))
-                pl.when((face == 2) & (zodd == 1))(lambda: put(take(zb_ref, above)))
-                above = above + (face == 2).astype(jnp.int32)
-            if s > 0:
-                pl.when(face == 3)(lambda: put(disp_ref[s - 1, rows, :]))
-            else:
-                pl.when((face == 3) & (zodd == 1))(lambda: put(take(za_ref, below)))
-                pl.when((face == 3) & (zodd == 0))(lambda: put(take(zb_ref, below)))
-                below = below + (face == 3).astype(jnp.int32)
+            if s + 1 == subs:
+                above = above + up
+            if s == 0:
+                below = below + down
             return n, above, below
 
         counts = lax.fori_loop(0, blocks, block, counts)
@@ -305,7 +319,7 @@
 
 
 def add_kernel(chunk, chunks, ways_in, ways_out, extra, *refs):
-    ins, outs = refs[:ways_in], refs[ways_in:]
+    ins, outs = refs[:ways_in], refs[-ways_out:]
     for c in range(chunks):
         rows = pl.ds(c * chunk, chunk)
         total = tree([r[rows, :].astype(F32) for r in ins]).astype(BF16)
@@ -366,18 +380,6 @@
     return [x] + [swap(x, "eight", q) for q in range(1, size)]
 
 
-def across_steps(x, chunk):
-    size = lax.axis_size("eight")
-    q = 1
-    while 2 * q < size:
-        (x,) = call(
-            functools.partial(add_kernel, chunk, 1, 2, 1, False), [sds(x.shape, BF16)], 0,
-            [x, swap(x, "eight", q)], 2 * x.size, 6 * x.size, vmem=8,
-        )
-        q *= 2
-    return [x, swap(x, "eight", q)]
-
-
 def gather(centre, wide):
     groups = stage_bits(wide)
     have = {0: centre}
@@ -399,7 +401,7 @@
     eight = lax.axis_size("eight")
     count = wide * eight * subs
     chunk = rows // wide
-    caps = (-(-subs * blocks * 9 // 16), -(-blocks * 3 // 4))
+    caps = (-(-subs * blocks * 5 // 8), -(-blocks * 3 // 4))
     away = [(i, (i + 1) % wide if i % 2 else (i - 1) % wide) for i in range(wide)]
     pairs_a = [(i, i ^ 1) for i in range(eight) if i ^ 1 < eight]
     pairs_b = [(i, i + 1 if i % 2 else i - 1) for i in range(1, eight - 1 + eight % 2)]
@@ -463,15 +465,26 @@
         za = lax.ppermute(za, "eight", pairs_a)
         zb = lax.ppermute(zb, "eight", pairs_b)
         chip = swap(disp, "wide", 1)
-        lam_parts = across_steps(own, chunk)
+        lam_parts = [own] + ([swap(own, "eight", 1)] if eight > 1 else [])
         direct, dkeep, dsend = call(
-            functools.partial(direct_kernel, chunk, wide, eight, caps, packed), [half, message, message], 3,
+            functools.partial(direct_kernel, chunk, wide, eight, caps, packed),
+            [half, message, message], 3,
             [info, side, powers, gap, disp, chip, za, zb, *offs, dirichlet, own],
             2 * mm, op_bytes + arr * 16,
-            scratch=[pltpu.VMEM((subs, rows, cols), F32), pltpu.VMEM((subs, rows, cols), BF16)],
+            scratch=[
+                pltpu.VMEM((subs, rows, cols), F32),
+                pltpu.VMEM((subs, rows, cols), BF16),
+            ],
         )
         dirs = stage([dkeep, dsend], 0, chunk, wide, True)
-        dir_parts = across(scatter(dirs, 1, chunk, wide, True))
+        for q in range(1, eight.bit_length() - 1):
+            (own,) = call(
+                functools.partial(add_kernel, chunk, 1, 2, 1, False), [sds(own.shape, BF16)], 0,
+                [*lam_parts, dkeep], 2 * own.size, 6 * own.size, vmem=8,
+            )
+            lam_parts = [own, swap(own, "eight", 1 << q)]
+        dirs = scatter(dirs, 1, chunk, wide, True)
+        dir_parts = across(dirs)
         centre, alpha = call(
             functools.partial(centre_kernel, chunk, eight, float(count)),
             [sds((chunk, cols), BF16), sds((8, cols), F32)], 0, dir_parts + lam_parts,

time: 204 us -> 206 us (level)
  starting transfers between devices: 76 us -> 79.7 us
    ppermute x3, waiting for transfers between devices: 0.01 us -> 23.9 us  [search(): offs[0] = lax.ppermute(offs[0], 'wide', away)]
    ppermute x3, waiting for transfers between devices: 36.9 us -> 19.6 us  [search(): offs[-1] = lax.ppermute(offs[-1], 'wide', away)]
    ppermute x63, waiting for transfers between devices: 55.3 us -> 48.5 us  [swap(): return lax.ppermute(x, axis, [(i, i ^ mask) for i in range(n)])]
    ppermute x3, starting transfers between devices: 0.82 us -> 3.24 us  [search(): offs[-1] = lax.ppermute(offs[-1], 'wide', away)]
  transfers between devices with their start and end apart: 78 -> 78, of which waited for: 33 -> 35; matrix products, arithmetic and copies ran while one was open for 0% -> 0% of each run, Pallas kernels for 3% -> 3%
where the time goes in v4:
time: 206 us
  waiting for transfers between devices  93.4 us (45%)
  starting transfers between devices  79.7 us (39%)
  Pallas kernels  28.9 us (14%)
  local copies, waits for them, and re-layouts  2.11 us (1%)
    ppermute x63, starting transfers between devices, swap(): return lax.ppermute(x, axis, [(i, i ^ mask) for i in range(n)])  62.5 us
    ppermute x63, waiting for transfers between devices, swap(): return lax.ppermute(x, axis, [(i, i ^ mask) for i in range(n)])  48.5 us
    pallas_call x28, Pallas kernels, call(): pl.pallas_call(kernel, out_shape=outs, in_specs=[SMEM if i < n_smem else...  28.9 us
    ppermute x3, waiting for transfers between devices, search(): offs[0] = lax.ppermute(offs[0], 'wide', away)  23.9 us
    ppermute x3, waiting for transfers between devices, search(): offs[-1] = lax.ppermute(offs[-1], 'wide', away)  19.6 us
    ppermute x3, starting transfers between devices, search(): za = lax.ppermute(za, 'eight', pairs_a)  4.6 us
  transfers between devices with their start and end apart: 78, of which 35 were waited for; matrix products, arithmetic and copies ran while one was open for 0% of the time, Pallas kernels for 3%

profile of v4, /device:TPU:0, one launch (start us, length us, event | category | flops | bytes accessed | tf_op | source)
XLA Modules:
  0.0 206.2 jit_solution(4994930231997122844)
XLA Ops:
  0.7 5.5 %shard_map.96 = (bf16[512,256]{1,0:T(8,128)(2,1)S(1)}, bf16[512,256]{1,0:T(8,128)(2,1)S(1)}, bf16[2,1024,256]{2,1,0:T(8,128)(2,1)S(1)}) custom-call(s32[2]{0:T(128)S(1)} %pad_add_fusion.info, f32[2,1024,256]{2,1,0:T(8,128)} %lam_ref.1, bf16[2,1024,1024]{2,1,0:T(8,128)(2,1)} %flex_ref.1), custom_call_target="tpu_custom_call" | custom-call | flops 1073741824 | bytes 7340032 | tf_op jit(solution)/shard_map/pallas_call | solution.py:21
  6.8 3.5 %collective-permute-start.123 = (s32[2,8]{1,0:T(2,128)S(1)}, s32[2,8]{1,0:T(2,128)S(1)}, u32[]{:S(2)}, u32[]{:S(2)}) collective-permute-start(s32[2,8]{1,0:T(2,128)S(1)} %copy-done.5), channel_id=1, source_target_pairs={{0,28},{4,8},{8,4},{12,16},{16,12},{20,24},{24,20},{28,0},{1,29},{... | collective-permute-start | bytes 200 | tf_op jit(solution)/shard_map/ppermute | solution.py:410
  10.4 1.6 collective-permute-start.124
  16.4 2.3 %collective-permute-start.133 = (bf16[128,256]{1,0:T(8,128)(2,1)S(1)}, bf16[128,256]{1,0:T(8,128)(2,1)S(1)}, u32[]{:S(2)}, u32[]{:S(2)}) collective-permute-start(bf16[128,256]{1,0:T(8,128)(2,1)S(1)} %get-tuple-element.291), channel_id=1, source_target_pairs={{0,24},{4,28},{8,16},{12,20},{16,8},{20,12},{24,0},{28,4},{1,25},{... | collective-permute-start | bytes 196616 | tf_op jit(solution)/shard_map/ppermute | solution.py:353
  18.6 4.6 %collective-permute-start.127 = (bf16[6,128,256]{2,1,0:T(8,128)(2,1)S(1)}, bf16[6,128,256]{2,1,0:T(8,128)(2,1)S(1)}, u32[]{:S(2)}, u32[]{:S(2)}) collective-permute-start(bf16[6,128,256]{2,1,0:T(8,128)(2,1)S(1)} %get-tuple-element.284), channel_id=1, source_target_pairs={{0,1},{1,0},{2,3},{3,2},{4,5},{5,4},{6,7},{7,6},{8,9},{9,8},{10,11... | collective-permute-start | bytes 1179656 | tf_op jit(solution)/shard_map/ppermute | solution.py:465
  24.0 2.6 %collective-permute-start.130 = (bf16[5,128,256]{2,1,0:T(8,128)(2,1)S(1)}, bf16[5,128,256]{2,1,0:T(8,128)(2,1)S(1)}, u32[]{:S(2)}, u32[]{:S(2)}) collective-permute-start(bf16[5,128,256]{2,1,0:T(8,128)(2,1)S(1)} %get-tuple-element.287), channel_id=1, source_target_pairs={{0,28},{4,8},{8,4},{12,16},{16,12},{20,24},{24,20},{28,0},{1,29},{... | collective-permute-start | bytes 983048 | tf_op jit(solution)/shard_map/ppermute | solution.py:464
  26.7 8.2 %collective-permute-done.129.refs_0_ = bf16[5,128,256]{2,1,0:T(8,128)(2,1)S(1)} collective-permute-done((bf16[5,128,256]{2,1,0:T(8,128)(2,1)S(1)}, bf16[5,128,256]{2,1,0:T(8,128)(2,1)S(1)}, u32[]{:S(2)}, u32[]{:S(2)}) %collective-permute-start.129) | collective-permute-done | bytes 327712 | tf_op jit(solution)/shard_map/ppermute | solution.py:462
  34.9 5.6 %collective-permute-done.130.refs_1_ = bf16[5,128,256]{2,1,0:T(8,128)(2,1)S(1)} collective-permute-done((bf16[5,128,256]{2,1,0:T(8,128)(2,1)S(1)}, bf16[5,128,256]{2,1,0:T(8,128)(2,1)S(1)}, u32[]{:S(2)}, u32[]{:S(2)}) %collective-permute-start.130) | collective-permute-done | bytes 327712 | tf_op jit(solution)/shard_map/ppermute | solution.py:464
  40.5 4.0 %shard_map.100 = (bf16[2,1024,256]{2,1,0:T(8,128)(2,1)S(1)}, bf16[528,256]{1,0:T(8,128)(2,1)S(1)}, bf16[528,256]{1,0:T(8,128)(2,1)S(1)}) custom-call(s32[2]{0:T(128)S(1)} %pad_add_fusion.info, s32[2,8]{1,0:T(2,128)S(1)} %copy-done.5, s32[2]{0:T(128)S(1)} %copy-done.6, f32[2,1024,256]{2,1,0:T(8,128)S(1)} %copy-done.2, ...), custom_call_target="tpu_custom_call" | custom-call | flops 2147483648 | bytes 12582912 | tf_op jit(solution)/shard_map/pallas_call | solution.py:21
  44.5 1.9 collective-permute-start.134
  47.8 3.4 %collective-permute-start.137 = (bf16[144,256]{1,0:T(8,128)(2,1)S(1)}, bf16[144,256]{1,0:T(8,128)(2,1)S(1)}, u32[]{:S(2)}, u32[]{:S(2)}) collective-permute-start(bf16[144,256]{1,0:T(8,128)(2,1)S(1)} %get-tuple-element.297), channel_id=1, source_target_pairs={{0,24},{4,28},{8,16},{12,20},{16,8},{20,12},{24,0},{28,4},{1,25},{... | collective-permute-start | bytes 221192 | tf_op jit(solution)/shard_map/ppermute | solution.py:353
  51.2 2.0 collective-permute-start.141
  54.0 4.3 %collective-permute-start.138 = (bf16[144,256]{1,0:T(8,128)(2,1)S(1)}, bf16[144,256]{1,0:T(8,128)(2,1)S(1)}, u32[]{:S(2)}, u32[]{:S(2)}) collective-permute-start(bf16[144,256]{1,0:T(8,128)(2,1)S(1)} %shard_map.102.refs_0_), channel_id=1, source_target_pairs={{0,1},{1,0},{2,3},{3,2},{4,5},{5,4},{6,7},{7,6},{8,9},{9,8},{10,11... | collective-permute-start | bytes 221192 | tf_op jit(solution)/shard_map/ppermute | solution.py:353
  58.3 2.4 %collective-permute-start.140 = (bf16[144,256]{1,0:T(8,128)(2,1)S(1)}, bf16[144,256]{1,0:T(8,128)(2,1)S(1)}, u32[]{:S(2)}, u32[]{:S(2)}) collective-permute-start(bf16[144,256]{1,0:T(8,128)(2,1)S(1)} %shard_map.102.refs_0_), channel_id=1, source_target_pairs={{0,3},{1,2},{2,1},{3,0},{4,7},{5,6},{6,5},{7,4},{8,11},{9,10},{10,... | collective-permute-start | bytes 221192 | tf_op jit(solution)/shard_map/ppermute | solution.py:353
  61.3 7.9 %collective-permute-done.142.refs_5_ = bf16[128,256]{1,0:T(8,128)(2,1)S(1)} collective-permute-done((bf16[128,256]{1,0:T(8,128)(2,1)S(1)}, bf16[128,256]{1,0:T(8,128)(2,1)S(1)}, u32[]{:S(2)}, u32[]{:S(2)}) %collective-permute-start.142) | collective-permute-done | bytes 65568 | tf_op jit(solution)/shard_map/ppermute | solution.py:353
  70.4 2.4 %collective-permute-start.148 = (bf16[128,256]{1,0:T(8,128)(2,1)S(1)}, bf16[128,256]{1,0:T(8,128)(2,1)S(1)}, u32[]{:S(2)}, u32[]{:S(2)}) collective-permute-start(bf16[128,256]{1,0:T(8,128)(2,1)S(1)} %get-tuple-element.300), channel_id=1, source_target_pairs={{0,24},{4,28},{8,16},{12,20},{16,8},{20,12},{24,0},{28,4},{1,25},{... | collective-permute-start | bytes 196616 | tf_op jit(solution)/shard_map/ppermute | solution.py:353
  76.9 128.7 %conditional.1 = (f32[2,1024,256]{2,1,0:T(8,128)}, f32[3,1024,256]{2,1,0:T(8,128)}, f32[3,256]{1,0:T(4,128)S(1)}) conditional(s32[]{:T(128)} %bitcast.8, (s32[2]{0:T(128)S(1)}, f32[2,1024,256]{2,1,0:T(8,128)S(1)}, bf16[2,1024,1024]{2,1,0:T(8,128)(2,1)S(1)}, s32[2,8]{1,0:T(2,128)S(1)}, s32[2]{0:T(128)S(1)}, /*index=5*/f32[2,1024,256]{2,1,0:T(8,128)S(1)}, ...), branch_computations={%region_0.1_spmd, %region_1.2_spmd} | conditional | flops 9677191168 | bytes 158391008 | solution.py:528
  79.1 2.4 %branch_1_fun.21 = (bf16[2,1024,256]{2,1,0:T(8,128)(2,1)S(1)}, bf16[6,128,256]{2,1,0:T(8,128)(2,1)S(1)}, bf16[6,128,256]{2,1,0:T(8,128)(2,1)S(1)}, bf16[5,128,25...) custom-call(s32[2]{0:T(128)S(1)} %get-tuple-element.151.info, ...), custom_call_target="tpu_custom_call" | custom-call | flops 1073741824 | bytes 7340032 | tf_op jit(solution)/shard_map/cond/branch_1_fun/pallas_call | solution.py:21
  81.7 1.5 collective-permute-start.78
  83.2 1.5 collective-permute-start.79
  90.1 7.6 %collective-permute-done.76.refs_0_ = bf16[5,128,256]{2,1,0:T(8,128)(2,1)S(1)} collective-permute-done((bf16[5,128,256]{2,1,0:T(8,128)(2,1)S(1)}, bf16[5,128,256]{2,1,0:T(8,128)(2,1)S(1)}, u32[]{:S(2)}, u32[]{:S(2)}) %collective-permute-start.76) | collective-permute-done | bytes 327712 | tf_op jit(solution)/shard_map/cond/branch_1_fun/ppermute | solution.py:462
  97.8 7.0 %collective-permute-done.77.refs_1_ = bf16[5,128,256]{2,1,0:T(8,128)(2,1)S(1)} collective-permute-done((bf16[5,128,256]{2,1,0:T(8,128)(2,1)S(1)}, bf16[5,128,256]{2,1,0:T(8,128)(2,1)S(1)}, u32[]{:S(2)}, u32[]{:S(2)}) %collective-permute-start.77) | collective-permute-done | bytes 327712 | tf_op jit(solution)/shard_map/cond/branch_1_fun/ppermute | solution.py:464
  104.8 4.0 %branch_1_fun.23 = (bf16[2,1024,256]{2,1,0:T(8,128)(2,1)S(1)}, bf16[528,256]{1,0:T(8,128)(2,1)S(1)}, bf16[528,256]{1,0:T(8,128)(2,1)S(1)}) custom-call(s32[2]{0:T(128)S(1)} %get-tuple-element.151.info, s32[2,8]{1,0:T(2,128)S(1)} %get-tuple-element.165.side, s32[2]{0:T(128)S(1)} %get-tuple-element.166.powers, f32[2,1024,256]{2,1,0:T(8,128)S(1)} %get-tuple-element.167.gap_ref, ...), custom_call_target="tpu_custom_call" | custom-call | flops 2147483648 | bytes 12582912 | tf_op jit(solution)/shard_map/cond/branch_1_fun/pallas_call | solution.py:21
  108.9 1.5 collective-permute-done.81.refs_1_
  110.5 1.5 collective-permute-start.82
  111.9 1.8 collective-permute-start.83
  114.0 2.1 %collective-permute-start.88 = (bf16[128,256]{1,0:T(8,128)(2,1)S(1)}, bf16[128,256]{1,0:T(8,128)(2,1)S(1)}, u32[]{:S(2)}, u32[]{:S(2)}) collective-permute-start(bf16[128,256]{1,0:T(8,128)(2,1)S(1)} %branch_1_fun.22.refs_3_.refs_0_), channel_id=1, source_target_pairs={{0,1},{1,0},{2,3},{3,2},{4,5},{5,4},{6,7},{7,6},{8,9},{9,8},{10,11... | collective-permute-start | bytes 196616 | tf_op jit(solution)/shard_map/cond/branch_1_fun/ppermute | solution.py:353
  117.2 1.8 collective-permute-done.84.refs_3_
  119.1 1.6 collective-permute-start.85
  121.2 2.3 %collective-permute-start.87 = (bf16[144,256]{1,0:T(8,128)(2,1)S(1)}, bf16[144,256]{1,0:T(8,128)(2,1)S(1)}, u32[]{:S(2)}, u32[]{:S(2)}) collective-permute-start(bf16[144,256]{1,0:T(8,128)(2,1)S(1)} %branch_1_fun.25.refs_0_), channel_id=1, source_target_pairs={{0,3},{1,2},{2,1},{3,0},{4,7},{5,6},{6,5},{7,4},{8,11},{9,10},{10,... | collective-permute-start | bytes 221192 | tf_op jit(solution)/shard_map/cond/branch_1_fun/ppermute | solution.py:353
  124.7 7.0 %collective-permute-done.89.refs_5_ = bf16[128,256]{1,0:T(8,128)(2,1)S(1)} collective-permute-done((bf16[128,256]{1,0:T(8,128)(2,1)S(1)}, bf16[128,256]{1,0:T(8,128)(2,1)S(1)}, u32[]{:S(2)}, u32[]{:S(2)}) %collective-permute-start.89) | collective-permute-done | bytes 65568 | tf_op jit(solution)/shard_map/cond/branch_1_fun/ppermute | solution.py:353
  133.6 1.7 collective-permute-start.95
  137.1 1.7 collective-permute-done.95.refs_6_
  141.7 2.4 %branch_1_fun.30 = (bf16[2,1024,256]{2,1,0:T(8,128)(2,1)S(1)}, bf16[6,128,256]{2,1,0:T(8,128)(2,1)S(1)}, bf16[6,128,256]{2,1,0:T(8,128)(2,1)S(1)}, bf16[5,128,25...) custom-call(s32[2]{0:T(128)S(1)} %get-tuple-element.151.info, ...), custom_call_target="tpu_custom_call", output_to_operand_aliasing={{5}: (7, {})} | custom-call | flops 1073741824 | bytes 7340032 | tf_op jit(solution)/shard_map/cond/branch_1_fun/pallas_call | solution.py:21
  150.2 1.9 collective-permute-done.105.refs_3_
  152.5 8.1 %collective-permute-done.101.refs_0_ = bf16[5,128,256]{2,1,0:T(8,128)(2,1)S(1)} collective-permute-done((bf16[5,128,256]{2,1,0:T(8,128)(2,1)S(1)}, bf16[5,128,256]{2,1,0:T(8,128)(2,1)S(1)}, u32[]{:S(2)}, u32[]{:S(2)}) %collective-permute-start.101) | collective-permute-done | bytes 327712 | tf_op jit(solution)/shard_map/cond/branch_1_fun/ppermute | solution.py:462
  160.7 7.0 %collective-permute-done.102.refs_1_ = bf16[5,128,256]{2,1,0:T(8,128)(2,1)S(1)} collective-permute-done((bf16[5,128,256]{2,1,0:T(8,128)(2,1)S(1)}, bf16[5,128,256]{2,1,0:T(8,128)(2,1)S(1)}, u32[]{:S(2)}, u32[]{:S(2)}) %collective-permute-start.102) | collective-permute-done | bytes 327712 | tf_op jit(solution)/shard_map/cond/branch_1_fun/ppermute | solution.py:464
  167.7 4.0 %branch_1_fun.32 = (bf16[2,1024,256]{2,1,0:T(8,128)(2,1)S(1)}, bf16[528,256]{1,0:T(8,128)(2,1)S(1)}, bf16[528,256]{1,0:T(8,128)(2,1)S(1)}) custom-call(s32[2]{0:T(128)S(1)} %get-tuple-element.151.info, s32[2,8]{1,0:T(2,128)S(1)} %get-tuple-element.165.side, s32[2]{0:T(128)S(1)} %get-tuple-element.166.powers, f32[2,1024,256]{2,1,0:T(8,128)S(1)} %get-tuple-element.167.gap_ref, ...), custom_call_target="tpu_custom_call" | custom-call | flops 2147483648 | bytes 12582912 | tf_op jit(solution)/shard_map/cond/branch_1_fun/pallas_call | solution.py:21
  171.8 1.5 collective-permute-done.106.refs_1_
  173.6 1.7 collective-permute-start.108
  175.3 1.7 collective-permute-start.109
  177.0 2.6 %collective-permute-start.113 = (bf16[128,256]{1,0:T(8,128)(2,1)S(1)}, bf16[128,256]{1,0:T(8,128)(2,1)S(1)}, u32[]{:S(2)}, u32[]{:S(2)}) collective-permute-start(bf16[128,256]{1,0:T(8,128)(2,1)S(1)} %branch_1_fun.31.refs_3_.refs_0_), channel_id=1, source_target_pairs={{0,1},{1,0},{2,3},{3,2},{4,5},{5,4},{6,7},{7,6},{8,9},{9,8},{10,11... | collective-permute-start | bytes 196616 | tf_op jit(solution)/shard_map/cond/branch_1_fun/ppermute | solution.py:353
  180.6 3.3 %collective-permute-start.110 = (bf16[144,256]{1,0:T(8,128)(2,1)S(1)}, bf16[144,256]{1,0:T(8,128)(2,1)S(1)}, u32[]{:S(2)}, u32[]{:S(2)}) collective-permute-start(bf16[144,256]{1,0:T(8,128)(2,1)S(1)} %branch_1_fun.34.refs_0_), channel_id=1, source_target_pairs={{0,1},{1,0},{2,3},{3,2},{4,5},{5,4},{6,7},{7,6},{8,9},{9,8},{10,11... | collective-permute-start | bytes 221192 | tf_op jit(solution)/shard_map/cond/branch_1_fun/ppermute | solution.py:353
  183.9 2.4 %collective-permute-start.112 = (bf16[144,256]{1,0:T(8,128)(2,1)S(1)}, bf16[144,256]{1,0:T(8,128)(2,1)S(1)}, u32[]{:S(2)}, u32[]{:S(2)}) collective-permute-start(bf16[144,256]{1,0:T(8,128)(2,1)S(1)} %branch_1_fun.34.refs_0_), channel_id=1, source_target_pairs={{0,3},{1,2},{2,1},{3,0},{4,7},{5,6},{6,5},{7,4},{8,11},{9,10},{10,... | collective-permute-start | bytes 221192 | tf_op jit(solution)/shard_map/cond/branch_1_fun/ppermute | solution.py:353
  187.2 7.5 %collective-permute-done.114.refs_5_ = bf16[128,256]{1,0:T(8,128)(2,1)S(1)} collective-permute-done((bf16[128,256]{1,0:T(8,128)(2,1)S(1)}, bf16[128,256]{1,0:T(8,128)(2,1)S(1)}, u32[]{:S(2)}, u32[]{:S(2)}) %collective-permute-start.114) | collective-permute-done | bytes 65568 | tf_op jit(solution)/shard_map/cond/branch_1_fun/ppermute | solution.py:353
  196.4 1.9 collective-permute-start.120
  198.3 1.4 collective-permute-done.116.refs_2_
  203.2 2.4 %branch_1_fun.37 = (f32[2,1024,256]{2,1,0:T(8,128)}, f32[3,1024,256]{2,1,0:T(8,128)}) custom-call(s32[2]{0:T(128)S(1)} %get-tuple-element.151.info, f32[2,1024,256]{2,1,0:T(8,128)S(1)} %get-tuple-element.204.lam_ref, bf16[2,1024,256]{2,1,0:T(8,128)(2,1)S(1)} %get-tuple-element.228.dir_ref, ...), custom_call_target="tpu_custom_call", output_to_operand_aliasing={{1}: (13, {})} | custom-call | flops 3145728 | bytes 8388608 | tf_op jit(solution)/shard_map/cond/branch_1_fun/pallas_call | solution.py:21
  (163 shorter events, 44.8 us)
Async XLA Ops:
  6.3 8.7 %collective-permute-start.122 = (bf16[512,256]{1,0:T(8,128)(2,1)S(1)}, bf16[512,256]{1,0:T(8,128)(2,1)S(1)}, u32[]{:S(2)}, u32[]{:S(2)}) collective-permute-start(bf16[512,256]{1,0:T(8,128)(2,1)S(1)} %get-tuple-element.273), channel_id=1, source_target_pairs={{0,4},{4,0},{8,12},{12,8},{16,20},{20,16},{24,28},{28,24},{1,5},{5... | collective-permute-start | bytes 786440 | tf_op jit(solution)/shard_map/ppermute | solution.py:353
  6.8 5.8 %collective-permute-start.123 = (s32[2,8]{1,0:T(2,128)S(1)}, s32[2,8]{1,0:T(2,128)S(1)}, u32[]{:S(2)}, u32[]{:S(2)}) collective-permute-start(s32[2,8]{1,0:T(2,128)S(1)} %copy-done.5), channel_id=1, source_target_pairs={{0,28},{4,8},{8,4},{12,16},{16,12},{20,24},{24,20},{28,0},{1,29},{... | collective-permute-start | bytes 200 | tf_op jit(solution)/shard_map/ppermute | solution.py:410
  15.0 25.5 %collective-permute-start.126 = (bf16[2,1024,256]{2,1,0:T(8,128)(2,1)S(1)}, bf16[2,1024,256]{2,1,0:T(8,128)(2,1)S(1)}, u32[]{:S(2)}, u32[]{:S(2)}) collective-permute-start(bf16[2,1024,256]{2,1,0:T(8,128)(2,1)S(1)} %get-tuple-element.283.refs_3_.disp_ref), channel_id=1, source_target_pairs={{0,4},{4,0},{8,12},{12,8},{16,20},{20,16},{24,28},{28,24},{1,5},{5... | collective-permute-start | bytes 3145736 | tf_op jit(solution)/shard_map/ppermute | solution.py:353
  15.1 8.2 %collective-permute-start.131 = (bf16[128,256]{1,0:T(8,128)(2,1)S(1)}, bf16[128,256]{1,0:T(8,128)(2,1)S(1)}, u32[]{:S(2)}, u32[]{:S(2)}) collective-permute-start(bf16[128,256]{1,0:T(8,128)(2,1)S(1)} %get-tuple-element.289), channel_id=1, source_target_pairs={{0,8},{4,12},{8,0},{12,4},{16,24},{20,28},{24,16},{28,20},{1,9},{5... | collective-permute-start | bytes 196616 | tf_op jit(solution)/shard_map/ppermute | solution.py:353
  15.2 8.8 %collective-permute-start.132 = (bf16[128,256]{1,0:T(8,128)(2,1)S(1)}, bf16[128,256]{1,0:T(8,128)(2,1)S(1)}, u32[]{:S(2)}, u32[]{:S(2)}) collective-permute-start(bf16[128,256]{1,0:T(8,128)(2,1)S(1)} %get-tuple-element.290), channel_id=1, source_target_pairs={{0,16},{4,20},{8,24},{12,28},{16,0},{20,4},{24,8},{28,12},{1,17},{... | collective-permute-start | bytes 196616 | tf_op jit(solution)/shard_map/ppermute | solution.py:353
  16.4 7.7 %collective-permute-start.133 = (bf16[128,256]{1,0:T(8,128)(2,1)S(1)}, bf16[128,256]{1,0:T(8,128)(2,1)S(1)}, u32[]{:S(2)}, u32[]{:S(2)}) collective-permute-start(bf16[128,256]{1,0:T(8,128)(2,1)S(1)} %get-tuple-element.291), channel_id=1, source_target_pairs={{0,24},{4,28},{8,16},{12,20},{16,8},{20,12},{24,0},{28,4},{1,25},{... | collective-permute-start | bytes 196616 | tf_op jit(solution)/shard_map/ppermute | solution.py:353
  18.6 21.8 %collective-permute-start.127 = (bf16[6,128,256]{2,1,0:T(8,128)(2,1)S(1)}, bf16[6,128,256]{2,1,0:T(8,128)(2,1)S(1)}, u32[]{:S(2)}, u32[]{:S(2)}) collective-permute-start(bf16[6,128,256]{2,1,0:T(8,128)(2,1)S(1)} %get-tuple-element.284), channel_id=1, source_target_pairs={{0,1},{1,0},{2,3},{3,2},{4,5},{5,4},{6,7},{7,6},{8,9},{9,8},{10,11... | collective-permute-start | bytes 1179656 | tf_op jit(solution)/shard_map/ppermute | solution.py:465
  23.2 17.2 %collective-permute-start.128 = (bf16[6,128,256]{2,1,0:T(8,128)(2,1)S(1)}, bf16[6,128,256]{2,1,0:T(8,128)(2,1)S(1)}, u32[]{:S(2)}, u32[]{:S(2)}) collective-permute-start(bf16[6,128,256]{2,1,0:T(8,128)(2,1)S(1)} %get-tuple-element.285), channel_id=1, source_target_pairs={{1,2},{2,1},{5,6},{6,5},{9,10},{10,9},{13,14},{14,13},{17,18},{18,... | collective-permute-start | bytes 1179656 | tf_op jit(solution)/shard_map/ppermute | solution.py:466
  23.9 11.0 %collective-permute-start.129 = (bf16[5,128,256]{2,1,0:T(8,128)(2,1)S(1)}, bf16[5,128,256]{2,1,0:T(8,128)(2,1)S(1)}, u32[]{:S(2)}, u32[]{:S(2)}) collective-permute-start(bf16[5,128,256]{2,1,0:T(8,128)(2,1)S(1)} %get-tuple-element.286), channel_id=1, source_target_pairs={{0,28},{4,8},{8,4},{12,16},{16,12},{20,24},{24,20},{28,0},{1,29},{... | collective-permute-start | bytes 983048 | tf_op jit(solution)/shard_map/ppermute | solution.py:462
  24.0 16.4 %collective-permute-start.130 = (bf16[5,128,256]{2,1,0:T(8,128)(2,1)S(1)}, bf16[5,128,256]{2,1,0:T(8,128)(2,1)S(1)}, u32[]{:S(2)}, u32[]{:S(2)}) collective-permute-start(bf16[5,128,256]{2,1,0:T(8,128)(2,1)S(1)} %get-tuple-element.287), channel_id=1, source_target_pairs={{0,28},{4,8},{8,4},{12,16},{16,12},{20,24},{24,20},{28,0},{1,29},{... | collective-permute-start | bytes 983048 | tf_op jit(solution)/shard_map/ppermute | solution.py:464
  47.7 5.6 %collective-permute-start.135 = (bf16[144,256]{1,0:T(8,128)(2,1)S(1)}, bf16[144,256]{1,0:T(8,128)(2,1)S(1)}, u32[]{:S(2)}, u32[]{:S(2)}) collective-permute-start(bf16[144,256]{1,0:T(8,128)(2,1)S(1)} %get-tuple-element.295), channel_id=1, source_target_pairs={{0,8},{4,12},{8,0},{12,4},{16,24},{20,28},{24,16},{28,20},{1,9},{5... | collective-permute-start | bytes 221192 | tf_op jit(solution)/shard_map/ppermute | solution.py:353
  47.8 6.2 %collective-permute-start.136 = (bf16[144,256]{1,0:T(8,128)(2,1)S(1)}, bf16[144,256]{1,0:T(8,128)(2,1)S(1)}, u32[]{:S(2)}, u32[]{:S(2)}) collective-permute-start(bf16[144,256]{1,0:T(8,128)(2,1)S(1)} %get-tuple-element.296), channel_id=1, source_target_pairs={{0,16},{4,20},{8,24},{12,28},{16,0},{20,4},{24,8},{28,12},{1,17},{... | collective-permute-start | bytes 221192 | tf_op jit(solution)/shard_map/ppermute | solution.py:353
  47.8 6.1 %collective-permute-start.137 = (bf16[144,256]{1,0:T(8,128)(2,1)S(1)}, bf16[144,256]{1,0:T(8,128)(2,1)S(1)}, u32[]{:S(2)}, u32[]{:S(2)}) collective-permute-start(bf16[144,256]{1,0:T(8,128)(2,1)S(1)} %get-tuple-element.297), channel_id=1, source_target_pairs={{0,24},{4,28},{8,16},{12,20},{16,8},{20,12},{24,0},{28,4},{1,25},{... | collective-permute-start | bytes 221192 | tf_op jit(solution)/shard_map/ppermute | solution.py:353
  51.2 9.5 %collective-permute-start.141 = (bf16[128,256]{1,0:T(8,128)(2,1)S(1)}, bf16[128,256]{1,0:T(8,128)(2,1)S(1)}, u32[]{:S(2)}, u32[]{:S(2)}) collective-permute-start(bf16[128,256]{1,0:T(8,128)(2,1)S(1)} %shard_map.99.refs_3_.refs_0_), channel_id=1, source_target_pairs={{0,1},{1,0},{2,3},{3,2},{4,5},{5,4},{6,7},{7,6},{8,9},{9,8},{10,11... | collective-permute-start | bytes 196616 | tf_op jit(solution)/shard_map/ppermute | solution.py:353
  54.0 15.2 %collective-permute-start.138 = (bf16[144,256]{1,0:T(8,128)(2,1)S(1)}, bf16[144,256]{1,0:T(8,128)(2,1)S(1)}, u32[]{:S(2)}, u32[]{:S(2)}) collective-permute-start(bf16[144,256]{1,0:T(8,128)(2,1)S(1)} %shard_map.102.refs_0_), channel_id=1, source_target_pairs={{0,1},{1,0},{2,3},{3,2},{4,5},{5,4},{6,7},{7,6},{8,9},{9,8},{10,11... | collective-permute-start | bytes 221192 | tf_op jit(solution)/shard_map/ppermute | solution.py:353
  58.3 10.9 %collective-permute-start.139 = (bf16[144,256]{1,0:T(8,128)(2,1)S(1)}, bf16[144,256]{1,0:T(8,128)(2,1)S(1)}, u32[]{:S(2)}, u32[]{:S(2)}) collective-permute-start(bf16[144,256]{1,0:T(8,128)(2,1)S(1)} %shard_map.102.refs_0_), channel_id=1, source_target_pairs={{0,2},{1,3},{2,0},{3,1},{4,6},{5,7},{6,4},{7,5},{8,10},{9,11},{10,... | collective-permute-start | bytes 221192 | tf_op jit(solution)/shard_map/ppermute | solution.py:353
  58.3 10.9 %collective-permute-start.140 = (bf16[144,256]{1,0:T(8,128)(2,1)S(1)}, bf16[144,256]{1,0:T(8,128)(2,1)S(1)}, u32[]{:S(2)}, u32[]{:S(2)}) collective-permute-start(bf16[144,256]{1,0:T(8,128)(2,1)S(1)} %shard_map.102.refs_0_), channel_id=1, source_target_pairs={{0,3},{1,2},{2,1},{3,0},{4,7},{5,6},{6,5},{7,4},{8,11},{9,10},{10,... | collective-permute-start | bytes 221192 | tf_op jit(solution)/shard_map/ppermute | solution.py:353
  60.8 8.4 %collective-permute-start.142 = (bf16[128,256]{1,0:T(8,128)(2,1)S(1)}, bf16[128,256]{1,0:T(8,128)(2,1)S(1)}, u32[]{:S(2)}, u32[]{:S(2)}) collective-permute-start(bf16[128,256]{1,0:T(8,128)(2,1)S(1)} %shard_map.103.refs_4_), channel_id=1, source_target_pairs={{0,2},{1,3},{2,0},{3,1},{4,6},{5,7},{6,4},{7,5},{8,10},{9,11},{10,... | collective-permute-start | bytes 196616 | tf_op jit(solution)/shard_map/ppermute | solution.py:353
  70.4 5.2 %collective-permute-start.148 = (bf16[128,256]{1,0:T(8,128)(2,1)S(1)}, bf16[128,256]{1,0:T(8,128)(2,1)S(1)}, u32[]{:S(2)}, u32[]{:S(2)}) collective-permute-start(bf16[128,256]{1,0:T(8,128)(2,1)S(1)} %get-tuple-element.300), channel_id=1, source_target_pairs={{0,24},{4,28},{8,16},{12,20},{16,8},{20,12},{24,0},{28,4},{1,25},{... | collective-permute-start | bytes 196616 | tf_op jit(solution)/shard_map/ppermute | solution.py:353
  81.6 23.2 %collective-permute-start.73 = (bf16[2,1024,256]{2,1,0:T(8,128)(2,1)S(1)}, bf16[2,1024,256]{2,1,0:T(8,128)(2,1)S(1)}, u32[]{:S(2)}, u32[]{:S(2)}) collective-permute-start(bf16[2,1024,256]{2,1,0:T(8,128)(2,1)S(1)} %get-tuple-element.185.disp_ref), channel_id=1, source_target_pairs={{0,4},{4,0},{8,12},{12,8},{16,20},{20,16},{24,28},{28,24},{1,5},{5... | collective-permute-start | bytes 3145736 | tf_op jit(solution)/shard_map/cond/branch_1_fun/ppermute | solution.py:353
  85.2 19.6 %collective-permute-start.74 = (bf16[6,128,256]{2,1,0:T(8,128)(2,1)S(1)}, bf16[6,128,256]{2,1,0:T(8,128)(2,1)S(1)}, u32[]{:S(2)}, u32[]{:S(2)}) collective-permute-start(bf16[6,128,256]{2,1,0:T(8,128)(2,1)S(1)} %get-tuple-element.186), channel_id=1, source_target_pairs={{0,1},{1,0},{2,3},{3,2},{4,5},{5,4},{6,7},{7,6},{8,9},{9,8},{10,11... | collective-permute-start | bytes 1179656 | tf_op jit(solution)/shard_map/cond/branch_1_fun/ppermute | solution.py:465
  86.2 18.6 %collective-permute-start.75 = (bf16[6,128,256]{2,1,0:T(8,128)(2,1)S(1)}, bf16[6,128,256]{2,1,0:T(8,128)(2,1)S(1)}, u32[]{:S(2)}, u32[]{:S(2)}) collective-permute-start(bf16[6,128,256]{2,1,0:T(8,128)(2,1)S(1)} %get-tuple-element.187), channel_id=1, source_target_pairs={{1,2},{2,1},{5,6},{6,5},{9,10},{10,9},{13,14},{14,13},{17,18},{18,... | collective-permute-start | bytes 1179656 | tf_op jit(solution)/shard_map/cond/branch_1_fun/ppermute | solution.py:466
  87.4 10.3 %collective-permute-start.76 = (bf16[5,128,256]{2,1,0:T(8,128)(2,1)S(1)}, bf16[5,128,256]{2,1,0:T(8,128)(2,1)S(1)}, u32[]{:S(2)}, u32[]{:S(2)}) collective-permute-start(bf16[5,128,256]{2,1,0:T(8,128)(2,1)S(1)} %get-tuple-element.188), channel_id=1, source_target_pairs={{0,28},{4,8},{8,4},{12,16},{16,12},{20,24},{24,20},{28,0},{1,29},{... | collective-permute-start | bytes 983048 | tf_op jit(solution)/shard_map/cond/branch_1_fun/ppermute | solution.py:462
  89.9 14.9 %collective-permute-start.77 = (bf16[5,128,256]{2,1,0:T(8,128)(2,1)S(1)}, bf16[5,128,256]{2,1,0:T(8,128)(2,1)S(1)}, u32[]{:S(2)}, u32[]{:S(2)}) collective-permute-start(bf16[5,128,256]{2,1,0:T(8,128)(2,1)S(1)} %get-tuple-element.189), channel_id=1, source_target_pairs={{0,28},{4,8},{8,4},{12,16},{16,12},{20,24},{24,20},{28,0},{1,29},{... | collective-permute-start | bytes 983048 | tf_op jit(solution)/shard_map/cond/branch_1_fun/ppermute | solution.py:464
  110.5 5.7 %collective-permute-start.82 = (bf16[144,256]{1,0:T(8,128)(2,1)S(1)}, bf16[144,256]{1,0:T(8,128)(2,1)S(1)}, u32[]{:S(2)}, u32[]{:S(2)}) collective-permute-start(bf16[144,256]{1,0:T(8,128)(2,1)S(1)} %get-tuple-element.199), channel_id=1, source_target_pairs={{0,8},{4,12},{8,0},{12,4},{16,24},{20,28},{24,16},{28,20},{1,9},{5... | collective-permute-start | bytes 221192 | tf_op jit(solution)/shard_map/cond/branch_1_fun/ppermute | solution.py:353
  111.9 5.3 %collective-permute-start.83 = (bf16[144,256]{1,0:T(8,128)(2,1)S(1)}, bf16[144,256]{1,0:T(8,128)(2,1)S(1)}, u32[]{:S(2)}, u32[]{:S(2)}) collective-permute-start(bf16[144,256]{1,0:T(8,128)(2,1)S(1)} %get-tuple-element.200), channel_id=1, source_target_pairs={{0,16},{4,20},{8,24},{12,28},{16,0},{20,4},{24,8},{28,12},{1,17},{... | collective-permute-start | bytes 221192 | tf_op jit(solution)/shard_map/cond/branch_1_fun/ppermute | solution.py:353
  113.8 5.3 %collective-permute-start.84 = (bf16[144,256]{1,0:T(8,128)(2,1)S(1)}, bf16[144,256]{1,0:T(8,128)(2,1)S(1)}, u32[]{:S(2)}, u32[]{:S(2)}) collective-permute-start(bf16[144,256]{1,0:T(8,128)(2,1)S(1)} %get-tuple-element.201), channel_id=1, source_target_pairs={{0,24},{4,28},{8,16},{12,20},{16,8},{20,12},{24,0},{28,4},{1,25},{... | collective-permute-start | bytes 221192 | tf_op jit(solution)/shard_map/cond/branch_1_fun/ppermute | solution.py:353
  114.0 9.5 %collective-permute-start.88 = (bf16[128,256]{1,0:T(8,128)(2,1)S(1)}, bf16[128,256]{1,0:T(8,128)(2,1)S(1)}, u32[]{:S(2)}, u32[]{:S(2)}) collective-permute-start(bf16[128,256]{1,0:T(8,128)(2,1)S(1)} %branch_1_fun.22.refs_3_.refs_0_), channel_id=1, source_target_pairs={{0,1},{1,0},{2,3},{3,2},{4,5},{5,4},{6,7},{7,6},{8,9},{9,8},{10,11... | collective-permute-start | bytes 196616 | tf_op jit(solution)/shard_map/cond/branch_1_fun/ppermute | solution.py:353
  119.1 12.7 %collective-permute-start.85 = (bf16[144,256]{1,0:T(8,128)(2,1)S(1)}, bf16[144,256]{1,0:T(8,128)(2,1)S(1)}, u32[]{:S(2)}, u32[]{:S(2)}) collective-permute-start(bf16[144,256]{1,0:T(8,128)(2,1)S(1)} %branch_1_fun.25.refs_0_), channel_id=1, source_target_pairs={{0,1},{1,0},{2,3},{3,2},{4,5},{5,4},{6,7},{7,6},{8,9},{9,8},{10,11... | collective-permute-start | bytes 221192 | tf_op jit(solution)/shard_map/cond/branch_1_fun/ppermute | solution.py:353
  120.6 11.1 %collective-permute-start.86 = (bf16[144,256]{1,0:T(8,128)(2,1)S(1)}, bf16[144,256]{1,0:T(8,128)(2,1)S(1)}, u32[]{:S(2)}, u32[]{:S(2)}) collective-permute-start(bf16[144,256]{1,0:T(8,128)(2,1)S(1)} %branch_1_fun.25.refs_0_), channel_id=1, source_target_pairs={{0,2},{1,3},{2,0},{3,1},{4,6},{5,7},{6,4},{7,5},{8,10},{9,11},{10,... | collective-permute-start | bytes 221192 | tf_op jit(solution)/shard_map/cond/branch_1_fun/ppermute | solution.py:353
  121.2 10.5 %collective-permute-start.87 = (bf16[144,256]{1,0:T(8,128)(2,1)S(1)}, bf16[144,256]{1,0:T(8,128)(2,1)S(1)}, u32[]{:S(2)}, u32[]{:S(2)}) collective-permute-start(bf16[144,256]{1,0:T(8,128)(2,1)S(1)} %branch_1_fun.25.refs_0_), channel_id=1, source_target_pairs={{0,3},{1,2},{2,1},{3,0},{4,7},{5,6},{6,5},{7,4},{8,11},{9,10},{10,... | collective-permute-start | bytes 221192 | tf_op jit(solution)/shard_map/cond/branch_1_fun/ppermute | solution.py:353
  123.5 8.2 %collective-permute-start.89 = (bf16[128,256]{1,0:T(8,128)(2,1)S(1)}, bf16[128,256]{1,0:T(8,128)(2,1)S(1)}, u32[]{:S(2)}, u32[]{:S(2)}) collective-permute-start(bf16[128,256]{1,0:T(8,128)(2,1)S(1)} %branch_1_fun.26.refs_4_), channel_id=1, source_target_pairs={{0,2},{1,3},{2,0},{3,1},{4,6},{5,7},{6,4},{7,5},{8,10},{9,11},{10,... | collective-permute-start | bytes 196616 | tf_op jit(solution)/shard_map/cond/branch_1_fun/ppermute | solution.py:353
  133.6 5.2 %collective-permute-start.95 = (bf16[128,256]{1,0:T(8,128)(2,1)S(1)}, bf16[128,256]{1,0:T(8,128)(2,1)S(1)}, u32[]{:S(2)}, u32[]{:S(2)}) collective-permute-start(bf16[128,256]{1,0:T(8,128)(2,1)S(1)} %get-tuple-element.203.refs_0_), channel_id=1, source_target_pairs={{0,24},{4,28},{8,16},{12,20},{16,8},{20,12},{24,0},{28,4},{1,25},{... | collective-permute-start | bytes 196616 | tf_op jit(solution)/shard_map/cond/branch_1_fun/ppermute | solution.py:353
  144.2 23.5 %collective-permute-start.98 = (bf16[2,1024,256]{2,1,0:T(8,128)(2,1)S(1)}, bf16[2,1024,256]{2,1,0:T(8,128)(2,1)S(1)}, u32[]{:S(2)}, u32[]{:S(2)}) collective-permute-start(bf16[2,1024,256]{2,1,0:T(8,128)(2,1)S(1)} %get-tuple-element.219.disp_ref), channel_id=1, source_target_pairs={{0,4},{4,0},{8,12},{12,8},{16,20},{20,16},{24,28},{28,24},{1,5},{5... | collective-permute-start | bytes 3145736 | tf_op jit(solution)/shard_map/cond/branch_1_fun/ppermute | solution.py:353
  146.9 5.2 %collective-permute-start.105 = (bf16[128,256]{1,0:T(8,128)(2,1)S(1)}, bf16[128,256]{1,0:T(8,128)(2,1)S(1)}, u32[]{:S(2)}, u32[]{:S(2)}) collective-permute-start(bf16[128,256]{1,0:T(8,128)(2,1)S(1)} %get-tuple-element.227), channel_id=1, source_target_pairs={{0,24},{4,28},{8,16},{12,20},{16,8},{20,12},{24,0},{28,4},{1,25},{... | collective-permute-start | bytes 196616 | tf_op jit(solution)/shard_map/cond/branch_1_fun/ppermute | solution.py:353
  148.1 19.6 %collective-permute-start.99 = (bf16[6,128,256]{2,1,0:T(8,128)(2,1)S(1)}, bf16[6,128,256]{2,1,0:T(8,128)(2,1)S(1)}, u32[]{:S(2)}, u32[]{:S(2)}) collective-permute-start(bf16[6,128,256]{2,1,0:T(8,128)(2,1)S(1)} %get-tuple-element.220), channel_id=1, source_target_pairs={{0,1},{1,0},{2,3},{3,2},{4,5},{5,4},{6,7},{7,6},{8,9},{9,8},{10,11... | collective-permute-start | bytes 1179656 | tf_op jit(solution)/shard_map/cond/branch_1_fun/ppermute | solution.py:465
  148.9 18.8 %collective-permute-start.100 = (bf16[6,128,256]{2,1,0:T(8,128)(2,1)S(1)}, bf16[6,128,256]{2,1,0:T(8,128)(2,1)S(1)}, u32[]{:S(2)}, u32[]{:S(2)}) collective-permute-start(bf16[6,128,256]{2,1,0:T(8,128)(2,1)S(1)} %get-tuple-element.221), channel_id=1, source_target_pairs={{1,2},{2,1},{5,6},{6,5},{9,10},{10,9},{13,14},{14,13},{17,18},{18,... | collective-permute-start | bytes 1179656 | tf_op jit(solution)/shard_map/cond/branch_1_fun/ppermute | solution.py:466
  149.9 10.8 %collective-permute-start.101 = (bf16[5,128,256]{2,1,0:T(8,128)(2,1)S(1)}, bf16[5,128,256]{2,1,0:T(8,128)(2,1)S(1)}, u32[]{:S(2)}, u32[]{:S(2)}) collective-permute-start(bf16[5,128,256]{2,1,0:T(8,128)(2,1)S(1)} %get-tuple-element.222), channel_id=1, source_target_pairs={{0,28},{4,8},{8,4},{12,16},{16,12},{20,24},{24,20},{28,0},{1,29},{... | collective-permute-start | bytes 983048 | tf_op jit(solution)/shard_map/cond/branch_1_fun/ppermute | solution.py:462
  152.1 15.6 %collective-permute-start.102 = (bf16[5,128,256]{2,1,0:T(8,128)(2,1)S(1)}, bf16[5,128,256]{2,1,0:T(8,128)(2,1)S(1)}, u32[]{:S(2)}, u32[]{:S(2)}) collective-permute-start(bf16[5,128,256]{2,1,0:T(8,128)(2,1)S(1)} %get-tuple-element.223), channel_id=1, source_target_pairs={{0,28},{4,8},{8,4},{12,16},{16,12},{20,24},{24,20},{28,0},{1,29},{... | collective-permute-start | bytes 983048 | tf_op jit(solution)/shard_map/cond/branch_1_fun/ppermute | solution.py:464
  173.4 6.2 %collective-permute-start.107 = (bf16[144,256]{1,0:T(8,128)(2,1)S(1)}, bf16[144,256]{1,0:T(8,128)(2,1)S(1)}, u32[]{:S(2)}, u32[]{:S(2)}) collective-permute-start(bf16[144,256]{1,0:T(8,128)(2,1)S(1)} %get-tuple-element.232), channel_id=1, source_target_pairs={{0,8},{4,12},{8,0},{12,4},{16,24},{20,28},{24,16},{28,20},{1,9},{5... | collective-permute-start | bytes 221192 | tf_op jit(solution)/shard_map/cond/branch_1_fun/ppermute | solution.py:353
  173.6 6.0 %collective-permute-start.108 = (bf16[144,256]{1,0:T(8,128)(2,1)S(1)}, bf16[144,256]{1,0:T(8,128)(2,1)S(1)}, u32[]{:S(2)}, u32[]{:S(2)}) collective-permute-start(bf16[144,256]{1,0:T(8,128)(2,1)S(1)} %get-tuple-element.233), channel_id=1, source_target_pairs={{0,16},{4,20},{8,24},{12,28},{16,0},{20,4},{24,8},{28,12},{1,17},{... | collective-permute-start | bytes 221192 | tf_op jit(solution)/shard_map/cond/branch_1_fun/ppermute | solution.py:353
  175.3 5.3 %collective-permute-start.109 = (bf16[144,256]{1,0:T(8,128)(2,1)S(1)}, bf16[144,256]{1,0:T(8,128)(2,1)S(1)}, u32[]{:S(2)}, u32[]{:S(2)}) collective-permute-start(bf16[144,256]{1,0:T(8,128)(2,1)S(1)} %get-tuple-element.234), channel_id=1, source_target_pairs={{0,24},{4,28},{8,16},{12,20},{16,8},{20,12},{24,0},{28,4},{1,25},{... | collective-permute-start | bytes 221192 | tf_op jit(solution)/shard_map/cond/branch_1_fun/ppermute | solution.py:353
  177.0 9.4 %collective-permute-start.113 = (bf16[128,256]{1,0:T(8,128)(2,1)S(1)}, bf16[128,256]{1,0:T(8,128)(2,1)S(1)}, u32[]{:S(2)}, u32[]{:S(2)}) collective-permute-start(bf16[128,256]{1,0:T(8,128)(2,1)S(1)} %branch_1_fun.31.refs_3_.refs_0_), channel_id=1, source_target_pairs={{0,1},{1,0},{2,3},{3,2},{4,5},{5,4},{6,7},{7,6},{8,9},{9,8},{10,11... | collective-permute-start | bytes 196616 | tf_op jit(solution)/shard_map/cond/branch_1_fun/ppermute | solution.py:353
  180.6 14.1 %collective-permute-start.110 = (bf16[144,256]{1,0:T(8,128)(2,1)S(1)}, bf16[144,256]{1,0:T(8,128)(2,1)S(1)}, u32[]{:S(2)}, u32[]{:S(2)}) collective-permute-start(bf16[144,256]{1,0:T(8,128)(2,1)S(1)} %branch_1_fun.34.refs_0_), channel_id=1, source_target_pairs={{0,1},{1,0},{2,3},{3,2},{4,5},{5,4},{6,7},{7,6},{8,9},{9,8},{10,11... | collective-permute-start | bytes 221192 | tf_op jit(solution)/shard_map/cond/branch_1_fun/ppermute | solution.py:353
  183.9 10.8 %collective-permute-start.111 = (bf16[144,256]{1,0:T(8,128)(2,1)S(1)}, bf16[144,256]{1,0:T(8,128)(2,1)S(1)}, u32[]{:S(2)}, u32[]{:S(2)}) collective-permute-start(bf16[144,256]{1,0:T(8,128)(2,1)S(1)} %branch_1_fun.34.refs_0_), channel_id=1, source_target_pairs={{0,2},{1,3},{2,0},{3,1},{4,6},{5,7},{6,4},{7,5},{8,10},{9,11},{10,... | collective-permute-start | bytes 221192 | tf_op jit(solution)/shard_map/cond/branch_1_fun/ppermute | solution.py:353
  183.9 10.8 %collective-permute-start.112 = (bf16[144,256]{1,0:T(8,128)(2,1)S(1)}, bf16[144,256]{1,0:T(8,128)(2,1)S(1)}, u32[]{:S(2)}, u32[]{:S(2)}) collective-permute-start(bf16[144,256]{1,0:T(8,128)(2,1)S(1)} %branch_1_fun.34.refs_0_), channel_id=1, source_target_pairs={{0,3},{1,2},{2,1},{3,0},{4,7},{5,6},{6,5},{7,4},{8,11},{9,10},{10,... | collective-permute-start | bytes 221192 | tf_op jit(solution)/shard_map/cond/branch_1_fun/ppermute | solution.py:353
  186.4 8.3 %collective-permute-start.114 = (bf16[128,256]{1,0:T(8,128)(2,1)S(1)}, bf16[128,256]{1,0:T(8,128)(2,1)S(1)}, u32[]{:S(2)}, u32[]{:S(2)}) collective-permute-start(bf16[128,256]{1,0:T(8,128)(2,1)S(1)} %branch_1_fun.35.refs_4_), channel_id=1, source_target_pairs={{0,2},{1,3},{2,0},{3,1},{4,6},{5,7},{6,4},{7,5},{8,10},{9,11},{10,... | collective-permute-start | bytes 196616 | tf_op jit(solution)/shard_map/cond/branch_1_fun/ppermute | solution.py:353
  196.4 5.2 %collective-permute-start.120 = (bf16[128,256]{1,0:T(8,128)(2,1)S(1)}, bf16[128,256]{1,0:T(8,128)(2,1)S(1)}, u32[]{:S(2)}, u32[]{:S(2)}) collective-permute-start(bf16[128,256]{1,0:T(8,128)(2,1)S(1)} %get-tuple-element.236.refs_0_), channel_id=1, source_target_pairs={{0,24},{4,28},{8,16},{12,20},{16,8},{20,12},{24,0},{28,4},{1,25},{... | collective-permute-start | bytes 196616 | tf_op jit(solution)/shard_map/cond/branch_1_fun/ppermute | solution.py:353
  (38 other events, 370.7 us)

commit v5 on v4

--- a/solution.py
+++ b/solution.py
@@ -36,15 +36,17 @@
     return jax.ShapeDtypeStruct(shape, dtype)
 
 
-def stage_bits(size):
+def paired_stages(size):
     total = size.bit_length() - 1
-    groups = [1]
-    left = total - 1
-    while left > 0:
-        take = 2 if left >= 2 else 1
-        groups.append(take)
-        left -= take
-    return groups
+    stages, shift = [(0, 1)], 1
+    while shift < total:
+        stages.append((shift, min(2, total - shift)))
+        shift += stages[-1][1]
+    return stages
+
+
+def single_stages(size):
+    return [(0, 1)] + [(shift, 1) for shift in range(size.bit_length() - 2, 0, -1)]
 
 
 def pack_products(inner, square, most):
@@ -249,29 +251,20 @@
             up = (face == 2).astype(jnp.int32)
             down = (face == 3).astype(jnp.int32)
 
-            @pl.when(face < 2)
-            def _():
-                pl.when(face == odd)(lambda: put(chip_ref[s, rows, :]))
-                pl.when(away & (n < size))(lambda: put(take(offs[0], n)))
-                if packed:
-                    pl.when(away & (n >= size))(lambda: put(take(offs[1], n - size)))
-
-            @pl.when(face == 2)
-            def _():
-                if s + 1 < subs:
-                    put(disp_ref[s + 1, rows, :])
-                else:
-                    pl.when(zodd == 0)(lambda: put(take(za_ref, above)))
-                    pl.when(zodd == 1)(lambda: put(take(zb_ref, above)))
-
-            @pl.when(face == 3)
-            def _():
-                if s > 0:
-                    put(disp_ref[s - 1, rows, :])
-                else:
-                    pl.when(zodd == 1)(lambda: put(take(za_ref, below)))
-                    pl.when(zodd == 0)(lambda: put(take(zb_ref, below)))
-
+            pl.when(face == odd)(lambda: put(chip_ref[s, rows, :]))
+            pl.when(away & (n < size))(lambda: put(take(offs[0], n)))
+            if packed:
+                pl.when(away & (n >= size))(lambda: put(take(offs[1], n - size)))
+            if s + 1 < subs:
+                pl.when(face == 2)(lambda: put(disp_ref[s + 1, rows, :]))
+            else:
+                pl.when((face == 2) & (zodd == 0))(lambda: put(take(za_ref, above)))
+                pl.when((face == 2) & (zodd == 1))(lambda: put(take(zb_ref, above)))
+            if s > 0:
+                pl.when(face == 3)(lambda: put(disp_ref[s - 1, rows, :]))
+            else:
+                pl.when((face == 3) & (zodd == 1))(lambda: put(take(za_ref, below)))
+                pl.when((face == 3) & (zodd == 0))(lambda: put(take(zb_ref, below)))
             n = n + away.astype(jnp.int32)
             if s + 1 == subs:
                 above = above + up
@@ -318,12 +311,13 @@
     )
 
 
-def add_kernel(chunk, chunks, ways_in, ways_out, extra, *refs):
+def add_kernel(chunk, chunks, ways_in, ways_out, high, extra, *refs):
     ins, outs = refs[:ways_in], refs[-ways_out:]
     for c in range(chunks):
         rows = pl.ds(c * chunk, chunk)
         total = tree([r[rows, :].astype(F32) for r in ins]).astype(BF16)
-        outs[c % ways_out][pl.ds((c // ways_out) * chunk, chunk), :] = total
+        way, spot = divmod(c, chunks // ways_out) if high else (c % ways_out, c // ways_out)
+        outs[way][pl.ds(spot * chunk, chunk), :] = total
     if extra:
         tail = pl.ds(chunks * chunk, EXTRA)
         tiles = [r[tail, :] for r in ins]
@@ -353,25 +347,25 @@
     return lax.ppermute(x, axis, [(i, i ^ mask) for i in range(n)])
 
 
-def stage(parts, g, chunk, wide, extra):
-    groups = stage_bits(wide)
-    shift = sum(groups[:g])
-    ways = 1 << groups[g]
-    chunks = wide >> (shift + groups[g])
+def stage(parts, stages, g, chunk, wide, extra):
+    shift, bits = stages[g]
+    ways = 1 << bits
+    chunks = wide >> sum(b for _, b in stages[: g + 1])
     cols = parts[0].shape[1]
     got = [parts[0]] + [swap(parts[q], "wide", q << shift) for q in range(1, ways)]
-    nxt = 1 << groups[g + 1] if g + 1 < len(groups) else 1
+    nxt = 1 << stages[g + 1][1] if g + 1 < len(stages) else 1
+    high = g + 1 < len(stages) and 1 << stages[g + 1][0] != wide // chunks
     shape = sds(((chunks // nxt) * chunk + (EXTRA if extra else 0), cols), BF16)
     return call(
-        functools.partial(add_kernel, chunk, chunks, ways, nxt, extra),
+        functools.partial(add_kernel, chunk, chunks, ways, nxt, high, extra),
         [shape] * nxt, 0, got, chunks * chunk * cols * ways,
         chunks * chunk * cols * 2 * (ways + 1), vmem=8,
     )
 
 
-def scatter(parts, first, chunk, wide, extra):
-    for g in range(first, len(stage_bits(wide))):
-        parts = stage(parts, g, chunk, wide, extra)
+def scatter(parts, stages, first, chunk, wide, extra):
+    for g in range(first, len(stages)):
+        parts = stage(parts, stages, g, chunk, wide, extra)
     return parts[0]
 
 
@@ -381,11 +375,8 @@
 
 
 def gather(centre, wide):
-    groups = stage_bits(wide)
     have = {0: centre}
-    shift = wide.bit_length() - 1
-    for bits in reversed(groups):
-        shift -= bits
+    for shift, bits in reversed(paired_stages(wide)):
         new = dict(have)
         for q in range(1, 1 << bits):
             for k, v in have.items():
@@ -419,7 +410,7 @@
     full = sds((subs, rows, cols), F32)
     half = sds((subs, rows, cols), BF16)
     one = sds((rows, cols), BF16)
-    few = [sds((cap, rows // blocks, cols), BF16) for cap in (caps[1], caps[1], -(-caps[0] // 2), caps[0] // 2)]
+    few = [sds((cap, rows // blocks, cols), BF16) for cap in (caps[1], caps[1], -(-caps[0] * 3 // 5), caps[0] * 2 // 5)]
     part = sds(((wide // 2) * chunk, cols), BF16)
     message = sds(((wide // 2) * chunk + EXTRA, cols), BF16)
     stack = sds((ITERS, rows, cols), F32)
@@ -454,13 +445,13 @@
                 functools.partial(halo_kernel, packed), outs, len(head), head + [disp],
                 arr, arr * 4, vmem=8,
             )]
-        lams = stage([lkeep, lsend], 0, chunk, wide, False)
+        lams = stage([lkeep, lsend], single_stages(wide), 0, chunk, wide, False)
         lams, sends = lax.optimization_barrier((lams, sends))
         disp, za, zb = sends[:3]
         offs = sends[3:] if packed else [disp]
         if packed:
             offs[0] = lax.ppermute(offs[0], "wide", away)
-        own = scatter(lams, 1, chunk, wide, False)
+        own = scatter(lams, single_stages(wide), 1, chunk, wide, False)
         offs[-1] = lax.ppermute(offs[-1], "wide", away)
         za = lax.ppermute(za, "eight", pairs_a)
         zb = lax.ppermute(zb, "eight", pairs_b)
@@ -476,14 +467,14 @@
                 pltpu.VMEM((subs, rows, cols), BF16),
             ],
         )
-        dirs = stage([dkeep, dsend], 0, chunk, wide, True)
+        dirs = stage([dkeep, dsend], paired_stages(wide), 0, chunk, wide, True)
         for q in range(1, eight.bit_length() - 1):
             (own,) = call(
-                functools.partial(add_kernel, chunk, 1, 2, 1, False), [sds(own.shape, BF16)], 0,
+                functools.partial(add_kernel, chunk, 1, 2, 1, False, False), [sds(own.shape, BF16)], 0,
                 [*lam_parts, dkeep], 2 * own.size, 6 * own.size, vmem=8,
             )
             lam_parts = [own, swap(own, "eight", 1 << q)]
-        dirs = scatter(dirs, 1, chunk, wide, True)
+        dirs = scatter(dirs, paired_stages(wide), 1, chunk, wide, True)
         dir_parts = across(dirs)
         centre, alpha = call(
             functools.partial(centre_kernel, chunk, eight, float(count)),

time: 206 us -> 211 us (1.024)
  waiting for transfers between devices: 93.4 us -> 99.1 us
    ppermute x63 -> x60, waiting for transfers between devices: 48.5 us -> 72.7 us  [swap(): return lax.ppermute(x, axis, [(i, i ^ mask) for i in range(n)])]
    ppermute x3, waiting for transfers between devices: 23.9 us -> 0.01 us  [search(): offs[0] = lax.ppermute(offs[0], 'wide', away)]
    ppermute x3, waiting for transfers between devices: 19.6 us -> 25 us  [search(): offs[-1] = lax.ppermute(offs[-1], 'wide', away)]
    ppermute x3, starting transfers between devices: 3.24 us -> 0.91 us  [search(): offs[-1] = lax.ppermute(offs[-1], 'wide', away)]
    pallas_call x28 -> x31, Pallas kernels: 28.9 us -> 29.5 us  [call(): pl.pallas_call(kernel, out_shape=outs, in_specs=[SMEM if i < n_smem else...]
    ppermute x63 -> x60, starting transfers between devices: 62.5 us -> 62.9 us  [swap(): return lax.ppermute(x, axis, [(i, i ^ mask) for i in range(n)])]
  transfers between devices with their start and end apart: 78 -> 75, of which waited for: 35 -> 32; matrix products, arithmetic and copies ran while one was open for 0% -> 0% of each run, Pallas kernels for 3% -> 3%
where the time goes in v5:
time: 211 us
  waiting for transfers between devices  99.1 us (47%)
  starting transfers between devices  77.7 us (37%)
  Pallas kernels  29.5 us (14%)
  local copies, waits for them, and re-layouts  2.11 us (1%)
    ppermute x60, waiting for transfers between devices, swap(): return lax.ppermute(x, axis, [(i, i ^ mask) for i in range(n)])  72.7 us
    ppermute x60, starting transfers between devices, swap(): return lax.ppermute(x, axis, [(i, i ^ mask) for i in range(n)])  62.9 us
    pallas_call x31, Pallas kernels, call(): pl.pallas_call(kernel, out_shape=outs, in_specs=[SMEM if i < n_smem else...  29.5 us
    ppermute x3, waiting for transfers between devices, search(): offs[-1] = lax.ppermute(offs[-1], 'wide', away)  25 us
    ppermute x3, starting transfers between devices, search(): za = lax.ppermute(za, 'eight', pairs_a)  4.6 us
  transfers between devices with their start and end apart: 75, of which 32 were waited for; matrix products, arithmetic and copies ran while one was open for 0% of the time, Pallas kernels for 3%

profile of v5, /device:TPU:0, one launch (start us, length us, event | category | flops | bytes accessed | tf_op | source)
XLA Modules:
  0.0 210.6 jit_solution(13175501341064717515)
XLA Ops:
  0.7 5.5 %shard_map.96 = (bf16[512,256]{1,0:T(8,128)(2,1)S(1)}, bf16[512,256]{1,0:T(8,128)(2,1)S(1)}, bf16[2,1024,256]{2,1,0:T(8,128)(2,1)S(1)}) custom-call(s32[2]{0:T(128)S(1)} %pad_add_fusion.info, f32[2,1024,256]{2,1,0:T(8,128)} %lam_ref.1, bf16[2,1024,1024]{2,1,0:T(8,128)(2,1)} %flex_ref.1), custom_call_target="tpu_custom_call" | custom-call | flops 1073741824 | bytes 7340032 | tf_op jit(solution)/shard_map/pallas_call | solution.py:21
  6.8 3.5 %collective-permute-start.118 = (s32[2,8]{1,0:T(2,128)S(1)}, s32[2,8]{1,0:T(2,128)S(1)}, u32[]{:S(2)}, u32[]{:S(2)}) collective-permute-start(s32[2,8]{1,0:T(2,128)S(1)} %copy-done.5), channel_id=1, source_target_pairs={{0,28},{4,8},{8,4},{12,16},{16,12},{20,24},{24,20},{28,0},{1,29},{... | collective-permute-start | bytes 200 | tf_op jit(solution)/shard_map/ppermute | solution.py:401
  10.4 1.6 collective-permute-start.119
  12.6 1.3 collective-permute-done.119.refs_1_
  15.7 4.6 %collective-permute-start.122 = (bf16[6,128,256]{2,1,0:T(8,128)(2,1)S(1)}, bf16[6,128,256]{2,1,0:T(8,128)(2,1)S(1)}, u32[]{:S(2)}, u32[]{:S(2)}) collective-permute-start(bf16[6,128,256]{2,1,0:T(8,128)(2,1)S(1)} %get-tuple-element.270), channel_id=1, source_target_pairs={{0,1},{1,0},{2,3},{3,2},{4,5},{5,4},{6,7},{7,6},{8,9},{9,8},{10,11... | collective-permute-start | bytes 1179656 | tf_op jit(solution)/shard_map/ppermute | solution.py:456
  21.1 1.5 collective-permute-start.127
  22.6 10.4 %collective-permute-done.127.refs_1_ = bf16[128,256]{1,0:T(8,128)(2,1)S(1)} collective-permute-done((bf16[128,256]{1,0:T(8,128)(2,1)S(1)}, bf16[128,256]{1,0:T(8,128)(2,1)S(1)}, u32[]{:S(2)}, u32[]{:S(2)}) %collective-permute-start.127) | collective-permute-done | bytes 65568 | tf_op jit(solution)/shard_map/ppermute | solution.py:347
  33.9 7.5 %collective-permute-done.125.refs_1_ = bf16[4,128,256]{2,1,0:T(8,128)(2,1)S(1)} collective-permute-done((bf16[4,128,256]{2,1,0:T(8,128)(2,1)S(1)}, bf16[4,128,256]{2,1,0:T(8,128)(2,1)S(1)}, u32[]{:S(2)}, u32[]{:S(2)}) %collective-permute-start.125) | collective-permute-done | bytes 262176 | tf_op jit(solution)/shard_map/ppermute | solution.py:455
  41.5 4.2 %shard_map.101 = (bf16[2,1024,256]{2,1,0:T(8,128)(2,1)S(1)}, bf16[528,256]{1,0:T(8,128)(2,1)S(1)}, bf16[528,256]{1,0:T(8,128)(2,1)S(1)}) custom-call(s32[2]{0:T(128)S(1)} %pad_add_fusion.info, s32[2,8]{1,0:T(2,128)S(1)} %copy-done.5, s32[2]{0:T(128)S(1)} %copy-done.6, f32[2,1024,256]{2,1,0:T(8,128)S(1)} %copy-done.2, ...), custom_call_target="tpu_custom_call" | custom-call | flops 2147483648 | bytes 12582912 | tf_op jit(solution)/shard_map/pallas_call | solution.py:21
  45.7 2.3 %collective-permute-start.128 = (bf16[528,256]{1,0:T(8,128)(2,1)S(1)}, bf16[528,256]{1,0:T(8,128)(2,1)S(1)}, u32[]{:S(2)}, u32[]{:S(2)}) collective-permute-start(bf16[528,256]{1,0:T(8,128)(2,1)S(1)} %get-tuple-element.279), channel_id=1, source_target_pairs={{0,4},{4,0},{8,12},{12,8},{16,20},{20,16},{24,28},{28,24},{1,5},{5... | collective-permute-start | bytes 811016 | tf_op jit(solution)/shard_map/ppermute | solution.py:347
  49.4 3.4 %collective-permute-start.131 = (bf16[144,256]{1,0:T(8,128)(2,1)S(1)}, bf16[144,256]{1,0:T(8,128)(2,1)S(1)}, u32[]{:S(2)}, u32[]{:S(2)}) collective-permute-start(bf16[144,256]{1,0:T(8,128)(2,1)S(1)} %get-tuple-element.283), channel_id=1, source_target_pairs={{0,24},{4,28},{8,16},{12,20},{16,8},{20,12},{24,0},{28,4},{1,25},{... | collective-permute-start | bytes 221192 | tf_op jit(solution)/shard_map/ppermute | solution.py:347
  54.2 1.3 collective-permute-done.130.refs_2_
  55.6 3.7 %collective-permute-start.132 = (bf16[144,256]{1,0:T(8,128)(2,1)S(1)}, bf16[144,256]{1,0:T(8,128)(2,1)S(1)}, u32[]{:S(2)}, u32[]{:S(2)}) collective-permute-start(bf16[144,256]{1,0:T(8,128)(2,1)S(1)} %shard_map.103.refs_0_), channel_id=1, source_target_pairs={{0,1},{1,0},{2,3},{3,2},{4,5},{5,4},{6,7},{7,6},{8,9},{9,8},{10,11... | collective-permute-start | bytes 221192 | tf_op jit(solution)/shard_map/ppermute | solution.py:347
  59.3 2.4 %collective-permute-start.134 = (bf16[144,256]{1,0:T(8,128)(2,1)S(1)}, bf16[144,256]{1,0:T(8,128)(2,1)S(1)}, u32[]{:S(2)}, u32[]{:S(2)}) collective-permute-start(bf16[144,256]{1,0:T(8,128)(2,1)S(1)} %shard_map.103.refs_0_), channel_id=1, source_target_pairs={{0,3},{1,2},{2,1},{3,0},{4,7},{5,6},{6,5},{7,4},{8,11},{9,10},{10,... | collective-permute-start | bytes 221192 | tf_op jit(solution)/shard_map/ppermute | solution.py:347
  62.3 7.8 %collective-permute-done.136.refs_5_ = bf16[128,256]{1,0:T(8,128)(2,1)S(1)} collective-permute-done((bf16[128,256]{1,0:T(8,128)(2,1)S(1)}, bf16[128,256]{1,0:T(8,128)(2,1)S(1)}, u32[]{:S(2)}, u32[]{:S(2)}) %collective-permute-start.136) | collective-permute-done | bytes 65568 | tf_op jit(solution)/shard_map/ppermute | solution.py:347
  71.3 2.4 %collective-permute-start.142 = (bf16[128,256]{1,0:T(8,128)(2,1)S(1)}, bf16[128,256]{1,0:T(8,128)(2,1)S(1)}, u32[]{:S(2)}, u32[]{:S(2)}) collective-permute-start(bf16[128,256]{1,0:T(8,128)(2,1)S(1)} %get-tuple-element.286), channel_id=1, source_target_pairs={{0,24},{4,28},{8,16},{12,20},{16,8},{20,12},{24,0},{28,4},{1,25},{... | collective-permute-start | bytes 196616 | tf_op jit(solution)/shard_map/ppermute | solution.py:347
  75.2 1.3 collective-permute-done.142
  77.8 132.2 %conditional.1 = (f32[2,1024,256]{2,1,0:T(8,128)}, f32[3,1024,256]{2,1,0:T(8,128)}, f32[3,256]{1,0:T(4,128)S(1)}) conditional(s32[]{:T(128)} %bitcast.8, (s32[2]{0:T(128)S(1)}, f32[2,1024,256]{2,1,0:T(8,128)S(1)}, bf16[2,1024,1024]{2,1,0:T(8,128)(2,1)S(1)}, s32[2,8]{1,0:T(2,128)S(1)}, s32[2]{0:T(128)S(1)}, /*index=5*/f32[2,1024,256]{2,1,0:T(8,128)S(1)}, ...), branch_computations={%region_0.1_spmd, %region_1.2_spmd} | conditional | flops 9677387776 | bytes 159177312 | solution.py:519
  80.1 2.4 %branch_1_fun.23 = (bf16[2,1024,256]{2,1,0:T(8,128)(2,1)S(1)}, bf16[6,128,256]{2,1,0:T(8,128)(2,1)S(1)}, bf16[6,128,256]{2,1,0:T(8,128)(2,1)S(1)}, bf16[6,128,25...) custom-call(s32[2]{0:T(128)S(1)} %get-tuple-element.145.info, ...), custom_call_target="tpu_custom_call" | custom-call | flops 1073741824 | bytes 7340032 | tf_op jit(solution)/shard_map/cond/branch_1_fun/pallas_call | solution.py:21
  82.6 1.7 collective-permute-start.75
  85.9 2.8 %collective-permute-done.75.refs_1_ = bf16[256,256]{1,0:T(8,128)(2,1)S(1)} collective-permute-done((bf16[256,256]{1,0:T(8,128)(2,1)S(1)}, bf16[256,256]{1,0:T(8,128)(2,1)S(1)}, u32[]{:S(2)}, u32[]{:S(2)}) %collective-permute-start.75) | collective-permute-done | bytes 131104 | tf_op jit(solution)/shard_map/cond/branch_1_fun/ppermute | solution.py:347
  89.9 7.8 %collective-permute-done.76.refs_1_ = bf16[128,256]{1,0:T(8,128)(2,1)S(1)} collective-permute-done((bf16[128,256]{1,0:T(8,128)(2,1)S(1)}, bf16[128,256]{1,0:T(8,128)(2,1)S(1)}, u32[]{:S(2)}, u32[]{:S(2)}) %collective-permute-start.76) | collective-permute-done | bytes 65568 | tf_op jit(solution)/shard_map/cond/branch_1_fun/ppermute | solution.py:347
  97.7 8.9 %collective-permute-done.74.refs_1_ = bf16[4,128,256]{2,1,0:T(8,128)(2,1)S(1)} collective-permute-done((bf16[4,128,256]{2,1,0:T(8,128)(2,1)S(1)}, bf16[4,128,256]{2,1,0:T(8,128)(2,1)S(1)}, u32[]{:S(2)}, u32[]{:S(2)}) %collective-permute-start.74) | collective-permute-done | bytes 262176 | tf_op jit(solution)/shard_map/cond/branch_1_fun/ppermute | solution.py:455
  106.7 4.2 %branch_1_fun.26 = (bf16[2,1024,256]{2,1,0:T(8,128)(2,1)S(1)}, bf16[528,256]{1,0:T(8,128)(2,1)S(1)}, bf16[528,256]{1,0:T(8,128)(2,1)S(1)}) custom-call(s32[2]{0:T(128)S(1)} %get-tuple-element.145.info, s32[2,8]{1,0:T(2,128)S(1)} %get-tuple-element.159.side, s32[2]{0:T(128)S(1)} %get-tuple-element.160.powers, f32[2,1024,256]{2,1,0:T(8,128)S(1)} %get-tuple-element.161.gap_ref, ...), custom_call_target="tpu_custom_call" | custom-call | flops 2147483648 | bytes 12582912 | tf_op jit(solution)/shard_map/cond/branch_1_fun/pallas_call | solution.py:21
  110.9 1.6 collective-permute-start.77
  113.9 3.4 %collective-permute-start.80 = (bf16[144,256]{1,0:T(8,128)(2,1)S(1)}, bf16[144,256]{1,0:T(8,128)(2,1)S(1)}, u32[]{:S(2)}, u32[]{:S(2)}) collective-permute-start(bf16[144,256]{1,0:T(8,128)(2,1)S(1)} %get-tuple-element.193), channel_id=1, source_target_pairs={{0,24},{4,28},{8,16},{12,20},{16,8},{20,12},{24,0},{28,4},{1,25},{... | collective-permute-start | bytes 221192 | tf_op jit(solution)/shard_map/cond/branch_1_fun/ppermute | solution.py:347
  117.3 2.1 collective-permute-start.84
  120.1 3.7 %collective-permute-start.81 = (bf16[144,256]{1,0:T(8,128)(2,1)S(1)}, bf16[144,256]{1,0:T(8,128)(2,1)S(1)}, u32[]{:S(2)}, u32[]{:S(2)}) collective-permute-start(bf16[144,256]{1,0:T(8,128)(2,1)S(1)} %branch_1_fun.28.refs_0_), channel_id=1, source_target_pairs={{0,1},{1,0},{2,3},{3,2},{4,5},{5,4},{6,7},{7,6},{8,9},{9,8},{10,11... | collective-permute-start | bytes 221192 | tf_op jit(solution)/shard_map/cond/branch_1_fun/ppermute | solution.py:347
  123.8 2.4 %collective-permute-start.83 = (bf16[144,256]{1,0:T(8,128)(2,1)S(1)}, bf16[144,256]{1,0:T(8,128)(2,1)S(1)}, u32[]{:S(2)}, u32[]{:S(2)}) collective-permute-start(bf16[144,256]{1,0:T(8,128)(2,1)S(1)} %branch_1_fun.28.refs_0_), channel_id=1, source_target_pairs={{0,3},{1,2},{2,1},{3,0},{4,7},{5,6},{6,5},{7,4},{8,11},{9,10},{10,... | collective-permute-start | bytes 221192 | tf_op jit(solution)/shard_map/cond/branch_1_fun/ppermute | solution.py:347
  127.1 7.4 %collective-permute-done.85.refs_5_ = bf16[128,256]{1,0:T(8,128)(2,1)S(1)} collective-permute-done((bf16[128,256]{1,0:T(8,128)(2,1)S(1)}, bf16[128,256]{1,0:T(8,128)(2,1)S(1)}, u32[]{:S(2)}, u32[]{:S(2)}) %collective-permute-start.85) | collective-permute-done | bytes 65568 | tf_op jit(solution)/shard_map/cond/branch_1_fun/ppermute | solution.py:347
  134.7 1.3 collective-permute-start.87
  136.2 2.0 collective-permute-start.91
  144.3 2.4 %branch_1_fun.33 = (bf16[2,1024,256]{2,1,0:T(8,128)(2,1)S(1)}, bf16[6,128,256]{2,1,0:T(8,128)(2,1)S(1)}, bf16[6,128,256]{2,1,0:T(8,128)(2,1)S(1)}, bf16[6,128,25...) custom-call(s32[2]{0:T(128)S(1)} %get-tuple-element.145.info, ...), custom_call_target="tpu_custom_call", output_to_operand_aliasing={{5}: (7, {})} | custom-call | flops 1073741824 | bytes 7340032 | tf_op jit(solution)/shard_map/cond/branch_1_fun/pallas_call | solution.py:21
  147.2 1.7 collective-permute-start.99
  150.1 2.7 %collective-permute-done.99.refs_1_ = bf16[256,256]{1,0:T(8,128)(2,1)S(1)} collective-permute-done((bf16[256,256]{1,0:T(8,128)(2,1)S(1)}, bf16[256,256]{1,0:T(8,128)(2,1)S(1)}, u32[]{:S(2)}, u32[]{:S(2)}) %collective-permute-start.99) | collective-permute-done | bytes 131104 | tf_op jit(solution)/shard_map/cond/branch_1_fun/ppermute | solution.py:347
  152.8 1.3 collective-permute-start.100
  154.1 8.2 %collective-permute-done.100.refs_1_ = bf16[128,256]{1,0:T(8,128)(2,1)S(1)} collective-permute-done((bf16[128,256]{1,0:T(8,128)(2,1)S(1)}, bf16[128,256]{1,0:T(8,128)(2,1)S(1)}, u32[]{:S(2)}, u32[]{:S(2)}) %collective-permute-start.100) | collective-permute-done | bytes 65568 | tf_op jit(solution)/shard_map/cond/branch_1_fun/ppermute | solution.py:347
  162.3 8.6 %collective-permute-done.98.refs_1_ = bf16[4,128,256]{2,1,0:T(8,128)(2,1)S(1)} collective-permute-done((bf16[4,128,256]{2,1,0:T(8,128)(2,1)S(1)}, bf16[4,128,256]{2,1,0:T(8,128)(2,1)S(1)}, u32[]{:S(2)}, u32[]{:S(2)}) %collective-permute-start.98) | collective-permute-done | bytes 262176 | tf_op jit(solution)/shard_map/cond/branch_1_fun/ppermute | solution.py:455
  170.9 4.2 %branch_1_fun.36 = (bf16[2,1024,256]{2,1,0:T(8,128)(2,1)S(1)}, bf16[528,256]{1,0:T(8,128)(2,1)S(1)}, bf16[528,256]{1,0:T(8,128)(2,1)S(1)}) custom-call(s32[2]{0:T(128)S(1)} %get-tuple-element.145.info, s32[2,8]{1,0:T(2,128)S(1)} %get-tuple-element.159.side, s32[2]{0:T(128)S(1)} %get-tuple-element.160.powers, f32[2,1024,256]{2,1,0:T(8,128)S(1)} %get-tuple-element.161.gap_ref, ...), custom_call_target="tpu_custom_call" | custom-call | flops 2147483648 | bytes 12582912 | tf_op jit(solution)/shard_map/cond/branch_1_fun/pallas_call | solution.py:21
  175.1 1.3 collective-permute-start.101
  177.8 3.4 %collective-permute-start.104 = (bf16[144,256]{1,0:T(8,128)(2,1)S(1)}, bf16[144,256]{1,0:T(8,128)(2,1)S(1)}, u32[]{:S(2)}, u32[]{:S(2)}) collective-permute-start(bf16[144,256]{1,0:T(8,128)(2,1)S(1)} %get-tuple-element.224), channel_id=1, source_target_pairs={{0,24},{4,28},{8,16},{12,20},{16,8},{20,12},{24,0},{28,4},{1,25},{... | collective-permute-start | bytes 221192 | tf_op jit(solution)/shard_map/cond/branch_1_fun/ppermute | solution.py:347
  181.2 2.1 collective-permute-start.108
  184.0 4.7 %collective-permute-start.105 = (bf16[144,256]{1,0:T(8,128)(2,1)S(1)}, bf16[144,256]{1,0:T(8,128)(2,1)S(1)}, u32[]{:S(2)}, u32[]{:S(2)}) collective-permute-start(bf16[144,256]{1,0:T(8,128)(2,1)S(1)} %branch_1_fun.38.refs_0_), channel_id=1, source_target_pairs={{0,1},{1,0},{2,3},{3,2},{4,5},{5,4},{6,7},{7,6},{8,9},{9,8},{10,11... | collective-permute-start | bytes 221192 | tf_op jit(solution)/shard_map/cond/branch_1_fun/ppermute | solution.py:347
  188.6 2.4 %collective-permute-start.107 = (bf16[144,256]{1,0:T(8,128)(2,1)S(1)}, bf16[144,256]{1,0:T(8,128)(2,1)S(1)}, u32[]{:S(2)}, u32[]{:S(2)}) collective-permute-start(bf16[144,256]{1,0:T(8,128)(2,1)S(1)} %branch_1_fun.38.refs_0_), channel_id=1, source_target_pairs={{0,3},{1,2},{2,1},{3,0},{4,7},{5,6},{6,5},{7,4},{8,11},{9,10},{10,... | collective-permute-start | bytes 221192 | tf_op jit(solution)/shard_map/cond/branch_1_fun/ppermute | solution.py:347
  191.7 7.8 %collective-permute-done.109.refs_5_ = bf16[128,256]{1,0:T(8,128)(2,1)S(1)} collective-permute-done((bf16[128,256]{1,0:T(8,128)(2,1)S(1)}, bf16[128,256]{1,0:T(8,128)(2,1)S(1)}, u32[]{:S(2)}, u32[]{:S(2)}) %collective-permute-start.109) | collective-permute-done | bytes 65568 | tf_op jit(solution)/shard_map/cond/branch_1_fun/ppermute | solution.py:347
  199.5 1.3 collective-permute-start.111
  200.8 2.3 %collective-permute-start.115 = (bf16[128,256]{1,0:T(8,128)(2,1)S(1)}, bf16[128,256]{1,0:T(8,128)(2,1)S(1)}, u32[]{:S(2)}, u32[]{:S(2)}) collective-permute-start(bf16[128,256]{1,0:T(8,128)(2,1)S(1)} %get-tuple-element.226.refs_0_), channel_id=1, source_target_pairs={{0,24},{4,28},{8,16},{12,20},{16,8},{20,12},{24,0},{28,4},{1,25},{... | collective-permute-start | bytes 196616 | tf_op jit(solution)/shard_map/cond/branch_1_fun/ppermute | solution.py:347
  207.6 2.4 %branch_1_fun.41 = (f32[2,1024,256]{2,1,0:T(8,128)}, f32[3,1024,256]{2,1,0:T(8,128)}) custom-call(s32[2]{0:T(128)S(1)} %get-tuple-element.145.info, f32[2,1024,256]{2,1,0:T(8,128)S(1)} %get-tuple-element.196.lam_ref, bf16[2,1024,256]{2,1,0:T(8,128)(2,1)S(1)} %get-tuple-element.218.dir_ref, ...), custom_call_target="tpu_custom_call", output_to_operand_aliasing={{1}: (13, {})} | custom-call | flops 3145728 | bytes 8388608 | tf_op jit(solution)/shard_map/cond/branch_1_fun/pallas_call | solution.py:21
  (160 shorter events, 35.5 us)
Async XLA Ops:
  6.3 8.6 %collective-permute-start.117 = (bf16[512,256]{1,0:T(8,128)(2,1)S(1)}, bf16[512,256]{1,0:T(8,128)(2,1)S(1)}, u32[]{:S(2)}, u32[]{:S(2)}) collective-permute-start(bf16[512,256]{1,0:T(8,128)(2,1)S(1)} %get-tuple-element.261), channel_id=1, source_target_pairs={{0,4},{4,0},{8,12},{12,8},{16,20},{20,16},{24,28},{28,24},{1,5},{5... | collective-permute-start | bytes 786440 | tf_op jit(solution)/shard_map/ppermute | solution.py:347
  6.8 5.8 %collective-permute-start.118 = (s32[2,8]{1,0:T(2,128)S(1)}, s32[2,8]{1,0:T(2,128)S(1)}, u32[]{:S(2)}, u32[]{:S(2)}) collective-permute-start(s32[2,8]{1,0:T(2,128)S(1)} %copy-done.5), channel_id=1, source_target_pairs={{0,28},{4,8},{8,4},{12,16},{16,12},{20,24},{24,20},{28,0},{1,29},{... | collective-permute-start | bytes 200 | tf_op jit(solution)/shard_map/ppermute | solution.py:401
  15.0 26.4 %collective-permute-start.121 = (bf16[2,1024,256]{2,1,0:T(8,128)(2,1)S(1)}, bf16[2,1024,256]{2,1,0:T(8,128)(2,1)S(1)}, u32[]{:S(2)}, u32[]{:S(2)}) collective-permute-start(bf16[2,1024,256]{2,1,0:T(8,128)(2,1)S(1)} %get-tuple-element.269.refs_3_.disp_ref), channel_id=1, source_target_pairs={{0,4},{4,0},{8,12},{12,8},{16,20},{20,16},{24,28},{28,24},{1,5},{5... | collective-permute-start | bytes 3145736 | tf_op jit(solution)/shard_map/ppermute | solution.py:347
  15.1 5.9 %collective-permute-start.126 = (bf16[256,256]{1,0:T(8,128)(2,1)S(1)}, bf16[256,256]{1,0:T(8,128)(2,1)S(1)}, u32[]{:S(2)}, u32[]{:S(2)}) collective-permute-start(bf16[256,256]{1,0:T(8,128)(2,1)S(1)} %get-tuple-element.275), channel_id=1, source_target_pairs={{0,16},{4,20},{8,24},{12,28},{16,0},{20,4},{24,8},{28,12},{1,17},{... | collective-permute-start | bytes 393224 | tf_op jit(solution)/shard_map/ppermute | solution.py:347
  15.7 25.8 %collective-permute-start.122 = (bf16[6,128,256]{2,1,0:T(8,128)(2,1)S(1)}, bf16[6,128,256]{2,1,0:T(8,128)(2,1)S(1)}, u32[]{:S(2)}, u32[]{:S(2)}) collective-permute-start(bf16[6,128,256]{2,1,0:T(8,128)(2,1)S(1)} %get-tuple-element.270), channel_id=1, source_target_pairs={{0,1},{1,0},{2,3},{3,2},{4,5},{5,4},{6,7},{7,6},{8,9},{9,8},{10,11... | collective-permute-start | bytes 1179656 | tf_op jit(solution)/shard_map/ppermute | solution.py:456
  20.2 21.2 %collective-permute-start.123 = (bf16[6,128,256]{2,1,0:T(8,128)(2,1)S(1)}, bf16[6,128,256]{2,1,0:T(8,128)(2,1)S(1)}, u32[]{:S(2)}, u32[]{:S(2)}) collective-permute-start(bf16[6,128,256]{2,1,0:T(8,128)(2,1)S(1)} %get-tuple-element.271), channel_id=1, source_target_pairs={{1,2},{2,1},{5,6},{6,5},{9,10},{10,9},{13,14},{14,13},{17,18},{18,... | collective-permute-start | bytes 1179656 | tf_op jit(solution)/shard_map/ppermute | solution.py:457
  20.9 20.5 %collective-permute-start.124 = (bf16[6,128,256]{2,1,0:T(8,128)(2,1)S(1)}, bf16[6,128,256]{2,1,0:T(8,128)(2,1)S(1)}, u32[]{:S(2)}, u32[]{:S(2)}) collective-permute-start(bf16[6,128,256]{2,1,0:T(8,128)(2,1)S(1)} %get-tuple-element.272), channel_id=1, source_target_pairs={{0,28},{4,8},{8,4},{12,16},{16,12},{20,24},{24,20},{28,0},{1,29},{... | collective-permute-start | bytes 1179656 | tf_op jit(solution)/shard_map/ppermute | solution.py:453
  21.1 11.9 %collective-permute-start.127 = (bf16[128,256]{1,0:T(8,128)(2,1)S(1)}, bf16[128,256]{1,0:T(8,128)(2,1)S(1)}, u32[]{:S(2)}, u32[]{:S(2)}) collective-permute-start(bf16[128,256]{1,0:T(8,128)(2,1)S(1)} %get-tuple-element.277), channel_id=1, source_target_pairs={{0,8},{4,12},{8,0},{12,4},{16,24},{20,28},{24,16},{28,20},{1,9},{5... | collective-permute-start | bytes 196616 | tf_op jit(solution)/shard_map/ppermute | solution.py:347
  33.0 8.5 %collective-permute-start.125 = (bf16[4,128,256]{2,1,0:T(8,128)(2,1)S(1)}, bf16[4,128,256]{2,1,0:T(8,128)(2,1)S(1)}, u32[]{:S(2)}, u32[]{:S(2)}) collective-permute-start(bf16[4,128,256]{2,1,0:T(8,128)(2,1)S(1)} %get-tuple-element.273), channel_id=1, source_target_pairs={{0,28},{4,8},{8,4},{12,16},{16,12},{20,24},{24,20},{28,0},{1,29},{... | collective-permute-start | bytes 786440 | tf_op jit(solution)/shard_map/ppermute | solution.py:455
  49.3 6.2 %collective-permute-start.130 = (bf16[144,256]{1,0:T(8,128)(2,1)S(1)}, bf16[144,256]{1,0:T(8,128)(2,1)S(1)}, u32[]{:S(2)}, u32[]{:S(2)}) collective-permute-start(bf16[144,256]{1,0:T(8,128)(2,1)S(1)} %get-tuple-element.282), channel_id=1, source_target_pairs={{0,16},{4,20},{8,24},{12,28},{16,0},{20,4},{24,8},{28,12},{1,17},{... | collective-permute-start | bytes 221192 | tf_op jit(solution)/shard_map/ppermute | solution.py:347
  49.4 6.1 %collective-permute-start.131 = (bf16[144,256]{1,0:T(8,128)(2,1)S(1)}, bf16[144,256]{1,0:T(8,128)(2,1)S(1)}, u32[]{:S(2)}, u32[]{:S(2)}) collective-permute-start(bf16[144,256]{1,0:T(8,128)(2,1)S(1)} %get-tuple-element.283), channel_id=1, source_target_pairs={{0,24},{4,28},{8,16},{12,20},{16,8},{20,12},{24,0},{28,4},{1,25},{... | collective-permute-start | bytes 221192 | tf_op jit(solution)/shard_map/ppermute | solution.py:347
  52.8 8.9 %collective-permute-start.135 = (bf16[128,256]{1,0:T(8,128)(2,1)S(1)}, bf16[128,256]{1,0:T(8,128)(2,1)S(1)}, u32[]{:S(2)}, u32[]{:S(2)}) collective-permute-start(bf16[128,256]{1,0:T(8,128)(2,1)S(1)} %shard_map.100.refs_3_.refs_0_), channel_id=1, source_target_pairs={{0,1},{1,0},{2,3},{3,2},{4,5},{5,4},{6,7},{7,6},{8,9},{9,8},{10,11... | collective-permute-start | bytes 196616 | tf_op jit(solution)/shard_map/ppermute | solution.py:347
  55.6 14.5 %collective-permute-start.132 = (bf16[144,256]{1,0:T(8,128)(2,1)S(1)}, bf16[144,256]{1,0:T(8,128)(2,1)S(1)}, u32[]{:S(2)}, u32[]{:S(2)}) collective-permute-start(bf16[144,256]{1,0:T(8,128)(2,1)S(1)} %shard_map.103.refs_0_), channel_id=1, source_target_pairs={{0,1},{1,0},{2,3},{3,2},{4,5},{5,4},{6,7},{7,6},{8,9},{9,8},{10,11... | collective-permute-start | bytes 221192 | tf_op jit(solution)/shard_map/ppermute | solution.py:347
  59.2 10.8 %collective-permute-start.133 = (bf16[144,256]{1,0:T(8,128)(2,1)S(1)}, bf16[144,256]{1,0:T(8,128)(2,1)S(1)}, u32[]{:S(2)}, u32[]{:S(2)}) collective-permute-start(bf16[144,256]{1,0:T(8,128)(2,1)S(1)} %shard_map.103.refs_0_), channel_id=1, source_target_pairs={{0,2},{1,3},{2,0},{3,1},{4,6},{5,7},{6,4},{7,5},{8,10},{9,11},{10,... | collective-permute-start | bytes 221192 | tf_op jit(solution)/shard_map/ppermute | solution.py:347
  59.3 10.8 %collective-permute-start.134 = (bf16[144,256]{1,0:T(8,128)(2,1)S(1)}, bf16[144,256]{1,0:T(8,128)(2,1)S(1)}, u32[]{:S(2)}, u32[]{:S(2)}) collective-permute-start(bf16[144,256]{1,0:T(8,128)(2,1)S(1)} %shard_map.103.refs_0_), channel_id=1, source_target_pairs={{0,3},{1,2},{2,1},{3,0},{4,7},{5,6},{6,5},{7,4},{8,11},{9,10},{10,... | collective-permute-start | bytes 221192 | tf_op jit(solution)/shard_map/ppermute | solution.py:347
  61.7 8.3 %collective-permute-start.136 = (bf16[128,256]{1,0:T(8,128)(2,1)S(1)}, bf16[128,256]{1,0:T(8,128)(2,1)S(1)}, u32[]{:S(2)}, u32[]{:S(2)}) collective-permute-start(bf16[128,256]{1,0:T(8,128)(2,1)S(1)} %shard_map.104.refs_4_), channel_id=1, source_target_pairs={{0,2},{1,3},{2,0},{3,1},{4,6},{5,7},{6,4},{7,5},{8,10},{9,11},{10,... | collective-permute-start | bytes 196616 | tf_op jit(solution)/shard_map/ppermute | solution.py:347
  71.3 5.2 %collective-permute-start.142 = (bf16[128,256]{1,0:T(8,128)(2,1)S(1)}, bf16[128,256]{1,0:T(8,128)(2,1)S(1)}, u32[]{:S(2)}, u32[]{:S(2)}) collective-permute-start(bf16[128,256]{1,0:T(8,128)(2,1)S(1)} %get-tuple-element.286), channel_id=1, source_target_pairs={{0,24},{4,28},{8,16},{12,20},{16,8},{20,12},{24,0},{28,4},{1,25},{... | collective-permute-start | bytes 196616 | tf_op jit(solution)/shard_map/ppermute | solution.py:347
  82.5 24.1 %collective-permute-start.70 = (bf16[2,1024,256]{2,1,0:T(8,128)(2,1)S(1)}, bf16[2,1024,256]{2,1,0:T(8,128)(2,1)S(1)}, u32[]{:S(2)}, u32[]{:S(2)}) collective-permute-start(bf16[2,1024,256]{2,1,0:T(8,128)(2,1)S(1)} %get-tuple-element.177.disp_ref), channel_id=1, source_target_pairs={{0,4},{4,0},{8,12},{12,8},{16,20},{20,16},{24,28},{28,24},{1,5},{5... | collective-permute-start | bytes 3145736 | tf_op jit(solution)/shard_map/cond/branch_1_fun/ppermute | solution.py:347
  82.6 6.1 %collective-permute-start.75 = (bf16[256,256]{1,0:T(8,128)(2,1)S(1)}, bf16[256,256]{1,0:T(8,128)(2,1)S(1)}, u32[]{:S(2)}, u32[]{:S(2)}) collective-permute-start(bf16[256,256]{1,0:T(8,128)(2,1)S(1)} %get-tuple-element.184), channel_id=1, source_target_pairs={{0,16},{4,20},{8,24},{12,28},{16,0},{20,4},{24,8},{28,12},{1,17},{... | collective-permute-start | bytes 393224 | tf_op jit(solution)/shard_map/cond/branch_1_fun/ppermute | solution.py:347
  84.3 22.4 %collective-permute-start.71 = (bf16[6,128,256]{2,1,0:T(8,128)(2,1)S(1)}, bf16[6,128,256]{2,1,0:T(8,128)(2,1)S(1)}, u32[]{:S(2)}, u32[]{:S(2)}) collective-permute-start(bf16[6,128,256]{2,1,0:T(8,128)(2,1)S(1)} %get-tuple-element.178), channel_id=1, source_target_pairs={{0,1},{1,0},{2,3},{3,2},{4,5},{5,4},{6,7},{7,6},{8,9},{9,8},{10,11... | collective-permute-start | bytes 1179656 | tf_op jit(solution)/shard_map/cond/branch_1_fun/ppermute | solution.py:456
  84.3 22.4 %collective-permute-start.72 = (bf16[6,128,256]{2,1,0:T(8,128)(2,1)S(1)}, bf16[6,128,256]{2,1,0:T(8,128)(2,1)S(1)}, u32[]{:S(2)}, u32[]{:S(2)}) collective-permute-start(bf16[6,128,256]{2,1,0:T(8,128)(2,1)S(1)} %get-tuple-element.179), channel_id=1, source_target_pairs={{1,2},{2,1},{5,6},{6,5},{9,10},{10,9},{13,14},{14,13},{17,18},{18,... | collective-permute-start | bytes 1179656 | tf_op jit(solution)/shard_map/cond/branch_1_fun/ppermute | solution.py:457
  85.0 21.7 %collective-permute-start.73 = (bf16[6,128,256]{2,1,0:T(8,128)(2,1)S(1)}, bf16[6,128,256]{2,1,0:T(8,128)(2,1)S(1)}, u32[]{:S(2)}, u32[]{:S(2)}) collective-permute-start(bf16[6,128,256]{2,1,0:T(8,128)(2,1)S(1)} %get-tuple-element.180), channel_id=1, source_target_pairs={{0,28},{4,8},{8,4},{12,16},{16,12},{20,24},{24,20},{28,0},{1,29},{... | collective-permute-start | bytes 1179656 | tf_op jit(solution)/shard_map/cond/branch_1_fun/ppermute | solution.py:453
  88.8 8.9 %collective-permute-start.76 = (bf16[128,256]{1,0:T(8,128)(2,1)S(1)}, bf16[128,256]{1,0:T(8,128)(2,1)S(1)}, u32[]{:S(2)}, u32[]{:S(2)}) collective-permute-start(bf16[128,256]{1,0:T(8,128)(2,1)S(1)} %get-tuple-element.186), channel_id=1, source_target_pairs={{0,8},{4,12},{8,0},{12,4},{16,24},{20,28},{24,16},{28,20},{1,9},{5... | collective-permute-start | bytes 196616 | tf_op jit(solution)/shard_map/cond/branch_1_fun/ppermute | solution.py:347
  97.7 8.9 %collective-permute-start.74 = (bf16[4,128,256]{2,1,0:T(8,128)(2,1)S(1)}, bf16[4,128,256]{2,1,0:T(8,128)(2,1)S(1)}, u32[]{:S(2)}, u32[]{:S(2)}) collective-permute-start(bf16[4,128,256]{2,1,0:T(8,128)(2,1)S(1)} %get-tuple-element.181), channel_id=1, source_target_pairs={{0,28},{4,8},{8,4},{12,16},{16,12},{20,24},{24,20},{28,0},{1,29},{... | collective-permute-start | bytes 786440 | tf_op jit(solution)/shard_map/cond/branch_1_fun/ppermute | solution.py:455
  113.7 5.6 %collective-permute-start.78 = (bf16[144,256]{1,0:T(8,128)(2,1)S(1)}, bf16[144,256]{1,0:T(8,128)(2,1)S(1)}, u32[]{:S(2)}, u32[]{:S(2)}) collective-permute-start(bf16[144,256]{1,0:T(8,128)(2,1)S(1)} %get-tuple-element.191), channel_id=1, source_target_pairs={{0,8},{4,12},{8,0},{12,4},{16,24},{20,28},{24,16},{28,20},{1,9},{5... | collective-permute-start | bytes 221192 | tf_op jit(solution)/shard_map/cond/branch_1_fun/ppermute | solution.py:347
  113.8 6.2 %collective-permute-start.79 = (bf16[144,256]{1,0:T(8,128)(2,1)S(1)}, bf16[144,256]{1,0:T(8,128)(2,1)S(1)}, u32[]{:S(2)}, u32[]{:S(2)}) collective-permute-start(bf16[144,256]{1,0:T(8,128)(2,1)S(1)} %get-tuple-element.192), channel_id=1, source_target_pairs={{0,16},{4,20},{8,24},{12,28},{16,0},{20,4},{24,8},{28,12},{1,17},{... | collective-permute-start | bytes 221192 | tf_op jit(solution)/shard_map/cond/branch_1_fun/ppermute | solution.py:347
  113.9 6.1 %collective-permute-start.80 = (bf16[144,256]{1,0:T(8,128)(2,1)S(1)}, bf16[144,256]{1,0:T(8,128)(2,1)S(1)}, u32[]{:S(2)}, u32[]{:S(2)}) collective-permute-start(bf16[144,256]{1,0:T(8,128)(2,1)S(1)} %get-tuple-element.193), channel_id=1, source_target_pairs={{0,24},{4,28},{8,16},{12,20},{16,8},{20,12},{24,0},{28,4},{1,25},{... | collective-permute-start | bytes 221192 | tf_op jit(solution)/shard_map/cond/branch_1_fun/ppermute | solution.py:347
  117.3 8.9 %collective-permute-start.84 = (bf16[128,256]{1,0:T(8,128)(2,1)S(1)}, bf16[128,256]{1,0:T(8,128)(2,1)S(1)}, u32[]{:S(2)}, u32[]{:S(2)}) collective-permute-start(bf16[128,256]{1,0:T(8,128)(2,1)S(1)} %branch_1_fun.25.refs_3_.refs_0_), channel_id=1, source_target_pairs={{0,1},{1,0},{2,3},{3,2},{4,5},{5,4},{6,7},{7,6},{8,9},{9,8},{10,11... | collective-permute-start | bytes 196616 | tf_op jit(solution)/shard_map/cond/branch_1_fun/ppermute | solution.py:347
  120.1 14.5 %collective-permute-start.81 = (bf16[144,256]{1,0:T(8,128)(2,1)S(1)}, bf16[144,256]{1,0:T(8,128)(2,1)S(1)}, u32[]{:S(2)}, u32[]{:S(2)}) collective-permute-start(bf16[144,256]{1,0:T(8,128)(2,1)S(1)} %branch_1_fun.28.refs_0_), channel_id=1, source_target_pairs={{0,1},{1,0},{2,3},{3,2},{4,5},{5,4},{6,7},{7,6},{8,9},{9,8},{10,11... | collective-permute-start | bytes 221192 | tf_op jit(solution)/shard_map/cond/branch_1_fun/ppermute | solution.py:347
  123.8 10.8 %collective-permute-start.82 = (bf16[144,256]{1,0:T(8,128)(2,1)S(1)}, bf16[144,256]{1,0:T(8,128)(2,1)S(1)}, u32[]{:S(2)}, u32[]{:S(2)}) collective-permute-start(bf16[144,256]{1,0:T(8,128)(2,1)S(1)} %branch_1_fun.28.refs_0_), channel_id=1, source_target_pairs={{0,2},{1,3},{2,0},{3,1},{4,6},{5,7},{6,4},{7,5},{8,10},{9,11},{10,... | collective-permute-start | bytes 221192 | tf_op jit(solution)/shard_map/cond/branch_1_fun/ppermute | solution.py:347
  123.8 10.8 %collective-permute-start.83 = (bf16[144,256]{1,0:T(8,128)(2,1)S(1)}, bf16[144,256]{1,0:T(8,128)(2,1)S(1)}, u32[]{:S(2)}, u32[]{:S(2)}) collective-permute-start(bf16[144,256]{1,0:T(8,128)(2,1)S(1)} %branch_1_fun.28.refs_0_), channel_id=1, source_target_pairs={{0,3},{1,2},{2,1},{3,0},{4,7},{5,6},{6,5},{7,4},{8,11},{9,10},{10,... | collective-permute-start | bytes 221192 | tf_op jit(solution)/shard_map/cond/branch_1_fun/ppermute | solution.py:347
  126.2 8.3 %collective-permute-start.85 = (bf16[128,256]{1,0:T(8,128)(2,1)S(1)}, bf16[128,256]{1,0:T(8,128)(2,1)S(1)}, u32[]{:S(2)}, u32[]{:S(2)}) collective-permute-start(bf16[128,256]{1,0:T(8,128)(2,1)S(1)} %branch_1_fun.29.refs_4_), channel_id=1, source_target_pairs={{0,2},{1,3},{2,0},{3,1},{4,6},{5,7},{6,4},{7,5},{8,10},{9,11},{10,... | collective-permute-start | bytes 196616 | tf_op jit(solution)/shard_map/cond/branch_1_fun/ppermute | solution.py:347
  136.2 5.2 %collective-permute-start.91 = (bf16[128,256]{1,0:T(8,128)(2,1)S(1)}, bf16[128,256]{1,0:T(8,128)(2,1)S(1)}, u32[]{:S(2)}, u32[]{:S(2)}) collective-permute-start(bf16[128,256]{1,0:T(8,128)(2,1)S(1)} %get-tuple-element.195.refs_0_), channel_id=1, source_target_pairs={{0,24},{4,28},{8,16},{12,20},{16,8},{20,12},{24,0},{28,4},{1,25},{... | collective-permute-start | bytes 196616 | tf_op jit(solution)/shard_map/cond/branch_1_fun/ppermute | solution.py:347
  146.8 24.1 %collective-permute-start.94 = (bf16[2,1024,256]{2,1,0:T(8,128)(2,1)S(1)}, bf16[2,1024,256]{2,1,0:T(8,128)(2,1)S(1)}, u32[]{:S(2)}, u32[]{:S(2)}) collective-permute-start(bf16[2,1024,256]{2,1,0:T(8,128)(2,1)S(1)} %get-tuple-element.209.disp_ref), channel_id=1, source_target_pairs={{0,4},{4,0},{8,12},{12,8},{16,20},{20,16},{24,28},{28,24},{1,5},{5... | collective-permute-start | bytes 3145736 | tf_op jit(solution)/shard_map/cond/branch_1_fun/ppermute | solution.py:347
  147.2 5.6 %collective-permute-start.99 = (bf16[256,256]{1,0:T(8,128)(2,1)S(1)}, bf16[256,256]{1,0:T(8,128)(2,1)S(1)}, u32[]{:S(2)}, u32[]{:S(2)}) collective-permute-start(bf16[256,256]{1,0:T(8,128)(2,1)S(1)} %get-tuple-element.215), channel_id=1, source_target_pairs={{0,16},{4,20},{8,24},{12,28},{16,0},{20,4},{24,8},{28,12},{1,17},{... | collective-permute-start | bytes 393224 | tf_op jit(solution)/shard_map/cond/branch_1_fun/ppermute | solution.py:347
  148.9 22.0 %collective-permute-start.95 = (bf16[6,128,256]{2,1,0:T(8,128)(2,1)S(1)}, bf16[6,128,256]{2,1,0:T(8,128)(2,1)S(1)}, u32[]{:S(2)}, u32[]{:S(2)}) collective-permute-start(bf16[6,128,256]{2,1,0:T(8,128)(2,1)S(1)} %get-tuple-element.210), channel_id=1, source_target_pairs={{0,1},{1,0},{2,3},{3,2},{4,5},{5,4},{6,7},{7,6},{8,9},{9,8},{10,11... | collective-permute-start | bytes 1179656 | tf_op jit(solution)/shard_map/cond/branch_1_fun/ppermute | solution.py:456
  148.9 22.0 %collective-permute-start.96 = (bf16[6,128,256]{2,1,0:T(8,128)(2,1)S(1)}, bf16[6,128,256]{2,1,0:T(8,128)(2,1)S(1)}, u32[]{:S(2)}, u32[]{:S(2)}) collective-permute-start(bf16[6,128,256]{2,1,0:T(8,128)(2,1)S(1)} %get-tuple-element.211), channel_id=1, source_target_pairs={{1,2},{2,1},{5,6},{6,5},{9,10},{10,9},{13,14},{14,13},{17,18},{18,... | collective-permute-start | bytes 1179656 | tf_op jit(solution)/shard_map/cond/branch_1_fun/ppermute | solution.py:457
  149.6 21.3 %collective-permute-start.97 = (bf16[6,128,256]{2,1,0:T(8,128)(2,1)S(1)}, bf16[6,128,256]{2,1,0:T(8,128)(2,1)S(1)}, u32[]{:S(2)}, u32[]{:S(2)}) collective-permute-start(bf16[6,128,256]{2,1,0:T(8,128)(2,1)S(1)} %get-tuple-element.212), channel_id=1, source_target_pairs={{0,28},{4,8},{8,4},{12,16},{16,12},{20,24},{24,20},{28,0},{1,29},{... | collective-permute-start | bytes 1179656 | tf_op jit(solution)/shard_map/cond/branch_1_fun/ppermute | solution.py:453
  152.8 9.4 %collective-permute-start.100 = (bf16[128,256]{1,0:T(8,128)(2,1)S(1)}, bf16[128,256]{1,0:T(8,128)(2,1)S(1)}, u32[]{:S(2)}, u32[]{:S(2)}) collective-permute-start(bf16[128,256]{1,0:T(8,128)(2,1)S(1)} %get-tuple-element.217), channel_id=1, source_target_pairs={{0,8},{4,12},{8,0},{12,4},{16,24},{20,28},{24,16},{28,20},{1,9},{5... | collective-permute-start | bytes 196616 | tf_op jit(solution)/shard_map/cond/branch_1_fun/ppermute | solution.py:347
  162.2 8.7 %collective-permute-start.98 = (bf16[4,128,256]{2,1,0:T(8,128)(2,1)S(1)}, bf16[4,128,256]{2,1,0:T(8,128)(2,1)S(1)}, u32[]{:S(2)}, u32[]{:S(2)}) collective-permute-start(bf16[4,128,256]{2,1,0:T(8,128)(2,1)S(1)} %get-tuple-element.213), channel_id=1, source_target_pairs={{0,28},{4,8},{8,4},{12,16},{16,12},{20,24},{24,20},{28,0},{1,29},{... | collective-permute-start | bytes 786440 | tf_op jit(solution)/shard_map/cond/branch_1_fun/ppermute | solution.py:455
  177.6 5.6 %collective-permute-start.102 = (bf16[144,256]{1,0:T(8,128)(2,1)S(1)}, bf16[144,256]{1,0:T(8,128)(2,1)S(1)}, u32[]{:S(2)}, u32[]{:S(2)}) collective-permute-start(bf16[144,256]{1,0:T(8,128)(2,1)S(1)} %get-tuple-element.222), channel_id=1, source_target_pairs={{0,8},{4,12},{8,0},{12,4},{16,24},{20,28},{24,16},{28,20},{1,9},{5... | collective-permute-start | bytes 221192 | tf_op jit(solution)/shard_map/cond/branch_1_fun/ppermute | solution.py:347
  177.7 6.2 %collective-permute-start.103 = (bf16[144,256]{1,0:T(8,128)(2,1)S(1)}, bf16[144,256]{1,0:T(8,128)(2,1)S(1)}, u32[]{:S(2)}, u32[]{:S(2)}) collective-permute-start(bf16[144,256]{1,0:T(8,128)(2,1)S(1)} %get-tuple-element.223), channel_id=1, source_target_pairs={{0,16},{4,20},{8,24},{12,28},{16,0},{20,4},{24,8},{28,12},{1,17},{... | collective-permute-start | bytes 221192 | tf_op jit(solution)/shard_map/cond/branch_1_fun/ppermute | solution.py:347
  177.8 6.1 %collective-permute-start.104 = (bf16[144,256]{1,0:T(8,128)(2,1)S(1)}, bf16[144,256]{1,0:T(8,128)(2,1)S(1)}, u32[]{:S(2)}, u32[]{:S(2)}) collective-permute-start(bf16[144,256]{1,0:T(8,128)(2,1)S(1)} %get-tuple-element.224), channel_id=1, source_target_pairs={{0,24},{4,28},{8,16},{12,20},{16,8},{20,12},{24,0},{28,4},{1,25},{... | collective-permute-start | bytes 221192 | tf_op jit(solution)/shard_map/cond/branch_1_fun/ppermute | solution.py:347
  181.2 9.9 %collective-permute-start.108 = (bf16[128,256]{1,0:T(8,128)(2,1)S(1)}, bf16[128,256]{1,0:T(8,128)(2,1)S(1)}, u32[]{:S(2)}, u32[]{:S(2)}) collective-permute-start(bf16[128,256]{1,0:T(8,128)(2,1)S(1)} %branch_1_fun.35.refs_3_.refs_0_), channel_id=1, source_target_pairs={{0,1},{1,0},{2,3},{3,2},{4,5},{5,4},{6,7},{7,6},{8,9},{9,8},{10,11... | collective-permute-start | bytes 196616 | tf_op jit(solution)/shard_map/cond/branch_1_fun/ppermute | solution.py:347
  184.0 15.5 %collective-permute-start.105 = (bf16[144,256]{1,0:T(8,128)(2,1)S(1)}, bf16[144,256]{1,0:T(8,128)(2,1)S(1)}, u32[]{:S(2)}, u32[]{:S(2)}) collective-permute-start(bf16[144,256]{1,0:T(8,128)(2,1)S(1)} %branch_1_fun.38.refs_0_), channel_id=1, source_target_pairs={{0,1},{1,0},{2,3},{3,2},{4,5},{5,4},{6,7},{7,6},{8,9},{9,8},{10,11... | collective-permute-start | bytes 221192 | tf_op jit(solution)/shard_map/cond/branch_1_fun/ppermute | solution.py:347
  188.6 10.8 %collective-permute-start.106 = (bf16[144,256]{1,0:T(8,128)(2,1)S(1)}, bf16[144,256]{1,0:T(8,128)(2,1)S(1)}, u32[]{:S(2)}, u32[]{:S(2)}) collective-permute-start(bf16[144,256]{1,0:T(8,128)(2,1)S(1)} %branch_1_fun.38.refs_0_), channel_id=1, source_target_pairs={{0,2},{1,3},{2,0},{3,1},{4,6},{5,7},{6,4},{7,5},{8,10},{9,11},{10,... | collective-permute-start | bytes 221192 | tf_op jit(solution)/shard_map/cond/branch_1_fun/ppermute | solution.py:347
  188.6 10.8 %collective-permute-start.107 = (bf16[144,256]{1,0:T(8,128)(2,1)S(1)}, bf16[144,256]{1,0:T(8,128)(2,1)S(1)}, u32[]{:S(2)}, u32[]{:S(2)}) collective-permute-start(bf16[144,256]{1,0:T(8,128)(2,1)S(1)} %branch_1_fun.38.refs_0_), channel_id=1, source_target_pairs={{0,3},{1,2},{2,1},{3,0},{4,7},{5,6},{6,5},{7,4},{8,11},{9,10},{10,... | collective-permute-start | bytes 221192 | tf_op jit(solution)/shard_map/cond/branch_1_fun/ppermute | solution.py:347
  191.1 8.3 %collective-permute-start.109 = (bf16[128,256]{1,0:T(8,128)(2,1)S(1)}, bf16[128,256]{1,0:T(8,128)(2,1)S(1)}, u32[]{:S(2)}, u32[]{:S(2)}) collective-permute-start(bf16[128,256]{1,0:T(8,128)(2,1)S(1)} %branch_1_fun.39.refs_4_), channel_id=1, source_target_pairs={{0,2},{1,3},{2,0},{3,1},{4,6},{5,7},{6,4},{7,5},{8,10},{9,11},{10,... | collective-permute-start | bytes 196616 | tf_op jit(solution)/shard_map/cond/branch_1_fun/ppermute | solution.py:347
  (35 other events, 343.0 us)

commit v6 on v4

--- a/solution.py
+++ b/solution.py
@@ -249,29 +249,20 @@
             up = (face == 2).astype(jnp.int32)
             down = (face == 3).astype(jnp.int32)
 
-            @pl.when(face < 2)
-            def _():
-                pl.when(face == odd)(lambda: put(chip_ref[s, rows, :]))
-                pl.when(away & (n < size))(lambda: put(take(offs[0], n)))
-                if packed:
-                    pl.when(away & (n >= size))(lambda: put(take(offs[1], n - size)))
-
-            @pl.when(face == 2)
-            def _():
-                if s + 1 < subs:
-                    put(disp_ref[s + 1, rows, :])
-                else:
-                    pl.when(zodd == 0)(lambda: put(take(za_ref, above)))
-                    pl.when(zodd == 1)(lambda: put(take(zb_ref, above)))
-
-            @pl.when(face == 3)
-            def _():
-                if s > 0:
-                    put(disp_ref[s - 1, rows, :])
-                else:
-                    pl.when(zodd == 1)(lambda: put(take(za_ref, below)))
-                    pl.when(zodd == 0)(lambda: put(take(zb_ref, below)))
-
+            pl.when(face == odd)(lambda: put(chip_ref[s, rows, :]))
+            pl.when(away & (n < size))(lambda: put(take(offs[0], n)))
+            if packed:
+                pl.when(away & (n >= size))(lambda: put(take(offs[1], n - size)))
+            if s + 1 < subs:
+                pl.when(face == 2)(lambda: put(disp_ref[s + 1, rows, :]))
+            else:
+                pl.when((face == 2) & (zodd == 0))(lambda: put(take(za_ref, above)))
+                pl.when((face == 2) & (zodd == 1))(lambda: put(take(zb_ref, above)))
+            if s > 0:
+                pl.when(face == 3)(lambda: put(disp_ref[s - 1, rows, :]))
+            else:
+                pl.when((face == 3) & (zodd == 1))(lambda: put(take(za_ref, below)))
+                pl.when((face == 3) & (zodd == 0))(lambda: put(take(zb_ref, below)))
             n = n + away.astype(jnp.int32)
             if s + 1 == subs:
                 above = above + up

time: 206 us -> 207 us (level)
  no operation moved by 1% of the time
where the time goes in v6:
time: 207 us
  waiting for transfers between devices  92.5 us (45%)
  starting transfers between devices  80.5 us (39%)
  Pallas kernels  29.4 us (14%)
  local copies, waits for them, and re-layouts  2.11 us (1%)
    ppermute x63, starting transfers between devices, swap(): return lax.ppermute(x, axis, [(i, i ^ mask) for i in range(n)])  63.4 us
    ppermute x63, waiting for transfers between devices, swap(): return lax.ppermute(x, axis, [(i, i ^ mask) for i in range(n)])  47.1 us
    pallas_call x28, Pallas kernels, call(): pl.pallas_call(kernel, out_shape=outs, in_specs=[SMEM if i < n_smem else...  29.4 us
    ppermute x3, waiting for transfers between devices, search(): offs[0] = lax.ppermute(offs[0], 'wide', away)  24.5 us
    ppermute x3, waiting for transfers between devices, search(): offs[-1] = lax.ppermute(offs[-1], 'wide', away)  19.5 us
    ppermute x3, starting transfers between devices, search(): za = lax.ppermute(za, 'eight', pairs_a)  4.6 us
  transfers between devices with their start and end apart: 78, of which 35 were waited for; matrix products, arithmetic and copies ran while one was open for 0% of the time, Pallas kernels for 3%

profile of v6, /device:TPU:0, one launch (start us, length us, event | category | flops | bytes accessed | tf_op | source)
XLA Modules:
  0.0 206.7 jit_solution(10086979834855584563)
XLA Ops:
  0.7 5.5 %shard_map.96 = (bf16[512,256]{1,0:T(8,128)(2,1)S(1)}, bf16[512,256]{1,0:T(8,128)(2,1)S(1)}, bf16[2,1024,256]{2,1,0:T(8,128)(2,1)S(1)}) custom-call(s32[2]{0:T(128)S(1)} %pad_add_fusion.info, f32[2,1024,256]{2,1,0:T(8,128)} %lam_ref.1, bf16[2,1024,1024]{2,1,0:T(8,128)(2,1)} %flex_ref.1), custom_call_target="tpu_custom_call" | custom-call | flops 1073741824 | bytes 7340032 | tf_op jit(solution)/shard_map/pallas_call | solution.py:21
  6.8 3.5 %collective-permute-start.123 = (s32[2,8]{1,0:T(2,128)S(1)}, s32[2,8]{1,0:T(2,128)S(1)}, u32[]{:S(2)}, u32[]{:S(2)}) collective-permute-start(s32[2,8]{1,0:T(2,128)S(1)} %copy-done.5), channel_id=1, source_target_pairs={{0,28},{4,8},{8,4},{12,16},{16,12},{20,24},{24,20},{28,0},{1,29},{... | collective-permute-start | bytes 200 | tf_op jit(solution)/shard_map/ppermute | solution.py:401
  10.4 1.6 collective-permute-start.124
  16.4 2.3 %collective-permute-start.133 = (bf16[128,256]{1,0:T(8,128)(2,1)S(1)}, bf16[128,256]{1,0:T(8,128)(2,1)S(1)}, u32[]{:S(2)}, u32[]{:S(2)}) collective-permute-start(bf16[128,256]{1,0:T(8,128)(2,1)S(1)} %get-tuple-element.291), channel_id=1, source_target_pairs={{0,24},{4,28},{8,16},{12,20},{16,8},{20,12},{24,0},{28,4},{1,25},{... | collective-permute-start | bytes 196616 | tf_op jit(solution)/shard_map/ppermute | solution.py:344
  18.6 4.6 %collective-permute-start.127 = (bf16[6,128,256]{2,1,0:T(8,128)(2,1)S(1)}, bf16[6,128,256]{2,1,0:T(8,128)(2,1)S(1)}, u32[]{:S(2)}, u32[]{:S(2)}) collective-permute-start(bf16[6,128,256]{2,1,0:T(8,128)(2,1)S(1)} %get-tuple-element.284), channel_id=1, source_target_pairs={{0,1},{1,0},{2,3},{3,2},{4,5},{5,4},{6,7},{7,6},{8,9},{9,8},{10,11... | collective-permute-start | bytes 1179656 | tf_op jit(solution)/shard_map/ppermute | solution.py:456
  24.0 2.6 %collective-permute-start.130 = (bf16[5,128,256]{2,1,0:T(8,128)(2,1)S(1)}, bf16[5,128,256]{2,1,0:T(8,128)(2,1)S(1)}, u32[]{:S(2)}, u32[]{:S(2)}) collective-permute-start(bf16[5,128,256]{2,1,0:T(8,128)(2,1)S(1)} %get-tuple-element.287), channel_id=1, source_target_pairs={{0,28},{4,8},{8,4},{12,16},{16,12},{20,24},{24,20},{28,0},{1,29},{... | collective-permute-start | bytes 983048 | tf_op jit(solution)/shard_map/ppermute | solution.py:455
  26.7 8.2 %collective-permute-done.129.refs_0_ = bf16[5,128,256]{2,1,0:T(8,128)(2,1)S(1)} collective-permute-done((bf16[5,128,256]{2,1,0:T(8,128)(2,1)S(1)}, bf16[5,128,256]{2,1,0:T(8,128)(2,1)S(1)}, u32[]{:S(2)}, u32[]{:S(2)}) %collective-permute-start.129) | collective-permute-done | bytes 327712 | tf_op jit(solution)/shard_map/ppermute | solution.py:453
  34.9 5.6 %collective-permute-done.130.refs_1_ = bf16[5,128,256]{2,1,0:T(8,128)(2,1)S(1)} collective-permute-done((bf16[5,128,256]{2,1,0:T(8,128)(2,1)S(1)}, bf16[5,128,256]{2,1,0:T(8,128)(2,1)S(1)}, u32[]{:S(2)}, u32[]{:S(2)}) %collective-permute-start.130) | collective-permute-done | bytes 327712 | tf_op jit(solution)/shard_map/ppermute | solution.py:455
  40.5 4.2 %shard_map.100 = (bf16[2,1024,256]{2,1,0:T(8,128)(2,1)S(1)}, bf16[528,256]{1,0:T(8,128)(2,1)S(1)}, bf16[528,256]{1,0:T(8,128)(2,1)S(1)}) custom-call(s32[2]{0:T(128)S(1)} %pad_add_fusion.info, s32[2,8]{1,0:T(2,128)S(1)} %copy-done.5, s32[2]{0:T(128)S(1)} %copy-done.6, f32[2,1024,256]{2,1,0:T(8,128)S(1)} %copy-done.2, ...), custom_call_target="tpu_custom_call" | custom-call | flops 2147483648 | bytes 12582912 | tf_op jit(solution)/shard_map/pallas_call | solution.py:21
  44.7 1.9 collective-permute-start.134
  48.0 3.4 %collective-permute-start.137 = (bf16[144,256]{1,0:T(8,128)(2,1)S(1)}, bf16[144,256]{1,0:T(8,128)(2,1)S(1)}, u32[]{:S(2)}, u32[]{:S(2)}) collective-permute-start(bf16[144,256]{1,0:T(8,128)(2,1)S(1)} %get-tuple-element.297), channel_id=1, source_target_pairs={{0,24},{4,28},{8,16},{12,20},{16,8},{20,12},{24,0},{28,4},{1,25},{... | collective-permute-start | bytes 221192 | tf_op jit(solution)/shard_map/ppermute | solution.py:344
  51.4 2.0 collective-permute-start.141
  54.2 4.3 %collective-permute-start.138 = (bf16[144,256]{1,0:T(8,128)(2,1)S(1)}, bf16[144,256]{1,0:T(8,128)(2,1)S(1)}, u32[]{:S(2)}, u32[]{:S(2)}) collective-permute-start(bf16[144,256]{1,0:T(8,128)(2,1)S(1)} %shard_map.102.refs_0_), channel_id=1, source_target_pairs={{0,1},{1,0},{2,3},{3,2},{4,5},{5,4},{6,7},{7,6},{8,9},{9,8},{10,11... | collective-permute-start | bytes 221192 | tf_op jit(solution)/shard_map/ppermute | solution.py:344
  58.5 2.4 %collective-permute-start.140 = (bf16[144,256]{1,0:T(8,128)(2,1)S(1)}, bf16[144,256]{1,0:T(8,128)(2,1)S(1)}, u32[]{:S(2)}, u32[]{:S(2)}) collective-permute-start(bf16[144,256]{1,0:T(8,128)(2,1)S(1)} %shard_map.102.refs_0_), channel_id=1, source_target_pairs={{0,3},{1,2},{2,1},{3,0},{4,7},{5,6},{6,5},{7,4},{8,11},{9,10},{10,... | collective-permute-start | bytes 221192 | tf_op jit(solution)/shard_map/ppermute | solution.py:344
  61.5 7.9 %collective-permute-done.142.refs_5_ = bf16[128,256]{1,0:T(8,128)(2,1)S(1)} collective-permute-done((bf16[128,256]{1,0:T(8,128)(2,1)S(1)}, bf16[128,256]{1,0:T(8,128)(2,1)S(1)}, u32[]{:S(2)}, u32[]{:S(2)}) %collective-permute-start.142) | collective-permute-done | bytes 65568 | tf_op jit(solution)/shard_map/ppermute | solution.py:344
  70.6 2.4 %collective-permute-start.148 = (bf16[128,256]{1,0:T(8,128)(2,1)S(1)}, bf16[128,256]{1,0:T(8,128)(2,1)S(1)}, u32[]{:S(2)}, u32[]{:S(2)}) collective-permute-start(bf16[128,256]{1,0:T(8,128)(2,1)S(1)} %get-tuple-element.300), channel_id=1, source_target_pairs={{0,24},{4,28},{8,16},{12,20},{16,8},{20,12},{24,0},{28,4},{1,25},{... | collective-permute-start | bytes 196616 | tf_op jit(solution)/shard_map/ppermute | solution.py:344
  77.0 129.0 %conditional.1 = (f32[2,1024,256]{2,1,0:T(8,128)}, f32[3,1024,256]{2,1,0:T(8,128)}, f32[3,256]{1,0:T(4,128)S(1)}) conditional(s32[]{:T(128)} %bitcast.8, (s32[2]{0:T(128)S(1)}, f32[2,1024,256]{2,1,0:T(8,128)S(1)}, bf16[2,1024,1024]{2,1,0:T(8,128)(2,1)S(1)}, s32[2,8]{1,0:T(2,128)S(1)}, s32[2]{0:T(128)S(1)}, /*index=5*/f32[2,1024,256]{2,1,0:T(8,128)S(1)}, ...), branch_computations={%region_0.1_spmd, %region_1.2_spmd} | conditional | flops 9677191168 | bytes 158391008 | solution.py:519
  79.3 2.4 %branch_1_fun.21 = (bf16[2,1024,256]{2,1,0:T(8,128)(2,1)S(1)}, bf16[6,128,256]{2,1,0:T(8,128)(2,1)S(1)}, bf16[6,128,256]{2,1,0:T(8,128)(2,1)S(1)}, bf16[5,128,25...) custom-call(s32[2]{0:T(128)S(1)} %get-tuple-element.151.info, ...), custom_call_target="tpu_custom_call" | custom-call | flops 1073741824 | bytes 7340032 | tf_op jit(solution)/shard_map/cond/branch_1_fun/pallas_call | solution.py:21
  81.8 1.5 collective-permute-start.78
  83.3 1.5 collective-permute-start.79
  88.7 1.4 collective-permute-done.80.refs_3_
  90.3 8.2 %collective-permute-done.76.refs_0_ = bf16[5,128,256]{2,1,0:T(8,128)(2,1)S(1)} collective-permute-done((bf16[5,128,256]{2,1,0:T(8,128)(2,1)S(1)}, bf16[5,128,256]{2,1,0:T(8,128)(2,1)S(1)}, u32[]{:S(2)}, u32[]{:S(2)}) %collective-permute-start.76) | collective-permute-done | bytes 327712 | tf_op jit(solution)/shard_map/cond/branch_1_fun/ppermute | solution.py:453
  98.5 6.9 %collective-permute-done.77.refs_1_ = bf16[5,128,256]{2,1,0:T(8,128)(2,1)S(1)} collective-permute-done((bf16[5,128,256]{2,1,0:T(8,128)(2,1)S(1)}, bf16[5,128,256]{2,1,0:T(8,128)(2,1)S(1)}, u32[]{:S(2)}, u32[]{:S(2)}) %collective-permute-start.77) | collective-permute-done | bytes 327712 | tf_op jit(solution)/shard_map/cond/branch_1_fun/ppermute | solution.py:455
  105.4 4.2 %branch_1_fun.23 = (bf16[2,1024,256]{2,1,0:T(8,128)(2,1)S(1)}, bf16[528,256]{1,0:T(8,128)(2,1)S(1)}, bf16[528,256]{1,0:T(8,128)(2,1)S(1)}) custom-call(s32[2]{0:T(128)S(1)} %get-tuple-element.151.info, s32[2,8]{1,0:T(2,128)S(1)} %get-tuple-element.165.side, s32[2]{0:T(128)S(1)} %get-tuple-element.166.powers, f32[2,1024,256]{2,1,0:T(8,128)S(1)} %get-tuple-element.167.gap_ref, ...), custom_call_target="tpu_custom_call" | custom-call | flops 2147483648 | bytes 12582912 | tf_op jit(solution)/shard_map/cond/branch_1_fun/pallas_call | solution.py:21
  109.7 1.5 collective-permute-done.81.refs_1_
  112.7 2.2 %collective-permute-start.84 = (bf16[144,256]{1,0:T(8,128)(2,1)S(1)}, bf16[144,256]{1,0:T(8,128)(2,1)S(1)}, u32[]{:S(2)}, u32[]{:S(2)}) collective-permute-start(bf16[144,256]{1,0:T(8,128)(2,1)S(1)} %get-tuple-element.201), channel_id=1, source_target_pairs={{0,24},{4,28},{8,16},{12,20},{16,8},{20,12},{24,0},{28,4},{1,25},{... | collective-permute-start | bytes 221192 | tf_op jit(solution)/shard_map/cond/branch_1_fun/ppermute | solution.py:344
  114.9 1.6 collective-permute-start.88
  118.0 3.0 %collective-permute-start.85 = (bf16[144,256]{1,0:T(8,128)(2,1)S(1)}, bf16[144,256]{1,0:T(8,128)(2,1)S(1)}, u32[]{:S(2)}, u32[]{:S(2)}) collective-permute-start(bf16[144,256]{1,0:T(8,128)(2,1)S(1)} %branch_1_fun.25.refs_0_), channel_id=1, source_target_pairs={{0,1},{1,0},{2,3},{3,2},{4,5},{5,4},{6,7},{7,6},{8,9},{9,8},{10,11... | collective-permute-start | bytes 221192 | tf_op jit(solution)/shard_map/cond/branch_1_fun/ppermute | solution.py:344
  121.5 1.9 collective-permute-start.87
  123.4 1.6 collective-permute-start.89
  125.0 7.0 %collective-permute-done.89.refs_5_ = bf16[128,256]{1,0:T(8,128)(2,1)S(1)} collective-permute-done((bf16[128,256]{1,0:T(8,128)(2,1)S(1)}, bf16[128,256]{1,0:T(8,128)(2,1)S(1)}, u32[]{:S(2)}, u32[]{:S(2)}) %collective-permute-start.89) | collective-permute-done | bytes 65568 | tf_op jit(solution)/shard_map/cond/branch_1_fun/ppermute | solution.py:344
  133.9 1.7 collective-permute-start.95
  137.4 1.7 collective-permute-done.95.refs_6_
  142.0 2.4 %branch_1_fun.30 = (bf16[2,1024,256]{2,1,0:T(8,128)(2,1)S(1)}, bf16[6,128,256]{2,1,0:T(8,128)(2,1)S(1)}, bf16[6,128,256]{2,1,0:T(8,128)(2,1)S(1)}, bf16[5,128,25...) custom-call(s32[2]{0:T(128)S(1)} %get-tuple-element.151.info, ...), custom_call_target="tpu_custom_call", output_to_operand_aliasing={{5}: (7, {})} | custom-call | flops 1073741824 | bytes 7340032 | tf_op jit(solution)/shard_map/cond/branch_1_fun/pallas_call | solution.py:21
  150.5 1.9 collective-permute-done.105.refs_3_
  152.8 8.1 %collective-permute-done.101.refs_0_ = bf16[5,128,256]{2,1,0:T(8,128)(2,1)S(1)} collective-permute-done((bf16[5,128,256]{2,1,0:T(8,128)(2,1)S(1)}, bf16[5,128,256]{2,1,0:T(8,128)(2,1)S(1)}, u32[]{:S(2)}, u32[]{:S(2)}) %collective-permute-start.101) | collective-permute-done | bytes 327712 | tf_op jit(solution)/shard_map/cond/branch_1_fun/ppermute | solution.py:453
  161.0 7.0 %collective-permute-done.102.refs_1_ = bf16[5,128,256]{2,1,0:T(8,128)(2,1)S(1)} collective-permute-done((bf16[5,128,256]{2,1,0:T(8,128)(2,1)S(1)}, bf16[5,128,256]{2,1,0:T(8,128)(2,1)S(1)}, u32[]{:S(2)}, u32[]{:S(2)}) %collective-permute-start.102) | collective-permute-done | bytes 327712 | tf_op jit(solution)/shard_map/cond/branch_1_fun/ppermute | solution.py:455
  168.0 4.2 %branch_1_fun.32 = (bf16[2,1024,256]{2,1,0:T(8,128)(2,1)S(1)}, bf16[528,256]{1,0:T(8,128)(2,1)S(1)}, bf16[528,256]{1,0:T(8,128)(2,1)S(1)}) custom-call(s32[2]{0:T(128)S(1)} %get-tuple-element.151.info, s32[2,8]{1,0:T(2,128)S(1)} %get-tuple-element.165.side, s32[2]{0:T(128)S(1)} %get-tuple-element.166.powers, f32[2,1024,256]{2,1,0:T(8,128)S(1)} %get-tuple-element.167.gap_ref, ...), custom_call_target="tpu_custom_call" | custom-call | flops 2147483648 | bytes 12582912 | tf_op jit(solution)/shard_map/cond/branch_1_fun/pallas_call | solution.py:21
  172.3 1.5 collective-permute-done.106.refs_1_
  174.1 1.7 collective-permute-start.108
  175.7 1.7 collective-permute-start.109
  177.4 2.6 %collective-permute-start.113 = (bf16[128,256]{1,0:T(8,128)(2,1)S(1)}, bf16[128,256]{1,0:T(8,128)(2,1)S(1)}, u32[]{:S(2)}, u32[]{:S(2)}) collective-permute-start(bf16[128,256]{1,0:T(8,128)(2,1)S(1)} %branch_1_fun.31.refs_3_.refs_0_), channel_id=1, source_target_pairs={{0,1},{1,0},{2,3},{3,2},{4,5},{5,4},{6,7},{7,6},{8,9},{9,8},{10,11... | collective-permute-start | bytes 196616 | tf_op jit(solution)/shard_map/cond/branch_1_fun/ppermute | solution.py:344
  181.1 3.3 %collective-permute-start.110 = (bf16[144,256]{1,0:T(8,128)(2,1)S(1)}, bf16[144,256]{1,0:T(8,128)(2,1)S(1)}, u32[]{:S(2)}, u32[]{:S(2)}) collective-permute-start(bf16[144,256]{1,0:T(8,128)(2,1)S(1)} %branch_1_fun.34.refs_0_), channel_id=1, source_target_pairs={{0,1},{1,0},{2,3},{3,2},{4,5},{5,4},{6,7},{7,6},{8,9},{9,8},{10,11... | collective-permute-start | bytes 221192 | tf_op jit(solution)/shard_map/cond/branch_1_fun/ppermute | solution.py:344
  184.3 2.4 %collective-permute-start.112 = (bf16[144,256]{1,0:T(8,128)(2,1)S(1)}, bf16[144,256]{1,0:T(8,128)(2,1)S(1)}, u32[]{:S(2)}, u32[]{:S(2)}) collective-permute-start(bf16[144,256]{1,0:T(8,128)(2,1)S(1)} %branch_1_fun.34.refs_0_), channel_id=1, source_target_pairs={{0,3},{1,2},{2,1},{3,0},{4,7},{5,6},{6,5},{7,4},{8,11},{9,10},{10,... | collective-permute-start | bytes 221192 | tf_op jit(solution)/shard_map/cond/branch_1_fun/ppermute | solution.py:344
  187.6 7.5 %collective-permute-done.114.refs_5_ = bf16[128,256]{1,0:T(8,128)(2,1)S(1)} collective-permute-done((bf16[128,256]{1,0:T(8,128)(2,1)S(1)}, bf16[128,256]{1,0:T(8,128)(2,1)S(1)}, u32[]{:S(2)}, u32[]{:S(2)}) %collective-permute-start.114) | collective-permute-done | bytes 65568 | tf_op jit(solution)/shard_map/cond/branch_1_fun/ppermute | solution.py:344
  196.9 1.9 collective-permute-start.120
  198.8 1.5 collective-permute-done.116.refs_2_
  203.6 2.4 %branch_1_fun.37 = (f32[2,1024,256]{2,1,0:T(8,128)}, f32[3,1024,256]{2,1,0:T(8,128)}) custom-call(s32[2]{0:T(128)S(1)} %get-tuple-element.151.info, f32[2,1024,256]{2,1,0:T(8,128)S(1)} %get-tuple-element.204.lam_ref, bf16[2,1024,256]{2,1,0:T(8,128)(2,1)S(1)} %get-tuple-element.228.dir_ref, ...), custom_call_target="tpu_custom_call", output_to_operand_aliasing={{1}: (13, {})} | custom-call | flops 3145728 | bytes 8388608 | tf_op jit(solution)/shard_map/cond/branch_1_fun/pallas_call | solution.py:21
  (163 shorter events, 43.8 us)
Async XLA Ops:
  6.3 8.7 %collective-permute-start.122 = (bf16[512,256]{1,0:T(8,128)(2,1)S(1)}, bf16[512,256]{1,0:T(8,128)(2,1)S(1)}, u32[]{:S(2)}, u32[]{:S(2)}) collective-permute-start(bf16[512,256]{1,0:T(8,128)(2,1)S(1)} %get-tuple-element.273), channel_id=1, source_target_pairs={{0,4},{4,0},{8,12},{12,8},{16,20},{20,16},{24,28},{28,24},{1,5},{5... | collective-permute-start | bytes 786440 | tf_op jit(solution)/shard_map/ppermute | solution.py:344
  6.8 5.8 %collective-permute-start.123 = (s32[2,8]{1,0:T(2,128)S(1)}, s32[2,8]{1,0:T(2,128)S(1)}, u32[]{:S(2)}, u32[]{:S(2)}) collective-permute-start(s32[2,8]{1,0:T(2,128)S(1)} %copy-done.5), channel_id=1, source_target_pairs={{0,28},{4,8},{8,4},{12,16},{16,12},{20,24},{24,20},{28,0},{1,29},{... | collective-permute-start | bytes 200 | tf_op jit(solution)/shard_map/ppermute | solution.py:401
  15.0 25.5 %collective-permute-start.126 = (bf16[2,1024,256]{2,1,0:T(8,128)(2,1)S(1)}, bf16[2,1024,256]{2,1,0:T(8,128)(2,1)S(1)}, u32[]{:S(2)}, u32[]{:S(2)}) collective-permute-start(bf16[2,1024,256]{2,1,0:T(8,128)(2,1)S(1)} %get-tuple-element.283.refs_3_.disp_ref), channel_id=1, source_target_pairs={{0,4},{4,0},{8,12},{12,8},{16,20},{20,16},{24,28},{28,24},{1,5},{5... | collective-permute-start | bytes 3145736 | tf_op jit(solution)/shard_map/ppermute | solution.py:344
  15.1 8.2 %collective-permute-start.131 = (bf16[128,256]{1,0:T(8,128)(2,1)S(1)}, bf16[128,256]{1,0:T(8,128)(2,1)S(1)}, u32[]{:S(2)}, u32[]{:S(2)}) collective-permute-start(bf16[128,256]{1,0:T(8,128)(2,1)S(1)} %get-tuple-element.289), channel_id=1, source_target_pairs={{0,8},{4,12},{8,0},{12,4},{16,24},{20,28},{24,16},{28,20},{1,9},{5... | collective-permute-start | bytes 196616 | tf_op jit(solution)/shard_map/ppermute | solution.py:344
  15.2 8.8 %collective-permute-start.132 = (bf16[128,256]{1,0:T(8,128)(2,1)S(1)}, bf16[128,256]{1,0:T(8,128)(2,1)S(1)}, u32[]{:S(2)}, u32[]{:S(2)}) collective-permute-start(bf16[128,256]{1,0:T(8,128)(2,1)S(1)} %get-tuple-element.290), channel_id=1, source_target_pairs={{0,16},{4,20},{8,24},{12,28},{16,0},{20,4},{24,8},{28,12},{1,17},{... | collective-permute-start | bytes 196616 | tf_op jit(solution)/shard_map/ppermute | solution.py:344
  16.4 7.7 %collective-permute-start.133 = (bf16[128,256]{1,0:T(8,128)(2,1)S(1)}, bf16[128,256]{1,0:T(8,128)(2,1)S(1)}, u32[]{:S(2)}, u32[]{:S(2)}) collective-permute-start(bf16[128,256]{1,0:T(8,128)(2,1)S(1)} %get-tuple-element.291), channel_id=1, source_target_pairs={{0,24},{4,28},{8,16},{12,20},{16,8},{20,12},{24,0},{28,4},{1,25},{... | collective-permute-start | bytes 196616 | tf_op jit(solution)/shard_map/ppermute | solution.py:344
  18.6 21.8 %collective-permute-start.127 = (bf16[6,128,256]{2,1,0:T(8,128)(2,1)S(1)}, bf16[6,128,256]{2,1,0:T(8,128)(2,1)S(1)}, u32[]{:S(2)}, u32[]{:S(2)}) collective-permute-start(bf16[6,128,256]{2,1,0:T(8,128)(2,1)S(1)} %get-tuple-element.284), channel_id=1, source_target_pairs={{0,1},{1,0},{2,3},{3,2},{4,5},{5,4},{6,7},{7,6},{8,9},{9,8},{10,11... | collective-permute-start | bytes 1179656 | tf_op jit(solution)/shard_map/ppermute | solution.py:456
  23.2 17.2 %collective-permute-start.128 = (bf16[6,128,256]{2,1,0:T(8,128)(2,1)S(1)}, bf16[6,128,256]{2,1,0:T(8,128)(2,1)S(1)}, u32[]{:S(2)}, u32[]{:S(2)}) collective-permute-start(bf16[6,128,256]{2,1,0:T(8,128)(2,1)S(1)} %get-tuple-element.285), channel_id=1, source_target_pairs={{1,2},{2,1},{5,6},{6,5},{9,10},{10,9},{13,14},{14,13},{17,18},{18,... | collective-permute-start | bytes 1179656 | tf_op jit(solution)/shard_map/ppermute | solution.py:457
  23.9 11.0 %collective-permute-start.129 = (bf16[5,128,256]{2,1,0:T(8,128)(2,1)S(1)}, bf16[5,128,256]{2,1,0:T(8,128)(2,1)S(1)}, u32[]{:S(2)}, u32[]{:S(2)}) collective-permute-start(bf16[5,128,256]{2,1,0:T(8,128)(2,1)S(1)} %get-tuple-element.286), channel_id=1, source_target_pairs={{0,28},{4,8},{8,4},{12,16},{16,12},{20,24},{24,20},{28,0},{1,29},{... | collective-permute-start | bytes 983048 | tf_op jit(solution)/shard_map/ppermute | solution.py:453
  24.0 16.4 %collective-permute-start.130 = (bf16[5,128,256]{2,1,0:T(8,128)(2,1)S(1)}, bf16[5,128,256]{2,1,0:T(8,128)(2,1)S(1)}, u32[]{:S(2)}, u32[]{:S(2)}) collective-permute-start(bf16[5,128,256]{2,1,0:T(8,128)(2,1)S(1)} %get-tuple-element.287), channel_id=1, source_target_pairs={{0,28},{4,8},{8,4},{12,16},{16,12},{20,24},{24,20},{28,0},{1,29},{... | collective-permute-start | bytes 983048 | tf_op jit(solution)/shard_map/ppermute | solution.py:455
  47.8 5.6 %collective-permute-start.135 = (bf16[144,256]{1,0:T(8,128)(2,1)S(1)}, bf16[144,256]{1,0:T(8,128)(2,1)S(1)}, u32[]{:S(2)}, u32[]{:S(2)}) collective-permute-start(bf16[144,256]{1,0:T(8,128)(2,1)S(1)} %get-tuple-element.295), channel_id=1, source_target_pairs={{0,8},{4,12},{8,0},{12,4},{16,24},{20,28},{24,16},{28,20},{1,9},{5... | collective-permute-start | bytes 221192 | tf_op jit(solution)/shard_map/ppermute | solution.py:344
  47.9 6.2 %collective-permute-start.136 = (bf16[144,256]{1,0:T(8,128)(2,1)S(1)}, bf16[144,256]{1,0:T(8,128)(2,1)S(1)}, u32[]{:S(2)}, u32[]{:S(2)}) collective-permute-start(bf16[144,256]{1,0:T(8,128)(2,1)S(1)} %get-tuple-element.296), channel_id=1, source_target_pairs={{0,16},{4,20},{8,24},{12,28},{16,0},{20,4},{24,8},{28,12},{1,17},{... | collective-permute-start | bytes 221192 | tf_op jit(solution)/shard_map/ppermute | solution.py:344
  48.0 6.1 %collective-permute-start.137 = (bf16[144,256]{1,0:T(8,128)(2,1)S(1)}, bf16[144,256]{1,0:T(8,128)(2,1)S(1)}, u32[]{:S(2)}, u32[]{:S(2)}) collective-permute-start(bf16[144,256]{1,0:T(8,128)(2,1)S(1)} %get-tuple-element.297), channel_id=1, source_target_pairs={{0,24},{4,28},{8,16},{12,20},{16,8},{20,12},{24,0},{28,4},{1,25},{... | collective-permute-start | bytes 221192 | tf_op jit(solution)/shard_map/ppermute | solution.py:344
  51.4 9.5 %collective-permute-start.141 = (bf16[128,256]{1,0:T(8,128)(2,1)S(1)}, bf16[128,256]{1,0:T(8,128)(2,1)S(1)}, u32[]{:S(2)}, u32[]{:S(2)}) collective-permute-start(bf16[128,256]{1,0:T(8,128)(2,1)S(1)} %shard_map.99.refs_3_.refs_0_), channel_id=1, source_target_pairs={{0,1},{1,0},{2,3},{3,2},{4,5},{5,4},{6,7},{7,6},{8,9},{9,8},{10,11... | collective-permute-start | bytes 196616 | tf_op jit(solution)/shard_map/ppermute | solution.py:344
  54.2 15.2 %collective-permute-start.138 = (bf16[144,256]{1,0:T(8,128)(2,1)S(1)}, bf16[144,256]{1,0:T(8,128)(2,1)S(1)}, u32[]{:S(2)}, u32[]{:S(2)}) collective-permute-start(bf16[144,256]{1,0:T(8,128)(2,1)S(1)} %shard_map.102.refs_0_), channel_id=1, source_target_pairs={{0,1},{1,0},{2,3},{3,2},{4,5},{5,4},{6,7},{7,6},{8,9},{9,8},{10,11... | collective-permute-start | bytes 221192 | tf_op jit(solution)/shard_map/ppermute | solution.py:344
  58.5 10.9 %collective-permute-start.139 = (bf16[144,256]{1,0:T(8,128)(2,1)S(1)}, bf16[144,256]{1,0:T(8,128)(2,1)S(1)}, u32[]{:S(2)}, u32[]{:S(2)}) collective-permute-start(bf16[144,256]{1,0:T(8,128)(2,1)S(1)} %shard_map.102.refs_0_), channel_id=1, source_target_pairs={{0,2},{1,3},{2,0},{3,1},{4,6},{5,7},{6,4},{7,5},{8,10},{9,11},{10,... | collective-permute-start | bytes 221192 | tf_op jit(solution)/shard_map/ppermute | solution.py:344
  58.5 10.9 %collective-permute-start.140 = (bf16[144,256]{1,0:T(8,128)(2,1)S(1)}, bf16[144,256]{1,0:T(8,128)(2,1)S(1)}, u32[]{:S(2)}, u32[]{:S(2)}) collective-permute-start(bf16[144,256]{1,0:T(8,128)(2,1)S(1)} %shard_map.102.refs_0_), channel_id=1, source_target_pairs={{0,3},{1,2},{2,1},{3,0},{4,7},{5,6},{6,5},{7,4},{8,11},{9,10},{10,... | collective-permute-start | bytes 221192 | tf_op jit(solution)/shard_map/ppermute | solution.py:344
  60.9 8.4 %collective-permute-start.142 = (bf16[128,256]{1,0:T(8,128)(2,1)S(1)}, bf16[128,256]{1,0:T(8,128)(2,1)S(1)}, u32[]{:S(2)}, u32[]{:S(2)}) collective-permute-start(bf16[128,256]{1,0:T(8,128)(2,1)S(1)} %shard_map.103.refs_4_), channel_id=1, source_target_pairs={{0,2},{1,3},{2,0},{3,1},{4,6},{5,7},{6,4},{7,5},{8,10},{9,11},{10,... | collective-permute-start | bytes 196616 | tf_op jit(solution)/shard_map/ppermute | solution.py:344
  70.6 5.2 %collective-permute-start.148 = (bf16[128,256]{1,0:T(8,128)(2,1)S(1)}, bf16[128,256]{1,0:T(8,128)(2,1)S(1)}, u32[]{:S(2)}, u32[]{:S(2)}) collective-permute-start(bf16[128,256]{1,0:T(8,128)(2,1)S(1)} %get-tuple-element.300), channel_id=1, source_target_pairs={{0,24},{4,28},{8,16},{12,20},{16,8},{20,12},{24,0},{28,4},{1,25},{... | collective-permute-start | bytes 196616 | tf_op jit(solution)/shard_map/ppermute | solution.py:344
  81.8 23.7 %collective-permute-start.73 = (bf16[2,1024,256]{2,1,0:T(8,128)(2,1)S(1)}, bf16[2,1024,256]{2,1,0:T(8,128)(2,1)S(1)}, u32[]{:S(2)}, u32[]{:S(2)}) collective-permute-start(bf16[2,1024,256]{2,1,0:T(8,128)(2,1)S(1)} %get-tuple-element.185.disp_ref), channel_id=1, source_target_pairs={{0,4},{4,0},{8,12},{12,8},{16,20},{20,16},{24,28},{28,24},{1,5},{5... | collective-permute-start | bytes 3145736 | tf_op jit(solution)/shard_map/cond/branch_1_fun/ppermute | solution.py:344
  84.9 5.2 %collective-permute-start.80 = (bf16[128,256]{1,0:T(8,128)(2,1)S(1)}, bf16[128,256]{1,0:T(8,128)(2,1)S(1)}, u32[]{:S(2)}, u32[]{:S(2)}) collective-permute-start(bf16[128,256]{1,0:T(8,128)(2,1)S(1)} %get-tuple-element.194), channel_id=1, source_target_pairs={{0,24},{4,28},{8,16},{12,20},{16,8},{20,12},{24,0},{28,4},{1,25},{... | collective-permute-start | bytes 196616 | tf_op jit(solution)/shard_map/cond/branch_1_fun/ppermute | solution.py:344
  85.4 20.0 %collective-permute-start.74 = (bf16[6,128,256]{2,1,0:T(8,128)(2,1)S(1)}, bf16[6,128,256]{2,1,0:T(8,128)(2,1)S(1)}, u32[]{:S(2)}, u32[]{:S(2)}) collective-permute-start(bf16[6,128,256]{2,1,0:T(8,128)(2,1)S(1)} %get-tuple-element.186), channel_id=1, source_target_pairs={{0,1},{1,0},{2,3},{3,2},{4,5},{5,4},{6,7},{7,6},{8,9},{9,8},{10,11... | collective-permute-start | bytes 1179656 | tf_op jit(solution)/shard_map/cond/branch_1_fun/ppermute | solution.py:456
  86.3 19.1 %collective-permute-start.75 = (bf16[6,128,256]{2,1,0:T(8,128)(2,1)S(1)}, bf16[6,128,256]{2,1,0:T(8,128)(2,1)S(1)}, u32[]{:S(2)}, u32[]{:S(2)}) collective-permute-start(bf16[6,128,256]{2,1,0:T(8,128)(2,1)S(1)} %get-tuple-element.187), channel_id=1, source_target_pairs={{1,2},{2,1},{5,6},{6,5},{9,10},{10,9},{13,14},{14,13},{17,18},{18,... | collective-permute-start | bytes 1179656 | tf_op jit(solution)/shard_map/cond/branch_1_fun/ppermute | solution.py:457
  87.6 10.9 %collective-permute-start.76 = (bf16[5,128,256]{2,1,0:T(8,128)(2,1)S(1)}, bf16[5,128,256]{2,1,0:T(8,128)(2,1)S(1)}, u32[]{:S(2)}, u32[]{:S(2)}) collective-permute-start(bf16[5,128,256]{2,1,0:T(8,128)(2,1)S(1)} %get-tuple-element.188), channel_id=1, source_target_pairs={{0,28},{4,8},{8,4},{12,16},{16,12},{20,24},{24,20},{28,0},{1,29},{... | collective-permute-start | bytes 983048 | tf_op jit(solution)/shard_map/cond/branch_1_fun/ppermute | solution.py:453
  90.0 15.4 %collective-permute-start.77 = (bf16[5,128,256]{2,1,0:T(8,128)(2,1)S(1)}, bf16[5,128,256]{2,1,0:T(8,128)(2,1)S(1)}, u32[]{:S(2)}, u32[]{:S(2)}) collective-permute-start(bf16[5,128,256]{2,1,0:T(8,128)(2,1)S(1)} %get-tuple-element.189), channel_id=1, source_target_pairs={{0,28},{4,8},{8,4},{12,16},{16,12},{20,24},{24,20},{28,0},{1,29},{... | collective-permute-start | bytes 983048 | tf_op jit(solution)/shard_map/cond/branch_1_fun/ppermute | solution.py:455
  111.3 5.2 %collective-permute-start.82 = (bf16[144,256]{1,0:T(8,128)(2,1)S(1)}, bf16[144,256]{1,0:T(8,128)(2,1)S(1)}, u32[]{:S(2)}, u32[]{:S(2)}) collective-permute-start(bf16[144,256]{1,0:T(8,128)(2,1)S(1)} %get-tuple-element.199), channel_id=1, source_target_pairs={{0,8},{4,12},{8,0},{12,4},{16,24},{20,28},{24,16},{28,20},{1,9},{5... | collective-permute-start | bytes 221192 | tf_op jit(solution)/shard_map/cond/branch_1_fun/ppermute | solution.py:344
  112.7 5.3 %collective-permute-start.84 = (bf16[144,256]{1,0:T(8,128)(2,1)S(1)}, bf16[144,256]{1,0:T(8,128)(2,1)S(1)}, u32[]{:S(2)}, u32[]{:S(2)}) collective-permute-start(bf16[144,256]{1,0:T(8,128)(2,1)S(1)} %get-tuple-element.201), channel_id=1, source_target_pairs={{0,24},{4,28},{8,16},{12,20},{16,8},{20,12},{24,0},{28,4},{1,25},{... | collective-permute-start | bytes 221192 | tf_op jit(solution)/shard_map/cond/branch_1_fun/ppermute | solution.py:344
  114.9 8.6 %collective-permute-start.88 = (bf16[128,256]{1,0:T(8,128)(2,1)S(1)}, bf16[128,256]{1,0:T(8,128)(2,1)S(1)}, u32[]{:S(2)}, u32[]{:S(2)}) collective-permute-start(bf16[128,256]{1,0:T(8,128)(2,1)S(1)} %branch_1_fun.22.refs_3_.refs_0_), channel_id=1, source_target_pairs={{0,1},{1,0},{2,3},{3,2},{4,5},{5,4},{6,7},{7,6},{8,9},{9,8},{10,11... | collective-permute-start | bytes 196616 | tf_op jit(solution)/shard_map/cond/branch_1_fun/ppermute | solution.py:344
  118.0 14.0 %collective-permute-start.85 = (bf16[144,256]{1,0:T(8,128)(2,1)S(1)}, bf16[144,256]{1,0:T(8,128)(2,1)S(1)}, u32[]{:S(2)}, u32[]{:S(2)}) collective-permute-start(bf16[144,256]{1,0:T(8,128)(2,1)S(1)} %branch_1_fun.25.refs_0_), channel_id=1, source_target_pairs={{0,1},{1,0},{2,3},{3,2},{4,5},{5,4},{6,7},{7,6},{8,9},{9,8},{10,11... | collective-permute-start | bytes 221192 | tf_op jit(solution)/shard_map/cond/branch_1_fun/ppermute | solution.py:344
  121.0 11.1 %collective-permute-start.86 = (bf16[144,256]{1,0:T(8,128)(2,1)S(1)}, bf16[144,256]{1,0:T(8,128)(2,1)S(1)}, u32[]{:S(2)}, u32[]{:S(2)}) collective-permute-start(bf16[144,256]{1,0:T(8,128)(2,1)S(1)} %branch_1_fun.25.refs_0_), channel_id=1, source_target_pairs={{0,2},{1,3},{2,0},{3,1},{4,6},{5,7},{6,4},{7,5},{8,10},{9,11},{10,... | collective-permute-start | bytes 221192 | tf_op jit(solution)/shard_map/cond/branch_1_fun/ppermute | solution.py:344
  121.5 10.5 %collective-permute-start.87 = (bf16[144,256]{1,0:T(8,128)(2,1)S(1)}, bf16[144,256]{1,0:T(8,128)(2,1)S(1)}, u32[]{:S(2)}, u32[]{:S(2)}) collective-permute-start(bf16[144,256]{1,0:T(8,128)(2,1)S(1)} %branch_1_fun.25.refs_0_), channel_id=1, source_target_pairs={{0,3},{1,2},{2,1},{3,0},{4,7},{5,6},{6,5},{7,4},{8,11},{9,10},{10,... | collective-permute-start | bytes 221192 | tf_op jit(solution)/shard_map/cond/branch_1_fun/ppermute | solution.py:344
  123.4 8.6 %collective-permute-start.89 = (bf16[128,256]{1,0:T(8,128)(2,1)S(1)}, bf16[128,256]{1,0:T(8,128)(2,1)S(1)}, u32[]{:S(2)}, u32[]{:S(2)}) collective-permute-start(bf16[128,256]{1,0:T(8,128)(2,1)S(1)} %branch_1_fun.26.refs_4_), channel_id=1, source_target_pairs={{0,2},{1,3},{2,0},{3,1},{4,6},{5,7},{6,4},{7,5},{8,10},{9,11},{10,... | collective-permute-start | bytes 196616 | tf_op jit(solution)/shard_map/cond/branch_1_fun/ppermute | solution.py:344
  133.9 5.2 %collective-permute-start.95 = (bf16[128,256]{1,0:T(8,128)(2,1)S(1)}, bf16[128,256]{1,0:T(8,128)(2,1)S(1)}, u32[]{:S(2)}, u32[]{:S(2)}) collective-permute-start(bf16[128,256]{1,0:T(8,128)(2,1)S(1)} %get-tuple-element.203.refs_0_), channel_id=1, source_target_pairs={{0,24},{4,28},{8,16},{12,20},{16,8},{20,12},{24,0},{28,4},{1,25},{... | collective-permute-start | bytes 196616 | tf_op jit(solution)/shard_map/cond/branch_1_fun/ppermute | solution.py:344
  144.5 23.5 %collective-permute-start.98 = (bf16[2,1024,256]{2,1,0:T(8,128)(2,1)S(1)}, bf16[2,1024,256]{2,1,0:T(8,128)(2,1)S(1)}, u32[]{:S(2)}, u32[]{:S(2)}) collective-permute-start(bf16[2,1024,256]{2,1,0:T(8,128)(2,1)S(1)} %get-tuple-element.219.disp_ref), channel_id=1, source_target_pairs={{0,4},{4,0},{8,12},{12,8},{16,20},{20,16},{24,28},{28,24},{1,5},{5... | collective-permute-start | bytes 3145736 | tf_op jit(solution)/shard_map/cond/branch_1_fun/ppermute | solution.py:344
  147.2 5.2 %collective-permute-start.105 = (bf16[128,256]{1,0:T(8,128)(2,1)S(1)}, bf16[128,256]{1,0:T(8,128)(2,1)S(1)}, u32[]{:S(2)}, u32[]{:S(2)}) collective-permute-start(bf16[128,256]{1,0:T(8,128)(2,1)S(1)} %get-tuple-element.227), channel_id=1, source_target_pairs={{0,24},{4,28},{8,16},{12,20},{16,8},{20,12},{24,0},{28,4},{1,25},{... | collective-permute-start | bytes 196616 | tf_op jit(solution)/shard_map/cond/branch_1_fun/ppermute | solution.py:344
  148.4 19.6 %collective-permute-start.99 = (bf16[6,128,256]{2,1,0:T(8,128)(2,1)S(1)}, bf16[6,128,256]{2,1,0:T(8,128)(2,1)S(1)}, u32[]{:S(2)}, u32[]{:S(2)}) collective-permute-start(bf16[6,128,256]{2,1,0:T(8,128)(2,1)S(1)} %get-tuple-element.220), channel_id=1, source_target_pairs={{0,1},{1,0},{2,3},{3,2},{4,5},{5,4},{6,7},{7,6},{8,9},{9,8},{10,11... | collective-permute-start | bytes 1179656 | tf_op jit(solution)/shard_map/cond/branch_1_fun/ppermute | solution.py:456
  149.2 18.8 %collective-permute-start.100 = (bf16[6,128,256]{2,1,0:T(8,128)(2,1)S(1)}, bf16[6,128,256]{2,1,0:T(8,128)(2,1)S(1)}, u32[]{:S(2)}, u32[]{:S(2)}) collective-permute-start(bf16[6,128,256]{2,1,0:T(8,128)(2,1)S(1)} %get-tuple-element.221), channel_id=1, source_target_pairs={{1,2},{2,1},{5,6},{6,5},{9,10},{10,9},{13,14},{14,13},{17,18},{18,... | collective-permute-start | bytes 1179656 | tf_op jit(solution)/shard_map/cond/branch_1_fun/ppermute | solution.py:457
  150.2 10.8 %collective-permute-start.101 = (bf16[5,128,256]{2,1,0:T(8,128)(2,1)S(1)}, bf16[5,128,256]{2,1,0:T(8,128)(2,1)S(1)}, u32[]{:S(2)}, u32[]{:S(2)}) collective-permute-start(bf16[5,128,256]{2,1,0:T(8,128)(2,1)S(1)} %get-tuple-element.222), channel_id=1, source_target_pairs={{0,28},{4,8},{8,4},{12,16},{16,12},{20,24},{24,20},{28,0},{1,29},{... | collective-permute-start | bytes 983048 | tf_op jit(solution)/shard_map/cond/branch_1_fun/ppermute | solution.py:453
  152.4 15.6 %collective-permute-start.102 = (bf16[5,128,256]{2,1,0:T(8,128)(2,1)S(1)}, bf16[5,128,256]{2,1,0:T(8,128)(2,1)S(1)}, u32[]{:S(2)}, u32[]{:S(2)}) collective-permute-start(bf16[5,128,256]{2,1,0:T(8,128)(2,1)S(1)} %get-tuple-element.223), channel_id=1, source_target_pairs={{0,28},{4,8},{8,4},{12,16},{16,12},{20,24},{24,20},{28,0},{1,29},{... | collective-permute-start | bytes 983048 | tf_op jit(solution)/shard_map/cond/branch_1_fun/ppermute | solution.py:455
  173.9 6.1 %collective-permute-start.107 = (bf16[144,256]{1,0:T(8,128)(2,1)S(1)}, bf16[144,256]{1,0:T(8,128)(2,1)S(1)}, u32[]{:S(2)}, u32[]{:S(2)}) collective-permute-start(bf16[144,256]{1,0:T(8,128)(2,1)S(1)} %get-tuple-element.232), channel_id=1, source_target_pairs={{0,8},{4,12},{8,0},{12,4},{16,24},{20,28},{24,16},{28,20},{1,9},{5... | collective-permute-start | bytes 221192 | tf_op jit(solution)/shard_map/cond/branch_1_fun/ppermute | solution.py:344
  174.1 6.0 %collective-permute-start.108 = (bf16[144,256]{1,0:T(8,128)(2,1)S(1)}, bf16[144,256]{1,0:T(8,128)(2,1)S(1)}, u32[]{:S(2)}, u32[]{:S(2)}) collective-permute-start(bf16[144,256]{1,0:T(8,128)(2,1)S(1)} %get-tuple-element.233), channel_id=1, source_target_pairs={{0,16},{4,20},{8,24},{12,28},{16,0},{20,4},{24,8},{28,12},{1,17},{... | collective-permute-start | bytes 221192 | tf_op jit(solution)/shard_map/cond/branch_1_fun/ppermute | solution.py:344
  175.7 5.3 %collective-permute-start.109 = (bf16[144,256]{1,0:T(8,128)(2,1)S(1)}, bf16[144,256]{1,0:T(8,128)(2,1)S(1)}, u32[]{:S(2)}, u32[]{:S(2)}) collective-permute-start(bf16[144,256]{1,0:T(8,128)(2,1)S(1)} %get-tuple-element.234), channel_id=1, source_target_pairs={{0,24},{4,28},{8,16},{12,20},{16,8},{20,12},{24,0},{28,4},{1,25},{... | collective-permute-start | bytes 221192 | tf_op jit(solution)/shard_map/cond/branch_1_fun/ppermute | solution.py:344
  177.4 9.4 %collective-permute-start.113 = (bf16[128,256]{1,0:T(8,128)(2,1)S(1)}, bf16[128,256]{1,0:T(8,128)(2,1)S(1)}, u32[]{:S(2)}, u32[]{:S(2)}) collective-permute-start(bf16[128,256]{1,0:T(8,128)(2,1)S(1)} %branch_1_fun.31.refs_3_.refs_0_), channel_id=1, source_target_pairs={{0,1},{1,0},{2,3},{3,2},{4,5},{5,4},{6,7},{7,6},{8,9},{9,8},{10,11... | collective-permute-start | bytes 196616 | tf_op jit(solution)/shard_map/cond/branch_1_fun/ppermute | solution.py:344
  181.1 14.1 %collective-permute-start.110 = (bf16[144,256]{1,0:T(8,128)(2,1)S(1)}, bf16[144,256]{1,0:T(8,128)(2,1)S(1)}, u32[]{:S(2)}, u32[]{:S(2)}) collective-permute-start(bf16[144,256]{1,0:T(8,128)(2,1)S(1)} %branch_1_fun.34.refs_0_), channel_id=1, source_target_pairs={{0,1},{1,0},{2,3},{3,2},{4,5},{5,4},{6,7},{7,6},{8,9},{9,8},{10,11... | collective-permute-start | bytes 221192 | tf_op jit(solution)/shard_map/cond/branch_1_fun/ppermute | solution.py:344
  184.3 10.8 %collective-permute-start.111 = (bf16[144,256]{1,0:T(8,128)(2,1)S(1)}, bf16[144,256]{1,0:T(8,128)(2,1)S(1)}, u32[]{:S(2)}, u32[]{:S(2)}) collective-permute-start(bf16[144,256]{1,0:T(8,128)(2,1)S(1)} %branch_1_fun.34.refs_0_), channel_id=1, source_target_pairs={{0,2},{1,3},{2,0},{3,1},{4,6},{5,7},{6,4},{7,5},{8,10},{9,11},{10,... | collective-permute-start | bytes 221192 | tf_op jit(solution)/shard_map/cond/branch_1_fun/ppermute | solution.py:344
  184.3 10.8 %collective-permute-start.112 = (bf16[144,256]{1,0:T(8,128)(2,1)S(1)}, bf16[144,256]{1,0:T(8,128)(2,1)S(1)}, u32[]{:S(2)}, u32[]{:S(2)}) collective-permute-start(bf16[144,256]{1,0:T(8,128)(2,1)S(1)} %branch_1_fun.34.refs_0_), channel_id=1, source_target_pairs={{0,3},{1,2},{2,1},{3,0},{4,7},{5,6},{6,5},{7,4},{8,11},{9,10},{10,... | collective-permute-start | bytes 221192 | tf_op jit(solution)/shard_map/cond/branch_1_fun/ppermute | solution.py:344
  186.8 8.3 %collective-permute-start.114 = (bf16[128,256]{1,0:T(8,128)(2,1)S(1)}, bf16[128,256]{1,0:T(8,128)(2,1)S(1)}, u32[]{:S(2)}, u32[]{:S(2)}) collective-permute-start(bf16[128,256]{1,0:T(8,128)(2,1)S(1)} %branch_1_fun.35.refs_4_), channel_id=1, source_target_pairs={{0,2},{1,3},{2,0},{3,1},{4,6},{5,7},{6,4},{7,5},{8,10},{9,11},{10,... | collective-permute-start | bytes 196616 | tf_op jit(solution)/shard_map/cond/branch_1_fun/ppermute | solution.py:344
  196.9 5.2 %collective-permute-start.120 = (bf16[128,256]{1,0:T(8,128)(2,1)S(1)}, bf16[128,256]{1,0:T(8,128)(2,1)S(1)}, u32[]{:S(2)}, u32[]{:S(2)}) collective-permute-start(bf16[128,256]{1,0:T(8,128)(2,1)S(1)} %get-tuple-element.236.refs_0_), channel_id=1, source_target_pairs={{0,24},{4,28},{8,16},{12,20},{16,8},{20,12},{24,0},{28,4},{1,25},{... | collective-permute-start | bytes 196616 | tf_op jit(solution)/shard_map/cond/branch_1_fun/ppermute | solution.py:344
  (38 other events, 371.2 us)
